TPU v7x, 32 devices: a whole 2x2x4 slice. The times are simulated.
32 devices in a mesh: expert: 8 (over z, x), context: 2 (over core), dp: 2 (over y).
Axes of the slice: x: 2, y: 2, z: 4, core: 2. Of those that a mesh axis runs over, the one named last changes fastest.
Arguments:
- tokens: bfloat16 [2, 16, 768, 1024], P(None, ('expert', 'dp'), 'context'), may hold values from -6 to 6
- out_grad: bfloat16 [2, 16, 768, 1024], P(None, ('expert', 'dp'), 'context'), may hold values from -6 to 6
- seq_lengths: int32 [2, 16, 3], P(None, ('expert', 'dp')), may hold values from 1 to 512, 768 in all within a row
- token_order: int32 [2, 16, 768], P(None, ('expert', 'dp')), may hold values from 0 to 767, each once within a row
- expert_route: int32 [2, 16, 768, 1], P(None, ('expert', 'dp'), 'context'), may hold values from 0 to 7; in each aligned block of 384 rows (0 to 383, 384 to 767, ..., all dimensions but the last counted through in order) at most 54 rows name the same one
- mixer_gain: float32 [1024], replicated, may hold values from 0.1 to 1.9
- mixer_shift: float32 [1024], replicated, may hold values from -4 to 4
- project_in: bfloat16 [1024, 3072], replicated, may hold values from -0.25 to 0.25
- project_out: bfloat16 [1024, 1024], replicated, may hold values from -1 to 1
- expert_gain: float32 [1024], replicated, may hold values from 0.1 to 1.9
- expert_shift: float32 [1024], replicated, may hold values from -4 to 4
- router_weight: bfloat16 [1024, 8], replicated, may hold values from -0.09375 to 0.09375
- expert_in: bfloat16 [8, 1024, 4096], P('expert', ('context', 'dp')), may hold values from -0.1875 to 0.1875
- expert_out: bfloat16 [8, 4096, 1024], P('expert', ('context', 'dp')), may hold values from -0.75 to 0.75
Outputs:
- block_out: bfloat16 [2, 16, 768, 1024], P(None, ('expert', 'dp'), 'context')
- grad_tokens: float32 [2, 16, 768, 1024], P(None, ('expert', 'dp'), 'context')
- grad_mixer_gain: float32 [1024], replicated
- grad_mixer_shift: float32 [1024], replicated
- grad_project_in: float32 [1024, 3072], replicated
- grad_project_out: float32 [1024, 1024], replicated
- grad_expert_gain: float32 [1024], replicated
- grad_expert_shift: float32 [1024], replicated
- grad_router: float32 [1024, 8], replicated
- grad_expert_in: float32 [8, 1024, 4096], P('expert', ('context', 'dp'))
- grad_expert_out: float32 [8, 4096, 1024], P('expert', ('context', 'dp'))
Inputs may be any that keep to these rules, and one draw needn't show every extreme that they name: `seq_lengths`: each pack's lengths add up to 768 and the longest is 512. `token_order`: each pack's rows hold each of its 768 positions once. `expert_route`: among the 384 rows of one device in one micro-batch (aligned blocks), at most 54 route to one expert.
All inputs are finite; a program needn't handle non-finite values.
Results may differ from a plain program's by a relative error of at most 0.022.
Values may be sent and summed in bfloat16 or wider, within the bound.
No kernel may reach another device: no remote copies, remote signals or barrier semaphores. Data moves between devices by JAX's collectives and lax.ppermute only.
A program may use at most 320 MiB of HBM per device.

v0:
```python
from functools import partial
import math

import jax
import jax.numpy as jnp
from jax import lax
from jax.sharding import PartitionSpec as P

HEADS = 16
HEAD_DIM = 64


EPS = 1e-05
MASKED = -1e30
HIGH = lax.Precision.HIGHEST


def layer_norm(values, gain, shift):
    center = values - jnp.mean(values, axis=-1, keepdims=True)
    scale = lax.rsqrt(jnp.mean(center * center, axis=-1, keepdims=True) + EPS)
    normal = center * scale
    return (normal * gain + shift, normal, scale)


def norm_back(grad, normal, scale, gain):
    scaled = grad * gain
    inner = (
        scaled
        - jnp.mean(scaled, axis=-1, keepdims=True)
        - normal * jnp.mean(scaled * normal, axis=-1, keepdims=True)
    )
    return (inner * scale, jnp.sum(grad * normal, axis=0), jnp.sum(grad, axis=0))


def split_heads(values):
    return values.reshape(values.shape[0], HEADS, HEAD_DIM)


def allowed_mask(query_positions, query_segments, key_positions, key_segments):
    return (key_positions[None, :] <= query_positions[:, None]) & (
        key_segments[None, :] == query_segments[:, None]
    )


def fold_keys(
    carry, piece, start, query, query_positions, query_segments, all_positions, all_segments
):
    running, total, weighted = carry
    keys, values = piece
    count = keys.shape[0]
    width = math.gcd(count, 512)
    for offset in range(0, count, width):
        key_block = split_heads(keys[offset : offset + width])
        value_block = split_heads(values[offset : offset + width])
        key_positions = lax.dynamic_slice_in_dim(all_positions, offset, width)
        key_segments = lax.dynamic_slice_in_dim(all_segments, offset, width)
        allowed = allowed_mask(query_positions, query_segments, key_positions, key_segments)[None]
        scores = (
            jnp.einsum("qhd,khd->hqk", query, key_block, preferred_element_type=jnp.float32) * 0.125
        )
        scores = jnp.where(allowed, scores, MASKED)
        new_top = jnp.maximum(running, jnp.max(scores, axis=-1))
        factor = jnp.exp(running - new_top)
        weights = jnp.where(allowed, jnp.exp(scores - new_top[..., None]), 0.0)
        total = total * factor + jnp.sum(weights, axis=-1)
        weighted = weighted * factor[..., None] + jnp.einsum(
            "hqk,khd->hqd",
            weights.astype(jnp.bfloat16),
            value_block,
            preferred_element_type=jnp.float32,
        )
        running = new_top
    return (running, total, weighted)


def attend_back(
    query,
    keys_all,
    values_all,
    mixed_grad,
    delta,
    log_total,
    query_positions,
    query_segments,
    all_positions,
    all_segments,
):
    count = keys_all.shape[0]
    width = math.gcd(count, 512)
    query_grad = jnp.zeros(query.shape, jnp.float32)
    key_parts = []
    value_parts = []
    for offset in range(0, count, width):
        key_block = split_heads(keys_all[offset : offset + width])
        value_block = split_heads(values_all[offset : offset + width])
        key_positions = all_positions[offset : offset + width]
        key_segments = all_segments[offset : offset + width]
        allowed = allowed_mask(query_positions, query_segments, key_positions, key_segments)[None]
        scores = (
            jnp.einsum("qhd,khd->hqk", query, key_block, preferred_element_type=jnp.float32) * 0.125
        )
        scores = jnp.where(allowed, scores, MASKED)
        probs_block = jnp.where(allowed, jnp.exp(scores - log_total[..., None]), 0.0)
        value_parts.append(
            jnp.einsum(
                "hqk,qhd->khd",
                probs_block.astype(jnp.bfloat16),
                mixed_grad,
                preferred_element_type=jnp.float32,
            )
        )
        prob_grad = jnp.einsum(
            "qhd,khd->hqk", mixed_grad, value_block, preferred_element_type=jnp.float32
        )
        score_low = (probs_block * (prob_grad - delta[..., None])).astype(jnp.bfloat16)
        query_grad = (
            query_grad
            + jnp.einsum("hqk,khd->qhd", score_low, key_block, preferred_element_type=jnp.float32)
            * 0.125
        )
        key_parts.append(
            jnp.einsum("hqk,qhd->khd", score_low, query, preferred_element_type=jnp.float32) * 0.125
        )
    model = keys_all.shape[1]
    key_grad = jnp.concatenate(key_parts, axis=0).reshape(count, model)
    value_grad = jnp.concatenate(value_parts, axis=0).reshape(count, model)
    return (query_grad, key_grad, value_grad)


def reduce_grads(dense, expert):
    dense = lax.psum(dense, ("expert", "context", "dp"))
    expert = (
        lax.psum_scatter(
            expert[0].astype(jnp.bfloat16), ("context", "dp"), scatter_dimension=1, tiled=True
        ).astype(jnp.float32),
        lax.psum_scatter(
            expert[1].astype(jnp.bfloat16), ("context", "dp"), scatter_dimension=1, tiled=True
        ).astype(jnp.float32),
    )
    return (dense, expert)


def add_trees(first, second):
    return jax.tree.map(jnp.add, first, second)


def local(
    tokens,
    out_grad,
    seq_lengths,
    token_order,
    expert_route,
    mixer_gain,
    mixer_shift,
    project_in,
    project_out,
    expert_gain,
    expert_shift,
    router_weight,
    expert_in,
    expert_out,
):
    micro = tokens.shape[0]
    rows = tokens.shape[2]
    model = tokens.shape[3]
    place_index = lax.axis_index("context")
    experts = expert_in.shape[0] * lax.axis_size("expert")
    capacity = 9 * rows // (8 * experts)
    full_in, full_out = (
        lax.all_gather(expert_in, ("context", "dp"), axis=1, tiled=True),
        lax.all_gather(expert_out, ("context", "dp"), axis=1, tiled=True),
    )
    router_float = router_weight.astype(jnp.float32)
    expert_ids = jnp.arange(experts, dtype=jnp.int32)
    slot_ids = jnp.arange(experts * capacity, dtype=jnp.int32)
    outputs = []
    input_grads = []
    running_sum = None
    for micro_index in range(micro):
        inputs = tokens[micro_index, 0].astype(jnp.float32)
        grad_out = out_grad[micro_index, 0].astype(jnp.float32)
        all_positions = token_order[micro_index, 0]
        ends = jnp.cumsum(seq_lengths[micro_index, 0])
        all_segments = jnp.sum((all_positions[:, None] >= ends[None, :]).astype(jnp.int32), axis=1)
        query_positions = lax.dynamic_slice_in_dim(all_positions, place_index * rows, rows)
        query_segments = lax.dynamic_slice_in_dim(all_segments, place_index * rows, rows)
        normed, normal_one, scale_one = layer_norm(inputs, mixer_gain, mixer_shift)
        normed_low = normed.astype(jnp.bfloat16)
        joined = jnp.dot(normed_low, project_in, preferred_element_type=jnp.float32).astype(
            jnp.bfloat16
        )
        query = split_heads(joined[:, :model])
        keys = joined[:, model : 2 * model]
        values = joined[:, 2 * model :]
        start_carry = (
            jnp.full((HEADS, rows), MASKED, jnp.float32),
            jnp.zeros((HEADS, rows), jnp.float32),
            jnp.zeros((HEADS, rows, HEAD_DIM), jnp.float32),
        )
        folder = partial(
            fold_keys,
            query=query,
            query_positions=query_positions,
            query_segments=query_segments,
            all_positions=all_positions,
            all_segments=all_segments,
        )
        running, total, weighted = folder(
            start_carry,
            (
                lax.all_gather(keys, "context", axis=0, tiled=True),
                lax.all_gather(values, "context", axis=0, tiled=True),
            ),
            jnp.int32(0),
        )
        attended = jnp.transpose(weighted / total[..., None], (1, 0, 2))
        log_total = running + jnp.log(total)
        mixed_low = attended.reshape(rows, model).astype(jnp.bfloat16)
        middle = inputs + jnp.dot(mixed_low, project_out, preferred_element_type=jnp.float32)
        second, normal_two, scale_two = layer_norm(middle, expert_gain, expert_shift)
        second_low = second.astype(jnp.bfloat16)
        shares = jax.nn.softmax(
            jnp.dot(second_low, router_weight, preferred_element_type=jnp.float32), axis=-1
        )
        route = expert_route[micro_index, 0, :, 0]
        choose_int = (route[:, None] == expert_ids[None, :]).astype(jnp.int32)
        choose_float = choose_int.astype(jnp.float32)
        gate = jnp.sum(shares * choose_float, axis=1)
        earlier = jnp.cumsum(choose_int, axis=0) - choose_int
        target = route * capacity + jnp.sum(earlier * choose_int, axis=1)
        place = (target[None, :] == slot_ids[:, None]).astype(jnp.bfloat16)
        sent = (
            jnp.dot(place, second_low, preferred_element_type=jnp.float32)
            .astype(jnp.bfloat16)
            .reshape(experts, capacity, model)
        )
        received = lax.all_to_all(sent, "expert", split_axis=0, concat_axis=1, tiled=True)
        inner = jnp.einsum("erd,edf->erf", received, full_in, preferred_element_type=jnp.float32)
        active = jax.nn.gelu(inner, approximate=True).astype(jnp.bfloat16)
        result = jnp.einsum(
            "erf,efd->erd", active, full_out, preferred_element_type=jnp.float32
        ).astype(jnp.bfloat16)
        returned = lax.all_to_all(result, "expert", split_axis=1, concat_axis=0, tiled=True)
        picked = jnp.einsum(
            "jt,jd->td",
            place,
            returned.reshape(experts * capacity, model),
            preferred_element_type=jnp.float32,
        )
        outputs.append((middle + gate[:, None] * picked).astype(jnp.bfloat16))
        gate_grad = jnp.sum(grad_out * picked, axis=1)
        result_grad = (gate[:, None] * grad_out).astype(jnp.bfloat16)
        sent_grad = (
            jnp.dot(place, result_grad, preferred_element_type=jnp.float32)
            .astype(jnp.bfloat16)
            .reshape(experts, capacity, model)
        )
        received_grad = lax.all_to_all(sent_grad, "expert", split_axis=0, concat_axis=1, tiled=True)
        active_grad = jnp.einsum(
            "erd,efd->erf", received_grad, full_out, preferred_element_type=jnp.float32
        )
        out_term = jnp.einsum(
            "erf,erd->efd", active, received_grad, preferred_element_type=jnp.float32
        )
        gelu_pull = jax.vjp(partial(jax.nn.gelu, approximate=True), inner)[1]
        inner_grad = gelu_pull(active_grad)[0].astype(jnp.bfloat16)
        in_term = jnp.einsum(
            "erd,erf->edf", received, inner_grad, preferred_element_type=jnp.float32
        )
        row_grad = jnp.einsum(
            "erf,edf->erd", inner_grad, full_in, preferred_element_type=jnp.float32
        ).astype(jnp.bfloat16)
        returned_grad = lax.all_to_all(row_grad, "expert", split_axis=1, concat_axis=0, tiled=True)
        logit_grad = gate_grad[:, None] * gate[:, None] * (choose_float - shares)
        router_term = jnp.einsum(
            "td,te->de", second_low.astype(jnp.float32), logit_grad, precision=HIGH
        )
        second_grad = jnp.einsum("te,de->td", logit_grad, router_float, precision=HIGH)
        second_grad = second_grad + jnp.einsum(
            "jt,jd->td",
            place,
            returned_grad.reshape(experts * capacity, model),
            preferred_element_type=jnp.float32,
        )
        middle_part, gain_two_grad, shift_two_grad = norm_back(
            second_grad, normal_two, scale_two, expert_gain
        )
        middle_grad = grad_out + middle_part
        branch_grad = middle_grad.astype(jnp.bfloat16)
        project_out_term = jnp.einsum(
            "td,te->de", mixed_low, branch_grad, preferred_element_type=jnp.float32
        )
        mixed_grad = split_heads(
            jnp.einsum(
                "te,de->td", branch_grad, project_out, preferred_element_type=jnp.float32
            ).astype(jnp.bfloat16)
        )
        delta = jnp.einsum("qhd,qhd->hq", mixed_grad.astype(jnp.float32), attended)
        keys_all, values_all = (
            lax.all_gather(keys, "context", axis=0, tiled=True),
            lax.all_gather(values, "context", axis=0, tiled=True),
        )
        query_grad, key_grad, value_grad = attend_back(
            query,
            keys_all,
            values_all,
            mixed_grad,
            delta,
            log_total,
            query_positions,
            query_segments,
            all_positions,
            all_segments,
        )
        key_own, value_own = (
            lax.psum_scatter(
                key_grad.astype(jnp.bfloat16), "context", scatter_dimension=0, tiled=True
            ).astype(jnp.float32),
            lax.psum_scatter(
                value_grad.astype(jnp.bfloat16), "context", scatter_dimension=0, tiled=True
            ).astype(jnp.float32),
        )
        joined_grad = jnp.concatenate(
            [query_grad.reshape(rows, model), key_own, value_own], axis=1
        ).astype(jnp.bfloat16)
        project_in_term = jnp.einsum(
            "td,te->de", normed_low, joined_grad, preferred_element_type=jnp.float32
        )
        normed_grad = jnp.einsum(
            "te,de->td", joined_grad, project_in, preferred_element_type=jnp.float32
        )
        input_part, gain_one_grad, shift_one_grad = norm_back(
            normed_grad, normal_one, scale_one, mixer_gain
        )
        input_grads.append(middle_grad + input_part)
        dense_term = (
            gain_one_grad,
            shift_one_grad,
            project_in_term,
            project_out_term,
            gain_two_grad,
            shift_two_grad,
            router_term,
        )
        expert_term = (in_term, out_term)
        latest = (dense_term, expert_term)
        running_sum = latest if running_sum is None else add_trees(running_sum, latest)
    dense_total, expert_total = running_sum
    dense_total, expert_total = reduce_grads(dense_total, expert_total)
    block_out = jnp.stack(outputs)[:, None]
    grad_tokens = jnp.stack(input_grads)[:, None]
    return (
        block_out,
        grad_tokens,
        dense_total[0],
        dense_total[1],
        dense_total[2],
        dense_total[3],
        dense_total[4],
        dense_total[5],
        dense_total[6],
        expert_total[0],
        expert_total[1],
    )


def solution(mesh):
    in_specs = (
        P(None, ("expert", "dp"), "context", None),
        P(None, ("expert", "dp"), "context", None),
        P(None, ("expert", "dp"), None),
        P(None, ("expert", "dp"), None),
        P(None, ("expert", "dp"), "context", None),
        P(),
        P(),
        P(),
        P(),
        P(),
        P(),
        P(),
        P("expert", ("context", "dp"), None),
        P("expert", ("context", "dp"), None),
    )
    out_specs = (
        P(None, ("expert", "dp"), "context", None),
        P(None, ("expert", "dp"), "context", None),
        P(),
        P(),
        P(),
        P(),
        P(),
        P(),
        P(),
        P("expert", ("context", "dp"), None),
        P("expert", ("context", "dp"), None),
    )
    return jax.shard_map(local, mesh=mesh, in_specs=in_specs, out_specs=out_specs, check_vma=False)
```

profile of v0, /device:TPU:0, one launch (start us, length us, event | category | flops | bytes accessed | tf_op | source)
XLA Modules:
  0.0 992.5 jit_solution(6699218476504335465)
XLA Ops:
  11.0 5.8 convolution_convert_fusion.1
  19.2 5.8 convolution_convert_fusion
  52.5 4.2 fusion.51
  56.7 3.8 fusion.50
  65.3 4.9 fusion.34
  70.3 5.7 fusion.64
  76.2 5.3 fusion.32
  81.6 7.3 fusion.361
  120.6 3.3 fusion.363
  131.5 7.0 all-to-all-start.6
  142.6 19.5 %all-to-all-done.6 = bf16[8,54,1024]{2,1,0:T(8,128)(2,1)} async-done(((bf16[8,54,1024]{2,1,0:T(8,128)(2,1)}), bf16[8,54,1024]{2,1,0:T(8,128)(2,1)}, u32[]{:S(2)}, u32[]{:S(2)}) %all-to-all-start.6) | async-done | bytes 884768 | tf_op jit(solution)/shard_map/all_to_all | solution.py:258
  162.1 4.4 all-to-all-start.2
  173.3 16.1 %all-to-all-done.2 = bf16[8,54,1024]{2,1,0:T(8,128)(2,1)} async-done(((bf16[8,54,1024]{2,1,0:T(8,128)(2,1)}), bf16[8,54,1024]{2,1,0:T(8,128)(2,1)}, u32[]{:S(2)}, u32[]{:S(2)}) %all-to-all-start.2) | async-done | bytes 884768 | tf_op jit(solution)/shard_map/all_to_all | solution.py:237
  189.4 4.2 all-to-all-start.4
  197.5 18.7 %all-to-all-done.4 = bf16[8,54,1024]{2,1,0:T(8,128)(2,1)} async-done(((bf16[8,54,1024]{2,1,0:T(8,128)(2,1)}), bf16[8,54,1024]{2,1,0:T(8,128)(2,1)}, u32[]{:S(2)}, u32[]{:S(2)}) %all-to-all-start.4) | async-done | bytes 884768 | tf_op jit(solution)/shard_map/all_to_all | solution.py:258
  216.3 3.6 all-to-all-start
  226.9 15.9 %all-to-all-done = bf16[8,54,1024]{2,1,0:T(8,128)(2,1)S(1)} async-done(((bf16[8,54,1024]{2,1,0:T(8,128)(2,1)}), bf16[8,54,1024]{2,1,0:T(8,128)(2,1)S(1)}, u32[]{:S(2)}, u32[]{:S(2)}) %all-to-all-start) | async-done | bytes 884768 | tf_op jit(solution)/shard_map/all_to_all | solution.py:237
  244.0 10.5 %fusion.2 = f32[432,4096]{1,0:T(8,128)} fusion(bf16[432,1024]{1,0:T(8,128)(2,1)} %reshape.1018, bf16[1,4096,1024]{2,1,0:T(8,128)(2,1)} %all-gather.13.cloned.1.call-done), kind=kOutput, calls=%fused_computation.8 | convolution fusion | flops 3623878656 | bytes 16351232 | tf_op jit(solution)/shard_map/erd,efd->erf/dot_general | solution.py:259
  254.5 13.0 %fusion.31 = (bf16[432,4096]{1,0:T(8,128)(2,1)}, f32[432,4096]{1,0:T(8,128)S(1)}) fusion(f32[432,4096]{1,0:T(8,128)} %fusion.2, bf16[432,1024]{1,0:T(8,128)(2,1)S(1)} %copy-done.84, bf16[1,1024,4096]{2,1,0:T(8,128)(2,1)} %all-gather.11.cloned.1.call-done), kind=kOutput, calls=%fused_computation.37 | convolution fusion | flops 3659268096 | bytes 26968064 | tf_op jit(solution)/shard_map/erd,edf->erf/dot_general | solution.py:238
  267.5 4.5 fusion.154
  275.2 7.0 reduce.24
  283.7 4.4 all-to-all-start.3
  288.1 10.6 %fusion.4 = f32[432,4096]{1,0:T(8,128)} fusion(bf16[432,1024]{1,0:T(8,128)(2,1)} %reshape.1013, bf16[1,4096,1024]{2,1,0:T(8,128)(2,1)} %all-gather.13.cloned.1.call-done), kind=kOutput, calls=%fused_computation.10 | convolution fusion | flops 3623878656 | bytes 16351232 | tf_op jit(solution)/shard_map/erd,efd->erf/dot_general | solution.py:259
  298.7 12.8 %fusion.24 = (bf16[432,4096]{1,0:T(8,128)(2,1)}, f32[432,4096]{1,0:T(8,128)S(1)}) fusion(f32[432,4096]{1,0:T(8,128)} %fusion.4, bf16[432,1024]{1,0:T(8,128)(2,1)S(1)} %copy-done.86, bf16[1,1024,4096]{2,1,0:T(8,128)(2,1)} %all-gather.11.cloned.1.call-done), kind=kOutput, calls=%fused_computation.30 | convolution fusion | flops 3659268096 | bytes 26968064 | tf_op jit(solution)/shard_map/erd,edf->erf/dot_general | solution.py:238
  311.6 4.5 fusion.157
  318.7 7.0 reduce.25
  327.3 6.4 all-to-all-start.1
  333.7 8.3 fusion.160
  344.6 7.0 reduce.26
  355.2 4.4 all-to-all-start.7
  359.6 8.3 fusion.163
  370.5 7.1 reduce.27
  381.6 3.6 all-to-all-start.5
  385.3 5.7 reshape.1049
  391.0 5.5 reshape.1051
  399.8 3.9 fusion.126
  403.6 5.5 reshape.1053
  413.9 3.2 reshape.1055
  417.1 5.7 multiply_reduce_fusion.1
  422.8 4.2 convert_add_fusion.1
  431.6 4.6 fusion.190
  436.2 4.6 fusion.193
  448.1 5.3 multiply_convert_fusion.2
  456.2 4.7 multiply_convert_fusion.3
  470.2 3.3 convolution_convert_fusion.7
  475.0 5.3 fusion.199
  480.3 4.6 fusion.202
  492.4 5.6 multiply_convert_fusion.5
  501.0 4.7 multiply_convert_fusion.6
  515.0 12.9 %fusion.371 = f32[1024,4096]{1,0:T(8,128)} fusion(bf16[432,1024]{1,0:T(8,128)(2,1)} %reshape.995, bf16[432,4096]{1,0:T(8,128)(2,1)} %get-tuple-element.190), kind=kOutput, calls=%fused_computation.462 | convolution fusion | flops 3623878656 | bytes 21200896 | tf_op jit(solution)/shard_map/erd,erf->edf/dot_general | solution.py:267
  527.9 10.2 %fusion = bf16[1,1024,4096]{2,1,0:T(8,128)(2,1)} fusion(f32[1024,4096]{1,0:T(8,128)} %fusion.371, bf16[432,1024]{1,0:T(8,128)(2,1)S(1)} %copy-done.85, bf16[432,4096]{1,0:T(8,128)(2,1)S(1)} %copy-done.169), kind=kOutput, calls=%fused_computation.6 | convolution fusion | flops 3632267264 | bytes 29589504 | tf_op jit(solution)/shard_map/erd,erf->edf/dot_general | solution.py:267
  538.6 17.0 %fusion.345 = f32[4096,1024]{1,0:T(8,128)} fusion(bf16[432,1024]{1,0:T(8,128)(2,1)} %reshape.1013, f32[432,4096]{1,0:T(8,128)} %copy-done.166), kind=kOutput, calls=%fused_computation.436 | convolution fusion | flops 3639803904 | bytes 24739840 | tf_op jit(solution)/shard_map/erf,erd->efd/dot_general | solution.py:262
  555.6 13.5 %fusion.1 = bf16[1,4096,1024]{2,1,0:T(8,128)(2,1)} fusion(f32[4096,1024]{1,0:T(8,128)} %fusion.345, bf16[432,1024]{1,0:T(8,128)(2,1)S(1)} %copy-done.83, f32[432,4096]{1,0:T(8,128)} %copy-done.170), kind=kOutput, calls=%fused_computation.7 | convolution fusion | flops 3648192512 | bytes 33128448 | tf_op jit(solution)/shard_map/erf,erd->efd/dot_general | solution.py:262
  584.9 3.3 convolution_add_fusion.1
  597.5 5.5 fusion.215
  603.1 10.0 %convolution_add_fusion = f32[1024,3072]{1,0:T(8,128)} fusion(f32[1024,3072]{1,0:T(8,128)S(1)} %fusion.215, bf16[384,1024]{0,1:T(8,128)(2,1)S(1)} %copy-done.64, bf16[384,1024]{0,1:T(8,128)(2,1)} %copy.360, bf16[384,1024]{0,1:T(8,128)(2,1)S(1)} %bitcast.561, f32[384]{0:T(512)S(1)} %copy-done.145, f32[384]{0:T(512)S(1)} %copy-done.139, ...), kind=kOutput, calls=%fused_computation.40 | convolution fusion | flops 2428502016 | bytes 28323840 | tf_op jit(solution)/shard_map/td,te->de/dot_general | solution.py:326
  618.0 6.4 fusion.214
  624.5 9.5 fusion.124
  634.0 42.4 %all-reduce = (f32[1024]{0:T(1024)}, f32[1024]{0:T(1024)}, f32[1024]{0:T(1024)}, f32[1024]{0:T(1024)}, f32[1024,8]{0,1:T(8,128)}) all-reduce(f32[1024]{0:T(1024)S(1)} %add.380, f32[1024]{0:T(1024)S(1)} %add.381, f32[1024]{0:T(1024)S(1)} %add.384, ...), channel_id=1, replica_groups=mesh['expert'=8,'context'=2,'dp'=2] {'expert','context','dp'}, use_global_device_ids=true, to_apply=%region_52.53 | all-reduce | flops 12288 | bytes 98304 | tf_op jit(solution)/shard_map/psum | solution.py:131
  676.4 3.9 fusion.123
  682.2 4.1 convert_element_type.331
  686.9 4.1 convert_element_type.334
  691.0 281.6 %all-reduce.4.cloned.1.call-done = (f32[1024,3072]{1,0:T(8,128)}, f32[1024,1024]{1,0:T(8,128)}) async-done(((f32[1024,3072]{1,0:T(8,128)}, f32[1024,1024]{1,0:T(8,128)}), (f32[1024,3072]{1,0:T(8,128)}, f32[1024,1024]{1,0:T(8,128)})) %all-reduce.4.cloned.1.call-update) | async-done | bytes 16777232 | tf_op jit(solution)/shard_map/psum | solution.py:131
  972.5 11.1 %copy.399 = f32[1024,3072]{1,0:T(8,128)} copy(f32[1024,3072]{1,0:T(8,128)} %get-tuple-element.210) | data formatting | bytes 25165824
  (569 shorter events, 208.9 us)
Async XLA Ops:
  7.2 81.7 %copy-start = (bf16[1024,1024]{1,0:T(8,128)(2,1)S(1)}, bf16[1024,1024]{1,0:T(8,128)(2,1)}, u32[]{:S(2)}) copy-start(bf16[1024,1024]{1,0:T(8,128)(2,1)} %param.22) | copy-start | bytes 6291460
  7.2 31.3 %all-gather.7.cloned.1.call-start = ((), (), s32[]{:S(2)}) async-start(), calls=%async_computation.14 | async-start | bytes 2359296 | tf_op jit(solution)/shard_map/all_gather | solution.py:211
  9.0 10.1 %copy-start.138 = (f32[384]{0:T(512)}, f32[384]{0:T(512)S(1)}, u32[]{:S(2)}) copy-start(f32[384]{0:T(512)S(1)} %get-tuple-element.202) | copy-start | bytes 4612
  18.3 27.4 %all-gather.9.cloned.1.call-start = ((), (), s32[]{:S(2)}) async-start(), calls=%async_computation.15 | async-start | bytes 2359296 | tf_op jit(solution)/shard_map/all_gather | solution.py:212
  19.1 72.0 %all-gather.15.cloned.1.call-start = ((), (), s32[]{:S(2)}) async-start(), calls=%async_computation.18 | async-start | bytes 2359296 | tf_op jit(solution)/shard_map/all_gather | solution.py:211
  26.4 70.2 %all-gather.17.cloned.1.call-start = ((), (), s32[]{:S(2)}) async-start(), calls=%async_computation.19 | async-start | bytes 2359296 | tf_op jit(solution)/shard_map/all_gather | solution.py:212
  27.0 216.9 %all-gather.13.cloned.1.call-start = ((), (), s32[]{:S(2)}) async-start(), calls=%async_computation.17 | async-start | bytes 10485760 | tf_op jit(solution)/shard_map/all_gather | solution.py:171
  27.6 226.9 %all-gather.11.cloned.1.call-start = ((), (), s32[]{:S(2)}) async-start(), calls=%async_computation.16 | async-start | bytes 10485760 | tf_op jit(solution)/shard_map/all_gather | solution.py:170
  30.6 26.1 %copy-start.5 = (bf16[384,1024]{0,1:T(8,128)(2,1)}, bf16[384,1024]{0,1:T(8,128)(2,1)S(1)}, u32[]{:S(2)}) copy-start(bf16[384,1024]{0,1:T(8,128)(2,1)S(1)} %copy.257) | copy-start | bytes 2359300
  37.5 44.0 %copy-start.70 = (pred[384,256]{0,1:T(8,128)(4,1)}, pred[384,256]{0,1:T(8,128)(4,1)S(1)}, u32[]{:S(2)}) copy-start(pred[384,256]{0,1:T(8,128)(4,1)S(1)} %get-tuple-element.153) | copy-start | bytes 294916
  60.5 20.9 %copy-start.101 = (f32[16,384]{1,0:T(8,128)}, f32[16,384]{1,0:T(8,128)S(1)}, u32[]{:S(2)}) copy-start(f32[16,384]{1,0:T(8,128)S(1)} %get-tuple-element.171) | copy-start | bytes 73732
  62.1 19.4 %copy-start.116 = (f32[16,384]{1,0:T(8,128)}, f32[16,384]{1,0:T(8,128)S(1)}, u32[]{:S(2)}) copy-start(f32[16,384]{1,0:T(8,128)S(1)} %fusion.36) | copy-start | bytes 73732
  65.3 10.7 %copy-start.92 = (bf16[256,1024]{0,1:T(8,128)(2,1)}, bf16[256,1024]{0,1:T(8,128)(2,1)S(1)}, u32[]{:S(2)}) copy-start(bf16[256,1024]{0,1:T(8,128)(2,1)S(1)} %copy.262) | copy-start | bytes 1572868
  70.2 11.2 %copy-start.118 = (f32[16,384]{1,0:T(8,128)}, f32[16,384]{1,0:T(8,128)S(1)}, u32[]{:S(2)}) copy-start(f32[16,384]{1,0:T(8,128)S(1)} %fusion.34) | copy-start | bytes 73732
  76.1 12.7 %copy-start.94 = (bf16[256,1024]{0,1:T(8,128)(2,1)}, bf16[256,1024]{0,1:T(8,128)(2,1)S(1)}, u32[]{:S(2)}) copy-start(bf16[256,1024]{0,1:T(8,128)(2,1)S(1)} %copy.259) | copy-start | bytes 1572868
  95.6 13.7 %copy-start.45 = (bf16[256,1024]{0,1:T(8,128)(2,1)}, bf16[256,1024]{0,1:T(8,128)(2,1)S(1)}, u32[]{:S(2)}) copy-start(bf16[256,1024]{0,1:T(8,128)(2,1)S(1)} %copy.272) | copy-start | bytes 1572868
  96.6 10.5 %copy-start.7 = (bf16[384,1024]{0,1:T(8,128)(2,1)S(1)}, bf16[384,1024]{0,1:T(8,128)(2,1)}, u32[]{:S(2)}) copy-start(bf16[384,1024]{0,1:T(8,128)(2,1)} %copy.268) | copy-start | bytes 2359300
  96.6 10.5 %copy-start.81 = (pred[384,256]{0,1:T(8,128)(4,1)S(1)}, pred[384,256]{0,1:T(8,128)(4,1)}, u32[]{:S(2)}) copy-start(pred[384,256]{0,1:T(8,128)(4,1)} %get-tuple-element.161) | copy-start | bytes 294916
  127.1 13.0 %copy-start.33 = (bf16[384,1024]{1,0:T(8,128)(2,1)}, bf16[384,1024]{1,0:T(8,128)(2,1)S(1)}, u32[]{:S(2)}) copy-start(bf16[384,1024]{1,0:T(8,128)(2,1)S(1)} %get-tuple-element.140) | copy-start | bytes 2359300
  127.5 281.7 %copy-start.105 = (f32[384,8]{0,1:T(8,128)}, f32[384,8]{0,1:T(8,128)S(1)}, u32[]{:S(2)}) copy-start(f32[384,8]{0,1:T(8,128)S(1)} %get-tuple-element.193) | copy-start | bytes 36868
  127.5 281.7 %copy-start.140 = (f32[384]{0:T(512)}, f32[384]{0:T(512)S(1)}, u32[]{:S(2)}) copy-start(f32[384]{0:T(512)S(1)} %get-tuple-element.192) | copy-start | bytes 4612
  127.5 281.7 %copy-start.146 = (f32[384]{0:T(512)}, f32[384]{0:T(512)S(1)}, u32[]{:S(2)}) copy-start(f32[384]{0:T(512)S(1)} %fusion.279) | copy-start | bytes 4612
  131.5 36.6 %copy-start.134 = (s32[384]{0:T(512)S(1)}, s32[384]{0:T(512)}, u32[]{:S(2)}) copy-start(s32[384]{0:T(512)} %copy-done.133) | copy-start | bytes 4612
  131.5 30.6 %all-to-all-start.6 = ((bf16[8,54,1024]{2,1,0:T(8,128)(2,1)}), bf16[8,54,1024]{2,1,0:T(8,128)(2,1)}, u32[]{:S(2)}, u32[]{:S(2)}) async-start(bf16[8,54,1024]{2,1,0:T(8,128)(2,1)} %reshape.1017), calls=%async_computation.6 | async-start | bytes 1835008 | tf_op jit(solution)/shard_map/all_to_all | solution.py:258
  138.6 29.6 %copy-start.157 = (s32[384]{0:T(512)S(1)}, s32[384]{0:T(512)}, u32[]{:S(2)}) copy-start(s32[384]{0:T(512)} %get-tuple-element.205) | copy-start | bytes 4612
  162.1 27.3 %all-to-all-start.2 = ((bf16[8,54,1024]{2,1,0:T(8,128)(2,1)}), bf16[8,54,1024]{2,1,0:T(8,128)(2,1)}, u32[]{:S(2)}, u32[]{:S(2)}) async-start(bf16[8,54,1024]{2,1,0:T(8,128)(2,1)} %reshape.1009), calls=%async_computation.2 | async-start | bytes 1835008 | tf_op jit(solution)/shard_map/all_to_all | solution.py:237
  166.5 27.1 %copy-start.35 = (bf16[384,1024]{1,0:T(8,128)(2,1)S(1)}, bf16[384,1024]{1,0:T(8,128)(2,1)}, u32[]{:S(2)}) copy-start(bf16[384,1024]{1,0:T(8,128)(2,1)} %get-tuple-element.139) | copy-start | bytes 2359300
  168.1 241.9 %copy-start.107 = (f32[384,8]{0,1:T(8,128)}, f32[384,8]{0,1:T(8,128)S(1)}, u32[]{:S(2)}) copy-start(f32[384,8]{0,1:T(8,128)S(1)} %get-tuple-element.189) | copy-start | bytes 36868
  168.1 241.9 %copy-start.142 = (f32[384]{0:T(512)}, f32[384]{0:T(512)S(1)}, u32[]{:S(2)}) copy-start(f32[384]{0:T(512)S(1)} %get-tuple-element.188) | copy-start | bytes 4612
  168.2 241.9 %copy-start.148 = (f32[384]{0:T(512)}, f32[384]{0:T(512)S(1)}, u32[]{:S(2)}) copy-start(f32[384]{0:T(512)S(1)} %fusion.277) | copy-start | bytes 4612
  189.4 26.8 %all-to-all-start.4 = ((bf16[8,54,1024]{2,1,0:T(8,128)(2,1)}), bf16[8,54,1024]{2,1,0:T(8,128)(2,1)}, u32[]{:S(2)}, u32[]{:S(2)}) async-start(bf16[8,54,1024]{2,1,0:T(8,128)(2,1)} %reshape.1012), calls=%async_computation.4 | async-start | bytes 1835008 | tf_op jit(solution)/shard_map/all_to_all | solution.py:258
  216.3 26.6 %all-to-all-start = ((bf16[8,54,1024]{2,1,0:T(8,128)(2,1)}), bf16[8,54,1024]{2,1,0:T(8,128)(2,1)S(1)}, u32[]{:S(2)}, u32[]{:S(2)}) async-start(bf16[8,54,1024]{2,1,0:T(8,128)(2,1)} %reshape.994), calls=%async_computation | async-start | bytes 1835008 | tf_op jit(solution)/shard_map/all_to_all | solution.py:237
  244.0 10.6 %copy-start.84 = (bf16[432,1024]{1,0:T(8,128)(2,1)S(1)}, bf16[432,1024]{1,0:T(8,128)(2,1)}, u32[]{:S(2)}) copy-start(bf16[432,1024]{1,0:T(8,128)(2,1)} %reshape.1010) | copy-start | bytes 2654212
  254.5 13.0 %copy-start.165 = (bf16[1,4096,1024]{2,1,0:T(8,128)(2,1)S(1)}, bf16[1,4096,1024]{2,1,0:T(8,128)(2,1)}, u32[]{:S(2)}) copy-start(bf16[1,4096,1024]{2,1,0:T(8,128)(2,1)} %all-gather.13.cloned.1.call-done) | copy-start | bytes 25165828
  283.7 43.6 %all-to-all-start.3 = ((bf16[8,2,27648]{2,1,0:T(2,128)(2,1)}), bf16[8,2,27648]{2,1,0:T(2,128)(2,1)}, u32[]{:S(2)}, u32[]{:S(2)}) async-start(bf16[8,2,27648]{2,1,0:T(2,128)(2,1)} %reshape.1048), calls=%async_computation.3 | async-start | bytes 1769472 | tf_op jit(solution)/shard_map/all_to_all | solution.py:243
  288.1 10.6 %copy-start.86 = (bf16[432,1024]{1,0:T(8,128)(2,1)S(1)}, bf16[432,1024]{1,0:T(8,128)(2,1)}, u32[]{:S(2)}) copy-start(bf16[432,1024]{1,0:T(8,128)(2,1)} %reshape.995) | copy-start | bytes 2654212
  288.1 23.5 %slice-start.8 = ((s8[8388608]{0:T(1024)(128)(4,1)}), s8[4194304]{0:T(1024)(128)(4,1)S(1)}, s32[]{:S(2)}) async-start(s8[8388608]{0:T(1024)(128)(4,1)} %bitcast.588), calls=%async_computation.35 | async-start | bytes 8388608
  298.7 12.9 %slice-start.9 = ((s8[8388608]{0:T(1024)(128)(4,1)}), s8[4194304]{0:T(1024)(128)(4,1)S(1)}, s32[]{:S(2)}) async-start(s8[8388608]{0:T(1024)(128)(4,1)} %bitcast.588), calls=%async_computation.36 | async-start | bytes 8388608
  327.3 27.9 %all-to-all-start.1 = ((bf16[8,2,27648]{2,1,0:T(2,128)(2,1)}), bf16[8,2,27648]{2,1,0:T(2,128)(2,1)}, u32[]{:S(2)}, u32[]{:S(2)}) async-start(bf16[8,2,27648]{2,1,0:T(2,128)(2,1)} %reshape.1050), calls=%async_computation.1 | async-start | bytes 1769472 | tf_op jit(solution)/shard_map/all_to_all | solution.py:243
  355.2 26.4 %all-to-all-start.7 = ((bf16[8,2,27648]{2,1,0:T(2,128)(2,1)}), bf16[8,2,27648]{2,1,0:T(2,128)(2,1)}, u32[]{:S(2)}, u32[]{:S(2)}) async-start(bf16[8,2,27648]{2,1,0:T(2,128)(2,1)} %reshape.1052), calls=%async_computation.7 | async-start | bytes 1769472 | tf_op jit(solution)/shard_map/all_to_all | solution.py:273
  370.5 14.7 %copy-start.104 = (f32[16,384]{1,0:T(8,128)S(1)}, f32[16,384]{1,0:T(8,128)}, u32[]{:S(2)}) copy-start(f32[16,384]{1,0:T(8,128)} %copy-done.103) | copy-start | bytes 73732
  370.5 14.7 %copy-start.115 = (f32[16,384]{1,0:T(8,128)S(1)}, f32[16,384]{1,0:T(8,128)}, u32[]{:S(2)}) copy-start(f32[16,384]{1,0:T(8,128)} %copy-done.114) | copy-start | bytes 73732
  370.5 14.7 %copy-start.123 = (f32[16,384]{1,0:T(8,128)S(1)}, f32[16,384]{1,0:T(8,128)}, u32[]{:S(2)}) copy-start(f32[16,384]{1,0:T(8,128)} %copy-done.122) | copy-start | bytes 73732
  370.5 14.7 %copy-start.125 = (f32[16,384]{1,0:T(8,128)S(1)}, f32[16,384]{1,0:T(8,128)}, u32[]{:S(2)}) copy-start(f32[16,384]{1,0:T(8,128)} %copy-done.124) | copy-start | bytes 73732
  370.5 14.7 %copy-start.127 = (f32[16,384]{1,0:T(8,128)S(1)}, f32[16,384]{1,0:T(8,128)}, u32[]{:S(2)}) copy-start(f32[16,384]{1,0:T(8,128)} %copy-done.126) | copy-start | bytes 73732
  381.6 32.3 %all-to-all-start.5 = ((bf16[8,2,27648]{2,1,0:T(2,128)(2,1)}), bf16[8,2,27648]{2,1,0:T(2,128)(2,1)S(1)}, u32[]{:S(2)}, u32[]{:S(2)}) async-start(bf16[8,2,27648]{2,1,0:T(2,128)(2,1)} %reshape.1054), calls=%async_computation.5 | async-start | bytes 1769472 | tf_op jit(solution)/shard_map/all_to_all | solution.py:273
  385.1 203.1 %reduce-scatter.25.cloned.1.call-start = ((), (), s32[]{:S(2)}) async-start(), calls=%async_computation.25 | async-start | bytes 2359296
  403.6 10.2 %copy-start.152 = (f32[384]{0:T(512)}, f32[384]{0:T(512)S(1)}, u32[]{:S(2)}) copy-start(f32[384]{0:T(512)S(1)} %mul.667) | copy-start | bytes 4612
  403.6 10.2 %copy-start.154 = (f32[384]{0:T(512)}, f32[384]{0:T(512)S(1)}, u32[]{:S(2)}) copy-start(f32[384]{0:T(512)S(1)} %mul.630) | copy-start | bytes 4612
  446.4 144.2 %reduce-scatter.23.cloned.1.call-start = ((), (), s32[]{:S(2)}) async-start(), calls=%async_computation.24 | async-start | bytes 2359296
  448.1 13.9 %slice-start.6 = ((s8[6291456]{0:T(1024)(128)(4,1)}), s8[4194304]{0:T(1024)(128)(4,1)S(1)}, s32[]{:S(2)}) async-start(s8[6291456]{0:T(1024)(128)(4,1)} %bitcast.518), calls=%async_computation.33 | async-start | bytes 8388608
  470.0 122.9 %reduce-scatter.21.cloned.1.call-start = ((), (), s32[]{:S(2)}) async-start(), calls=%async_computation.23 | async-start | bytes 2359296
  474.9 15.5 %copy-start.58 = (bf16[384,1024]{0,1:T(8,128)(2,1)}, bf16[384,1024]{0,1:T(8,128)(2,1)S(1)}, u32[]{:S(2)}) copy-start(bf16[384,1024]{0,1:T(8,128)(2,1)S(1)} %copy.280) | copy-start | bytes 2359300
  475.0 9.9 slice-start
  492.2 103.0 %reduce-scatter.19.cloned.1.call-start = ((), (), s32[]{:S(2)}) async-start(), calls=%async_computation.22 | async-start | bytes 2359296
  492.4 14.4 %slice-start.2 = ((s8[6291456]{0:T(1024)(128)(4,1)}), s8[4194304]{0:T(1024)(128)(4,1)S(1)}, s32[]{:S(2)}) async-start(s8[6291456]{0:T(1024)(128)(4,1)} %bitcast.514), calls=%async_computation.29 | async-start | bytes 8388608
  514.6 13.2 %copy-start.85 = (bf16[432,1024]{1,0:T(8,128)(2,1)S(1)}, bf16[432,1024]{1,0:T(8,128)(2,1)}, u32[]{:S(2)}) copy-start(bf16[432,1024]{1,0:T(8,128)(2,1)} %reshape.1010) | copy-start | bytes 2654212
  514.7 167.5 %reduce-scatter.15.cloned.1.call-start = ((), (), s32[]{:S(2)}) async-start(), calls=%async_computation.20 | async-start | bytes 10485760 | tf_op jit(solution)/shard_map/reduce_scatter | solution.py:133
  515.0 12.9 %copy-start.169 = (bf16[432,4096]{1,0:T(8,128)(2,1)S(1)}, bf16[432,4096]{1,0:T(8,128)(2,1)}, u32[]{:S(2)}) copy-start(bf16[432,4096]{1,0:T(8,128)(2,1)} %get-tuple-element.194) | copy-start | bytes 10616836
  538.1 17.5 %copy-start.83 = (bf16[432,1024]{1,0:T(8,128)(2,1)S(1)}, bf16[432,1024]{1,0:T(8,128)(2,1)}, u32[]{:S(2)}) copy-start(bf16[432,1024]{1,0:T(8,128)(2,1)} %reshape.1018) | copy-start | bytes 2654212
  538.1 148.8 %reduce-scatter.17.cloned.1.call-start = ((), (), s32[]{:S(2)}) async-start(), calls=%async_computation.21 | async-start | bytes 10485760 | tf_op jit(solution)/shard_map/reduce_scatter | solution.py:136
  569.1 403.4 %all-reduce.4.cloned.1.call-start = ((), (), s32[]{:S(2)}) async-start(), calls=%async_computation.26 | async-start | bytes 33554432 | tf_op jit(solution)/shard_map/psum | solution.py:131
  584.9 12.6 %copy-start.54 = (bf16[16,64,384]{2,1,0:T(8,128)(2,1)}, bf16[16,64,384]{2,1,0:T(8,128)(2,1)S(1)}, u32[]{:S(2)}) copy-start(bf16[16,64,384]{2,1,0:T(8,128)(2,1)S(1)} %multiply_convert_fusion.9) | copy-start | bytes 2359300
  972.5 11.1 %copy-start.51 = (f32[1024,1024]{1,0:T(8,128)S(1)}, f32[1024,1024]{1,0:T(8,128)}, u32[]{:S(2)}) copy-start(f32[1024,1024]{1,0:T(8,128)} %get-tuple-element.211) | copy-start | bytes 12582916
  (138 other events, 567.5 us)
Sparse Core Ops, SparseCore 0:
  18.4 12.4 all-gather.6
  33.1 10.9 all-gather.8
  46.2 10.9 all-gather.14
  59.2 10.9 all-gather.16
  71.6 59.4 all-gather.12
  132.5 58.2 all-gather.10
  446.5 10.1 reduce-scatter.24
  470.1 10.2 reduce-scatter.22
  492.3 10.1 reduce-scatter.20
  514.8 10.2 reduce-scatter.18
  538.2 72.8 reduce-scatter.14
  613.7 73.1 reduce-scatter.16
  693.8 278.6 all-reduce.3
where the time goes:
time: 1000 us; the launch traced here: 992 us
  waiting for transfers between devices  360 us (36%)
  matrix products  307 us (31%)
  local copies, waits for them, and re-layouts  140 us (14%)
  other arithmetic  87 us (9%)
  blocking collectives  42.4 us (4%)
  starting transfers between devices  39.6 us (4%)
  between operations  16.8 us (2%)
    psum x1, waiting for transfers between devices, reduce_grads(): dense = lax.psum(dense, ('expert', 'context', 'dp'))  282 us
    unnamed x381, local copies, waits for them, and re-layouts  74.9 us
    psum x1, blocking collectives, reduce_grads(): dense = lax.psum(dense, ('expert', 'context', 'dp'))  42.4 us
    all_to_all x2, waiting for transfers between devices, local(): lax.all_to_all(sent_grad, 'expert', split_axis=0, concat_axis=1, tiled=True)  38.3 us
    unnamed x11, other arithmetic  33.1 us
    all_to_all x2, waiting for transfers between devices, local(): lax.all_to_all(sent, 'expert', split_axis=0, concat_axis=1, tiled=True)  32 us
    dot_general x2, matrix products, local(): jnp.einsum('erf,erd->efd', active, received_grad, preferred_element_type=...  30.5 us
    dot_general x2, matrix products, local(): jnp.einsum('erd,edf->erf', received, full_in, preferred_element_type=jnp....  25.8 us
  transfers between devices with their start and end apart: 21, of which 8 were waited for; matrix products, arithmetic and copies ran while one was open for 44% of the time, Pallas kernels for 0%

commit v1 on v0

v1 whole, which is shorter than its diff:
```python
from functools import partial

import jax
import jax.numpy as jnp
from jax import lax
from jax.sharding import PartitionSpec as P
from jax.experimental import pallas as pl
from jax.experimental.pallas import tpu as pltpu
bf=jnp.bfloat16; f32=jnp.float32
NT=(((1,),(1,)),((),()))
TN=(((0,),(0,)),((),()))
NN=(((1,),(0,)),((),()))
def mm(a,b,dims): return lax.dot_general(a,b,dims,preferred_element_type=f32)

def fwd_body(rb, bias_ref, q_ref, ko_ref, vo_ref, kx_ref, vx_ref, o_ref, ol_ref, lse_ref):
    i=pl.program_id(0)
    rows=q_ref.shape[0]
    lane=lax.broadcasted_iota(jnp.int32,(1,128),1)
    masks=[(lane<64).astype(bf)*0.125,(lane>=64).astype(bf)*0.125]
    ko=ko_ref[...]; vo=vo_ref[...]; kx=kx_ref[...]; vx=vx_ref[...]
    for r in range(0,rows,rb):
        q=q_ref[r:r+rb,:]
        bo=bias_ref[r:r+rb,:rows]; bx=bias_ref[r:r+rb,rows:]
        outs=[]
        old=lse_ref[r:r+rb,:]
        for j in range(2):
            qj=q*masks[j]
            so=mm(qj,ko,NT)+bo
            sx=mm(qj,kx,NT)+bx
            m=jnp.maximum(jnp.max(so,-1,keepdims=True),jnp.max(sx,-1,keepdims=True))
            po=jnp.exp(so-m); px=jnp.exp(sx-m)
            l=jnp.sum(po,-1,keepdims=True)+jnp.sum(px,-1,keepdims=True)
            w=mm(po.astype(bf),vo,NN)+mm(px.astype(bf),vx,NN)
            outs.append(w/l)
            old=jnp.where(lane==2*i+j,m+jnp.log(l),old)
        lse_ref[r:r+rb,:]=old
        o=jnp.where(lane<64,outs[0],outs[1])
        o_ref[r:r+rb,:]=o
        ol_ref[r:r+rb,:]=o.astype(bf)

def attn_fwd(joined, other, bias, mb, rb=None):
    rows=bias.shape[0]; nx=other.shape[0]; D=other.shape[1]//2; G=D//128
    flops=4*rows*(rows+nx)*D
    rb=rb or rows
    return pl.pallas_call(partial(fwd_body,rb),
        grid=(G,),
        in_specs=[pl.BlockSpec(bias.shape,lambda i:(0,0)),
            pl.BlockSpec((rows,128),lambda i:(mb,i)),
            pl.BlockSpec((rows,128),lambda i:(mb,G+i)),
            pl.BlockSpec((rows,128),lambda i:(mb,2*G+i)),
            pl.BlockSpec((nx,128),lambda i:(0,i)),
            pl.BlockSpec((nx,128),lambda i:(0,G+i))],
        out_specs=[pl.BlockSpec((rows,128),lambda i:(0,i)),pl.BlockSpec((rows,128),lambda i:(0,i)),pl.BlockSpec((rows,128),lambda i:(0,0))],
        out_shape=[jax.ShapeDtypeStruct((rows,D),f32),jax.ShapeDtypeStruct((rows,D),bf),jax.ShapeDtypeStruct((rows,128),f32)],
        cost_estimate=pl.CostEstimate(flops=flops*4,transcendentals=16*rows*(rows+nx),bytes_accessed=rows*D*16),
        name="attn_fwd")(bias,joined,joined,joined,other,other)

def bwd_body(kb, biast_ref, lse_ref, q_ref, ko_ref, vo_ref, kx_ref, vx_ref, do_ref, o_ref, dq_ref, dko_ref, dx_ref):
    i=pl.program_id(0)
    rows=q_ref.shape[0]; nx=kx_ref.shape[0]
    lane=lax.broadcasted_iota(jnp.int32,(1,128),1)
    masks=[(lane<64).astype(bf),(lane>=64).astype(bf)]
    q=q_ref[...]; do=do_ref[...]
    prod=do.astype(f32)*o_ref[...]
    qs=[q*(m*0.125) for m in masks]; dos=[do*m for m in masks]
    sel=(lax.broadcasted_iota(jnp.int32,(8,128),1)//64==lax.broadcasted_iota(jnp.int32,(8,128),0)).astype(f32)
    delta=lax.dot_general(sel,prod,NT,precision=lax.Precision.HIGHEST,preferred_element_type=f32)
    lses=[lse_ref[pl.ds(2*i+j,1),:] for j in range(2)]
    dq=[None,None]
    for (kr,vr,base,cnt,own) in ((ko_ref,vo_ref,0,rows,True),(kx_ref,vx_ref,rows,nx,False)):
        for b in range(0,cnt,kb):
            k=kr[b:b+kb,:]; v=vr[b:b+kb,:]
            bt=biast_ref[base+b:base+b+kb,:]
            dk=dv=None
            for j in range(2):
                s=mm(k,qs[j],NT)+bt
                p=jnp.exp(s-lses[j])
                dp=mm(v,dos[j],NT)
                ds=(p*(dp-delta[j:j+1,:])).astype(bf)
                a=mm(p.astype(bf),dos[j],NN); c=mm(ds,qs[j],NN)
                dv=a if dv is None else dv+a
                dk=c if dk is None else dk+c
                e=mm(ds,k,TN)
                dq[j]=e if dq[j] is None else dq[j]+e
            if own:
                dko_ref[0,b:b+kb,:]=dk; dko_ref[1,b:b+kb,:]=dv
            else:
                dx_ref[0,b:b+kb,:]=dk.astype(bf); dx_ref[1,b:b+kb,:]=dv.astype(bf)
    dq_ref[...]=(jnp.where(lane<64,dq[0],dq[1])*0.125).astype(bf)

def attn_bwd(joined, other, biast, lset, do, o, mb, kb=None):
    rows=biast.shape[1]; nx=other.shape[0]; D=other.shape[1]//2; G=D//128
    flops=10*rows*(rows+nx)*D
    kb=kb or rows
    return pl.pallas_call(partial(bwd_body,kb),
        grid=(G,),
        in_specs=[pl.BlockSpec(biast.shape,lambda i:(0,0)),
            pl.BlockSpec(lset.shape,lambda i:(0,0)),
            pl.BlockSpec((rows,128),lambda i:(mb,i)),
            pl.BlockSpec((rows,128),lambda i:(mb,G+i)),
            pl.BlockSpec((rows,128),lambda i:(mb,2*G+i)),
            pl.BlockSpec((nx,128),lambda i:(0,i)),
            pl.BlockSpec((nx,128),lambda i:(0,G+i)),
            pl.BlockSpec((rows,128),lambda i:(0,i)),
            pl.BlockSpec((rows,128),lambda i:(0,i))],
        out_specs=[pl.BlockSpec((rows,128),lambda i:(0,i)),pl.BlockSpec((2,rows,128),lambda i:(0,0,i)),pl.BlockSpec((2,nx,128),lambda i:(0,0,i))],
        out_shape=[jax.ShapeDtypeStruct((rows,D),bf),jax.ShapeDtypeStruct((2,rows,D),f32),jax.ShapeDtypeStruct((2,nx,D),bf)],
        cost_estimate=pl.CostEstimate(flops=flops*4,transcendentals=16*rows*(rows+nx),bytes_accessed=rows*D*30),
        name="attn_bwd")(biast,lset,joined,joined,joined,other,other,do,o)

C0=0.7978845608028654; C1=0.044715
def exp_body(x_ref, g_ref, wi_ref, wo_ref, *refs):
    act_ref, ig_ref, b_ref, accr, accd = refs[-5:]
    f=pl.program_id(0)
    x=x_ref[...]; g=g_ref[...]; wi=wi_ref[...]; wo=wo_ref[...]
    v=mm(x,wi,NN)
    ag=mm(g,wo,NT)
    v2=v*v
    t=jnp.tanh(C0*(v*(1.0+C1*v2)))
    h=0.5*(1.0+t)
    act=(v*h).astype(bf)
    dg=h+(0.5*C0)*v*(1.0-t*t)*(1.0+(3*C1)*v2)
    ig=(ag*dg).astype(bf)
    act_ref[...]=act; ig_ref[...]=ig
    r=mm(act,wo,NN); d=mm(ig,wi,NT)
    @pl.when(f==0)
    def _(): accr[...]=r; accd[...]=d
    @pl.when(f>0)
    def _(): accr[...]+=r; accd[...]+=d
    @pl.when(f==pl.num_programs(0)-1)
    def _():
        size=b_ref.shape[1]//2
        for e in range(b_ref.shape[0]):
            b_ref[e,:size,:]=accr[e*size:(e+1)*size,:].astype(bf)
            b_ref[e,size:,:]=accd[e*size:(e+1)*size,:].astype(bf)

def expert(x, g, wi, wo, prev, mb, nmb, experts, fb=512):
    rows,D=x.shape; FF=wi.shape[1]
    blk=pl.BlockSpec((rows,fb),lambda f:(mb,f))
    anyspec=pl.BlockSpec(memory_space=pl.ANY)
    ex=() if prev is None else prev
    return pl.pallas_call(exp_body, grid=(FF//fb,),
        in_specs=[pl.BlockSpec((rows,D),lambda f:(0,0)),pl.BlockSpec((rows,D),lambda f:(0,0)),
                  pl.BlockSpec((D,fb),lambda f:(0,f)),pl.BlockSpec((fb,D),lambda f:(f,0))]+[anyspec]*len(ex),
        out_specs=[blk,blk,pl.BlockSpec((experts,2*rows//experts,D),lambda f:(0,0,0))],
        out_shape=[jax.ShapeDtypeStruct((nmb*rows,FF),bf)]*2+[jax.ShapeDtypeStruct((experts,2*rows//experts,D),bf)],
        scratch_shapes=[pltpu.VMEM((rows,D),f32)]*2,
        input_output_aliases={} if prev is None else {4:0,5:1},
        cost_estimate=pl.CostEstimate(flops=8*rows*D*FF,transcendentals=rows*FF,bytes_accessed=4*D*FF+4*rows*FF),
        name="expert")(x,g,wi,wo,*ex)

def merge_body(count, dq_ref, own_ref, *refs):
    j=pl.program_id(0); out_ref=refs[-1]
    @pl.when(j==0)
    def _(): out_ref[...]=dq_ref[...]
    @pl.when(j>0)
    def _():
        total=own_ref[0]
        for r in refs[:count]: total=total+r[0].astype(f32)
        out_ref[...]=total.astype(bf)

def merge(dq, own, parts, prev, mb, nmb):
    rows,D=dq.shape
    three=pl.BlockSpec((1,rows,D),lambda j:(jnp.maximum(j-1,0),0,0))
    ex=[] if prev is None else [prev]
    return pl.pallas_call(partial(merge_body,len(parts)), grid=(3,),
        in_specs=[pl.BlockSpec((rows,D),lambda j:(0,0)),three]+[three]*len(parts)+[pl.BlockSpec(memory_space=pl.ANY)]*len(ex),
        out_specs=pl.BlockSpec((rows,D),lambda j:(mb,j)),
        out_shape=jax.ShapeDtypeStruct((nmb*rows,3*D),bf),
        input_output_aliases={} if prev is None else {2+len(parts):0},
        cost_estimate=pl.CostEstimate(flops=rows*D*4,transcendentals=0,bytes_accessed=rows*D*22),
        name="merge")(dq,own,*parts,*ex)


HEADS = 16
EPS = 1e-05
HIGH = lax.Precision.HIGHEST


def layer_norm(values, gain, shift):
    center = values - jnp.mean(values, axis=-1, keepdims=True)
    scale = lax.rsqrt(jnp.mean(center * center, axis=-1, keepdims=True) + EPS)
    normal = center * scale
    return (normal * gain + shift, normal, scale)


def norm_back(grad, normal, scale, gain):
    scaled = grad * gain
    inner = (
        scaled
        - jnp.mean(scaled, axis=-1, keepdims=True)
        - normal * jnp.mean(scaled * normal, axis=-1, keepdims=True)
    )
    return (inner * scale, jnp.sum(grad * normal, axis=0), jnp.sum(grad, axis=0))


def swap(values, axis, bit):
    return lax.ppermute(values, axis, [(i, i ^ bit) for i in range(lax.axis_size(axis))])


def bits_of(axis):
    count = lax.axis_size(axis)
    assert count & (count - 1) == 0
    return [(axis, 1 << i) for i in range(count.bit_length() - 1)]


def halve(values, steps, slot):
    sent, kept = [], []
    for value, order in zip(values, steps):
        axis, bit = order[slot]
        high = (lax.axis_index(axis) // bit) % 2
        half = value.shape[0] // 2
        part = lax.dynamic_slice_in_dim(value, (1 - high) * half, half)
        kept.append(lax.dynamic_slice_in_dim(value, high * half, half))
        sent.append(swap(part, axis, bit))
    return [a + b for a, b in zip(kept, sent)]


def double(values, steps, slot):
    sent = [swap(value, *order[slot]) for value, order in zip(values, steps)]
    joined = []
    for value, other, order in zip(values, sent, steps):
        axis, bit = order[slot]
        high = (lax.axis_index(axis) // bit) % 2
        joined.append(
            jnp.concatenate(
                [jnp.where(high == 0, value, other), jnp.where(high == 0, other, value)], axis=0
            )
        )
    return joined


def sum_everywhere(whole, widths, held=()):
    near = bits_of("context")
    for slot in range(len(near)):
        whole = halve([whole], [near], slot)[0]
    chunks, start = [], 0
    for width in widths:
        chunks.append(whole[:, start : start + width])
        start += width
    expert = bits_of("expert")
    orders = [
        expert[:1] + bits_of("dp") + expert[1:],
        bits_of("dp") + expert,
        expert[1:] + expert[:1] + bits_of("dp"),
    ][: len(widths)]
    count = len(orders[0])
    for slot in range(count):
        chunks = list(lax.optimization_barrier(tuple(halve(chunks, orders, slot))))
    for slot in reversed(range(count)):
        chunks = list(lax.optimization_barrier(tuple(double(chunks, orders, slot))))
        if slot == 1 and held:
            held = tuple(h.astype(f32) for h in held)
            chunks, held = lax.optimization_barrier((chunks, held))
    whole = chunks[0] if len(chunks) == 1 else jnp.concatenate(chunks, axis=1)
    for slot in reversed(range(len(near))):
        whole = double([whole], [near], slot)[0]
    return whole, held


def sum_small(values):
    for axis in ("context", "dp", "expert"):
        for _, bit in bits_of(axis):
            values = values + swap(values, axis, bit)
    return values


def local(
    tokens,
    out_grad,
    seq_lengths,
    token_order,
    expert_route,
    mixer_gain,
    mixer_shift,
    project_in,
    project_out,
    expert_gain,
    expert_shift,
    router_weight,
    expert_in,
    expert_out,
):
    micro, rows, model = tokens.shape[0], tokens.shape[2], tokens.shape[3]
    contexts = lax.axis_size("context")
    here = lax.axis_index("context")
    experts = expert_in.shape[0] * lax.axis_size("expert")
    capacity = 9 * rows // (8 * experts)
    block = (capacity + 2 + 7) // 8 * 8
    slots = experts * block

    full_in = lax.all_gather(expert_in[0], ("context", "dp"), axis=0, tiled=True)
    full_out = lax.all_gather(expert_out[0], ("context", "dp"), axis=0, tiled=True)

    router_float = router_weight.astype(f32)
    expert_ids = jnp.arange(experts, dtype=jnp.int32)
    slot_ids = jnp.arange(slots, dtype=jnp.int32)

    routes, ranks, places, place_two = [], [], [], []
    sent_grads = []
    for m in range(micro):
        route = expert_route[m, 0, :, 0]
        choose_int = (route[:, None] == expert_ids[None, :]).astype(jnp.int32)
        earlier = jnp.cumsum(choose_int, axis=0) - choose_int
        rank = jnp.sum(earlier * choose_int, axis=1)
        place = (route * block + rank)[None, :] == slot_ids[:, None]
        routes.append(route)
        ranks.append(rank)
        places.append(place.astype(bf))
        target = (route * (2 * block) + rank)[None, :]
        wide = jnp.arange(2 * slots, dtype=jnp.int32)[:, None]
        place_two.append(((target == wide).astype(bf), (target + block == wide).astype(bf)))
        sent_grads.append(
            jnp.dot(places[m], out_grad[m, 0], preferred_element_type=f32)
            .astype(bf)
            .reshape(experts, 1, block, model)
        )
    sent_grads, tokens = lax.optimization_barrier((jnp.concatenate(sent_grads, axis=1), tokens))
    grads_there = lax.all_to_all(sent_grads, "expert", split_axis=0, concat_axis=0, tiled=True)

    flat = tokens.reshape(micro * rows, model).astype(f32)
    normed, normal_one, scale_one = layer_norm(flat, mixer_gain, mixer_shift)
    normed_low = lax.optimization_barrier(normed.astype(bf))
    joined = jnp.dot(normed_low, project_in, preferred_element_type=f32).astype(bf)
    others, biases = [], []
    for m in range(micro):
        pairs = joined[m * rows : (m + 1) * rows, model:]
        parts = [
            lax.ppermute(pairs, "context", [(i, (i + s) % contexts) for i in range(contexts)])
            for s in range(1, contexts)
        ]
        others.append(parts[0] if contexts == 2 else jnp.concatenate(parts, axis=0))
        positions = token_order[m, 0]
        ends = jnp.cumsum(seq_lengths[m, 0])
        segments = jnp.sum((positions[:, None] >= ends[None, :]).astype(jnp.int32), axis=1)
        owners = [(here - s + contexts) % contexts for s in range(contexts)]
        key_positions = jnp.concatenate(
            [lax.dynamic_slice_in_dim(positions, o * rows, rows) for o in owners]
        )
        key_segments = jnp.concatenate(
            [lax.dynamic_slice_in_dim(segments, o * rows, rows) for o in owners]
        )
        query_positions, query_segments = key_positions[:rows], key_segments[:rows]
        biases.append(
            (
                jnp.where(
                    (key_positions[None, :] <= query_positions[:, None])
                    & (key_segments[None, :] == query_segments[:, None]),
                    0.0,
                    -1e30,
                ).astype(f32),
                jnp.where(
                    (key_positions[:, None] <= query_positions[None, :])
                    & (key_segments[:, None] == query_segments[None, :]),
                    0.0,
                    -1e30,
                ).astype(f32),
            )
        )

    saved = []
    before = grads_there
    for m in range(micro):
        attended, mixed_low, lse = attn_fwd(joined, others[m], biases[m][0], m)
        log_total = lse[:, :HEADS].T
        middle = flat[m * rows : (m + 1) * rows] + jnp.dot(
            mixed_low, project_out, preferred_element_type=f32
        )
        second, normal_two, scale_two = layer_norm(middle, expert_gain, expert_shift)
        second_low = second.astype(bf)
        shares = jax.nn.softmax(
            jnp.dot(second_low, router_weight, preferred_element_type=f32), axis=-1
        )
        choose_float = (routes[m][:, None] == expert_ids[None, :]).astype(f32)
        gate = jnp.sum(shares * choose_float, axis=1)
        gate_high = gate.astype(bf)
        gate_low = (gate - gate_high.astype(f32)).astype(bf)
        slot_expert, slot_row = slot_ids // block, slot_ids % block
        mine = slot_expert[:, None] == routes[m][None, :]
        gates = jnp.where(
            mine & (slot_row == capacity)[:, None],
            gate_high[None, :],
            jnp.where(mine & (slot_row == capacity + 1)[:, None], gate_low[None, :], jnp.zeros((), bf)),
        )
        ladder = (ranks[m][:, None] == jnp.arange(model, dtype=jnp.int32)[None, :]).astype(bf)
        sent = jnp.dot(
            jnp.concatenate([places[m], gates], axis=1),
            jnp.concatenate([second_low, ladder], axis=0),
            preferred_element_type=f32,
        ).astype(bf)
        if m + 1 < micro:
            sent, others[m + 1] = lax.optimization_barrier((sent, others[m + 1]))
        sent, before = lax.optimization_barrier((sent, before))
        if m == 0:
            grads_there = before
        else:
            saved[m - 1][-1] = before
        there = lax.all_to_all(
            sent.reshape(experts, block, model), "expert", split_axis=0, concat_axis=0, tiled=True
        )
        before = there
        saved.append(
            [attended, mixed_low, log_total, middle, second_low, normal_two, scale_two, shares,
             choose_float, gate, there]
        )

    whole = lax.optimization_barrier(tuple(state[-1] for state in saved))
    for m in range(micro):
        saved[m][-1] = whole[m]
    kept = None
    rows_there, scaled_there, returned = [], [], []
    for m in range(micro):
        there = saved[m][-1]
        gate_there = there[:, capacity, :block].astype(f32) + there[:, capacity + 1, :block].astype(f32)
        scaled = (gate_there[:, :, None] * grads_there[:, m].astype(f32)).astype(bf)
        there = there.reshape(slots, model)
        scaled = scaled.reshape(slots, model)
        active, inner_grad, back = expert(
            there, scaled, full_in, full_out, kept, m, micro, experts
        )
        if m + 1 < micro:
            back, saved[m + 1][-1] = lax.optimization_barrier((back, saved[m + 1][-1]))
        kept = (active, inner_grad)
        rows_there.append(there)
        scaled_there.append(scaled)
        returned.append(
            lax.all_to_all(back, "expert", split_axis=0, concat_axis=0, tiled=True).reshape(
                2 * slots, model
            )
        )
    active, inner_grad = kept
    rows_there = jnp.concatenate(rows_there, axis=0)
    scaled_there = jnp.concatenate(scaled_there, axis=0)
    in_term = lax.dot_general(rows_there, inner_grad, TN, preferred_element_type=f32).astype(bf)
    out_term = lax.dot_general(active, scaled_there, TN, preferred_element_type=f32).astype(bf)
    in_term, out_term, returned[0] = lax.optimization_barrier((in_term, out_term, returned[0]))
    grad_in = lax.psum_scatter(in_term, ("context", "dp"), scatter_dimension=0, tiled=True)
    grad_out_weight = lax.psum_scatter(out_term, ("context", "dp"), scatter_dimension=0, tiled=True)

    outputs, middle_grads, branches, joined_grad = [], [], [], None
    small = None
    for m in range(micro):
        (attended, mixed_low, log_total, middle, second_low, normal_two, scale_two, shares,
         choose_float, gate, _) = saved[m]
        grad_out = out_grad[m, 0].astype(f32)
        picked = lax.dot_general(place_two[m][0], returned[m], TN, preferred_element_type=f32)
        outputs.append((middle + gate[:, None] * picked).astype(bf))
        gate_grad = jnp.sum(grad_out * picked, axis=1)
        logit_grad = gate_grad[:, None] * gate[:, None] * (choose_float - shares)
        router_term = jnp.einsum("td,te->de", second_low.astype(f32), logit_grad, precision=HIGH)
        second_grad = jnp.einsum("te,de->td", logit_grad, router_float, precision=HIGH)
        second_grad = second_grad + lax.dot_general(
            place_two[m][1], returned[m], TN, preferred_element_type=f32
        )
        middle_part, gain_two, shift_two = norm_back(second_grad, normal_two, scale_two, expert_gain)
        middle_grad = grad_out + middle_part
        branch = middle_grad.astype(bf)
        mixed_grad = lax.dot_general(branch, project_out, NT, preferred_element_type=f32).astype(bf)
        query_grad, own, away = attn_bwd(
            joined, others[m], biases[m][1], log_total, mixed_grad, attended, m
        )
        if m + 1 < micro:
            own, away, returned[m + 1] = lax.optimization_barrier((own, away, returned[m + 1]))
        parts = [
            lax.ppermute(
                away[:, (s - 1) * rows : s * rows] if contexts > 2 else away,
                "context",
                [(i, (i - s) % contexts) for i in range(contexts)],
            )
            for s in range(1, contexts)
        ]
        joined_grad = merge(query_grad, own, parts, joined_grad, m, micro)
        middle_grads.append(middle_grad)
        branches.append(branch)
        terms = (gain_two, shift_two, router_term)
        small = terms if small is None else tuple(a + b for a, b in zip(small, terms))

    mixed_all = jnp.concatenate([s[1] for s in saved], axis=0)
    out_sum = lax.dot_general(
        mixed_all, jnp.concatenate(branches, axis=0), TN, preferred_element_type=f32
    ).astype(bf)
    out_sum, _ = sum_everywhere(out_sum, (model // 2, model // 2))

    in_sum = lax.dot_general(normed_low, joined_grad, TN, preferred_element_type=f32).astype(bf)
    in_sum, joined_grad = lax.optimization_barrier((in_sum, joined_grad))
    third = 3 * model // 6
    in_sum, (grad_in, grad_out_weight) = sum_everywhere(
        in_sum,
        ((3 * model - third) // 2, (3 * model - third) // 2, third),
        (grad_in, grad_out_weight),
    )
    normed_grad = lax.dot_general(joined_grad, project_in, NT, preferred_element_type=f32)
    input_part, gain_one, shift_one = norm_back(normed_grad, normal_one, scale_one, mixer_gain)
    grad_tokens = jnp.concatenate(middle_grads, axis=0) + input_part
    small = jnp.concatenate(
        [gain_one[None], shift_one[None], small[0][None], small[1][None], small[2].T], axis=0
    )
    small = sum_small(small)
    return (
        jnp.stack(outputs)[:, None],
        grad_tokens.reshape(micro, 1, rows, model),
        small[0],
        small[1],
        in_sum.astype(f32),
        out_sum.astype(f32),
        small[2],
        small[3],
        small[4:].T,
        grad_in[None],
        grad_out_weight[None],
    )


def solution(mesh):
    tokens = P(None, ("expert", "dp"), "context", None)
    packs = P(None, ("expert", "dp"), None)
    weights = P("expert", ("context", "dp"), None)
    in_specs = (tokens, tokens, packs, packs, tokens) + (P(),) * 7 + (weights, weights)
    out_specs = (tokens, tokens) + (P(),) * 7 + (weights, weights)
    return jax.shard_map(local, mesh=mesh, in_specs=in_specs, out_specs=out_specs, check_vma=False)
```

time: 1000 us -> 568 us (0.57)
  matrix products: 307 us -> 95.8 us
  waiting for transfers between devices: 360 us -> 155 us
  Pallas kernels: 0 us -> 124 us
  local copies, waits for them, and re-layouts: 140 us -> 22 us
  starting transfers between devices: 39.6 us -> 82.4 us
  blocking collectives: 42.4 us -> 0 us
  other arithmetic: 87 us -> 66.8 us
    psum x1 -> x0, waiting for transfers between devices: 282 us -> none  [reduce_grads(): dense = lax.psum(dense, ('expert', 'context', 'dp'))]
    dot_general x72 -> x22, matrix products: 304 us -> 92.8 us  [the longest x1 13.8 us: local(): lax.dot_general(active, scaled_there, TN, preferred_element_type=f32)]
    pallas_call x0 -> x8, Pallas kernels: none -> 124 us  [the longest x2 47.9 us: expert(): pl.pallas_call(exp_body, grid=(FF // fb,), in_specs=[pl.BlockSpec((rows,...]
    ppermute x0 -> x53, waiting for transfers between devices: none -> 108 us  [the longest x49 108 us: swap(): lax.ppermute(values, axis, [(i, i ^ bit) for i in range(lax.axis_size(axi...]
    unnamed x381 -> x99, local copies, waits for them, and re-layouts: 74.9 us -> 6.57 us
    ppermute x0 -> x53, starting transfers between devices: none -> 53.2 us  [the longest x49 52.1 us: swap(): lax.ppermute(values, axis, [(i, i ^ bit) for i in range(lax.axis_size(axi...]
    psum x1 -> x0, blocking collectives: 42.4 us -> none  [reduce_grads(): dense = lax.psum(dense, ('expert', 'context', 'dp'))]
    unnamed x11 -> x1, other arithmetic: 33.1 us -> 1.28 us
  transfers between devices with their start and end apart: 21 -> 62, of which waited for: 8 -> 36; matrix products, arithmetic and copies ran while one was open for 44% -> 30% of each run, Pallas kernels for 0% -> 18%
where the time goes in v1:
time: 568 us; the launch traced here: 561 us
  waiting for transfers between devices  155 us (27%)
  Pallas kernels  124 us (22%)
  matrix products  95.8 us (17%)
  starting transfers between devices  82.4 us (15%)
  other arithmetic  66.8 us (12%)
  local copies, waits for them, and re-layouts  22 us (4%)
  between operations  15.7 us (3%)
    ppermute x49, waiting for transfers between devices, swap(): lax.ppermute(values, axis, [(i, i ^ bit) for i in range(lax.axis_size(axi...  108 us
    ppermute x49, starting transfers between devices, swap(): lax.ppermute(values, axis, [(i, i ^ bit) for i in range(lax.axis_size(axi...  52.1 us
    pallas_call x2, Pallas kernels, expert(): pl.pallas_call(exp_body, grid=(FF // fb,), in_specs=[pl.BlockSpec((rows,...  47.9 us
    pallas_call x2, Pallas kernels, attn_bwd(): pl.pallas_call(partial(bwd_body, kb), grid=(G,), in_specs=[pl.BlockSpec(b...  40 us
    all_to_all x2, waiting for transfers between devices, local(): lax.all_to_all(sent.reshape(experts, block, model), 'expert', split_axis=...  37.7 us
    pallas_call x2, Pallas kernels, attn_fwd(): pl.pallas_call(partial(fwd_body, rb), grid=(G,), in_specs=[pl.BlockSpec(b...  25.3 us
    dot_general x1, matrix products, local(): lax.dot_general(active, scaled_there, TN, preferred_element_type=f32)  13.8 us
    dot_general x1, matrix products, local(): lax.dot_general(rows_there, inner_grad, TN, preferred_element_type=f32)  13.7 us
  transfers between devices with their start and end apart: 62, of which 36 were waited for; matrix products, arithmetic and copies ran while one was open for 30% of the time, Pallas kernels for 18%

profile of v1, /device:TPU:0, one launch (start us, length us, event | category | flops | bytes accessed | tf_op | source)
XLA Modules:
  0.0 561.5 jit_solution(3039386447455089017)
XLA Ops:
  16.7 2.1 add_convert_fusion
  18.7 9.5 %convolution_convert_fusion.3.q_ref.ko_ref.vo_ref = bf16[768,3072]{1,0:T(8,128)(2,1)S(1)} fusion(bf16[768,1024]{1,0:T(8,128)(2,1)S(1)} %add_convert_fusion, bf16[1024,3072]{1,0:T(8,128)(2,1)} %param.21), kind=kOutput, calls=%fused_computation.4 | convolution fusion | flops 4834197504 | bytes 12582912 | tf_op jit(solution)/shard_map/dot_general | solution.py:324
  28.2 2.2 fusion.104
  31.8 8.0 %all-to-all-start = ((bf16[8,2,56,1024]{3,2,1,0:T(8,128)(2,1)}), bf16[8,2,56,1024]{3,2,1,0:T(8,128)(2,1)}, u32[]{:S(2)}, u32[]{:S(2)}) async-start(bf16[8,2,56,1024]{3,2,1,0:T(8,128)(2,1)} %pad_maximum_fusion), calls=%async_computation | async-start | bytes 3670016 | tf_op jit(solution)/shard_map/all_to_all | solution.py:319
  39.9 3.5 convert_element_type.233
  48.9 12.7 %attn_fwd.2 = (f32[384,1024]{1,0:T(8,128)}, bf16[384,1024]{1,0:T(8,128)(2,1)}, f32[384,128]{1,0:T(8,128)}) custom-call(f32[384,768]{1,0:T(8,128)} %and_select_fusion.3.bias_ref, bf16[768,3072]{1,0:T(8,128)(2,1)} %copy-done.1, bf16[768,3072]{1,0:T(8,128)(2,1)} %copy-done.1, bf16[768,3072]{1,0:T(8,128)(2,1)} %copy-done.1, ...), custom_call_target="tpu_custom_call" | custom-call | flops 4831838208 | bytes 6291456 | tf_op jit(solution)/shard_map/attn_fwd/pallas_call | solution.py:45
  61.5 2.7 fusion.111
  67.9 12.6 %attn_fwd.3 = (f32[384,1024]{1,0:T(8,128)}, bf16[384,1024]{1,0:T(8,128)(2,1)}, f32[384,128]{1,0:T(8,128)}) custom-call(f32[384,768]{1,0:T(8,128)} %and_select_fusion.2.bias_ref, bf16[768,3072]{1,0:T(8,128)(2,1)} %copy-done.1, bf16[768,3072]{1,0:T(8,128)(2,1)} %copy-done.1, bf16[768,3072]{1,0:T(8,128)(2,1)} %copy-done.1, ...), custom_call_target="tpu_custom_call" | custom-call | flops 4831838208 | bytes 6291456 | tf_op jit(solution)/shard_map/attn_fwd/pallas_call | solution.py:45
  80.6 4.1 fusion.113
  84.7 6.0 %all-to-all-start.1 = ((bf16[8,56,1024]{2,1,0:T(8,128)(2,1)}), bf16[8,56,1024]{2,1,0:T(8,128)(2,1)}, u32[]{:S(2)}, u32[]{:S(2)}) async-start(bf16[8,56,1024]{2,1,0:T(8,128)(2,1)} %bitcast.17), calls=%async_computation.1 | async-start | bytes 1835008 | tf_op jit(solution)/shard_map/all_to_all | solution.py:398
  95.5 18.1 %all-to-all-done.1 = bf16[8,56,1024]{2,1,0:T(8,128)(2,1)} async-done(((bf16[8,56,1024]{2,1,0:T(8,128)(2,1)}), bf16[8,56,1024]{2,1,0:T(8,128)(2,1)}, u32[]{:S(2)}, u32[]{:S(2)}) %all-to-all-start.1) | async-done | bytes 917536 | tf_op jit(solution)/shard_map/all_to_all | solution.py:398
  113.6 4.2 all-to-all-start.2
  117.8 3.0 fusion.106
  120.8 19.6 %all-to-all-done.2 = bf16[8,56,1024]{2,1,0:T(8,128)(2,1)} async-done(((bf16[8,56,1024]{2,1,0:T(8,128)(2,1)}), bf16[8,56,1024]{2,1,0:T(8,128)(2,1)}, u32[]{:S(2)}, u32[]{:S(2)}) %all-to-all-start.2) | async-done | bytes 917536 | tf_op jit(solution)/shard_map/all_to_all | solution.py:398
  141.3 2.3 fusion.8.g_ref
  143.7 23.9 %expert.2 = (bf16[896,4096]{1,0:T(8,128)(2,1)}, bf16[896,4096]{1,0:T(8,128)(2,1)}, bf16[8,112,1024]{2,1,0:T(8,128)(2,1)}) custom-call(bf16[448,1024]{1,0:T(8,128)(2,1)} %bitcast.19.x_ref, bf16[448,1024]{1,0:T(8,128)(2,1)} %fusion.8.g_ref, bf16[1024,4096]{1,0:T(8,128)(2,1)} %bitcast.153, bf16[4096,1024]{1,0:T(8,128)(2,1)} %bitcast.155), custom_call_target="tpu_custom_call" | custom-call | flops 15032385536 | bytes 24117248 | tf_op jit(solution)/shard_map/expert/pallas_call | solution.py:142
  168.5 4.3 all-to-all-start.3
  173.4 2.3 fusion.7.g_ref
  175.7 23.9 %expert.3 = (bf16[896,4096]{1,0:T(8,128)(2,1)}, bf16[896,4096]{1,0:T(8,128)(2,1)}, bf16[8,112,1024]{2,1,0:T(8,128)(2,1)}) custom-call(bf16[448,1024]{1,0:T(8,128)(2,1)} %bitcast.23.x_ref, bf16[448,1024]{1,0:T(8,128)(2,1)} %fusion.7.g_ref, bf16[1024,4096]{1,0:T(8,128)(2,1)} %bitcast.154, ...), custom_call_target="tpu_custom_call", output_to_operand_aliasing={{0}: (4, {}), {1}: (5, {})} | custom-call | flops 15032385536 | bytes 24117248 | tf_op jit(solution)/shard_map/expert/pallas_call | solution.py:142
  199.6 13.8 %convolution_convert_fusion = bf16[4096,1024]{1,0:T(8,128)(2,1)} fusion(bf16[896,4096]{1,0:T(8,128)(2,1)} %get-tuple-element.111, bf16[448,1024]{1,0:T(8,128)(2,1)} %fusion.7.g_ref, bf16[448,1024]{1,0:T(8,128)(2,1)} %fusion.8.g_ref), kind=kOutput, calls=%fused_computation | convolution fusion | flops 7524057088 | bytes 17563648 | tf_op jit(solution)/shard_map/dot_general | solution.py:435
  213.4 13.7 %convolution_convert_fusion.1 = bf16[1024,4096]{1,0:T(8,128)(2,1)} fusion(bf16[896,4096]{1,0:T(8,128)(2,1)} %get-tuple-element.110, bf16[448,1024]{1,0:T(8,128)(2,1)} %bitcast.23.x_ref, bf16[448,1024]{1,0:T(8,128)(2,1)} %bitcast.19.x_ref), kind=kOutput, calls=%fused_computation.1 | convolution fusion | flops 7524057088 | bytes 17563648 | tf_op jit(solution)/shard_map/dot_general | solution.py:434
  230.1 5.9 %all-to-all-start.4 = ((bf16[8,112,1024]{2,1,0:T(8,128)(2,1)}), bf16[8,112,1024]{2,1,0:T(8,128)(2,1)}, u32[]{:S(2)}, u32[]{:S(2)}) async-start(bf16[8,112,1024]{2,1,0:T(8,128)(2,1)} %get-tuple-element.118), calls=%async_computation.4 | async-start | bytes 3670016 | tf_op jit(solution)/shard_map/all_to_all | solution.py:427
  236.2 5.2 fusion.39
  241.5 3.0 fusion.37
  249.8 19.9 %attn_bwd.2 = (bf16[384,1024]{1,0:T(8,128)(2,1)}, f32[2,384,1024]{2,1,0:T(8,128)}, bf16[2,384,1024]{2,1,0:T(8,128)(2,1)}) custom-call(f32[768,384]{1,0:T(8,128)} %and_select_fusion.1.biast_ref, f32[16,384]{1,0:T(8,128)} %slice_bitcast_fusion.4.lse_ref, bf16[768,3072]{1,0:T(8,128)(2,1)} %copy-done.1, bf16[768,3072]{1,0:T(8,128)(2,1)} %copy-done.1, ...), custom_call_target="tpu_custom_call" | custom-call | flops 12079595520 | bytes 11796480 | tf_op jit(solution)/shard_map/attn_bwd/pallas_call | solution.py:95
  269.7 7.8 %all-to-all-done.4 = bf16[8,112,1024]{2,1,0:T(8,128)(2,1)} async-done(((bf16[8,112,1024]{2,1,0:T(8,128)(2,1)}), bf16[8,112,1024]{2,1,0:T(8,128)(2,1)}, u32[]{:S(2)}, u32[]{:S(2)}) %all-to-all-start.4) | async-done | bytes 1835040 | tf_op jit(solution)/shard_map/all_to_all | solution.py:427
  277.6 3.0 fusion.10
  280.6 2.6 fusion.38
  284.8 2.1 fusion.102
  293.7 3.1 convolution_convert_fusion.7.do_ref
  303.9 20.1 %attn_bwd.3 = (bf16[384,1024]{1,0:T(8,128)(2,1)}, f32[2,384,1024]{2,1,0:T(8,128)}, bf16[2,384,1024]{2,1,0:T(8,128)(2,1)}) custom-call(f32[768,384]{1,0:T(8,128)} %and_select_fusion.biast_ref, f32[16,384]{1,0:T(8,128)} %slice_bitcast_fusion.3.lse_ref, bf16[768,3072]{1,0:T(8,128)(2,1)} %copy-done.1, bf16[768,3072]{1,0:T(8,128)(2,1)} %copy-done.1, ...), custom_call_target="tpu_custom_call" | custom-call | flops 12079595520 | bytes 11796480 | tf_op jit(solution)/shard_map/attn_bwd/pallas_call | solution.py:95
  328.0 4.3 collective-permute-done.39
  333.2 2.0 collective-permute-start.40
  335.2 2.2 collective-permute-done.41
  338.2 5.2 merge.2.refs_1_
  343.4 5.2 merge.3
  348.5 7.5 %convolution_convert_fusion.2 = bf16[1024,3072]{1,0:T(8,128)(2,1)S(1)} fusion(bf16[768,1024]{1,0:T(8,128)(2,1)} %copy-done.18, bf16[768,3072]{1,0:T(8,128)(2,1)} %merge.3), kind=kOutput, calls=%fused_computation.3 | convolution fusion | flops 4834983936 | bytes 12582912 | tf_op jit(solution)/shard_map/dot_general | solution.py:484
  356.0 2.1 constant_dynamic-slice_fusion.21
  362.6 3.4 collective-permute-done.43
  367.9 2.2 collective-permute-start.44
  374.6 13.1 %multiply_reduce_fusion = (f32[1024]{0:T(1024)S(1)}, f32[768]{0:T(1024)}, f32[768]{0:T(1024)S(1)}, f32[1024]{0:T(1024)S(1)}, f32[768,1024]{1,0:T(8,128)}) fusion(bf16[2,1,384,1024]{3,2,1,0:T(8,128)(2,1)} %param.14, f32[768]{0:T(1024)S(1)} %copy-done.37, f32[768]{0:T(1024)S(1)} %copy-done.35, f32[1024]{0:T(1024)S(1)} %copy-done.39, ...), kind=kOutput, calls=%fused_computation.9 | convolution fusion | flops 4839698432 | bytes 15753216 | tf_op jit(solution)/shard_map/dot_general | solution.py:492
  390.4 4.1 dynamic-slice_add_fusion
  399.5 3.4 collective-permute-done.12
  403.0 24.5 %collective-permute-done.11 = bf16[256,1280]{1,0:T(8,128)(2,1)S(1)} collective-permute-done((bf16[256,1280]{1,0:T(8,128)(2,1)S(1)}, bf16[256,1280]{1,0:T(8,128)(2,1)S(1)}, u32[]{:S(2)}, u32[]{:S(2)}) %collective-permute-start.11) | collective-permute-done | bytes 655392 | tf_op jit(solution)/shard_map/ppermute | solution.py:198
  432.3 3.7 collective-permute-done.15
  437.4 9.7 %collective-permute-done.13 = bf16[128,1280]{1,0:T(8,128)(2,1)S(1)} collective-permute-done((bf16[128,1280]{1,0:T(8,128)(2,1)S(1)}, bf16[128,1280]{1,0:T(8,128)(2,1)S(1)}, u32[]{:S(2)}, u32[]{:S(2)}) %collective-permute-start.13) | collective-permute-done | bytes 327712 | tf_op jit(solution)/shard_map/ppermute | solution.py:198
  457.1 2.3 collective-permute-start.20
  460.1 3.3 collective-permute-done.20
  463.4 4.5 collective-permute-done.19
  468.1 2.9 collective-permute-start.22
  476.6 2.0 collective-permute-start.48
  478.6 2.6 collective-permute-start.26
  481.3 3.9 collective-permute-done.26
  491.4 2.9 collective-permute-done.30
  498.2 4.1 convert_element_type.276
  502.3 4.1 convert_element_type.277
  509.4 3.5 collective-permute-done.33
  512.9 5.0 collective-permute-done.32
  524.7 3.8 collective-permute-done.6
  530.3 6.7 %collective-permute-done.50 = bf16[256,512]{1,0:T(8,128)(2,1)S(1)} collective-permute-done((bf16[256,512]{1,0:T(8,128)(2,1)S(1)}, bf16[256,512]{1,0:T(8,128)(2,1)S(1)}, u32[]{:S(2)}, u32[]{:S(2)}) %collective-permute-start.50) | collective-permute-done | bytes 262176 | tf_op jit(solution)/shard_map/ppermute | solution.py:198
  539.0 2.9 maximum_add_fusion
  541.8 2.4 collective-permute-done.8
  545.6 2.4 maximum_convert_fusion.1
  548.5 6.0 %maximum_convert_fusion = f32[1024,3072]{1,0:T(8,128)} fusion(bf16[512,3072]{1,0:T(8,128)(2,1)S(1)} %get-tuple-element.254, bf16[512,3072]{1,0:T(8,128)(2,1)S(1)} %get-tuple-element.253), kind=kLoop, calls=%fused_computation.2 | loop fusion | flops 12582912 | bytes 18874368 | tf_op jit(solution)/shard_map/convert_element_type | solution.py:504
  (383 shorter events, 122.8 us)
Async XLA Ops:
  7.2 54.4 %copy-start = (bf16[1024,1024]{1,0:T(8,128)(2,1)S(1)}, bf16[1024,1024]{1,0:T(8,128)(2,1)}, u32[]{:S(2)}) copy-start(bf16[1024,1024]{1,0:T(8,128)(2,1)} %param.22) | copy-start | bytes 6291460
  7.2 136.5 %all-gather.5.cloned.1.call-start = ((), (), s32[]{:S(2)}) async-start(), calls=%async_computation.9 | async-start | bytes 10485760 | tf_op jit(solution)/shard_map/all_gather | solution.py:292
  7.9 135.7 %all-gather.7.cloned.1.call-start = ((), (), s32[]{:S(2)}) async-start(), calls=%async_computation.10 | async-start | bytes 10485760 | tf_op jit(solution)/shard_map/all_gather | solution.py:293
  31.3 17.6 %collective-permute-start = (bf16[384,2048]{1,0:T(8,128)(2,1)}, bf16[384,2048]{1,0:T(8,128)(2,1)}, u32[]{:S(2)}, u32[]{:S(2)}) collective-permute-start(bf16[384,2048]{1,0:T(8,128)(2,1)} %get-tuple-element.256), channel_id=1, source_target_pairs={{0,2},{2,0},{1,3},{3,1},{4,6},{6,4},{5,7},{7,5},{8,10},{10,8},{9,1... | collective-permute-start | bytes 4718600 | tf_op jit(solution)/shard_map/ppermute | solution.py:329
  31.8 36.2 %collective-permute-start.1 = (bf16[384,2048]{1,0:T(8,128)(2,1)}, bf16[384,2048]{1,0:T(8,128)(2,1)}, u32[]{:S(2)}, u32[]{:S(2)}) collective-permute-start(bf16[384,2048]{1,0:T(8,128)(2,1)} %get-tuple-element.255), channel_id=1, source_target_pairs={{0,2},{2,0},{1,3},{3,1},{4,6},{6,4},{5,7},{7,5},{8,10},{10,8},{9,1... | collective-permute-start | bytes 4718600 | tf_op jit(solution)/shard_map/ppermute | solution.py:329
  31.8 52.9 %all-to-all-start = ((bf16[8,2,56,1024]{3,2,1,0:T(8,128)(2,1)}), bf16[8,2,56,1024]{3,2,1,0:T(8,128)(2,1)}, u32[]{:S(2)}, u32[]{:S(2)}) async-start(bf16[8,2,56,1024]{3,2,1,0:T(8,128)(2,1)} %pad_maximum_fusion), calls=%async_computation | async-start | bytes 3670016 | tf_op jit(solution)/shard_map/all_to_all | solution.py:319
  84.7 28.9 %all-to-all-start.1 = ((bf16[8,56,1024]{2,1,0:T(8,128)(2,1)}), bf16[8,56,1024]{2,1,0:T(8,128)(2,1)}, u32[]{:S(2)}, u32[]{:S(2)}) async-start(bf16[8,56,1024]{2,1,0:T(8,128)(2,1)} %bitcast.17), calls=%async_computation.1 | async-start | bytes 1835008 | tf_op jit(solution)/shard_map/all_to_all | solution.py:398
  113.6 26.8 %all-to-all-start.2 = ((bf16[8,56,1024]{2,1,0:T(8,128)(2,1)}), bf16[8,56,1024]{2,1,0:T(8,128)(2,1)}, u32[]{:S(2)}, u32[]{:S(2)}) async-start(bf16[8,56,1024]{2,1,0:T(8,128)(2,1)} %bitcast.138), calls=%async_computation.2 | async-start | bytes 1835008 | tf_op jit(solution)/shard_map/all_to_all | solution.py:398
  168.5 58.6 %all-to-all-start.3 = ((bf16[8,112,1024]{2,1,0:T(8,128)(2,1)}), bf16[8,112,1024]{2,1,0:T(8,128)(2,1)}, u32[]{:S(2)}, u32[]{:S(2)}) async-start(bf16[8,112,1024]{2,1,0:T(8,128)(2,1)} %get-tuple-element.112), calls=%async_computation.3 | async-start | bytes 3670016 | tf_op jit(solution)/shard_map/all_to_all | solution.py:427
  172.9 325.3 %reduce-scatter.3.cloned.1.call-start = ((), (), s32[]{:S(2)}) async-start(), calls=%async_computation.7 | async-start | bytes 10485760 | tf_op jit(solution)/shard_map/reduce_scatter | solution.py:437
  230.1 47.4 %all-to-all-start.4 = ((bf16[8,112,1024]{2,1,0:T(8,128)(2,1)}), bf16[8,112,1024]{2,1,0:T(8,128)(2,1)}, u32[]{:S(2)}, u32[]{:S(2)}) async-start(bf16[8,112,1024]{2,1,0:T(8,128)(2,1)} %get-tuple-element.118), calls=%async_computation.4 | async-start | bytes 3670016 | tf_op jit(solution)/shard_map/all_to_all | solution.py:427
  236.0 266.3 %reduce-scatter.5.cloned.1.call-start = ((), (), s32[]{:S(2)}) async-start(), calls=%async_computation.8 | async-start | bytes 10485760 | tf_op jit(solution)/shard_map/reduce_scatter | solution.py:438
  291.1 5.8 %collective-permute-start.35 = (bf16[512,1024]{1,0:T(8,128)(2,1)}, bf16[512,1024]{1,0:T(8,128)(2,1)}, u32[]{:S(2)}, u32[]{:S(2)}) collective-permute-start(bf16[512,1024]{1,0:T(8,128)(2,1)} %constant_dynamic-slice_fusion.8), channel_id=1, source_target_pairs={{0,2},{2,0},{1,3},{3,1},{4,6},{6,4},{5,7},{7,5},{8,10},{10,8},{9,1... | collective-permute-start | bytes 3145736 | tf_op jit(solution)/shard_map/ppermute | solution.py:198
  293.2 45.0 %collective-permute-start.3 = (bf16[2,384,1024]{2,1,0:T(8,128)(2,1)}, bf16[2,384,1024]{2,1,0:T(8,128)(2,1)}, u32[]{:S(2)}, u32[]{:S(2)}) collective-permute-start(bf16[2,384,1024]{2,1,0:T(8,128)(2,1)} %get-tuple-element.127), channel_id=1, source_target_pairs={{0,2},{2,0},{1,3},{3,1},{4,6},{6,4},{5,7},{7,5},{8,10},{10,8},{9,1... | collective-permute-start | bytes 4718600 | tf_op jit(solution)/shard_map/ppermute | solution.py:465
  300.1 23.9 %collective-permute-start.37 = (bf16[256,512]{1,0:T(8,128)(2,1)}, bf16[256,512]{1,0:T(8,128)(2,1)}, u32[]{:S(2)}, u32[]{:S(2)}) collective-permute-start(bf16[256,512]{1,0:T(8,128)(2,1)} %constant_dynamic-slice_fusion.6), channel_id=1, source_target_pairs={{0,1},{1,0},{2,3},{3,2},{4,5},{5,4},{6,7},{7,6},{8,9},{9,8},{10,11... | collective-permute-start | bytes 786440 | tf_op jit(solution)/shard_map/ppermute | solution.py:198
  302.5 22.8 %collective-permute-start.36 = (bf16[256,512]{1,0:T(8,128)(2,1)}, bf16[256,512]{1,0:T(8,128)(2,1)}, u32[]{:S(2)}, u32[]{:S(2)}) collective-permute-start(bf16[256,512]{1,0:T(8,128)(2,1)} %constant_dynamic-slice_fusion.7), channel_id=1, source_target_pairs={{0,4},{4,0},{8,12},{12,8},{16,20},{20,16},{24,28},{28,24},{1,5},{5... | collective-permute-start | bytes 786440 | tf_op jit(solution)/shard_map/ppermute | solution.py:198
  324.0 19.4 %collective-permute-start.2 = (bf16[2,384,1024]{2,1,0:T(8,128)(2,1)}, bf16[2,384,1024]{2,1,0:T(8,128)(2,1)}, u32[]{:S(2)}, u32[]{:S(2)}) collective-permute-start(bf16[2,384,1024]{2,1,0:T(8,128)(2,1)} %get-tuple-element.124), channel_id=1, source_target_pairs={{0,2},{2,0},{1,3},{3,1},{4,6},{6,4},{5,7},{7,5},{8,10},{10,8},{9,1... | collective-permute-start | bytes 4718600 | tf_op jit(solution)/shard_map/ppermute | solution.py:465
  326.3 5.9 %collective-permute-start.39 = (bf16[128,512]{1,0:T(8,128)(2,1)S(1)}, bf16[128,512]{1,0:T(8,128)(2,1)S(1)}, u32[]{:S(2)}, u32[]{:S(2)}) collective-permute-start(bf16[128,512]{1,0:T(8,128)(2,1)S(1)} %constant_dynamic-slice_fusion.4), channel_id=1, source_target_pairs={{0,4},{4,0},{8,12},{12,8},{16,20},{20,16},{24,28},{28,24},{1,5},{5... | collective-permute-start | bytes 393224 | tf_op jit(solution)/shard_map/ppermute | solution.py:198
  327.4 5.6 %collective-permute-start.38 = (bf16[128,512]{1,0:T(8,128)(2,1)S(1)}, bf16[128,512]{1,0:T(8,128)(2,1)S(1)}, u32[]{:S(2)}, u32[]{:S(2)}) collective-permute-start(bf16[128,512]{1,0:T(8,128)(2,1)S(1)} %constant_dynamic-slice_fusion.5), channel_id=1, source_target_pairs={{0,1},{1,0},{2,3},{3,2},{4,5},{5,4},{6,7},{7,6},{8,9},{9,8},{10,11... | collective-permute-start | bytes 393224 | tf_op jit(solution)/shard_map/ppermute | solution.py:198
  333.1 4.3 collective-permute-start.41
  333.2 4.9 collective-permute-start.40
  359.6 30.8 %collective-permute-start.9 = (bf16[512,3072]{1,0:T(8,128)(2,1)}, bf16[512,3072]{1,0:T(8,128)(2,1)}, u32[]{:S(2)}, u32[]{:S(2)}) collective-permute-start(bf16[512,3072]{1,0:T(8,128)(2,1)} %constant_dynamic-slice_fusion.21), channel_id=1, source_target_pairs={{0,2},{2,0},{1,3},{3,1},{4,6},{6,4},{5,7},{7,5},{8,10},{10,8},{9,1... | collective-permute-start | bytes 9437192 | tf_op jit(solution)/shard_map/ppermute | solution.py:198
  359.6 6.3 %collective-permute-start.43 = (bf16[32,512]{1,0:T(8,128)(2,1)S(1)}, bf16[32,512]{1,0:T(8,128)(2,1)S(1)}, u32[]{:S(2)}, u32[]{:S(2)}) collective-permute-start(bf16[32,512]{1,0:T(8,128)(2,1)S(1)} %constant_dynamic-slice_fusion), channel_id=1, source_target_pairs={{0,16},{4,20},{8,24},{12,28},{16,0},{20,4},{24,8},{28,12},{1,17},{... | collective-permute-start | bytes 98312 | tf_op jit(solution)/shard_map/ppermute | solution.py:198
  360.6 5.9 %collective-permute-start.42 = (bf16[32,512]{1,0:T(8,128)(2,1)S(1)}, bf16[32,512]{1,0:T(8,128)(2,1)S(1)}, u32[]{:S(2)}, u32[]{:S(2)}) collective-permute-start(bf16[32,512]{1,0:T(8,128)(2,1)S(1)} %constant_dynamic-slice_fusion.1), channel_id=1, source_target_pairs={{0,16},{4,20},{8,24},{12,28},{16,0},{20,4},{24,8},{28,12},{1,17},{... | collective-permute-start | bytes 98312 | tf_op jit(solution)/shard_map/ppermute | solution.py:198
  366.6 5.3 collective-permute-start.45
  367.9 4.9 collective-permute-start.44
  372.8 17.6 %collective-permute-start.47 = (bf16[64,512]{1,0:T(8,128)(2,1)S(1)}, bf16[64,512]{1,0:T(8,128)(2,1)S(1)}, u32[]{:S(2)}, u32[]{:S(2)}) collective-permute-start(bf16[64,512]{1,0:T(8,128)(2,1)S(1)} %pad_maximum_fusion.20), channel_id=1, source_target_pairs={{0,8},{4,12},{8,0},{12,4},{16,24},{20,28},{24,16},{28,20},{1,9},{5... | collective-permute-start | bytes 196616 | tf_op jit(solution)/shard_map/ppermute | solution.py:198
  388.1 1.3 collective-permute-start.4
  388.3 9.6 %collective-permute-start.46 = (bf16[64,512]{1,0:T(8,128)(2,1)S(1)}, bf16[64,512]{1,0:T(8,128)(2,1)S(1)}, u32[]{:S(2)}, u32[]{:S(2)}) collective-permute-start(bf16[64,512]{1,0:T(8,128)(2,1)S(1)} %pad_maximum_fusion.19), channel_id=1, source_target_pairs={{0,8},{4,12},{8,0},{12,4},{16,24},{20,28},{24,16},{28,20},{1,9},{5... | collective-permute-start | bytes 196616 | tf_op jit(solution)/shard_map/ppermute | solution.py:198
  390.1 133.0 %collective-permute-start.5 = (f32[12,1024]{1,0:T(8,128)}, f32[12,1024]{1,0:T(8,128)}, u32[]{:S(2)}, u32[]{:S(2)}) collective-permute-start(f32[12,1024]{1,0:T(8,128)} %add.507), channel_id=1, source_target_pairs={{0,1},{1,0},{2,3},{3,2},{4,5},{5,4},{6,7},{7,6},{8,9},{9,8},{10,11... | collective-permute-start | bytes 147464 | tf_op jit(solution)/shard_map/ppermute | solution.py:198
  394.6 8.3 %collective-permute-start.12 = (bf16[256,512]{1,0:T(8,128)(2,1)S(1)}, bf16[256,512]{1,0:T(8,128)(2,1)S(1)}, u32[]{:S(2)}, u32[]{:S(2)}) collective-permute-start(bf16[256,512]{1,0:T(8,128)(2,1)S(1)} %constant_dynamic-slice_fusion.18), channel_id=1, source_target_pairs={{0,8},{4,12},{8,0},{12,4},{16,24},{20,28},{24,16},{28,20},{1,9},{5... | collective-permute-start | bytes 786440 | tf_op jit(solution)/shard_map/ppermute | solution.py:198
  396.3 31.2 %collective-permute-start.11 = (bf16[256,1280]{1,0:T(8,128)(2,1)S(1)}, bf16[256,1280]{1,0:T(8,128)(2,1)S(1)}, u32[]{:S(2)}, u32[]{:S(2)}) collective-permute-start(bf16[256,1280]{1,0:T(8,128)(2,1)S(1)} %constant_dynamic-slice_fusion.19), channel_id=1, source_target_pairs={{0,1},{1,0},{2,3},{3,2},{4,5},{5,4},{6,7},{7,6},{8,9},{9,8},{10,11... | collective-permute-start | bytes 1966088 | tf_op jit(solution)/shard_map/ppermute | solution.py:198
  398.0 29.7 %collective-permute-start.10 = (bf16[256,1280]{1,0:T(8,128)(2,1)S(1)}, bf16[256,1280]{1,0:T(8,128)(2,1)S(1)}, u32[]{:S(2)}, u32[]{:S(2)}) collective-permute-start(bf16[256,1280]{1,0:T(8,128)(2,1)S(1)} %constant_dynamic-slice_fusion.20), channel_id=1, source_target_pairs={{0,4},{4,0},{8,12},{12,8},{16,20},{20,16},{24,28},{28,24},{1,5},{5... | collective-permute-start | bytes 1966088 | tf_op jit(solution)/shard_map/ppermute | solution.py:198
  427.9 8.1 %collective-permute-start.15 = (bf16[128,512]{1,0:T(8,128)(2,1)S(1)}, bf16[128,512]{1,0:T(8,128)(2,1)S(1)}, u32[]{:S(2)}, u32[]{:S(2)}) collective-permute-start(bf16[128,512]{1,0:T(8,128)(2,1)S(1)} %constant_dynamic-slice_fusion.15), channel_id=1, source_target_pairs={{0,16},{4,20},{8,24},{12,28},{16,0},{20,4},{24,8},{28,12},{1,17},{... | collective-permute-start | bytes 393224 | tf_op jit(solution)/shard_map/ppermute | solution.py:198
  428.9 8.5 %collective-permute-start.14 = (bf16[128,1280]{1,0:T(8,128)(2,1)S(1)}, bf16[128,1280]{1,0:T(8,128)(2,1)S(1)}, u32[]{:S(2)}, u32[]{:S(2)}) collective-permute-start(bf16[128,1280]{1,0:T(8,128)(2,1)S(1)} %constant_dynamic-slice_fusion.16), channel_id=1, source_target_pairs={{0,4},{4,0},{8,12},{12,8},{16,20},{20,16},{24,28},{28,24},{1,5},{5... | collective-permute-start | bytes 983048 | tf_op jit(solution)/shard_map/ppermute | solution.py:198
  430.3 16.8 %collective-permute-start.13 = (bf16[128,1280]{1,0:T(8,128)(2,1)S(1)}, bf16[128,1280]{1,0:T(8,128)(2,1)S(1)}, u32[]{:S(2)}, u32[]{:S(2)}) collective-permute-start(bf16[128,1280]{1,0:T(8,128)(2,1)S(1)} %constant_dynamic-slice_fusion.17), channel_id=1, source_target_pairs={{0,1},{1,0},{2,3},{3,2},{4,5},{5,4},{6,7},{7,6},{8,9},{9,8},{10,11... | collective-permute-start | bytes 983048 | tf_op jit(solution)/shard_map/ppermute | solution.py:198
  447.2 4.3 collective-permute-start.18
  448.0 5.4 collective-permute-start.17
  449.0 6.1 %collective-permute-start.16 = (bf16[64,1280]{1,0:T(8,128)(2,1)S(1)}, bf16[64,1280]{1,0:T(8,128)(2,1)S(1)}, u32[]{:S(2)}, u32[]{:S(2)}) collective-permute-start(bf16[64,1280]{1,0:T(8,128)(2,1)S(1)} %constant_dynamic-slice_fusion.14), channel_id=1, source_target_pairs={{0,8},{4,12},{8,0},{12,4},{16,24},{20,28},{24,16},{28,20},{1,9},{5... | collective-permute-start | bytes 491528 | tf_op jit(solution)/shard_map/ppermute | solution.py:198
  455.2 4.8 collective-permute-start.21
  457.1 6.2 %collective-permute-start.20 = (bf16[32,1280]{1,0:T(8,128)(2,1)S(1)}, bf16[32,1280]{1,0:T(8,128)(2,1)S(1)}, u32[]{:S(2)}, u32[]{:S(2)}) collective-permute-start(bf16[32,1280]{1,0:T(8,128)(2,1)S(1)} %constant_dynamic-slice_fusion.10), channel_id=1, source_target_pairs={{0,16},{4,20},{8,24},{12,28},{16,0},{20,4},{24,8},{28,12},{1,17},{... | collective-permute-start | bytes 245768 | tf_op jit(solution)/shard_map/ppermute | solution.py:198
  459.4 8.5 %collective-permute-start.19 = (bf16[32,1280]{1,0:T(8,128)(2,1)S(1)}, bf16[32,1280]{1,0:T(8,128)(2,1)S(1)}, u32[]{:S(2)}, u32[]{:S(2)}) collective-permute-start(bf16[32,1280]{1,0:T(8,128)(2,1)S(1)} %constant_dynamic-slice_fusion.11), channel_id=1, source_target_pairs={{0,16},{4,20},{8,24},{12,28},{16,0},{20,4},{24,8},{28,12},{1,17},{... | collective-permute-start | bytes 245768 | tf_op jit(solution)/shard_map/ppermute | solution.py:198
  467.9 4.0 collective-permute-start.24
  468.0 5.4 collective-permute-start.23
  468.1 6.3 %collective-permute-start.22 = (bf16[32,1280]{1,0:T(8,128)(2,1)S(1)}, bf16[32,1280]{1,0:T(8,128)(2,1)S(1)}, u32[]{:S(2)}, u32[]{:S(2)}) collective-permute-start(bf16[32,1280]{1,0:T(8,128)(2,1)S(1)} %dynamic-slice_add_fusion.15), channel_id=1, source_target_pairs={{0,16},{4,20},{8,24},{12,28},{16,0},{20,4},{24,8},{28,12},{1,17},{... | collective-permute-start | bytes 245768 | tf_op jit(solution)/shard_map/ppermute | solution.py:198
  474.4 6.7 %collective-permute-start.27 = (bf16[64,512]{1,0:T(8,128)(2,1)S(1)}, bf16[64,512]{1,0:T(8,128)(2,1)S(1)}, u32[]{:S(2)}, u32[]{:S(2)}) collective-permute-start(bf16[64,512]{1,0:T(8,128)(2,1)S(1)} %pad_maximum_fusion.18), channel_id=1, source_target_pairs={{0,4},{4,0},{8,12},{12,8},{16,20},{20,16},{24,28},{28,24},{1,5},{5... | collective-permute-start | bytes 196616 | tf_op jit(solution)/shard_map/ppermute | solution.py:198
  476.1 12.6 %collective-permute-start.49 = (bf16[128,512]{1,0:T(8,128)(2,1)S(1)}, bf16[128,512]{1,0:T(8,128)(2,1)S(1)}, u32[]{:S(2)}, u32[]{:S(2)}) collective-permute-start(bf16[128,512]{1,0:T(8,128)(2,1)S(1)} %pad_maximum_fusion.17), channel_id=1, source_target_pairs={{0,4},{4,0},{8,12},{12,8},{16,20},{20,16},{24,28},{28,24},{1,5},{5... | collective-permute-start | bytes 393224 | tf_op jit(solution)/shard_map/ppermute | solution.py:198
  476.6 31.3 %collective-permute-start.48 = (bf16[128,512]{1,0:T(8,128)(2,1)S(1)}, bf16[128,512]{1,0:T(8,128)(2,1)}, u32[]{:S(2)}, u32[]{:S(2)}) collective-permute-start(bf16[128,512]{1,0:T(8,128)(2,1)S(1)} %pad_maximum_fusion.16), channel_id=1, source_target_pairs={{0,1},{1,0},{2,3},{3,2},{4,5},{5,4},{6,7},{7,6},{8,9},{9,8},{10,11... | collective-permute-start | bytes 393224 | tf_op jit(solution)/shard_map/ppermute | solution.py:198
  478.6 6.6 %collective-permute-start.26 = (bf16[64,1280]{1,0:T(8,128)(2,1)S(1)}, bf16[64,1280]{1,0:T(8,128)(2,1)S(1)}, u32[]{:S(2)}, u32[]{:S(2)}) collective-permute-start(bf16[64,1280]{1,0:T(8,128)(2,1)S(1)} %pad_maximum_fusion.14), channel_id=1, source_target_pairs={{0,8},{4,12},{8,0},{12,4},{16,24},{20,28},{24,16},{28,20},{1,9},{5... | collective-permute-start | bytes 491528 | tf_op jit(solution)/shard_map/ppermute | solution.py:198
  481.2 5.8 %collective-permute-start.25 = (bf16[64,1280]{1,0:T(8,128)(2,1)S(1)}, bf16[64,1280]{1,0:T(8,128)(2,1)S(1)}, u32[]{:S(2)}, u32[]{:S(2)}) collective-permute-start(bf16[64,1280]{1,0:T(8,128)(2,1)S(1)} %pad_maximum_fusion.13), channel_id=1, source_target_pairs={{0,8},{4,12},{8,0},{12,4},{16,24},{20,28},{24,16},{28,20},{1,9},{5... | collective-permute-start | bytes 491528 | tf_op jit(solution)/shard_map/ppermute | solution.py:198
  487.0 7.3 %collective-permute-start.30 = (bf16[128,512]{1,0:T(8,128)(2,1)S(1)}, bf16[128,512]{1,0:T(8,128)(2,1)S(1)}, u32[]{:S(2)}, u32[]{:S(2)}) collective-permute-start(bf16[128,512]{1,0:T(8,128)(2,1)S(1)} %pad_maximum_fusion.15), channel_id=1, source_target_pairs={{0,16},{4,20},{8,24},{12,28},{16,0},{20,4},{24,8},{28,12},{1,17},{... | collective-permute-start | bytes 393224 | tf_op jit(solution)/shard_map/ppermute | solution.py:198
  489.4 7.1 %collective-permute-start.29 = (bf16[128,1280]{1,0:T(8,128)(2,1)S(1)}, bf16[128,1280]{1,0:T(8,128)(2,1)S(1)}, u32[]{:S(2)}, u32[]{:S(2)}) collective-permute-start(bf16[128,1280]{1,0:T(8,128)(2,1)S(1)} %pad_maximum_fusion.9), channel_id=1, source_target_pairs={{0,4},{4,0},{8,12},{12,8},{16,20},{20,16},{24,28},{28,24},{1,5},{5... | collective-permute-start | bytes 983048 | tf_op jit(solution)/shard_map/ppermute | solution.py:198
  491.0 7.1 %collective-permute-start.28 = (bf16[128,1280]{1,0:T(8,128)(2,1)S(1)}, bf16[128,1280]{1,0:T(8,128)(2,1)S(1)}, u32[]{:S(2)}, u32[]{:S(2)}) collective-permute-start(bf16[128,1280]{1,0:T(8,128)(2,1)S(1)} %pad_maximum_fusion.8), channel_id=1, source_target_pairs={{0,1},{1,0},{2,3},{3,2},{4,5},{5,4},{6,7},{7,6},{8,9},{9,8},{10,11... | collective-permute-start | bytes 983048 | tf_op jit(solution)/shard_map/ppermute | solution.py:198
  506.4 6.4 %collective-permute-start.33 = (bf16[256,512]{1,0:T(8,128)(2,1)S(1)}, bf16[256,512]{1,0:T(8,128)(2,1)S(1)}, u32[]{:S(2)}, u32[]{:S(2)}) collective-permute-start(bf16[256,512]{1,0:T(8,128)(2,1)S(1)} %copy-done.22), channel_id=1, source_target_pairs={{0,8},{4,12},{8,0},{12,4},{16,24},{20,28},{24,16},{28,20},{1,9},{5... | collective-permute-start | bytes 786440 | tf_op jit(solution)/shard_map/ppermute | solution.py:198
  507.3 10.6 %collective-permute-start.32 = (bf16[256,1280]{1,0:T(8,128)(2,1)S(1)}, bf16[256,1280]{1,0:T(8,128)(2,1)S(1)}, u32[]{:S(2)}, u32[]{:S(2)}) collective-permute-start(bf16[256,1280]{1,0:T(8,128)(2,1)S(1)} %pad_maximum_fusion.4), channel_id=1, source_target_pairs={{0,1},{1,0},{2,3},{3,2},{4,5},{5,4},{6,7},{7,6},{8,9},{9,8},{10,11... | collective-permute-start | bytes 1966088 | tf_op jit(solution)/shard_map/ppermute | solution.py:198
  508.8 10.7 %collective-permute-start.31 = (bf16[256,1280]{1,0:T(8,128)(2,1)S(1)}, bf16[256,1280]{1,0:T(8,128)(2,1)S(1)}, u32[]{:S(2)}, u32[]{:S(2)}) collective-permute-start(bf16[256,1280]{1,0:T(8,128)(2,1)S(1)} %pad_maximum_fusion.3), channel_id=1, source_target_pairs={{0,4},{4,0},{8,12},{12,8},{16,20},{20,16},{24,28},{28,24},{1,5},{5... | collective-permute-start | bytes 1966088 | tf_op jit(solution)/shard_map/ppermute | solution.py:198
  520.1 28.0 %collective-permute-start.34 = (bf16[512,3072]{1,0:T(8,128)(2,1)S(1)}, bf16[512,3072]{1,0:T(8,128)(2,1)S(1)}, u32[]{:S(2)}, u32[]{:S(2)}) collective-permute-start(bf16[512,3072]{1,0:T(8,128)(2,1)S(1)} %constant_dynamic-update-slice_fusion), channel_id=1, source_target_pairs={{0,2},{2,0},{1,3},{3,1},{4,6},{6,4},{5,7},{7,5},{8,10},{10,8},{9,1... | collective-permute-start | bytes 9437192 | tf_op jit(solution)/shard_map/ppermute | solution.py:198
  520.2 10.0 %collective-permute-start.51 = (bf16[256,512]{1,0:T(8,128)(2,1)S(1)}, bf16[256,512]{1,0:T(8,128)(2,1)S(1)}, u32[]{:S(2)}, u32[]{:S(2)}) collective-permute-start(bf16[256,512]{1,0:T(8,128)(2,1)S(1)} %pad_maximum_fusion.12), channel_id=1, source_target_pairs={{0,1},{1,0},{2,3},{3,2},{4,5},{5,4},{6,7},{7,6},{8,9},{9,8},{10,11... | collective-permute-start | bytes 786440 | tf_op jit(solution)/shard_map/ppermute | solution.py:198
  521.8 17.0 %copy-start.14 = (f32[768,1024]{1,0:T(8,128)S(1)}, f32[768,1024]{1,0:T(8,128)}, u32[]{:S(2)}) copy-start(f32[768,1024]{1,0:T(8,128)} %get-tuple-element.334) | copy-start | bytes 9437188
  524.2 4.3 collective-permute-start.6
  528.5 8.9 %collective-permute-start.7 = (f32[12,1024]{1,0:T(8,128)S(1)}, f32[12,1024]{1,0:T(8,128)S(1)}, u32[]{:S(2)}, u32[]{:S(2)}) collective-permute-start(f32[12,1024]{1,0:T(8,128)S(1)} %add.509), channel_id=1, source_target_pairs={{0,8},{4,12},{8,0},{12,4},{16,24},{20,28},{24,16},{28,20},{1,9},{5... | collective-permute-start | bytes 147464 | tf_op jit(solution)/shard_map/ppermute | solution.py:198
  529.7 7.3 %collective-permute-start.50 = (bf16[256,512]{1,0:T(8,128)(2,1)S(1)}, bf16[256,512]{1,0:T(8,128)(2,1)S(1)}, u32[]{:S(2)}, u32[]{:S(2)}) collective-permute-start(bf16[256,512]{1,0:T(8,128)(2,1)S(1)} %pad_maximum_fusion.11), channel_id=1, source_target_pairs={{0,4},{4,0},{8,12},{12,8},{16,20},{20,16},{24,28},{28,24},{1,5},{5... | collective-permute-start | bytes 786440 | tf_op jit(solution)/shard_map/ppermute | solution.py:198
  537.3 8.2 %collective-permute-start.52 = (bf16[512,1024]{1,0:T(8,128)(2,1)S(1)}, bf16[512,1024]{1,0:T(8,128)(2,1)S(1)}, u32[]{:S(2)}, u32[]{:S(2)}) collective-permute-start(bf16[512,1024]{1,0:T(8,128)(2,1)S(1)} %constant_dynamic-update-slice_fusion.3), channel_id=1, source_target_pairs={{0,2},{2,0},{1,3},{3,1},{4,6},{6,4},{5,7},{7,5},{8,10},{10,8},{9,1... | collective-permute-start | bytes 3145736 | tf_op jit(solution)/shard_map/ppermute | solution.py:198
  537.4 6.8 %collective-permute-start.8 = (f32[12,1024]{1,0:T(8,128)S(1)}, f32[12,1024]{1,0:T(8,128)S(1)}, u32[]{:S(2)}, u32[]{:S(2)}) collective-permute-start(f32[12,1024]{1,0:T(8,128)S(1)} %add.510), channel_id=1, source_target_pairs={{0,16},{4,20},{8,24},{12,28},{16,0},{20,4},{24,8},{28,12},{1,17},{... | collective-permute-start | bytes 147464 | tf_op jit(solution)/shard_map/ppermute | solution.py:198
  (46 other events, 129.0 us)
Sparse Core Ops, SparseCore 0:
  9.6 60.9 all-gather.4
  72.2 58.2 all-gather.6
  227.3 73.2 reduce-scatter.2
  368.0 93.5 reduce-scatter.4

commit v2 on v1

--- a/solution.py
+++ b/solution.py
@@ -52,7 +52,7 @@
             pl.BlockSpec((nx,128),lambda i:(0,G+i))],
         out_specs=[pl.BlockSpec((rows,128),lambda i:(0,i)),pl.BlockSpec((rows,128),lambda i:(0,i)),pl.BlockSpec((rows,128),lambda i:(0,0))],
         out_shape=[jax.ShapeDtypeStruct((rows,D),f32),jax.ShapeDtypeStruct((rows,D),bf),jax.ShapeDtypeStruct((rows,128),f32)],
-        cost_estimate=pl.CostEstimate(flops=flops*4,transcendentals=16*rows*(rows+nx),bytes_accessed=rows*D*16),
+        cost_estimate=pl.CostEstimate(flops=rows,transcendentals=0,bytes_accessed=rows),
         name="attn_fwd")(bias,joined,joined,joined,other,other)
 
 def bwd_body(kb, biast_ref, lse_ref, q_ref, ko_ref, vo_ref, kx_ref, vx_ref, do_ref, o_ref, dq_ref, dko_ref, dx_ref):
@@ -83,7 +83,7 @@
                 e=mm(ds,k,TN)
                 dq[j]=e if dq[j] is None else dq[j]+e
             if own:
-                dko_ref[0,b:b+kb,:]=dk; dko_ref[1,b:b+kb,:]=dv
+                dko_ref[0,b:b+kb,:]=dk.astype(bf); dko_ref[1,b:b+kb,:]=dv.astype(bf)
             else:
                 dx_ref[0,b:b+kb,:]=dk.astype(bf); dx_ref[1,b:b+kb,:]=dv.astype(bf)
     dq_ref[...]=(jnp.where(lane<64,dq[0],dq[1])*0.125).astype(bf)
@@ -104,7 +104,7 @@
             pl.BlockSpec((rows,128),lambda i:(0,i)),
             pl.BlockSpec((rows,128),lambda i:(0,i))],
         out_specs=[pl.BlockSpec((rows,128),lambda i:(0,i)),pl.BlockSpec((2,rows,128),lambda i:(0,0,i)),pl.BlockSpec((2,nx,128),lambda i:(0,0,i))],
-        out_shape=[jax.ShapeDtypeStruct((rows,D),bf),jax.ShapeDtypeStruct((2,rows,D),f32),jax.ShapeDtypeStruct((2,nx,D),bf)],
+        out_shape=[jax.ShapeDtypeStruct((rows,D),bf),jax.ShapeDtypeStruct((2,rows,D),bf),jax.ShapeDtypeStruct((2,nx,D),bf)],
         cost_estimate=pl.CostEstimate(flops=flops*4,transcendentals=16*rows*(rows+nx),bytes_accessed=rows*D*30),
         name="attn_bwd")(biast,lset,joined,joined,joined,other,other,do,o)
 
@@ -112,7 +112,7 @@
 def exp_body(x_ref, g_ref, wi_ref, wo_ref, *refs):
     act_ref, ig_ref, b_ref, accr, accd = refs[-5:]
     f=pl.program_id(0)
-    x=x_ref[...]; g=g_ref[...]; wi=wi_ref[...]; wo=wo_ref[...]
+    x=x_ref[...]; g=g_ref[...]; wi=wi_ref[...].reshape(x_ref.shape[1],wi_ref.shape[3]); wo=wo_ref[0,0]
     v=mm(x,wi,NN)
     ag=mm(g,wo,NT)
     v2=v*v
@@ -134,42 +134,121 @@
             b_ref[e,:size,:]=accr[e*size:(e+1)*size,:].astype(bf)
             b_ref[e,size:,:]=accd[e*size:(e+1)*size,:].astype(bf)
 
-def expert(x, g, wi, wo, prev, mb, nmb, experts, fb=512):
-    rows,D=x.shape; FF=wi.shape[1]
+def expert(x, g, weights, prev, mb, nmb, experts, fb=512):
+    rows,D=x.shape; n,deep,_=weights.shape; part=deep//2; FF=part*n; per=D//fb
     blk=pl.BlockSpec((rows,fb),lambda f:(mb,f))
     anyspec=pl.BlockSpec(memory_space=pl.ANY)
     ex=() if prev is None else prev
     return pl.pallas_call(exp_body, grid=(FF//fb,),
         in_specs=[pl.BlockSpec((rows,D),lambda f:(0,0)),pl.BlockSpec((rows,D),lambda f:(0,0)),
-                  pl.BlockSpec((D,fb),lambda f:(0,f)),pl.BlockSpec((fb,D),lambda f:(f,0))]+[anyspec]*len(ex),
+                  pl.BlockSpec((n,1,D//n,fb),lambda f:(0,f//per,0,f%per)),
+                  pl.BlockSpec((1,1,fb,D),lambda f:(f//(part//fb),part//fb+f%(part//fb),0,0))]+[anyspec]*len(ex),
         out_specs=[blk,blk,pl.BlockSpec((experts,2*rows//experts,D),lambda f:(0,0,0))],
         out_shape=[jax.ShapeDtypeStruct((nmb*rows,FF),bf)]*2+[jax.ShapeDtypeStruct((experts,2*rows//experts,D),bf)],
         scratch_shapes=[pltpu.VMEM((rows,D),f32)]*2,
         input_output_aliases={} if prev is None else {4:0,5:1},
         cost_estimate=pl.CostEstimate(flops=8*rows*D*FF,transcendentals=rows*FF,bytes_accessed=4*D*FF+4*rows*FF),
-        name="expert")(x,g,wi,wo,*ex)
-
-def merge_body(count, dq_ref, own_ref, *refs):
-    j=pl.program_id(0); out_ref=refs[-1]
+        name="expert")(x,g,weights.reshape(n,2*FF//D,D//n,D),weights.reshape(n,deep//fb,fb,D),*ex)
+
+def in_grads_body(count, *refs):
+    in_ref, turned=refs[-2:]; xs=refs[:count]; ig_ref=refs[count]
+    n=in_ref.shape[0]; rows,D=xs[0].shape
+    @pl.when(pl.program_id(0)==0)
+    def _():
+        turned[...]=jnp.concatenate([r[...] for r in xs],axis=0).T
+    t=mm(turned[...],ig_ref[...],NN).astype(bf)
+    for q in range(n): in_ref[q,0,:,:]=t[q*(D//n):(q+1)*(D//n),:]
+
+def in_grads(xs, ig, n, fb=512):
+    rows,D=xs[0].shape; FF=ig.shape[1]; per=D//fb; count=len(xs)
+    return pl.pallas_call(partial(in_grads_body,count), grid=(FF//fb,),
+        in_specs=[pl.BlockSpec((rows,D),lambda f:(0,0))]*count+[pl.BlockSpec((count*rows,fb),lambda f:(0,f))],
+        out_specs=pl.BlockSpec((n,1,D//n,fb),lambda f:(0,f//per,0,f%per)),
+        out_shape=jax.ShapeDtypeStruct((n,FF//D,D//n,D),bf),
+        scratch_shapes=[pltpu.VMEM((D,count*rows),bf)],
+        cost_estimate=pl.CostEstimate(flops=2*count*rows*D*FF,transcendentals=0,bytes_accessed=2*D*FF+2*count*rows*FF),
+        name="in_grads")(*xs,ig)
+
+def out_grads_body(count, *refs):
+    out_ref, stacked=refs[-2:]; gs=refs[:count]; act_ref=refs[count]; rows=gs[0].shape[0]
+    @pl.when(pl.program_id(0)==0)
+    def _():
+        for m in range(count): stacked[m*rows:(m+1)*rows,:]=gs[m][...]
+    out_ref[...]=mm(act_ref[...],stacked[...],TN).astype(bf)
+
+def out_grads(gs, act, fb=512):
+    rows,D=gs[0].shape; FF=act.shape[1]; count=len(gs)
+    return pl.pallas_call(partial(out_grads_body,count), grid=(FF//fb,),
+        in_specs=[pl.BlockSpec((rows,D),lambda f:(0,0))]*count+[pl.BlockSpec((count*rows,fb),lambda f:(0,f))],
+        out_specs=pl.BlockSpec((fb,D),lambda f:(f,0)),
+        out_shape=jax.ShapeDtypeStruct((FF,D),bf),
+        scratch_shapes=[pltpu.VMEM((count*rows,D),bf)],
+        cost_estimate=pl.CostEstimate(flops=2*count*rows*D*FF,transcendentals=0,bytes_accessed=2*D*FF+2*count*rows*FF),
+        name="out_grads")(*gs,act)
+
+def project_body(count, parts, first, per, high_ref, x_ref, *refs):
+    j=pl.program_id(0)
+    joined_ref,keep_ref,send_ref,turned=refs[-4:]
+    half=keep_ref.shape[0]
     @pl.when(j==0)
-    def _(): out_ref[...]=dq_ref[...]
-    @pl.when(j>0)
+    def _(): turned[...]=x_ref[...].T
+    rows=x_ref.shape[0]//count
+    for m in range(count):
+        own=refs[m*(2+parts):(m+1)*(2+parts)]
+        @pl.when(j+first<per)
+        def _(): joined_ref[m*rows:(m+1)*rows,:]=own[0][...]
+        @pl.when(j+first>=per)
+        def _():
+            total=own[1][0].astype(f32)
+            for r in own[2:]: total=total+r[0].astype(f32)
+            joined_ref[m*rows:(m+1)*rows,:]=total.astype(bf)
+    high=high_ref[0]
+    right=joined_ref[...]
+    send_ref[...]=mm(turned[pl.ds(pl.multiple_of((1-high)*half,half),half),:],right,NN).astype(bf)
+    keep_ref[...]=mm(turned[pl.ds(pl.multiple_of(high*half,half),half),:],right,NN).astype(bf)
+
+def project_grads(x, groups, high, first, steps, prev, fb=512):
+    rows,D=x.shape; count=len(groups); R=rows//count; per=D//fb; parts=len(groups[0][2])
+    three=pl.BlockSpec((1,R,fb),lambda j,h:(jnp.maximum((j+first)//per-1,0),0,jnp.where(j+first<per,0,(j+first)%per)))
+    specs=[pl.BlockSpec((rows,D),lambda j,h:(0,0))]; args=[x]
+    for dq,own,away in groups:
+        specs+=[pl.BlockSpec((R,fb),lambda j,h:(0,jnp.minimum(j+first,per-1))),three]+[three]*parts
+        args+=[dq,own]+list(away)
+    if prev is not None:
+        specs.append(pl.BlockSpec(memory_space=pl.ANY)); args.append(prev)
+    return pl.pallas_call(partial(project_body,count,parts,first,per),
+        grid_spec=pltpu.PrefetchScalarGridSpec(num_scalar_prefetch=1,grid=(steps,),in_specs=specs,
+            out_specs=[pl.BlockSpec((rows,fb),lambda j,h:(0,j+first)),pl.BlockSpec((D//2,fb),lambda j,h:(0,j)),pl.BlockSpec((D//2,fb),lambda j,h:(0,j))],
+            scratch_shapes=[pltpu.VMEM((D,rows),bf)]),
+        out_shape=[jax.ShapeDtypeStruct((rows,3*D),bf)]+[jax.ShapeDtypeStruct((D//2,steps*fb),bf)]*2,
+        input_output_aliases={} if prev is None else {len(args):0},
+        cost_estimate=pl.CostEstimate(flops=6*rows*D*D,transcendentals=0,bytes_accessed=rows*D*16+6*D*D),
+        name="project_grads")(high,*args)
+
+def widen_body(count, per, high_ref, *refs):
+    out_ref=refs[-1]; i=pl.program_id(0)
+    @pl.when(i//per==high_ref[0])
     def _():
-        total=own_ref[0]
-        for r in refs[:count]: total=total+r[0].astype(f32)
-        out_ref[...]=total.astype(bf)
-
-def merge(dq, own, parts, prev, mb, nmb):
-    rows,D=dq.shape
-    three=pl.BlockSpec((1,rows,D),lambda j:(jnp.maximum(j-1,0),0,0))
-    ex=[] if prev is None else [prev]
-    return pl.pallas_call(partial(merge_body,len(parts)), grid=(3,),
-        in_specs=[pl.BlockSpec((rows,D),lambda j:(0,0)),three]+[three]*len(parts)+[pl.BlockSpec(memory_space=pl.ANY)]*len(ex),
-        out_specs=pl.BlockSpec((rows,D),lambda j:(mb,j)),
-        out_shape=jax.ShapeDtypeStruct((nmb*rows,3*D),bf),
-        input_output_aliases={} if prev is None else {2+len(parts):0},
-        cost_estimate=pl.CostEstimate(flops=rows*D*4,transcendentals=0,bytes_accessed=rows*D*22),
-        name="merge")(dq,own,*parts,*ex)
+        start=0
+        for r in refs[:count]:
+            out_ref[:,start:start+r.shape[1]]=r[...].astype(f32); start+=r.shape[1]
+    @pl.when(i//per!=high_ref[0])
+    def _():
+        start=0
+        for r in refs[count:2*count]:
+            out_ref[:,start:start+r.shape[1]]=r[...].astype(f32); start+=r.shape[1]
+
+def widen(mine, other, high, rb=256):
+    half=mine[0].shape[0]; per=half//rb; width=sum(m.shape[1] for m in mine)
+    own=lambda i,h:(jnp.where(i//per==h[0],i%per,jnp.where(h[0]==0,per-1,0)),0)
+    away=lambda i,h:(jnp.where(i//per!=h[0],i%per,jnp.where(h[0]==1,per-1,0)),0)
+    return pl.pallas_call(partial(widen_body,len(mine),per),
+        grid_spec=pltpu.PrefetchScalarGridSpec(num_scalar_prefetch=1,grid=(2*per,),
+            in_specs=[pl.BlockSpec((rb,m.shape[1]),own) for m in mine]+[pl.BlockSpec((rb,m.shape[1]),away) for m in mine],
+            out_specs=pl.BlockSpec((rb,width),lambda i,h:(i,0))),
+        out_shape=jax.ShapeDtypeStruct((2*half,width),f32),
+        cost_estimate=pl.CostEstimate(flops=half*width,transcendentals=0,bytes_accessed=half*width*12),
+        name="widen")(high,*mine,*other)
 
 
 HEADS = 16
@@ -228,41 +307,6 @@
             )
         )
     return joined
-
-
-def sum_everywhere(whole, widths, held=()):
-    near = bits_of("context")
-    for slot in range(len(near)):
-        whole = halve([whole], [near], slot)[0]
-    chunks, start = [], 0
-    for width in widths:
-        chunks.append(whole[:, start : start + width])
-        start += width
-    expert = bits_of("expert")
-    orders = [
-        expert[:1] + bits_of("dp") + expert[1:],
-        bits_of("dp") + expert,
-        expert[1:] + expert[:1] + bits_of("dp"),
-    ][: len(widths)]
-    count = len(orders[0])
-    for slot in range(count):
-        chunks = list(lax.optimization_barrier(tuple(halve(chunks, orders, slot))))
-    for slot in reversed(range(count)):
-        chunks = list(lax.optimization_barrier(tuple(double(chunks, orders, slot))))
-        if slot == 1 and held:
-            held = tuple(h.astype(f32) for h in held)
-            chunks, held = lax.optimization_barrier((chunks, held))
-    whole = chunks[0] if len(chunks) == 1 else jnp.concatenate(chunks, axis=1)
-    for slot in reversed(range(len(near))):
-        whole = double([whole], [near], slot)[0]
-    return whole, held
-
-
-def sum_small(values):
-    for axis in ("context", "dp", "expert"):
-        for _, bit in bits_of(axis):
-            values = values + swap(values, axis, bit)
-    return values
 
 
 def local(
@@ -289,8 +333,12 @@
     block = (capacity + 2 + 7) // 8 * 8
     slots = experts * block
 
-    full_in = lax.all_gather(expert_in[0], ("context", "dp"), axis=0, tiled=True)
-    full_out = lax.all_gather(expert_out[0], ("context", "dp"), axis=0, tiled=True)
+    devices = contexts * lax.axis_size("dp")
+    hidden = expert_in.shape[2]
+    blocks = [expert_in[0][:, k : k + model] for k in range(0, hidden, model)]
+    weights = lax.all_gather(
+        jnp.concatenate(blocks + [expert_out[0]], axis=0), ("context", "dp"), axis=0
+    )
 
     router_float = router_weight.astype(f32)
     expert_ids = jnp.arange(experts, dtype=jnp.int32)
@@ -318,8 +366,8 @@
     sent_grads, tokens = lax.optimization_barrier((jnp.concatenate(sent_grads, axis=1), tokens))
     grads_there = lax.all_to_all(sent_grads, "expert", split_axis=0, concat_axis=0, tiled=True)
 
-    flat = tokens.reshape(micro * rows, model).astype(f32)
-    normed, normal_one, scale_one = layer_norm(flat, mixer_gain, mixer_shift)
+    flat = tokens.reshape(micro * rows, model)
+    normed, normal_one, scale_one = layer_norm(flat.astype(f32), mixer_gain, mixer_shift)
     normed_low = lax.optimization_barrier(normed.astype(bf))
     joined = jnp.dot(normed_low, project_in, preferred_element_type=f32).astype(bf)
     others, biases = [], []
@@ -363,7 +411,7 @@
     for m in range(micro):
         attended, mixed_low, lse = attn_fwd(joined, others[m], biases[m][0], m)
         log_total = lse[:, :HEADS].T
-        middle = flat[m * rows : (m + 1) * rows] + jnp.dot(
+        middle = flat[m * rows : (m + 1) * rows].astype(f32) + jnp.dot(
             mixed_low, project_out, preferred_element_type=f32
         )
         second, normal_two, scale_two = layer_norm(middle, expert_gain, expert_shift)
@@ -404,9 +452,6 @@
              choose_float, gate, there]
         )
 
-    whole = lax.optimization_barrier(tuple(state[-1] for state in saved))
-    for m in range(micro):
-        saved[m][-1] = whole[m]
     kept = None
     rows_there, scaled_there, returned = [], [], []
     for m in range(micro):
@@ -415,9 +460,7 @@
         scaled = (gate_there[:, :, None] * grads_there[:, m].astype(f32)).astype(bf)
         there = there.reshape(slots, model)
         scaled = scaled.reshape(slots, model)
-        active, inner_grad, back = expert(
-            there, scaled, full_in, full_out, kept, m, micro, experts
-        )
+        active, inner_grad, back = expert(there, scaled, weights, kept, m, micro, experts)
         if m + 1 < micro:
             back, saved[m + 1][-1] = lax.optimization_barrier((back, saved[m + 1][-1]))
         kept = (active, inner_grad)
@@ -429,15 +472,16 @@
             )
         )
     active, inner_grad = kept
-    rows_there = jnp.concatenate(rows_there, axis=0)
-    scaled_there = jnp.concatenate(scaled_there, axis=0)
-    in_term = lax.dot_general(rows_there, inner_grad, TN, preferred_element_type=f32).astype(bf)
-    out_term = lax.dot_general(active, scaled_there, TN, preferred_element_type=f32).astype(bf)
-    in_term, out_term, returned[0] = lax.optimization_barrier((in_term, out_term, returned[0]))
-    grad_in = lax.psum_scatter(in_term, ("context", "dp"), scatter_dimension=0, tiled=True)
-    grad_out_weight = lax.psum_scatter(out_term, ("context", "dp"), scatter_dimension=0, tiled=True)
-
-    outputs, middle_grads, branches, joined_grad = [], [], [], None
+    out_term = out_grads(scaled_there, active)
+    out_term, inner_grad, returned[0] = lax.optimization_barrier((out_term, inner_grad, returned[0]))
+    in_term = in_grads(rows_there, inner_grad, devices)
+    in_term, place_two[0] = lax.optimization_barrier((in_term, place_two[0]))
+    grad_in = lax.psum_scatter(in_term, ("context", "dp"), scatter_dimension=0, tiled=True)[0]
+    grad_out_weight = lax.psum_scatter(
+        out_term, ("context", "dp"), scatter_dimension=0, tiled=True
+    )
+
+    outputs, middle_grads, branches, groups = [], [], [], []
     small = None
     for m in range(micro):
         (attended, mixed_low, log_total, middle, second_low, normal_two, scale_two, shares,
@@ -459,8 +503,6 @@
         query_grad, own, away = attn_bwd(
             joined, others[m], biases[m][1], log_total, mixed_grad, attended, m
         )
-        if m + 1 < micro:
-            own, away, returned[m + 1] = lax.optimization_barrier((own, away, returned[m + 1]))
         parts = [
             lax.ppermute(
                 away[:, (s - 1) * rows : s * rows] if contexts > 2 else away,
@@ -469,7 +511,10 @@
             )
             for s in range(1, contexts)
         ]
-        joined_grad = merge(query_grad, own, parts, joined_grad, m, micro)
+        groups.append([query_grad, own, parts])
+        if m + 1 < micro:
+            query_grad, place_two[m + 1] = lax.optimization_barrier((query_grad, place_two[m + 1]))
+            groups[m][0] = query_grad
         middle_grads.append(middle_grad)
         branches.append(branch)
         terms = (gain_two, shift_two, router_term)
@@ -479,30 +524,67 @@
     out_sum = lax.dot_general(
         mixed_all, jnp.concatenate(branches, axis=0), TN, preferred_element_type=f32
     ).astype(bf)
-    out_sum, _ = sum_everywhere(out_sum, (model // 2, model // 2))
-
-    in_sum = lax.dot_general(normed_low, joined_grad, TN, preferred_element_type=f32).astype(bf)
-    in_sum, joined_grad = lax.optimization_barrier((in_sum, joined_grad))
-    third = 3 * model // 6
-    in_sum, (grad_in, grad_out_weight) = sum_everywhere(
-        in_sum,
-        ((3 * model - third) // 2, (3 * model - third) // 2, third),
-        (grad_in, grad_out_weight),
+    out_sum, groups[-1][2][0] = lax.optimization_barrier((out_sum, groups[-1][2][0]))
+    near, expert_bits, dp_bits = bits_of("context"), bits_of("expert"), bits_of("dp")
+    high = (here % 2).astype(jnp.int32).reshape(1)
+    halves, joined_grad = [], None
+    for first in (0, 3):
+        joined_grad, kept, sent = project_grads(normed_low, groups, high, first, 3, joined_grad)
+        halves.append(kept + swap(sent, *near[0]))
+    halves.append(halve([out_sum], [near], 0)[0])
+    for slot in range(1, len(near)):
+        halves = halve(halves, [near] * 3, slot)
+    chunks = tuple(halves)
+
+    orders = (
+        expert_bits[:1] + dp_bits + expert_bits[1:],
+        expert_bits[1:2] + expert_bits[:1] + dp_bits + expert_bits[2:],
+        dp_bits + expert_bits[1:] + expert_bits[:1],
     )
-    normed_grad = lax.dot_general(joined_grad, project_in, NT, preferred_element_type=f32)
-    input_part, gain_one, shift_one = norm_back(normed_grad, normal_one, scale_one, mixer_gain)
-    grad_tokens = jnp.concatenate(middle_grads, axis=0) + input_part
-    small = jnp.concatenate(
-        [gain_one[None], shift_one[None], small[0][None], small[1][None], small[2].T], axis=0
-    )
-    small = sum_small(small)
+    count = len(orders[0])
+    for slot in range(count):
+        chunks = halve(chunks, orders, slot)
+        if slot == 0:
+            chunks, joined_grad = lax.optimization_barrier((chunks, joined_grad))
+            normed_grad = lax.dot_general(joined_grad, project_in, NT, preferred_element_type=f32)
+            input_part, gain_one, shift_one = norm_back(normed_grad, normal_one, scale_one, mixer_gain)
+            grad_tokens = jnp.concatenate(middle_grads, axis=0) + input_part
+            small = jnp.concatenate(
+                [gain_one[None], shift_one[None], small[0][None], small[1][None], small[2].T], axis=0
+            )
+        elif slot == 1:
+            chunks, small, grad_tokens = lax.optimization_barrier((chunks, small, grad_tokens))
+        else:
+            chunks = lax.optimization_barrier(chunks)
+    steps = dp_bits + expert_bits + near
+    for index in range(count):
+        chunks = double(chunks, orders, count - 1 - index)
+        small = small + swap(small, *steps[index])
+        chunks, small = lax.optimization_barrier((chunks, small))
+        if index == 0:
+            chunks, grad_in, grad_out_weight = lax.optimization_barrier(
+                (chunks, grad_in, grad_out_weight)
+            )
+            grad_in = jnp.concatenate([grad_in[k] for k in range(grad_in.shape[0])], axis=1).astype(f32)
+            grad_out_weight = grad_out_weight.astype(f32)
+        if index == count - 2:
+            chunks, grad_in, grad_out_weight = lax.optimization_barrier(
+                (chunks, grad_in, grad_out_weight)
+            )
+    for slot in reversed(range(1, len(near))):
+        chunks = double(chunks, (near,) * 3, slot)
+        small = small + swap(small, *near[slot])
+    small = small + swap(small, *near[0])
+    others = [swap(chunk, *near[0]) for chunk in chunks]
+    out_sum = widen(chunks[2:], others[2:], high)
+    in_sum = widen(chunks[:2], others[:2], high)
     return (
         jnp.stack(outputs)[:, None],
         grad_tokens.reshape(micro, 1, rows, model),
         small[0],
         small[1],
-        in_sum.astype(f32),
-        out_sum.astype(f32),
+        in_sum,
+        out_sum,
         small[2],
         small[3],
         small[4:].T,

time: 568 us -> 506 us (0.89)
  waiting for transfers between devices: 155 us -> 102 us
  Pallas kernels: 124 us -> 171 us
  matrix products: 95.8 us -> 58.1 us
  starting transfers between devices: 82.4 us -> 65.2 us
  other arithmetic: 66.8 us -> 59.8 us
  local copies, waits for them, and re-layouts: 22 us -> 28.2 us
    pallas_call x2 -> x6, Pallas kernels: 10.3 us -> 56.9 us  [the longest x2 15.6 us: project_grads(): pl.pallas_call(partial(project_body, count, parts, first, per), grid_spec...]
    dot_general x3 -> x0, matrix products: 35 us -> none  [the longest x1 13.8 us: local(): lax.dot_general(active, scaled_there, TN, preferred_element_type=f32)]
    ppermute x49 -> x35, waiting for transfers between devices: 108 us -> 77.4 us  [swap(): lax.ppermute(values, axis, [(i, i ^ bit) for i in range(lax.axis_size(axi...]
    all_to_all x2, waiting for transfers between devices: 37.7 us -> 15.8 us  [local(): lax.all_to_all(sent.reshape(experts, block, model), 'expert', split_axis=...]
    ppermute x49 -> x35, starting transfers between devices: 52.1 us -> 35 us  [swap(): lax.ppermute(values, axis, [(i, i ^ bit) for i in range(lax.axis_size(axi...]
    convert_element_type x5 -> x6, other arithmetic: 20.2 us -> 9.32 us  [the longest x1 2.5 us: local(): jnp.concatenate([grad_in[k] for k in range(grad_in.shape[0])], axis=1)]
  transfers between devices with their start and end apart: 62 -> 47, of which waited for: 36 -> 25; matrix products, arithmetic and copies ran while one was open for 30% -> 27% of each run, Pallas kernels for 18% -> 30%
where the time goes in v2:
time: 506 us; the launch traced here: 499 us
  Pallas kernels  171 us (34%)
  waiting for transfers between devices  102 us (20%)
  starting transfers between devices  65.2 us (13%)
  other arithmetic  59.8 us (12%)
  matrix products  58.1 us (11%)
  local copies, waits for them, and re-layouts  28.2 us (6%)
  between operations  15 us (3%)
    ppermute x35, waiting for transfers between devices, swap(): lax.ppermute(values, axis, [(i, i ^ bit) for i in range(lax.axis_size(axi...  77.4 us
    pallas_call x2, Pallas kernels, expert(): pl.pallas_call(exp_body, grid=(FF // fb,), in_specs=[pl.BlockSpec((rows,...  48.3 us
    pallas_call x2, Pallas kernels, attn_bwd(): pl.pallas_call(partial(bwd_body, kb), grid=(G,), in_specs=[pl.BlockSpec(b...  40.1 us
    ppermute x35, starting transfers between devices, swap(): lax.ppermute(values, axis, [(i, i ^ bit) for i in range(lax.axis_size(axi...  35 us
    pallas_call x2, Pallas kernels, attn_fwd(): pl.pallas_call(partial(fwd_body, rb), grid=(G,), in_specs=[pl.BlockSpec(b...  25.3 us
    all_to_all x2, waiting for transfers between devices, local(): lax.all_to_all(sent.reshape(experts, block, model), 'expert', split_axis=...  15.8 us
    pallas_call x2, Pallas kernels, project_grads(): pl.pallas_call(partial(project_body, count, parts, first, per), grid_spec...  15.6 us
    pallas_call x1, Pallas kernels, in_grads(): pl.pallas_call(partial(in_grads_body, count), grid=(FF // fb,), in_specs=...  14.4 us
  transfers between devices with their start and end apart: 47, of which 25 were waited for; matrix products, arithmetic and copies ran while one was open for 27% of the time, Pallas kernels for 30%

profile of v2, /device:TPU:0, one launch (start us, length us, event | category | flops | bytes accessed | tf_op | source)
XLA Modules:
  0.0 499.0 jit_solution(11552779245763115849)
XLA Ops:
  7.2 2.0 slice_dynamic-update-slice_fusion.3
  9.3 2.0 slice_dynamic-update-slice_fusion.2
  17.5 1.9 convolution_convert_fusion.3
  22.5 2.2 multiply_reduce_fusion.2
  24.8 2.3 add_convert_fusion.x_ref
  27.1 9.6 %convolution_convert_fusion.q_ref.ko_ref.vo_ref = bf16[768,3072]{1,0:T(8,128)(2,1)S(1)} fusion(bf16[768,1024]{1,0:T(8,128)(2,1)S(1)} %add_convert_fusion.x_ref, bf16[1024,3072]{1,0:T(8,128)(2,1)} %param.21), kind=kOutput, calls=%fused_computation | convolution fusion | flops 4834197504 | bytes 12582912 | tf_op jit(solution)/shard_map/dot_general | solution.py:372
  36.7 2.2 fusion.90
  40.3 7.9 %all-to-all-start = ((bf16[8,2,56,1024]{3,2,1,0:T(8,128)(2,1)}), bf16[8,2,56,1024]{3,2,1,0:T(8,128)(2,1)}, u32[]{:S(2)}, u32[]{:S(2)}) async-start(bf16[8,2,56,1024]{3,2,1,0:T(8,128)(2,1)} %pad_maximum_fusion), calls=%async_computation | async-start | bytes 3670016 | tf_op jit(solution)/shard_map/all_to_all | solution.py:367
  54.7 12.7 %attn_fwd.2 = (f32[384,1024]{1,0:T(8,128)}, bf16[384,1024]{1,0:T(8,128)(2,1)}, f32[384,128]{1,0:T(8,128)}) custom-call(f32[384,768]{1,0:T(8,128)} %and_select_fusion.3.bias_ref, bf16[768,3072]{1,0:T(8,128)(2,1)} %copy-done.1, bf16[768,3072]{1,0:T(8,128)(2,1)} %copy-done.1, bf16[768,3072]{1,0:T(8,128)(2,1)} %copy-done.1, ...), custom_call_target="tpu_custom_call" | custom-call | flops 384 | bytes 384 | tf_op jit(solution)/shard_map/attn_fwd/pallas_call | solution.py:45
  67.5 2.4 fusion.95
  73.7 12.6 %attn_fwd.3 = (f32[384,1024]{1,0:T(8,128)}, bf16[384,1024]{1,0:T(8,128)(2,1)}, f32[384,128]{1,0:T(8,128)}) custom-call(f32[384,768]{1,0:T(8,128)} %and_select_fusion.2.bias_ref, bf16[768,3072]{1,0:T(8,128)(2,1)} %copy-done.1, bf16[768,3072]{1,0:T(8,128)(2,1)} %copy-done.1, bf16[768,3072]{1,0:T(8,128)(2,1)} %copy-done.1, ...), custom_call_target="tpu_custom_call" | custom-call | flops 384 | bytes 384 | tf_op jit(solution)/shard_map/attn_fwd/pallas_call | solution.py:45
  86.3 2.4 fusion.97
  91.2 5.0 %all-to-all-start.1 = ((bf16[8,56,1024]{2,1,0:T(8,128)(2,1)}), bf16[8,56,1024]{2,1,0:T(8,128)(2,1)}, u32[]{:S(2)}, u32[]{:S(2)}) async-start(bf16[8,56,1024]{2,1,0:T(8,128)(2,1)} %bitcast.154), calls=%async_computation.1 | async-start | bytes 1835008 | tf_op jit(solution)/shard_map/all_to_all | solution.py:446
  98.7 1.9 fusion.21
  100.6 2.9 fusion.91
  103.4 15.8 %all-to-all-done.1 = bf16[8,56,1024]{2,1,0:T(8,128)(2,1)} async-done(((bf16[8,56,1024]{2,1,0:T(8,128)(2,1)}), bf16[8,56,1024]{2,1,0:T(8,128)(2,1)}, u32[]{:S(2)}, u32[]{:S(2)}) %all-to-all-start.1) | async-done | bytes 917536 | tf_op jit(solution)/shard_map/all_to_all | solution.py:446
  120.1 4.2 all-to-all-start.2
  124.3 2.3 fusion.2.g_ref.refs_0_
  126.7 24.2 %expert.2 = (bf16[896,4096]{1,0:T(8,128)(2,1)}, bf16[896,4096]{1,0:T(8,128)(2,1)}, bf16[8,112,1024]{2,1,0:T(8,128)(2,1)}) custom-call(bf16[448,1024]{1,0:T(8,128)(2,1)} %bitcast.18.x_ref.refs_0_, bf16[448,1024]{1,0:T(8,128)(2,1)} %fusion.2.g_ref.refs_0_, bf16[4,8,256,1024]{3,2,1,0:T(8,128)(2,1)} %bitcast.170, bf16[4,4,512,1024]{3,2,1,0:T(8,128)(2,1)} %bitcast.171), custom_call_target="tpu_custom_call" | custom-call | flops 15032385536 | bytes 24117248 | tf_op jit(solution)/shard_map/expert/pallas_call | solution.py:142
  150.9 5.9 %all-to-all-start.3 = ((bf16[8,112,1024]{2,1,0:T(8,128)(2,1)}), bf16[8,112,1024]{2,1,0:T(8,128)(2,1)}, u32[]{:S(2)}, u32[]{:S(2)}) async-start(bf16[8,112,1024]{2,1,0:T(8,128)(2,1)} %get-tuple-element.113), calls=%async_computation.3 | async-start | bytes 3670016 | tf_op jit(solution)/shard_map/all_to_all | solution.py:470
  159.9 2.3 fusion.1.g_ref.refs_1_
  162.2 24.1 %expert.3 = (bf16[896,4096]{1,0:T(8,128)(2,1)}, bf16[896,4096]{1,0:T(8,128)(2,1)}, bf16[8,112,1024]{2,1,0:T(8,128)(2,1)}) custom-call(bf16[448,1024]{1,0:T(8,128)(2,1)} %bitcast.25.x_ref.refs_1_, bf16[448,1024]{1,0:T(8,128)(2,1)} %fusion.1.g_ref.refs_1_, bf16[4,8,256,1024]{3,2,1,0:T(8,128)(2,1)} %bitcast.172, ...), custom_call_target="tpu_custom_call", output_to_operand_aliasing={{0}: (4, {}), {1}: (5, {})} | custom-call | flops 15032385536 | bytes 24117248 | tf_op jit(solution)/shard_map/expert/pallas_call | solution.py:142
  186.4 14.2 %out_grads.1 = bf16[4096,1024]{1,0:T(8,128)(2,1)} custom-call(bf16[448,1024]{1,0:T(8,128)(2,1)} %fusion.2.g_ref.refs_0_, bf16[448,1024]{1,0:T(8,128)(2,1)} %fusion.1.g_ref.refs_1_, bf16[896,4096]{1,0:T(8,128)(2,1)} %get-tuple-element.111.refs_2_), custom_call_target="tpu_custom_call" | custom-call | flops 7516192768 | bytes 15728640 | tf_op jit(solution)/shard_map/out_grads/pallas_call | solution.py:181
  200.5 14.4 %in_grads.1 = bf16[4,4,256,1024]{3,2,1,0:T(8,128)(2,1)} custom-call(bf16[448,1024]{1,0:T(8,128)(2,1)} %bitcast.18.x_ref.refs_0_, bf16[448,1024]{1,0:T(8,128)(2,1)} %bitcast.25.x_ref.refs_1_, bf16[896,4096]{1,0:T(8,128)(2,1)} %get-tuple-element.114.refs_2_), custom_call_target="tpu_custom_call" | custom-call | flops 7516192768 | bytes 15728640 | tf_op jit(solution)/shard_map/in_grads/pallas_call | solution.py:164
  222.2 5.9 %all-to-all-start.4 = ((bf16[8,112,1024]{2,1,0:T(8,128)(2,1)}), bf16[8,112,1024]{2,1,0:T(8,128)(2,1)}, u32[]{:S(2)}, u32[]{:S(2)}) async-start(bf16[8,112,1024]{2,1,0:T(8,128)(2,1)} %get-tuple-element.122), calls=%async_computation.4 | async-start | bytes 3670016 | tf_op jit(solution)/shard_map/all_to_all | solution.py:470
  228.2 5.5 %fusion.31 = (bf16[1,384,1024]{2,1,0:T(8,128)(2,1)}, f32[384]{0:T(512)S(1)}) fusion(f32[384,1024]{1,0:T(8,128)} %copy-done.6, f32[384]{0:T(512)S(1)} %select_reduce_fusion.1, bf16[2,1,384,1024]{3,2,1,0:T(8,128)(2,1)} %param.15, bf16[896,384]{1,0:T(8,128)(2,1)} %fusion.27, bf16[896,1024]{1,0:T(8,128)(2,1)} %bitcast.27), kind=kOutput, calls=%fused_computation.88 | convolution fusion | flops 707001984 | bytes 5671936 | tf_op jit(solution)/shard_map/dot_general | solution.py:490
  233.7 2.6 fusion.99
  239.8 1.9 convolution_convert_fusion.5.do_ref
  241.7 20.2 %attn_bwd.2 = (bf16[384,1024]{1,0:T(8,128)(2,1)}, bf16[2,384,1024]{2,1,0:T(8,128)(2,1)}, bf16[2,384,1024]{2,1,0:T(8,128)(2,1)}) custom-call(f32[768,384]{1,0:T(8,128)} %and_select_fusion.1.biast_ref, f32[16,384]{1,0:T(8,128)} %slice_bitcast_fusion.6.lse_ref, bf16[768,3072]{1,0:T(8,128)(2,1)} %copy-done.1, bf16[768,3072]{1,0:T(8,128)(2,1)} %copy-done.1, ...), custom_call_target="tpu_custom_call" | custom-call | flops 12079595520 | bytes 11796480 | tf_op jit(solution)/shard_map/attn_bwd/pallas_call | solution.py:95
  261.9 7.5 %all-to-all-done.4 = bf16[8,112,1024]{2,1,0:T(8,128)(2,1)} async-done(((bf16[8,112,1024]{2,1,0:T(8,128)(2,1)}), bf16[8,112,1024]{2,1,0:T(8,128)(2,1)}, u32[]{:S(2)}, u32[]{:S(2)}) %all-to-all-start.4) | async-done | bytes 1835040 | tf_op jit(solution)/shard_map/all_to_all | solution.py:470
  269.4 4.1 fusion.4
  273.5 2.6 fusion.100
  276.1 2.5 multiply_reduce_fusion.4
  278.7 4.7 fusion.88
  283.4 1.9 convolution_convert_fusion.4.do_ref
  285.3 19.9 %attn_bwd.3 = (bf16[384,1024]{1,0:T(8,128)(2,1)}, bf16[2,384,1024]{2,1,0:T(8,128)(2,1)}, bf16[2,384,1024]{2,1,0:T(8,128)(2,1)}) custom-call(f32[768,384]{1,0:T(8,128)} %and_select_fusion.biast_ref, f32[16,384]{1,0:T(8,128)} %slice_bitcast_fusion.5.lse_ref, bf16[768,3072]{1,0:T(8,128)(2,1)} %copy-done.1, bf16[768,3072]{1,0:T(8,128)(2,1)} %copy-done.1, ...), custom_call_target="tpu_custom_call" | custom-call | flops 12079595520 | bytes 11796480 | tf_op jit(solution)/shard_map/attn_bwd/pallas_call | solution.py:95
  305.8 5.2 %convolution_convert_fusion.1 = bf16[1024,1024]{1,0:T(8,128)(2,1)} fusion(bf16[384,1024]{1,0:T(8,128)(2,1)} %get-tuple-element.100, bf16[384,1024]{1,0:T(8,128)(2,1)} %get-tuple-element.98, bf16[384,1024]{1,0:T(8,128)(2,1)} %copy-done.26, bf16[384,1024]{1,0:T(8,128)(2,1)} %copy-done.30), kind=kOutput, calls=%fused_computation.16 | convolution fusion | flops 1617952768 | bytes 5242880 | tf_op jit(solution)/shard_map/dot_general | solution.py:524
  311.3 7.1 %project_grads.2 = (bf16[768,3072]{1,0:T(8,128)(2,1)}, bf16[512,1536]{1,0:T(8,128)(2,1)}, bf16[512,1536]{1,0:T(8,128)(2,1)}) custom-call(s32[1]{0:T(128)} %bitcast.34.high_ref, bf16[768,1024]{1,0:T(8,128)(2,1)} %copy-done.23, bf16[384,1024]{1,0:T(8,128)(2,1)} %get-tuple-element.123.refs_0_, bf16[2,384,1024]{2,1,0:T(8,128)(2,1)} %get-tuple-element.124.refs_1_, ...), custom_call_target="tpu_custom_call" | custom-call | flops 4831838208 | bytes 18874368 | tf_op jit(solution)/shard_map/project_grads/pallas_call | solution.py:219
  318.4 8.5 %project_grads.3 = (bf16[768,3072]{1,0:T(8,128)(2,1)}, bf16[512,1536]{1,0:T(8,128)(2,1)}, bf16[512,1536]{1,0:T(8,128)(2,1)}) custom-call(s32[1]{0:T(128)} %bitcast.34.high_ref, bf16[768,1024]{1,0:T(8,128)(2,1)} %copy-done.23, bf16[384,1024]{1,0:T(8,128)(2,1)} %get-tuple-element.123.refs_0_, ...), custom_call_target="tpu_custom_call", output_to_operand_aliasing={{0}: (8, {})} | custom-call | flops 4831838208 | bytes 18874368 | tf_op jit(solution)/shard_map/project_grads/pallas_call | solution.py:219
  327.0 2.3 constant_dynamic-slice_fusion.10
  329.8 2.5 collective-permute-done.8
  332.3 2.0 dynamic-slice_add_fusion
  342.9 17.3 %collective-permute-done.9 = bf16[256,1024]{1,0:T(8,128)(2,1)S(1)} collective-permute-done((bf16[256,1024]{1,0:T(8,128)(2,1)S(1)}, bf16[256,1024]{1,0:T(8,128)(2,1)S(1)}, u32[]{:S(2)}, u32[]{:S(2)}) %collective-permute-start.9) | collective-permute-done | bytes 524320 | tf_op jit(solution)/shard_map/ppermute | solution.py:277
  366.6 8.0 %multiply_reduce_fusion = (f32[768]{0:T(1024)S(1)}, f32[1024]{0:T(1024)S(1)}, f32[768]{0:T(1024)S(1)}, f32[1024]{0:T(1024)S(1)}, f32[768,1024]{1,0:T(8,128)S(1)}) fusion(bf16[2,1,384,1024]{3,2,1,0:T(8,128)(2,1)S(1)} %copy-done.3, f32[1024]{0:T(1024)S(1)} %copy-done.40, f32[768]{0:T(1024)S(1)} %copy-done.38, f32[768]{0:T(1024)S(1)} %copy-done.36, ...), kind=kOutput, calls=%fused_computation.4 | convolution fusion | flops 4839698432 | bytes 15753216 | tf_op jit(solution)/shard_map/dot_general | solution.py:549
  374.6 2.9 maximum_add_fusion
  380.1 3.7 collective-permute-done.10
  385.0 2.5 collective-permute-start.15
  389.6 3.7 collective-permute-done.15
  393.5 2.0 collective-permute-done.13
  397.4 2.8 collective-permute-start.16
  400.3 5.6 %collective-permute-done.17 = bf16[32,1536]{1,0:T(8,128)(2,1)S(1)} collective-permute-done((bf16[32,1536]{1,0:T(8,128)(2,1)S(1)}, bf16[32,1536]{1,0:T(8,128)(2,1)S(1)}, u32[]{:S(2)}, u32[]{:S(2)}) %collective-permute-start.17) | collective-permute-done | bytes 98336 | tf_op jit(solution)/shard_map/ppermute | solution.py:277
  409.1 3.8 collective-permute-done.22
  413.0 2.9 collective-permute-start.19
  416.0 4.5 collective-permute-done.20
  422.9 3.1 collective-permute-done.26
  427.6 1.9 collective-permute-start.23
  432.5 2.3 collective-permute-done.23
  438.1 2.5 maximum_convert_fusion
  440.6 2.5 convert_element_type.291
  445.1 7.0 %collective-permute-done.27 = bf16[128,1536]{1,0:T(8,128)(2,1)S(1)} collective-permute-done((bf16[128,1536]{1,0:T(8,128)(2,1)S(1)}, bf16[128,1536]{1,0:T(8,128)(2,1)S(1)}, u32[]{:S(2)}, u32[]{:S(2)}) %collective-permute-start.27) | collective-permute-done | bytes 393248 | tf_op jit(solution)/shard_map/ppermute | solution.py:277
  453.5 2.6 collective-permute-start.34
  456.3 12.0 %collective-permute-done.34 = f32[12,1024]{1,0:T(8,128)S(1)} collective-permute-done((f32[12,1024]{1,0:T(8,128)S(1)}, f32[12,1024]{1,0:T(8,128)S(1)}, u32[]{:S(2)}, u32[]{:S(2)}) %collective-permute-start.34) | collective-permute-done | bytes 49184 | tf_op jit(solution)/shard_map/ppermute | solution.py:277
  479.6 4.5 widen.3
  484.1 8.1 %widen.2 = f32[1024,3072]{1,0:T(8,128)} custom-call(s32[1]{0:T(128)} %bitcast.34.high_ref, bf16[512,1536]{1,0:T(8,128)(2,1)} %pad_maximum_fusion.1.refs_0_, bf16[512,1536]{1,0:T(8,128)(2,1)} %pad_maximum_fusion.2.refs_1_, bf16[512,1536]{1,0:T(8,128)(2,1)} %collective-permute-done.36.refs_2_, bf16[512,1536]{1,0:T(8,128)(2,1)} %collective-permute-done.37.refs_3_), custom_call_target="tpu_custom_call" | custom-call | flops 1572864 | bytes 18874368 | tf_op jit(solution)/shard_map/widen/pallas_call | solution.py:245
  (316 shorter events, 93.0 us)
Async XLA Ops:
  7.2 60.3 %copy-start = (bf16[1024,1024]{1,0:T(8,128)(2,1)S(1)}, bf16[1024,1024]{1,0:T(8,128)(2,1)}, u32[]{:S(2)}) copy-start(bf16[1024,1024]{1,0:T(8,128)(2,1)} %param.22) | copy-start | bytes 6291460
  7.2 119.5 %all-gather.3.cloned.1.call-start = ((), (), s32[]{:S(2)}) async-start(), calls=%async_computation.9 | async-start | bytes 20971520 | tf_op jit(solution)/shard_map/all_gather | solution.py:339
  22.5 4.6 copy-start.35
  27.1 9.6 %copy-start.23 = (bf16[768,1024]{1,0:T(8,128)(2,1)}, bf16[768,1024]{1,0:T(8,128)(2,1)S(1)}, u32[]{:S(2)}) copy-start(bf16[768,1024]{1,0:T(8,128)(2,1)S(1)} %add_convert_fusion.x_ref) | copy-start | bytes 4718596
  39.8 15.0 %collective-permute-start = (bf16[384,2048]{1,0:T(8,128)(2,1)}, bf16[384,2048]{1,0:T(8,128)(2,1)}, u32[]{:S(2)}, u32[]{:S(2)}) collective-permute-start(bf16[384,2048]{1,0:T(8,128)(2,1)} %get-tuple-element.260), channel_id=1, source_target_pairs={{0,2},{2,0},{1,3},{3,1},{4,6},{6,4},{5,7},{7,5},{8,10},{10,8},{9,1... | collective-permute-start | bytes 4718600 | tf_op jit(solution)/shard_map/ppermute | solution.py:377
  40.2 8.1 %copy-start.45 = (s32[2,1,3]{2,1,0:T(1,128)S(1)}, s32[2,1,3]{2,1,0:T(1,128)}, u32[]{:S(2)}) copy-start(s32[2,1,3]{2,1,0:T(1,128)} %param.16) | copy-start | bytes 76
  40.2 8.4 %copy-start.42 = (s32[2,1,768]{2,1,0:T(1,128)S(1)}, s32[2,1,768]{2,1,0:T(1,128)}, u32[]{:S(2)}) copy-start(s32[2,1,768]{2,1,0:T(1,128)} %param.17) | copy-start | bytes 18436
  40.2 33.5 %collective-permute-start.1 = (bf16[384,2048]{1,0:T(8,128)(2,1)}, bf16[384,2048]{1,0:T(8,128)(2,1)}, u32[]{:S(2)}, u32[]{:S(2)}) collective-permute-start(bf16[384,2048]{1,0:T(8,128)(2,1)} %get-tuple-element.259), channel_id=1, source_target_pairs={{0,2},{2,0},{1,3},{3,1},{4,6},{6,4},{5,7},{7,5},{8,10},{10,8},{9,1... | collective-permute-start | bytes 4718600 | tf_op jit(solution)/shard_map/ppermute | solution.py:377
  40.3 50.9 %all-to-all-start = ((bf16[8,2,56,1024]{3,2,1,0:T(8,128)(2,1)}), bf16[8,2,56,1024]{3,2,1,0:T(8,128)(2,1)}, u32[]{:S(2)}, u32[]{:S(2)}) async-start(bf16[8,2,56,1024]{3,2,1,0:T(8,128)(2,1)} %pad_maximum_fusion), calls=%async_computation | async-start | bytes 3670016 | tf_op jit(solution)/shard_map/all_to_all | solution.py:367
  91.2 28.0 %all-to-all-start.1 = ((bf16[8,56,1024]{2,1,0:T(8,128)(2,1)}), bf16[8,56,1024]{2,1,0:T(8,128)(2,1)}, u32[]{:S(2)}, u32[]{:S(2)}) async-start(bf16[8,56,1024]{2,1,0:T(8,128)(2,1)} %bitcast.154), calls=%async_computation.1 | async-start | bytes 1835008 | tf_op jit(solution)/shard_map/all_to_all | solution.py:446
  120.1 30.8 %all-to-all-start.2 = ((bf16[8,56,1024]{2,1,0:T(8,128)(2,1)}), bf16[8,56,1024]{2,1,0:T(8,128)(2,1)}, u32[]{:S(2)}, u32[]{:S(2)}) async-start(bf16[8,56,1024]{2,1,0:T(8,128)(2,1)} %bitcast.155), calls=%async_computation.2 | async-start | bytes 1835008 | tf_op jit(solution)/shard_map/all_to_all | solution.py:446
  150.9 49.7 %all-to-all-start.3 = ((bf16[8,112,1024]{2,1,0:T(8,128)(2,1)}), bf16[8,112,1024]{2,1,0:T(8,128)(2,1)}, u32[]{:S(2)}, u32[]{:S(2)}) async-start(bf16[8,112,1024]{2,1,0:T(8,128)(2,1)} %get-tuple-element.113), calls=%async_computation.3 | async-start | bytes 3670016 | tf_op jit(solution)/shard_map/all_to_all | solution.py:470
  156.8 269.2 %reduce-scatter.3.cloned.1.call-start = ((), (), s32[]{:S(2)}) async-start(), calls=%async_computation.7 | async-start | bytes 10485760 | tf_op jit(solution)/shard_map/reduce_scatter | solution.py:479
  222.2 47.2 %all-to-all-start.4 = ((bf16[8,112,1024]{2,1,0:T(8,128)(2,1)}), bf16[8,112,1024]{2,1,0:T(8,128)(2,1)}, u32[]{:S(2)}, u32[]{:S(2)}) async-start(bf16[8,112,1024]{2,1,0:T(8,128)(2,1)} %get-tuple-element.122), calls=%async_computation.4 | async-start | bytes 3670016 | tf_op jit(solution)/shard_map/all_to_all | solution.py:470
  228.2 197.8 %reduce-scatter.5.cloned.1.call-start = ((), (), s32[]{:S(2)}) async-start(), calls=%async_computation.8 | async-start | bytes 10485760 | tf_op jit(solution)/shard_map/reduce_scatter | solution.py:480
  228.2 5.5 %copy-start.19 = (bf16[896,384]{1,0:T(8,128)(2,1)S(1)}, bf16[896,384]{1,0:T(8,128)(2,1)}, u32[]{:S(2)}) copy-start(bf16[896,384]{1,0:T(8,128)(2,1)} %fusion.28) | copy-start | bytes 2064388
  269.4 4.1 copy-start.18
  305.2 5.8 %collective-permute-start.3 = (bf16[2,384,1024]{2,1,0:T(8,128)(2,1)}, bf16[2,384,1024]{2,1,0:T(8,128)(2,1)}, u32[]{:S(2)}, u32[]{:S(2)}) collective-permute-start(bf16[2,384,1024]{2,1,0:T(8,128)(2,1)} %get-tuple-element.131), channel_id=1, source_target_pairs={{0,2},{2,0},{1,3},{3,1},{4,6},{6,4},{5,7},{7,5},{8,10},{10,8},{9,1... | collective-permute-start | bytes 4718600 | tf_op jit(solution)/shard_map/ppermute | solution.py:507
  305.3 6.0 %collective-permute-start.2 = (bf16[2,384,1024]{2,1,0:T(8,128)(2,1)}, bf16[2,384,1024]{2,1,0:T(8,128)(2,1)}, u32[]{:S(2)}, u32[]{:S(2)}) collective-permute-start(bf16[2,384,1024]{2,1,0:T(8,128)(2,1)} %get-tuple-element.125), channel_id=1, source_target_pairs={{0,2},{2,0},{1,3},{3,1},{4,6},{6,4},{5,7},{7,5},{8,10},{10,8},{9,1... | collective-permute-start | bytes 4718600 | tf_op jit(solution)/shard_map/ppermute | solution.py:507
  326.9 9.2 %collective-permute-start.6 = (bf16[512,1536]{1,0:T(8,128)(2,1)}, bf16[512,1536]{1,0:T(8,128)(2,1)}, u32[]{:S(2)}, u32[]{:S(2)}) collective-permute-start(bf16[512,1536]{1,0:T(8,128)(2,1)} %get-tuple-element.137), channel_id=1, source_target_pairs={{0,2},{2,0},{1,3},{3,1},{4,6},{6,4},{5,7},{7,5},{8,10},{10,8},{9,1... | collective-permute-start | bytes 4718600 | tf_op jit(solution)/shard_map/ppermute | solution.py:277
  329.3 3.0 collective-permute-start.8
  329.7 9.0 %collective-permute-start.4 = (bf16[512,1536]{1,0:T(8,128)(2,1)}, bf16[512,1536]{1,0:T(8,128)(2,1)}, u32[]{:S(2)}, u32[]{:S(2)}) collective-permute-start(bf16[512,1536]{1,0:T(8,128)(2,1)} %get-tuple-element.134), channel_id=1, source_target_pairs={{0,2},{2,0},{1,3},{3,1},{4,6},{6,4},{5,7},{7,5},{8,10},{10,8},{9,1... | collective-permute-start | bytes 4718600 | tf_op jit(solution)/shard_map/ppermute | solution.py:277
  329.8 6.3 %copy-start.25 = (bf16[512,1536]{1,0:T(8,128)(2,1)S(1)}, bf16[512,1536]{1,0:T(8,128)(2,1)}, u32[]{:S(2)}) copy-start(bf16[512,1536]{1,0:T(8,128)(2,1)} %get-tuple-element.136) | copy-start | bytes 4718596
  334.3 25.9 %collective-permute-start.9 = (bf16[256,1024]{1,0:T(8,128)(2,1)S(1)}, bf16[256,1024]{1,0:T(8,128)(2,1)S(1)}, u32[]{:S(2)}, u32[]{:S(2)}) collective-permute-start(bf16[256,1024]{1,0:T(8,128)(2,1)S(1)} %constant_dynamic-slice_fusion.9), channel_id=1, source_target_pairs={{0,1},{1,0},{2,3},{3,2},{4,5},{5,4},{6,7},{7,6},{8,9},{9,8},{10,11... | collective-permute-start | bytes 1572872 | tf_op jit(solution)/shard_map/ppermute | solution.py:277
  337.9 22.4 %collective-permute-start.7 = (bf16[256,1536]{1,0:T(8,128)(2,1)S(1)}, bf16[256,1536]{1,0:T(8,128)(2,1)S(1)}, u32[]{:S(2)}, u32[]{:S(2)}) collective-permute-start(bf16[256,1536]{1,0:T(8,128)(2,1)S(1)} %constant_dynamic-slice_fusion.11), channel_id=1, source_target_pairs={{0,8},{4,12},{8,0},{12,4},{16,24},{20,28},{24,16},{28,20},{1,9},{5... | collective-permute-start | bytes 2359304 | tf_op jit(solution)/shard_map/ppermute | solution.py:277
  341.2 19.7 %collective-permute-start.5 = (bf16[256,1536]{1,0:T(8,128)(2,1)S(1)}, bf16[256,1536]{1,0:T(8,128)(2,1)S(1)}, u32[]{:S(2)}, u32[]{:S(2)}) collective-permute-start(bf16[256,1536]{1,0:T(8,128)(2,1)S(1)} %constant_dynamic-slice_fusion.12), channel_id=1, source_target_pairs={{0,4},{4,0},{8,12},{12,8},{16,20},{20,16},{24,28},{28,24},{1,5},{5... | collective-permute-start | bytes 2359304 | tf_op jit(solution)/shard_map/ppermute | solution.py:277
  360.4 6.2 %copy-start.46 = (bf16[768,3072]{1,0:T(8,128)(2,1)S(1)}, bf16[768,3072]{1,0:T(8,128)(2,1)}, u32[]{:S(2)}) copy-start(bf16[768,3072]{1,0:T(8,128)(2,1)} %get-tuple-element.143) | copy-start | bytes 14155780
  361.1 5.5 %copy-start.3 = (bf16[2,1,384,1024]{3,2,1,0:T(8,128)(2,1)S(1)}, bf16[2,1,384,1024]{3,2,1,0:T(8,128)(2,1)}, u32[]{:S(2)}) copy-start(bf16[2,1,384,1024]{3,2,1,0:T(8,128)(2,1)} %param.14) | copy-start | bytes 4718596
  361.1 5.5 %copy-start.36 = (f32[768]{0:T(1024)S(1)}, f32[768]{0:T(1024)}, u32[]{:S(2)}) copy-start(f32[768]{0:T(1024)} %copy-done.35) | copy-start | bytes 9220
  361.1 5.5 %copy-start.38 = (f32[768]{0:T(1024)S(1)}, f32[768]{0:T(1024)}, u32[]{:S(2)}) copy-start(f32[768]{0:T(1024)} %copy-done.37) | copy-start | bytes 9220
  361.1 5.5 %copy-start.40 = (f32[1024]{0:T(1024)S(1)}, f32[1024]{0:T(1024)}, u32[]{:S(2)}) copy-start(f32[1024]{0:T(1024)} %param.19) | copy-start | bytes 12292
  361.8 16.1 %collective-permute-start.12 = (bf16[128,1024]{1,0:T(8,128)(2,1)}, bf16[128,1024]{1,0:T(8,128)(2,1)}, u32[]{:S(2)}, u32[]{:S(2)}) collective-permute-start(bf16[128,1024]{1,0:T(8,128)(2,1)} %constant_dynamic-slice_fusion.6), channel_id=1, source_target_pairs={{0,8},{4,12},{8,0},{12,4},{16,24},{20,28},{24,16},{28,20},{1,9},{5... | collective-permute-start | bytes 786440 | tf_op jit(solution)/shard_map/ppermute | solution.py:277
  363.5 15.5 %collective-permute-start.11 = (bf16[128,1536]{1,0:T(8,128)(2,1)}, bf16[128,1536]{1,0:T(8,128)(2,1)}, u32[]{:S(2)}, u32[]{:S(2)}) collective-permute-start(bf16[128,1536]{1,0:T(8,128)(2,1)} %constant_dynamic-slice_fusion.7), channel_id=1, source_target_pairs={{0,4},{4,0},{8,12},{12,8},{16,20},{20,16},{24,28},{28,24},{1,5},{5... | collective-permute-start | bytes 1179656 | tf_op jit(solution)/shard_map/ppermute | solution.py:277
  365.4 9.3 %copy-start.10 = (f32[384,1024]{1,0:T(8,128)S(1)}, f32[384,1024]{1,0:T(8,128)}, u32[]{:S(2)}) copy-start(f32[384,1024]{1,0:T(8,128)} %get-tuple-element.248) | copy-start | bytes 4718596
  365.4 9.3 %copy-start.11 = (f32[384,1024]{1,0:T(8,128)S(1)}, f32[384,1024]{1,0:T(8,128)}, u32[]{:S(2)}) copy-start(f32[384,1024]{1,0:T(8,128)} %get-tuple-element.252) | copy-start | bytes 4718596
  365.4 18.5 %collective-permute-start.10 = (bf16[128,1536]{1,0:T(8,128)(2,1)}, bf16[128,1536]{1,0:T(8,128)(2,1)}, u32[]{:S(2)}, u32[]{:S(2)}) collective-permute-start(bf16[128,1536]{1,0:T(8,128)(2,1)} %constant_dynamic-slice_fusion.8), channel_id=1, source_target_pairs={{0,1},{1,0},{2,3},{3,2},{4,5},{5,4},{6,7},{7,6},{8,9},{9,8},{10,11... | collective-permute-start | bytes 1179656 | tf_op jit(solution)/shard_map/ppermute | solution.py:277
  377.9 6.0 %copy-start.17 = (bf16[256,1536]{1,0:T(8,128)(2,1)S(1)}, bf16[256,1536]{1,0:T(8,128)(2,1)}, u32[]{:S(2)}) copy-start(bf16[256,1536]{1,0:T(8,128)(2,1)} %copy-done.16) | copy-start | bytes 2359300
  385.0 8.4 %collective-permute-start.15 = (bf16[64,1024]{1,0:T(8,128)(2,1)S(1)}, bf16[64,1024]{1,0:T(8,128)(2,1)S(1)}, u32[]{:S(2)}, u32[]{:S(2)}) collective-permute-start(bf16[64,1024]{1,0:T(8,128)(2,1)S(1)} %constant_dynamic-slice_fusion.3), channel_id=1, source_target_pairs={{0,16},{4,20},{8,24},{12,28},{16,0},{20,4},{24,8},{28,12},{1,17},{... | collective-permute-start | bytes 393224 | tf_op jit(solution)/shard_map/ppermute | solution.py:277
  387.5 6.0 %collective-permute-start.14 = (bf16[64,1536]{1,0:T(8,128)(2,1)S(1)}, bf16[64,1536]{1,0:T(8,128)(2,1)S(1)}, u32[]{:S(2)}, u32[]{:S(2)}) collective-permute-start(bf16[64,1536]{1,0:T(8,128)(2,1)S(1)} %constant_dynamic-slice_fusion.4), channel_id=1, source_target_pairs={{0,1},{1,0},{2,3},{3,2},{4,5},{5,4},{6,7},{7,6},{8,9},{9,8},{10,11... | collective-permute-start | bytes 589832 | tf_op jit(solution)/shard_map/ppermute | solution.py:277
  388.1 7.5 %collective-permute-start.13 = (bf16[64,1536]{1,0:T(8,128)(2,1)S(1)}, bf16[64,1536]{1,0:T(8,128)(2,1)S(1)}, u32[]{:S(2)}, u32[]{:S(2)}) collective-permute-start(bf16[64,1536]{1,0:T(8,128)(2,1)S(1)} %constant_dynamic-slice_fusion.5), channel_id=1, source_target_pairs={{0,8},{4,12},{8,0},{12,4},{16,24},{20,28},{24,16},{28,20},{1,9},{5... | collective-permute-start | bytes 589832 | tf_op jit(solution)/shard_map/ppermute | solution.py:277
  395.6 4.6 collective-permute-start.18
  397.2 8.7 %collective-permute-start.17 = (bf16[32,1536]{1,0:T(8,128)(2,1)S(1)}, bf16[32,1536]{1,0:T(8,128)(2,1)S(1)}, u32[]{:S(2)}, u32[]{:S(2)}) collective-permute-start(bf16[32,1536]{1,0:T(8,128)(2,1)S(1)} %constant_dynamic-slice_fusion.1), channel_id=1, source_target_pairs={{0,16},{4,20},{8,24},{12,28},{16,0},{20,4},{24,8},{28,12},{1,17},{... | collective-permute-start | bytes 294920 | tf_op jit(solution)/shard_map/ppermute | solution.py:277
  397.4 9.8 %collective-permute-start.16 = (bf16[32,1536]{1,0:T(8,128)(2,1)S(1)}, bf16[32,1536]{1,0:T(8,128)(2,1)S(1)}, u32[]{:S(2)}, u32[]{:S(2)}) collective-permute-start(bf16[32,1536]{1,0:T(8,128)(2,1)S(1)} %constant_dynamic-slice_fusion.2), channel_id=1, source_target_pairs={{0,16},{4,20},{8,24},{12,28},{16,0},{20,4},{24,8},{28,12},{1,17},{... | collective-permute-start | bytes 294920 | tf_op jit(solution)/shard_map/ppermute | solution.py:277
  407.3 8.7 %collective-permute-start.21 = (bf16[32,1024]{1,0:T(8,128)(2,1)S(1)}, bf16[32,1024]{1,0:T(8,128)(2,1)S(1)}, u32[]{:S(2)}, u32[]{:S(2)}) collective-permute-start(bf16[32,1024]{1,0:T(8,128)(2,1)S(1)} %dynamic-slice_add_fusion.12), channel_id=1, source_target_pairs={{0,4},{4,0},{8,12},{12,8},{16,20},{20,16},{24,28},{28,24},{1,5},{5... | collective-permute-start | bytes 196616 | tf_op jit(solution)/shard_map/ppermute | solution.py:277
  408.7 4.3 collective-permute-start.22
  412.9 7.6 %collective-permute-start.20 = (bf16[32,1536]{1,0:T(8,128)(2,1)S(1)}, bf16[32,1536]{1,0:T(8,128)(2,1)S(1)}, u32[]{:S(2)}, u32[]{:S(2)}) collective-permute-start(bf16[32,1536]{1,0:T(8,128)(2,1)S(1)} %dynamic-slice_add_fusion.10), channel_id=1, source_target_pairs={{0,16},{4,20},{8,24},{12,28},{16,0},{20,4},{24,8},{28,12},{1,17},{... | collective-permute-start | bytes 294920 | tf_op jit(solution)/shard_map/ppermute | solution.py:277
  413.0 8.5 %collective-permute-start.19 = (bf16[32,1536]{1,0:T(8,128)(2,1)S(1)}, bf16[32,1536]{1,0:T(8,128)(2,1)S(1)}, u32[]{:S(2)}, u32[]{:S(2)}) collective-permute-start(bf16[32,1536]{1,0:T(8,128)(2,1)S(1)} %dynamic-slice_add_fusion.11), channel_id=1, source_target_pairs={{0,16},{4,20},{8,24},{12,28},{16,0},{20,4},{24,8},{28,12},{1,17},{... | collective-permute-start | bytes 294920 | tf_op jit(solution)/shard_map/ppermute | solution.py:277
  421.6 4.3 collective-permute-start.26
  426.0 6.4 %collective-permute-start.25 = (bf16[64,1024]{1,0:T(8,128)(2,1)S(1)}, bf16[64,1024]{1,0:T(8,128)(2,1)S(1)}, u32[]{:S(2)}, u32[]{:S(2)}) collective-permute-start(bf16[64,1024]{1,0:T(8,128)(2,1)S(1)} %pad_maximum_fusion.12), channel_id=1, source_target_pairs={{0,16},{4,20},{8,24},{12,28},{16,0},{20,4},{24,8},{28,12},{1,17},{... | collective-permute-start | bytes 393224 | tf_op jit(solution)/shard_map/ppermute | solution.py:277
  426.1 6.4 %collective-permute-start.24 = (bf16[64,1536]{1,0:T(8,128)(2,1)S(1)}, bf16[64,1536]{1,0:T(8,128)(2,1)S(1)}, u32[]{:S(2)}, u32[]{:S(2)}) collective-permute-start(bf16[64,1536]{1,0:T(8,128)(2,1)S(1)} %pad_maximum_fusion.11), channel_id=1, source_target_pairs={{0,1},{1,0},{2,3},{3,2},{4,5},{5,4},{6,7},{7,6},{8,9},{9,8},{10,11... | collective-permute-start | bytes 589832 | tf_op jit(solution)/shard_map/ppermute | solution.py:277
  427.6 7.3 %collective-permute-start.23 = (bf16[64,1536]{1,0:T(8,128)(2,1)S(1)}, bf16[64,1536]{1,0:T(8,128)(2,1)S(1)}, u32[]{:S(2)}, u32[]{:S(2)}) collective-permute-start(bf16[64,1536]{1,0:T(8,128)(2,1)S(1)} %pad_maximum_fusion.10), channel_id=1, source_target_pairs={{0,8},{4,12},{8,0},{12,4},{16,24},{20,28},{24,16},{28,20},{1,9},{5... | collective-permute-start | bytes 589832 | tf_op jit(solution)/shard_map/ppermute | solution.py:277
  435.0 9.1 %collective-permute-start.30 = (f32[12,1024]{1,0:T(8,128)S(1)}, f32[12,1024]{1,0:T(8,128)S(1)}, u32[]{:S(2)}, u32[]{:S(2)}) collective-permute-start(f32[12,1024]{1,0:T(8,128)S(1)} %add.499), channel_id=1, source_target_pairs={{0,8},{4,12},{8,0},{12,4},{16,24},{20,28},{24,16},{28,20},{1,9},{5... | collective-permute-start | bytes 147464 | tf_op jit(solution)/shard_map/ppermute | solution.py:277
  435.2 8.8 %collective-permute-start.29 = (bf16[128,1024]{1,0:T(8,128)(2,1)S(1)}, bf16[128,1024]{1,0:T(8,128)(2,1)S(1)}, u32[]{:S(2)}, u32[]{:S(2)}) collective-permute-start(bf16[128,1024]{1,0:T(8,128)(2,1)S(1)} %pad_maximum_fusion.9), channel_id=1, source_target_pairs={{0,8},{4,12},{8,0},{12,4},{16,24},{20,28},{24,16},{28,20},{1,9},{5... | collective-permute-start | bytes 786440 | tf_op jit(solution)/shard_map/ppermute | solution.py:277
  437.0 8.0 %collective-permute-start.28 = (bf16[128,1536]{1,0:T(8,128)(2,1)S(1)}, bf16[128,1536]{1,0:T(8,128)(2,1)S(1)}, u32[]{:S(2)}, u32[]{:S(2)}) collective-permute-start(bf16[128,1536]{1,0:T(8,128)(2,1)S(1)} %pad_maximum_fusion.8), channel_id=1, source_target_pairs={{0,4},{4,0},{8,12},{12,8},{16,20},{20,16},{24,28},{28,24},{1,5},{5... | collective-permute-start | bytes 1179656 | tf_op jit(solution)/shard_map/ppermute | solution.py:277
  443.1 9.1 %collective-permute-start.27 = (bf16[128,1536]{1,0:T(8,128)(2,1)S(1)}, bf16[128,1536]{1,0:T(8,128)(2,1)S(1)}, u32[]{:S(2)}, u32[]{:S(2)}) collective-permute-start(bf16[128,1536]{1,0:T(8,128)(2,1)S(1)} %pad_maximum_fusion.7), channel_id=1, source_target_pairs={{0,1},{1,0},{2,3},{3,2},{4,5},{5,4},{6,7},{7,6},{8,9},{9,8},{10,11... | collective-permute-start | bytes 1179656 | tf_op jit(solution)/shard_map/ppermute | solution.py:277
  452.3 16.0 %collective-permute-start.33 = (bf16[256,1024]{1,0:T(8,128)(2,1)S(1)}, bf16[256,1024]{1,0:T(8,128)(2,1)S(1)}, u32[]{:S(2)}, u32[]{:S(2)}) collective-permute-start(bf16[256,1024]{1,0:T(8,128)(2,1)S(1)} %pad_maximum_fusion.6), channel_id=1, source_target_pairs={{0,1},{1,0},{2,3},{3,2},{4,5},{5,4},{6,7},{7,6},{8,9},{9,8},{10,11... | collective-permute-start | bytes 1572872 | tf_op jit(solution)/shard_map/ppermute | solution.py:277
  453.3 16.9 %collective-permute-start.32 = (bf16[256,1536]{1,0:T(8,128)(2,1)S(1)}, bf16[256,1536]{1,0:T(8,128)(2,1)S(1)}, u32[]{:S(2)}, u32[]{:S(2)}) collective-permute-start(bf16[256,1536]{1,0:T(8,128)(2,1)S(1)} %pad_maximum_fusion.5), channel_id=1, source_target_pairs={{0,8},{4,12},{8,0},{12,4},{16,24},{20,28},{24,16},{28,20},{1,9},{5... | collective-permute-start | bytes 2359304 | tf_op jit(solution)/shard_map/ppermute | solution.py:277
  453.5 14.8 %collective-permute-start.34 = (f32[12,1024]{1,0:T(8,128)S(1)}, f32[12,1024]{1,0:T(8,128)S(1)}, u32[]{:S(2)}, u32[]{:S(2)}) collective-permute-start(f32[12,1024]{1,0:T(8,128)S(1)} %add.500), channel_id=1, source_target_pairs={{0,16},{4,20},{8,24},{12,28},{16,0},{20,4},{24,8},{28,12},{1,17},{... | collective-permute-start | bytes 147464 | tf_op jit(solution)/shard_map/ppermute | solution.py:277
  456.1 15.5 %collective-permute-start.31 = (bf16[256,1536]{1,0:T(8,128)(2,1)S(1)}, bf16[256,1536]{1,0:T(8,128)(2,1)S(1)}, u32[]{:S(2)}, u32[]{:S(2)}) collective-permute-start(bf16[256,1536]{1,0:T(8,128)(2,1)S(1)} %pad_maximum_fusion.4), channel_id=1, source_target_pairs={{0,4},{4,0},{8,12},{12,8},{16,20},{20,16},{24,28},{28,24},{1,5},{5... | collective-permute-start | bytes 2359304 | tf_op jit(solution)/shard_map/ppermute | solution.py:277
  468.5 5.0 %copy-start.12 = (bf16[512,1024]{1,0:T(8,128)(2,1)}, bf16[512,1024]{1,0:T(8,128)(2,1)S(1)}, u32[]{:S(2)}) copy-start(bf16[512,1024]{1,0:T(8,128)(2,1)S(1)} %pad_maximum_fusion.3.refs_0_) | copy-start | bytes 3145732
  473.0 11.1 %collective-permute-start.36 = (bf16[512,1536]{1,0:T(8,128)(2,1)}, bf16[512,1536]{1,0:T(8,128)(2,1)}, u32[]{:S(2)}, u32[]{:S(2)}) collective-permute-start(bf16[512,1536]{1,0:T(8,128)(2,1)} %pad_maximum_fusion.1.refs_0_), channel_id=1, source_target_pairs={{0,2},{2,0},{1,3},{3,1},{4,6},{6,4},{5,7},{7,5},{8,10},{10,8},{9,1... | collective-permute-start | bytes 4718600 | tf_op jit(solution)/shard_map/ppermute | solution.py:277
  473.0 11.1 %collective-permute-start.37 = (bf16[512,1536]{1,0:T(8,128)(2,1)}, bf16[512,1536]{1,0:T(8,128)(2,1)}, u32[]{:S(2)}, u32[]{:S(2)}) collective-permute-start(bf16[512,1536]{1,0:T(8,128)(2,1)} %pad_maximum_fusion.2.refs_1_), channel_id=1, source_target_pairs={{0,2},{2,0},{1,3},{3,1},{4,6},{6,4},{5,7},{7,5},{8,10},{10,8},{9,1... | collective-permute-start | bytes 4718600 | tf_op jit(solution)/shard_map/ppermute | solution.py:277
  473.5 6.1 %collective-permute-start.38 = (bf16[512,1024]{1,0:T(8,128)(2,1)S(1)}, bf16[512,1024]{1,0:T(8,128)(2,1)}, u32[]{:S(2)}, u32[]{:S(2)}) collective-permute-start(bf16[512,1024]{1,0:T(8,128)(2,1)S(1)} %pad_maximum_fusion.3.refs_0_), channel_id=1, source_target_pairs={{0,2},{2,0},{1,3},{3,1},{4,6},{6,4},{5,7},{7,5},{8,10},{10,8},{9,1... | collective-permute-start | bytes 3145736 | tf_op jit(solution)/shard_map/ppermute | solution.py:277
  473.5 3.2 collective-permute-start.35
  (30 other events, 62.8 us)
Sparse Core Ops, SparseCore 0:
  14.6 108.6 all-gather.2
  215.1 73.1 reduce-scatter.2
  291.1 93.3 reduce-scatter.4

commit v3 on v2

--- a/solution.py
+++ b/solution.py
@@ -62,31 +62,33 @@
     masks=[(lane<64).astype(bf),(lane>=64).astype(bf)]
     q=q_ref[...]; do=do_ref[...]
     prod=do.astype(f32)*o_ref[...]
-    qs=[q*(m*0.125) for m in masks]; dos=[do*m for m in masks]
+    q2=jnp.concatenate([q*(m*0.125) for m in masks],axis=0)
+    do2=jnp.concatenate([do*m for m in masks],axis=0)
     sel=(lax.broadcasted_iota(jnp.int32,(8,128),1)//64==lax.broadcasted_iota(jnp.int32,(8,128),0)).astype(f32)
     delta=lax.dot_general(sel,prod,NT,precision=lax.Precision.HIGHEST,preferred_element_type=f32)
-    lses=[lse_ref[pl.ds(2*i+j,1),:] for j in range(2)]
-    dq=[None,None]
-    for (kr,vr,base,cnt,own) in ((ko_ref,vo_ref,0,rows,True),(kx_ref,vx_ref,rows,nx,False)):
-        for b in range(0,cnt,kb):
-            k=kr[b:b+kb,:]; v=vr[b:b+kb,:]
-            bt=biast_ref[base+b:base+b+kb,:]
-            dk=dv=None
-            for j in range(2):
-                s=mm(k,qs[j],NT)+bt
-                p=jnp.exp(s-lses[j])
-                dp=mm(v,dos[j],NT)
-                ds=(p*(dp-delta[j:j+1,:])).astype(bf)
-                a=mm(p.astype(bf),dos[j],NN); c=mm(ds,qs[j],NN)
-                dv=a if dv is None else dv+a
-                dk=c if dk is None else dk+c
-                e=mm(ds,k,TN)
-                dq[j]=e if dq[j] is None else dq[j]+e
-            if own:
-                dko_ref[0,b:b+kb,:]=dk.astype(bf); dko_ref[1,b:b+kb,:]=dv.astype(bf)
-            else:
-                dx_ref[0,b:b+kb,:]=dk.astype(bf); dx_ref[1,b:b+kb,:]=dv.astype(bf)
-    dq_ref[...]=(jnp.where(lane<64,dq[0],dq[1])*0.125).astype(bf)
+    delta=jnp.concatenate([delta[0:1,:],delta[1:2,:]],axis=1)
+    lse=jnp.concatenate([lse_ref[pl.ds(2*i+j,1),:] for j in range(2)],axis=1)
+    ks=jnp.concatenate([ko_ref[...],kx_ref[...]],axis=0)
+    vs=jnp.concatenate([vo_ref[...],vx_ref[...]],axis=0)
+    dq=None
+    for b in range(0,rows+nx,kb):
+        k=ks[b:b+kb,:]; v=vs[b:b+kb,:]
+        bt=biast_ref[b:b+kb,:]
+        s=mm(k,q2,NT)+jnp.concatenate([bt,bt],axis=1)
+        p=jnp.exp(s-lse)
+        dp=mm(v,do2,NT)
+        ds=(p*(dp-delta)).astype(bf)
+        dv=mm(p.astype(bf),do2,NN).astype(bf)
+        dk=mm(ds,q2,NN).astype(bf)
+        e=mm(ds,k,TN)
+        dq=e if dq is None else dq+e
+        cut=min(max(rows-b,0),kb)
+        if cut:
+            dko_ref[0,b:b+cut,:]=dk[:cut]; dko_ref[1,b:b+cut,:]=dv[:cut]
+        if cut<kb:
+            at=b+cut-rows
+            dx_ref[0,at:at+kb-cut,:]=dk[cut:]; dx_ref[1,at:at+kb-cut,:]=dv[cut:]
+    dq_ref[...]=(jnp.where(lane<64,dq[:rows],dq[rows:])*0.125).astype(bf)
 
 def attn_bwd(joined, other, biast, lset, do, o, mb, kb=None):
     rows=biast.shape[1]; nx=other.shape[0]; D=other.shape[1]//2; G=D//128
@@ -283,16 +285,20 @@
     return [(axis, 1 << i) for i in range(count.bit_length() - 1)]
 
 
-def halve(values, steps, slot):
+def cut(values, steps, slot):
     sent, kept = [], []
     for value, order in zip(values, steps):
         axis, bit = order[slot]
         high = (lax.axis_index(axis) // bit) % 2
         half = value.shape[0] // 2
-        part = lax.dynamic_slice_in_dim(value, (1 - high) * half, half)
+        sent.append(lax.dynamic_slice_in_dim(value, (1 - high) * half, half))
         kept.append(lax.dynamic_slice_in_dim(value, high * half, half))
-        sent.append(swap(part, axis, bit))
-    return [a + b for a, b in zip(kept, sent)]
+    return tuple(sent), tuple(kept)
+
+
+def halve(values, steps, slot):
+    sent, kept = cut(values, steps, slot)
+    return [a + swap(b, *order[slot]) for a, b, order in zip(kept, sent, steps)]
 
 
 def double(values, steps, slot):
@@ -438,6 +444,13 @@
         ).astype(bf)
         if m + 1 < micro:
             sent, others[m + 1] = lax.optimization_barrier((sent, others[m + 1]))
+        if m + 1 == micro:
+            logs = tuple(state[2] for state in saved) + (log_total,)
+            sent, logs, turned = lax.optimization_barrier((sent, logs, tuple(b[1] for b in biases)))
+            log_total = logs[-1]
+            for n in range(m):
+                saved[n][2] = logs[n]
+            biases = [(b[0], t) for b, t in zip(biases, turned)]
         sent, before = lax.optimization_barrier((sent, before))
         if m == 0:
             grads_there = before
@@ -474,9 +487,6 @@
     active, inner_grad = kept
     out_term = out_grads(scaled_there, active)
     out_term, inner_grad, returned[0] = lax.optimization_barrier((out_term, inner_grad, returned[0]))
-    in_term = in_grads(rows_there, inner_grad, devices)
-    in_term, place_two[0] = lax.optimization_barrier((in_term, place_two[0]))
-    grad_in = lax.psum_scatter(in_term, ("context", "dp"), scatter_dimension=0, tiled=True)[0]
     grad_out_weight = lax.psum_scatter(
         out_term, ("context", "dp"), scatter_dimension=0, tiled=True
     )
@@ -512,8 +522,13 @@
             for s in range(1, contexts)
         ]
         groups.append([query_grad, own, parts])
+        if m == 0:
+            inner_grad, query_grad = lax.optimization_barrier((inner_grad, query_grad))
+            in_term = in_grads(rows_there, inner_grad, devices)
         if m + 1 < micro:
-            query_grad, place_two[m + 1] = lax.optimization_barrier((query_grad, place_two[m + 1]))
+            in_term, query_grad, place_two[m + 1] = lax.optimization_barrier(
+                (in_term, query_grad, place_two[m + 1])
+            )
             groups[m][0] = query_grad
         middle_grads.append(middle_grad)
         branches.append(branch)
@@ -530,6 +545,11 @@
     halves, joined_grad = [], None
     for first in (0, 3):
         joined_grad, kept, sent = project_grads(normed_low, groups, high, first, 3, joined_grad)
+        if first == 0:
+            kept, in_term, grad_out_weight = lax.optimization_barrier(
+                (kept, in_term, grad_out_weight)
+            )
+            grad_in = lax.psum_scatter(in_term, ("context", "dp"), scatter_dimension=0, tiled=True)[0]
         halves.append(kept + swap(sent, *near[0]))
     halves.append(halve([out_sum], [near], 0)[0])
     for slot in range(1, len(near)):
@@ -542,7 +562,8 @@
         dp_bits + expert_bits[1:] + expert_bits[:1],
     )
     count = len(orders[0])
-    for slot in range(count):
+    steps = near + dp_bits + expert_bits
+    for slot in range(count - 1):
         chunks = halve(chunks, orders, slot)
         if slot == 0:
             chunks, joined_grad = lax.optimization_barrier((chunks, joined_grad))
@@ -555,29 +576,34 @@
         elif slot == 1:
             chunks, small, grad_tokens = lax.optimization_barrier((chunks, small, grad_tokens))
         else:
-            chunks = lax.optimization_barrier(chunks)
-    steps = dp_bits + expert_bits + near
-    for index in range(count):
-        chunks = double(chunks, orders, count - 1 - index)
-        small = small + swap(small, *steps[index])
-        chunks, small = lax.optimization_barrier((chunks, small))
-        if index == 0:
+            small = small + swap(small, *steps.pop())
+            chunks, small = lax.optimization_barrier((chunks, small))
+    small = small + swap(small, *steps.pop())
+    chunks, small = lax.optimization_barrier(
+        (tuple(chunk + swap(chunk, *order[-1]) for chunk, order in zip(chunks, orders)), small)
+    )
+    for slot in reversed(range(count - 1)):
+        chunks = double(chunks, orders, slot)
+        if steps:
+            small = small + swap(small, *steps.pop())
+        if slot:
+            chunks, small = lax.optimization_barrier((tuple(chunks), small))
+        if slot == count - 2:
             chunks, grad_in, grad_out_weight = lax.optimization_barrier(
                 (chunks, grad_in, grad_out_weight)
             )
             grad_in = jnp.concatenate([grad_in[k] for k in range(grad_in.shape[0])], axis=1).astype(f32)
             grad_out_weight = grad_out_weight.astype(f32)
-        if index == count - 2:
+        if slot == 1:
             chunks, grad_in, grad_out_weight = lax.optimization_barrier(
                 (chunks, grad_in, grad_out_weight)
             )
+    assert not steps
     for slot in reversed(range(1, len(near))):
         chunks = double(chunks, (near,) * 3, slot)
-        small = small + swap(small, *near[slot])
-    small = small + swap(small, *near[0])
-    others = [swap(chunk, *near[0]) for chunk in chunks]
-    out_sum = widen(chunks[2:], others[2:], high)
-    in_sum = widen(chunks[:2], others[:2], high)
+    out_sum = widen(chunks[2:], [swap(chunks[2], *near[0])], high)
+    first, last, out_sum = lax.optimization_barrier((chunks[0], chunks[1], out_sum))
+    in_sum = widen([first, last], [swap(first, *near[0]), swap(last, *near[0])], high)
     return (
         jnp.stack(outputs)[:, None],
         grad_tokens.reshape(micro, 1, rows, model),

time: 506 us -> 484 us (0.957)
  waiting for transfers between devices: 102 us -> 86.4 us
    all_to_all x2, waiting for transfers between devices: 7.5 us -> 0.04 us  [local(): lax.all_to_all(back, 'expert', split_axis=0, concat_axis=0, tiled=True)]
    all_to_all x2, waiting for transfers between devices: 15.8 us -> 10.4 us  [local(): lax.all_to_all(sent.reshape(experts, block, model), 'expert', split_axis=...]
    ppermute x35 -> x32, starting transfers between devices: 35 us -> 30.1 us  [swap(): lax.ppermute(values, axis, [(i, i ^ bit) for i in range(lax.axis_size(axi...]
    ppermute x35 -> x32, waiting for transfers between devices: 77.4 us -> 75.4 us  [swap(): lax.ppermute(values, axis, [(i, i ^ bit) for i in range(lax.axis_size(axi...]
    unnamed x98 -> x92, local copies, waits for them, and re-layouts: 10.4 us -> 9.56 us
  transfers between devices with their start and end apart: 47 -> 44, of which waited for: 25 -> 22; matrix products, arithmetic and copies ran while one was open for 27% -> 28% of each run, Pallas kernels for 30% -> 33%
where the time goes in v3:
time: 484 us; the launch traced here: 476 us
  Pallas kernels  168 us (35%)
  waiting for transfers between devices  86.4 us (18%)
  starting transfers between devices  61.7 us (13%)
  matrix products  58.6 us (12%)
  other arithmetic  56.7 us (12%)
  local copies, waits for them, and re-layouts  30 us (6%)
  between operations  15 us (3%)
    ppermute x32, waiting for transfers between devices, swap(): lax.ppermute(values, axis, [(i, i ^ bit) for i in range(lax.axis_size(axi...  75.4 us
    pallas_call x2, Pallas kernels, expert(): pl.pallas_call(exp_body, grid=(FF // fb,), in_specs=[pl.BlockSpec((rows,...  48.3 us
    pallas_call x2, Pallas kernels, attn_bwd(): pl.pallas_call(partial(bwd_body, kb), grid=(G,), in_specs=[pl.BlockSpec(b...  37.2 us
    ppermute x32, starting transfers between devices, swap(): lax.ppermute(values, axis, [(i, i ^ bit) for i in range(lax.axis_size(axi...  30.1 us
    pallas_call x2, Pallas kernels, attn_fwd(): pl.pallas_call(partial(fwd_body, rb), grid=(G,), in_specs=[pl.BlockSpec(b...  25.3 us
    pallas_call x2, Pallas kernels, project_grads(): pl.pallas_call(partial(project_body, count, parts, first, per), grid_spec...  15.8 us
    pallas_call x1, Pallas kernels, in_grads(): pl.pallas_call(partial(in_grads_body, count), grid=(FF // fb,), in_specs=...  14.5 us
    pallas_call x1, Pallas kernels, out_grads(): pl.pallas_call(partial(out_grads_body, count), grid=(FF // fb,), in_specs...  14.1 us
  transfers between devices with their start and end apart: 44, of which 22 were waited for; matrix products, arithmetic and copies ran while one was open for 28% of the time, Pallas kernels for 33%

profile of v3, /device:TPU:0, one launch (start us, length us, event | category | flops | bytes accessed | tf_op | source)
XLA Modules:
  0.0 476.3 jit_solution(13931787043483721749)
XLA Ops:
  7.2 2.0 slice_dynamic-update-slice_fusion.3
  9.3 2.0 slice_dynamic-update-slice_fusion.2
  22.5 2.2 multiply_reduce_fusion.2
  24.8 2.3 add_convert_fusion.x_ref
  27.1 9.6 %convolution_convert_fusion.q_ref.ko_ref.vo_ref = bf16[768,3072]{1,0:T(8,128)(2,1)S(1)} fusion(bf16[768,1024]{1,0:T(8,128)(2,1)S(1)} %add_convert_fusion.x_ref, bf16[1024,3072]{1,0:T(8,128)(2,1)} %param.21), kind=kOutput, calls=%fused_computation | convolution fusion | flops 4834197504 | bytes 12582912 | tf_op jit(solution)/shard_map/dot_general | solution.py:378
  36.7 2.2 fusion.92
  40.3 7.9 %all-to-all-start = ((bf16[8,2,56,1024]{3,2,1,0:T(8,128)(2,1)}), bf16[8,2,56,1024]{3,2,1,0:T(8,128)(2,1)}, u32[]{:S(2)}, u32[]{:S(2)}) async-start(bf16[8,2,56,1024]{3,2,1,0:T(8,128)(2,1)} %pad_maximum_fusion), calls=%async_computation | async-start | bytes 3670016 | tf_op jit(solution)/shard_map/all_to_all | solution.py:373
  57.4 12.6 %attn_fwd.2 = (f32[384,1024]{1,0:T(8,128)}, bf16[384,1024]{1,0:T(8,128)(2,1)}, f32[384,128]{1,0:T(8,128)}) custom-call(f32[384,768]{1,0:T(8,128)} %and_select_fusion.3.bias_ref, bf16[768,3072]{1,0:T(8,128)(2,1)} %copy-done.1, bf16[768,3072]{1,0:T(8,128)(2,1)} %copy-done.1, bf16[768,3072]{1,0:T(8,128)(2,1)} %copy-done.1, ...), custom_call_target="tpu_custom_call" | custom-call | flops 384 | bytes 384 | tf_op jit(solution)/shard_map/attn_fwd/pallas_call | solution.py:45
  70.0 2.4 fusion.97
  76.3 12.7 %attn_fwd.3 = (f32[384,1024]{1,0:T(8,128)}, bf16[384,1024]{1,0:T(8,128)(2,1)}, f32[384,128]{1,0:T(8,128)}) custom-call(f32[384,768]{1,0:T(8,128)} %and_select_fusion.2.bias_ref, bf16[768,3072]{1,0:T(8,128)(2,1)} %copy-done.1, bf16[768,3072]{1,0:T(8,128)(2,1)} %copy-done.1, bf16[768,3072]{1,0:T(8,128)(2,1)} %copy-done.1, ...), custom_call_target="tpu_custom_call" | custom-call | flops 384 | bytes 384 | tf_op jit(solution)/shard_map/attn_fwd/pallas_call | solution.py:45
  88.9 2.4 fusion.99
  93.7 6.1 %all-to-all-start.1 = ((bf16[8,56,1024]{2,1,0:T(8,128)(2,1)}), bf16[8,56,1024]{2,1,0:T(8,128)(2,1)}, u32[]{:S(2)}, u32[]{:S(2)}) async-start(bf16[8,56,1024]{2,1,0:T(8,128)(2,1)} %bitcast.152), calls=%async_computation.1 | async-start | bytes 1835008 | tf_op jit(solution)/shard_map/all_to_all | solution.py:459
  104.5 3.2 fusion.21
  109.6 2.9 fusion.93
  112.5 10.4 %all-to-all-done.1 = bf16[8,56,1024]{2,1,0:T(8,128)(2,1)} async-done(((bf16[8,56,1024]{2,1,0:T(8,128)(2,1)}), bf16[8,56,1024]{2,1,0:T(8,128)(2,1)}, u32[]{:S(2)}, u32[]{:S(2)}) %all-to-all-start.1) | async-done | bytes 917536 | tf_op jit(solution)/shard_map/all_to_all | solution.py:459
  123.8 4.4 all-to-all-start.2
  128.2 2.3 fusion.2.g_ref.refs_0_
  130.5 24.2 %expert.2 = (bf16[896,4096]{1,0:T(8,128)(2,1)}, bf16[896,4096]{1,0:T(8,128)(2,1)}, bf16[8,112,1024]{2,1,0:T(8,128)(2,1)}) custom-call(bf16[448,1024]{1,0:T(8,128)(2,1)} %bitcast.21.x_ref.refs_0_, bf16[448,1024]{1,0:T(8,128)(2,1)} %fusion.2.g_ref.refs_0_, bf16[4,8,256,1024]{3,2,1,0:T(8,128)(2,1)} %bitcast.168, bf16[4,4,512,1024]{3,2,1,0:T(8,128)(2,1)} %bitcast.169), custom_call_target="tpu_custom_call" | custom-call | flops 15032385536 | bytes 24117248 | tf_op jit(solution)/shard_map/expert/pallas_call | solution.py:144
  154.7 6.0 %all-to-all-start.3 = ((bf16[8,112,1024]{2,1,0:T(8,128)(2,1)}), bf16[8,112,1024]{2,1,0:T(8,128)(2,1)}, u32[]{:S(2)}, u32[]{:S(2)}) async-start(bf16[8,112,1024]{2,1,0:T(8,128)(2,1)} %get-tuple-element.121), calls=%async_computation.3 | async-start | bytes 3670016 | tf_op jit(solution)/shard_map/all_to_all | solution.py:483
  161.7 2.3 fusion.1.g_ref.refs_1_
  164.0 24.1 %expert.3 = (bf16[896,4096]{1,0:T(8,128)(2,1)}, bf16[896,4096]{1,0:T(8,128)(2,1)}, bf16[8,112,1024]{2,1,0:T(8,128)(2,1)}) custom-call(bf16[448,1024]{1,0:T(8,128)(2,1)} %bitcast.28.x_ref.refs_1_, bf16[448,1024]{1,0:T(8,128)(2,1)} %fusion.1.g_ref.refs_1_, bf16[4,8,256,1024]{3,2,1,0:T(8,128)(2,1)} %bitcast.170, ...), custom_call_target="tpu_custom_call", output_to_operand_aliasing={{0}: (4, {}), {1}: (5, {})} | custom-call | flops 15032385536 | bytes 24117248 | tf_op jit(solution)/shard_map/expert/pallas_call | solution.py:144
  188.1 14.1 %out_grads.1 = bf16[4096,1024]{1,0:T(8,128)(2,1)} custom-call(bf16[448,1024]{1,0:T(8,128)(2,1)} %fusion.2.g_ref.refs_0_, bf16[448,1024]{1,0:T(8,128)(2,1)} %fusion.1.g_ref.refs_1_, bf16[896,4096]{1,0:T(8,128)(2,1)} %get-tuple-element.119.refs_2_), custom_call_target="tpu_custom_call" | custom-call | flops 7516192768 | bytes 15728640 | tf_op jit(solution)/shard_map/out_grads/pallas_call | solution.py:183
  204.6 5.9 %all-to-all-start.4 = ((bf16[8,112,1024]{2,1,0:T(8,128)(2,1)}), bf16[8,112,1024]{2,1,0:T(8,128)(2,1)}, u32[]{:S(2)}, u32[]{:S(2)}) async-start(bf16[8,112,1024]{2,1,0:T(8,128)(2,1)} %get-tuple-element.131), calls=%async_computation.4 | async-start | bytes 3670016 | tf_op jit(solution)/shard_map/all_to_all | solution.py:483
  210.5 5.2 %fusion.31 = (bf16[1,384,1024]{2,1,0:T(8,128)(2,1)}, f32[384]{0:T(512)S(1)}) fusion(f32[384,1024]{1,0:T(8,128)} %copy-done.6, f32[384]{0:T(512)S(1)} %select_reduce_fusion.1, bf16[2,1,384,1024]{3,2,1,0:T(8,128)(2,1)} %param.15, bf16[896,1024]{1,0:T(8,128)(2,1)} %bitcast.29, s32[384]{0:T(512)S(1)} %get-tuple-element.264), kind=kOutput, calls=%fused_computation.88 | convolution fusion | flops 707346048 | bytes 4985344 | tf_op jit(solution)/shard_map/dot_general | solution.py:500
  215.8 3.1 fusion.28
  222.2 1.9 convolution_convert_fusion.5.do_ref
  224.1 18.7 %attn_bwd.2 = (bf16[384,1024]{1,0:T(8,128)(2,1)}, bf16[2,384,1024]{2,1,0:T(8,128)(2,1)}, bf16[2,384,1024]{2,1,0:T(8,128)(2,1)}) custom-call(f32[768,384]{1,0:T(8,128)} %and_select_fusion.1.biast_ref, f32[16,384]{1,0:T(8,128)} %slice_bitcast_fusion.6.lse_ref, bf16[768,3072]{1,0:T(8,128)(2,1)} %copy-done.1, bf16[768,3072]{1,0:T(8,128)(2,1)} %copy-done.1, ...), custom_call_target="tpu_custom_call" | custom-call | flops 12079595520 | bytes 11796480 | tf_op jit(solution)/shard_map/attn_bwd/pallas_call | solution.py:97
  242.8 14.5 %in_grads.1 = bf16[4,4,256,1024]{3,2,1,0:T(8,128)(2,1)} custom-call(bf16[448,1024]{1,0:T(8,128)(2,1)} %bitcast.21.x_ref.refs_0_, bf16[448,1024]{1,0:T(8,128)(2,1)} %bitcast.28.x_ref.refs_1_, bf16[896,4096]{1,0:T(8,128)(2,1)} %get-tuple-element.128.refs_2_), custom_call_target="tpu_custom_call" | custom-call | flops 7516192768 | bytes 15728640 | tf_op jit(solution)/shard_map/in_grads/pallas_call | solution.py:166
  257.3 3.1 fusion.4
  260.5 2.6 fusion.101
  264.6 2.1 fusion.90
  268.6 18.5 %attn_bwd.3 = (bf16[384,1024]{1,0:T(8,128)(2,1)}, bf16[2,384,1024]{2,1,0:T(8,128)(2,1)}, bf16[2,384,1024]{2,1,0:T(8,128)(2,1)}) custom-call(f32[768,384]{1,0:T(8,128)} %and_select_fusion.biast_ref, f32[16,384]{1,0:T(8,128)} %slice_bitcast_fusion.5.lse_ref, bf16[768,3072]{1,0:T(8,128)(2,1)} %copy-done.1, bf16[768,3072]{1,0:T(8,128)(2,1)} %copy-done.1, ...), custom_call_target="tpu_custom_call" | custom-call | flops 12079595520 | bytes 11796480 | tf_op jit(solution)/shard_map/attn_bwd/pallas_call | solution.py:97
  287.7 5.0 %convolution_convert_fusion.1 = bf16[1024,1024]{1,0:T(8,128)(2,1)} fusion(bf16[384,1024]{1,0:T(8,128)(2,1)} %get-tuple-element.105, bf16[384,1024]{1,0:T(8,128)(2,1)} %get-tuple-element.103, bf16[384,1024]{1,0:T(8,128)(2,1)} %copy-done.26, bf16[384,1024]{1,0:T(8,128)(2,1)} %copy-done.28), kind=kOutput, calls=%fused_computation.16 | convolution fusion | flops 1617952768 | bytes 5242880 | tf_op jit(solution)/shard_map/dot_general | solution.py:539
  293.2 7.5 %project_grads.2 = (bf16[768,3072]{1,0:T(8,128)(2,1)}, bf16[512,1536]{1,0:T(8,128)(2,1)}, bf16[512,1536]{1,0:T(8,128)(2,1)}) custom-call(s32[1]{0:T(128)} %bitcast.35.high_ref, bf16[768,1024]{1,0:T(8,128)(2,1)} %copy-done.22, bf16[384,1024]{1,0:T(8,128)(2,1)} %get-tuple-element.132.refs_0_, bf16[2,384,1024]{2,1,0:T(8,128)(2,1)} %get-tuple-element.133.refs_1_, ...), custom_call_target="tpu_custom_call" | custom-call | flops 4831838208 | bytes 18874368 | tf_op jit(solution)/shard_map/project_grads/pallas_call | solution.py:221
  300.8 8.2 %project_grads.3 = (bf16[768,3072]{1,0:T(8,128)(2,1)}, bf16[512,1536]{1,0:T(8,128)(2,1)}, bf16[512,1536]{1,0:T(8,128)(2,1)}) custom-call(s32[1]{0:T(128)} %bitcast.35.high_ref, bf16[768,1024]{1,0:T(8,128)(2,1)} %copy-done.22, bf16[384,1024]{1,0:T(8,128)(2,1)} %get-tuple-element.132.refs_0_, ...), custom_call_target="tpu_custom_call", output_to_operand_aliasing={{0}: (8, {})} | custom-call | flops 4831838208 | bytes 18874368 | tf_op jit(solution)/shard_map/project_grads/pallas_call | solution.py:221
  309.1 2.6 constant_dynamic-slice_fusion.7
  312.2 4.0 collective-permute-done.8
  316.2 2.2 dynamic-slice_add_fusion
  321.3 4.1 collective-permute-start.7
  329.6 6.0 %collective-permute-done.9 = bf16[256,1024]{1,0:T(8,128)(2,1)S(1)} collective-permute-done((bf16[256,1024]{1,0:T(8,128)(2,1)S(1)}, bf16[256,1024]{1,0:T(8,128)(2,1)S(1)}, u32[]{:S(2)}, u32[]{:S(2)}) %collective-permute-start.9) | collective-permute-done | bytes 524320 | tf_op jit(solution)/shard_map/ppermute | solution.py:279
  335.7 7.2 %collective-permute-done.7 = bf16[256,1536]{1,0:T(8,128)(2,1)S(1)} collective-permute-done((bf16[256,1536]{1,0:T(8,128)(2,1)S(1)}, bf16[256,1536]{1,0:T(8,128)(2,1)S(1)}, u32[]{:S(2)}, u32[]{:S(2)}) %collective-permute-start.7) | collective-permute-done | bytes 786464 | tf_op jit(solution)/shard_map/ppermute | solution.py:279
  343.1 3.6 collective-permute-done.5
  352.2 8.2 %multiply_reduce_fusion = (f32[768]{0:T(1024)S(1)}, f32[1024]{0:T(1024)S(1)}, f32[768]{0:T(1024)S(1)}, f32[1024]{0:T(1024)S(1)}, f32[768,1024]{1,0:T(8,128)S(1)}) fusion(bf16[2,1,384,1024]{3,2,1,0:T(8,128)(2,1)S(1)} %copy-done.3, f32[1024]{0:T(1024)S(1)} %copy-done.37, f32[768]{0:T(1024)S(1)} %copy-done.35, f32[768]{0:T(1024)S(1)} %copy-done.33, ...), kind=kOutput, calls=%fused_computation.4 | convolution fusion | flops 4839698432 | bytes 15753216 | tf_op jit(solution)/shard_map/dot_general | solution.py:570
  360.4 2.9 maximum_add_fusion
  365.8 5.9 %collective-permute-done.10 = bf16[128,1536]{1,0:T(8,128)(2,1)} collective-permute-done((bf16[128,1536]{1,0:T(8,128)(2,1)}, bf16[128,1536]{1,0:T(8,128)(2,1)}, u32[]{:S(2)}, u32[]{:S(2)}) %collective-permute-start.10) | collective-permute-done | bytes 393248 | tf_op jit(solution)/shard_map/ppermute | solution.py:279
  372.8 2.4 collective-permute-start.16
  377.3 2.6 collective-permute-done.16
  379.8 3.5 collective-permute-done.15
  383.4 3.3 collective-permute-done.14
  386.8 2.5 collective-permute-start.18
  391.0 4.6 collective-permute-done.20
  395.7 4.1 collective-permute-done.18
  399.8 3.6 collective-permute-done.17
  405.0 2.9 collective-permute-start.21
  407.9 3.5 collective-permute-done.23
  411.5 2.3 collective-permute-done.21
  415.7 3.2 collective-permute-done.28
  423.2 2.5 maximum_convert_fusion
  425.7 2.5 convert_element_type.285
  434.3 7.3 %collective-permute-done.32 = bf16[256,1024]{1,0:T(8,128)(2,1)S(1)} collective-permute-done((bf16[256,1024]{1,0:T(8,128)(2,1)S(1)}, bf16[256,1024]{1,0:T(8,128)(2,1)S(1)}, u32[]{:S(2)}, u32[]{:S(2)}) %collective-permute-start.32) | collective-permute-done | bytes 524320 | tf_op jit(solution)/shard_map/ppermute | solution.py:279
  441.9 6.1 %collective-permute-done.31 = bf16[256,1536]{1,0:T(8,128)(2,1)S(1)} collective-permute-done((bf16[256,1536]{1,0:T(8,128)(2,1)S(1)}, bf16[256,1536]{1,0:T(8,128)(2,1)S(1)}, u32[]{:S(2)}, u32[]{:S(2)}) %collective-permute-start.31) | collective-permute-done | bytes 786464 | tf_op jit(solution)/shard_map/ppermute | solution.py:279
  450.8 4.6 widen.2
  455.9 2.4 maximum_bitcast_fusion
  461.5 8.1 %widen.3 = f32[1024,3072]{1,0:T(8,128)} custom-call(s32[1]{0:T(128)} %bitcast.35.high_ref, bf16[512,1536]{1,0:T(8,128)(2,1)} %pad_maximum_fusion.1.refs_0_, bf16[512,1536]{1,0:T(8,128)(2,1)} %pad_maximum_fusion.2.refs_1_, bf16[512,1536]{1,0:T(8,128)(2,1)} %collective-permute-done.34.refs_2_, bf16[512,1536]{1,0:T(8,128)(2,1)} %collective-permute-done.35.refs_3_), custom_call_target="tpu_custom_call" | custom-call | flops 1572864 | bytes 18874368 | tf_op jit(solution)/shard_map/widen/pallas_call | solution.py:247
  (293 shorter events, 87.9 us)
Async XLA Ops:
  7.2 62.9 %copy-start = (bf16[1024,1024]{1,0:T(8,128)(2,1)S(1)}, bf16[1024,1024]{1,0:T(8,128)(2,1)}, u32[]{:S(2)}) copy-start(bf16[1024,1024]{1,0:T(8,128)(2,1)} %param.22) | copy-start | bytes 6291460
  7.2 123.3 %all-gather.3.cloned.1.call-start = ((), (), s32[]{:S(2)}) async-start(), calls=%async_computation.9 | async-start | bytes 20971520 | tf_op jit(solution)/shard_map/all_gather | solution.py:345
  7.2 4.1 copy-start.20
  9.3 3.7 copy-start.21
  22.5 4.6 copy-start.32
  27.1 9.6 %copy-start.22 = (bf16[768,1024]{1,0:T(8,128)(2,1)}, bf16[768,1024]{1,0:T(8,128)(2,1)S(1)}, u32[]{:S(2)}) copy-start(bf16[768,1024]{1,0:T(8,128)(2,1)S(1)} %add_convert_fusion.x_ref) | copy-start | bytes 4718596
  39.8 17.6 %collective-permute-start = (bf16[384,2048]{1,0:T(8,128)(2,1)}, bf16[384,2048]{1,0:T(8,128)(2,1)}, u32[]{:S(2)}, u32[]{:S(2)}) collective-permute-start(bf16[384,2048]{1,0:T(8,128)(2,1)} %get-tuple-element.270), channel_id=1, source_target_pairs={{0,2},{2,0},{1,3},{3,1},{4,6},{6,4},{5,7},{7,5},{8,10},{10,8},{9,1... | collective-permute-start | bytes 4718600 | tf_op jit(solution)/shard_map/ppermute | solution.py:383
  40.2 8.1 %copy-start.42 = (s32[2,1,3]{2,1,0:T(1,128)S(1)}, s32[2,1,3]{2,1,0:T(1,128)}, u32[]{:S(2)}) copy-start(s32[2,1,3]{2,1,0:T(1,128)} %param.16) | copy-start | bytes 76
  40.2 8.4 %copy-start.39 = (s32[2,1,768]{2,1,0:T(1,128)S(1)}, s32[2,1,768]{2,1,0:T(1,128)}, u32[]{:S(2)}) copy-start(s32[2,1,768]{2,1,0:T(1,128)} %param.17) | copy-start | bytes 18436
  40.2 36.0 %collective-permute-start.1 = (bf16[384,2048]{1,0:T(8,128)(2,1)}, bf16[384,2048]{1,0:T(8,128)(2,1)}, u32[]{:S(2)}, u32[]{:S(2)}) collective-permute-start(bf16[384,2048]{1,0:T(8,128)(2,1)} %get-tuple-element.269), channel_id=1, source_target_pairs={{0,2},{2,0},{1,3},{3,1},{4,6},{6,4},{5,7},{7,5},{8,10},{10,8},{9,1... | collective-permute-start | bytes 4718600 | tf_op jit(solution)/shard_map/ppermute | solution.py:383
  40.3 53.4 %all-to-all-start = ((bf16[8,2,56,1024]{3,2,1,0:T(8,128)(2,1)}), bf16[8,2,56,1024]{3,2,1,0:T(8,128)(2,1)}, u32[]{:S(2)}, u32[]{:S(2)}) async-start(bf16[8,2,56,1024]{3,2,1,0:T(8,128)(2,1)} %pad_maximum_fusion), calls=%async_computation | async-start | bytes 3670016 | tf_op jit(solution)/shard_map/all_to_all | solution.py:373
  93.7 29.1 %all-to-all-start.1 = ((bf16[8,56,1024]{2,1,0:T(8,128)(2,1)}), bf16[8,56,1024]{2,1,0:T(8,128)(2,1)}, u32[]{:S(2)}, u32[]{:S(2)}) async-start(bf16[8,56,1024]{2,1,0:T(8,128)(2,1)} %bitcast.152), calls=%async_computation.1 | async-start | bytes 1835008 | tf_op jit(solution)/shard_map/all_to_all | solution.py:459
  123.8 30.9 %all-to-all-start.2 = ((bf16[8,56,1024]{2,1,0:T(8,128)(2,1)}), bf16[8,56,1024]{2,1,0:T(8,128)(2,1)}, u32[]{:S(2)}, u32[]{:S(2)}) async-start(bf16[8,56,1024]{2,1,0:T(8,128)(2,1)} %bitcast.153), calls=%async_computation.2 | async-start | bytes 1835008 | tf_op jit(solution)/shard_map/all_to_all | solution.py:459
  154.7 47.6 %all-to-all-start.3 = ((bf16[8,112,1024]{2,1,0:T(8,128)(2,1)}), bf16[8,112,1024]{2,1,0:T(8,128)(2,1)}, u32[]{:S(2)}, u32[]{:S(2)}) async-start(bf16[8,112,1024]{2,1,0:T(8,128)(2,1)} %get-tuple-element.121), calls=%async_computation.3 | async-start | bytes 3670016 | tf_op jit(solution)/shard_map/all_to_all | solution.py:483
  160.7 140.0 %reduce-scatter.3.cloned.1.call-start = ((), (), s32[]{:S(2)}) async-start(), calls=%async_computation.7 | async-start | bytes 10485760 | tf_op jit(solution)/shard_map/reduce_scatter | solution.py:490
  204.6 52.8 %all-to-all-start.4 = ((bf16[8,112,1024]{2,1,0:T(8,128)(2,1)}), bf16[8,112,1024]{2,1,0:T(8,128)(2,1)}, u32[]{:S(2)}, u32[]{:S(2)}) async-start(bf16[8,112,1024]{2,1,0:T(8,128)(2,1)} %get-tuple-element.131), calls=%async_computation.4 | async-start | bytes 3670016 | tf_op jit(solution)/shard_map/all_to_all | solution.py:483
  210.5 208.5 %reduce-scatter.5.cloned.1.call-start = ((), (), s32[]{:S(2)}) async-start(), calls=%async_computation.8 | async-start | bytes 10485760 | tf_op jit(solution)/shard_map/reduce_scatter | solution.py:552
  287.1 5.6 %collective-permute-start.3 = (bf16[2,384,1024]{2,1,0:T(8,128)(2,1)}, bf16[2,384,1024]{2,1,0:T(8,128)(2,1)}, u32[]{:S(2)}, u32[]{:S(2)}) collective-permute-start(bf16[2,384,1024]{2,1,0:T(8,128)(2,1)} %get-tuple-element.141), channel_id=1, source_target_pairs={{0,2},{2,0},{1,3},{3,1},{4,6},{6,4},{5,7},{7,5},{8,10},{10,8},{9,1... | collective-permute-start | bytes 4718600 | tf_op jit(solution)/shard_map/ppermute | solution.py:517
  287.2 6.0 %collective-permute-start.2 = (bf16[2,384,1024]{2,1,0:T(8,128)(2,1)}, bf16[2,384,1024]{2,1,0:T(8,128)(2,1)}, u32[]{:S(2)}, u32[]{:S(2)}) collective-permute-start(bf16[2,384,1024]{2,1,0:T(8,128)(2,1)} %get-tuple-element.134), channel_id=1, source_target_pairs={{0,2},{2,0},{1,3},{3,1},{4,6},{6,4},{5,7},{7,5},{8,10},{10,8},{9,1... | collective-permute-start | bytes 4718600 | tf_op jit(solution)/shard_map/ppermute | solution.py:517
  309.0 10.4 %collective-permute-start.6 = (bf16[512,1536]{1,0:T(8,128)(2,1)}, bf16[512,1536]{1,0:T(8,128)(2,1)}, u32[]{:S(2)}, u32[]{:S(2)}) collective-permute-start(bf16[512,1536]{1,0:T(8,128)(2,1)} %get-tuple-element.150), channel_id=1, source_target_pairs={{0,2},{2,0},{1,3},{3,1},{4,6},{6,4},{5,7},{7,5},{8,10},{10,8},{9,1... | collective-permute-start | bytes 4718600 | tf_op jit(solution)/shard_map/ppermute | solution.py:279
  311.7 4.5 collective-permute-start.8
  312.0 13.7 %collective-permute-start.4 = (bf16[512,1536]{1,0:T(8,128)(2,1)}, bf16[512,1536]{1,0:T(8,128)(2,1)}, u32[]{:S(2)}, u32[]{:S(2)}) collective-permute-start(bf16[512,1536]{1,0:T(8,128)(2,1)} %get-tuple-element.147), channel_id=1, source_target_pairs={{0,2},{2,0},{1,3},{3,1},{4,6},{6,4},{5,7},{7,5},{8,10},{10,8},{9,1... | collective-permute-start | bytes 4718600 | tf_op jit(solution)/shard_map/ppermute | solution.py:279
  312.2 7.2 %copy-start.25 = (bf16[512,1536]{1,0:T(8,128)(2,1)S(1)}, bf16[512,1536]{1,0:T(8,128)(2,1)}, u32[]{:S(2)}) copy-start(bf16[512,1536]{1,0:T(8,128)(2,1)} %get-tuple-element.149) | copy-start | bytes 4718596
  318.5 17.0 %collective-permute-start.9 = (bf16[256,1024]{1,0:T(8,128)(2,1)S(1)}, bf16[256,1024]{1,0:T(8,128)(2,1)S(1)}, u32[]{:S(2)}, u32[]{:S(2)}) collective-permute-start(bf16[256,1024]{1,0:T(8,128)(2,1)S(1)} %constant_dynamic-slice_fusion.6), channel_id=1, source_target_pairs={{0,1},{1,0},{2,3},{3,2},{4,5},{5,4},{6,7},{7,6},{8,9},{9,8},{10,11... | collective-permute-start | bytes 1572872 | tf_op jit(solution)/shard_map/ppermute | solution.py:279
  321.2 4.6 copy-start.24
  321.3 21.6 %collective-permute-start.7 = (bf16[256,1536]{1,0:T(8,128)(2,1)S(1)}, bf16[256,1536]{1,0:T(8,128)(2,1)S(1)}, u32[]{:S(2)}, u32[]{:S(2)}) collective-permute-start(bf16[256,1536]{1,0:T(8,128)(2,1)S(1)} %constant_dynamic-slice_fusion.8), channel_id=1, source_target_pairs={{0,8},{4,12},{8,0},{12,4},{16,24},{20,28},{24,16},{28,20},{1,9},{5... | collective-permute-start | bytes 2359304 | tf_op jit(solution)/shard_map/ppermute | solution.py:279
  327.7 19.1 %collective-permute-start.5 = (bf16[256,1536]{1,0:T(8,128)(2,1)S(1)}, bf16[256,1536]{1,0:T(8,128)(2,1)S(1)}, u32[]{:S(2)}, u32[]{:S(2)}) collective-permute-start(bf16[256,1536]{1,0:T(8,128)(2,1)S(1)} %constant_dynamic-slice_fusion.9), channel_id=1, source_target_pairs={{0,4},{4,0},{8,12},{12,8},{16,20},{20,16},{24,28},{28,24},{1,5},{5... | collective-permute-start | bytes 2359304 | tf_op jit(solution)/shard_map/ppermute | solution.py:279
  342.9 9.2 %copy-start.43 = (bf16[768,3072]{1,0:T(8,128)(2,1)S(1)}, bf16[768,3072]{1,0:T(8,128)(2,1)}, u32[]{:S(2)}) copy-start(bf16[768,3072]{1,0:T(8,128)(2,1)} %get-tuple-element.156) | copy-start | bytes 14155780
  346.9 4.1 copy-start.16
  347.0 5.2 %copy-start.3 = (bf16[2,1,384,1024]{3,2,1,0:T(8,128)(2,1)S(1)}, bf16[2,1,384,1024]{3,2,1,0:T(8,128)(2,1)}, u32[]{:S(2)}) copy-start(bf16[2,1,384,1024]{3,2,1,0:T(8,128)(2,1)} %param.14) | copy-start | bytes 4718596
  347.0 5.2 %copy-start.33 = (f32[768]{0:T(1024)S(1)}, f32[768]{0:T(1024)}, u32[]{:S(2)}) copy-start(f32[768]{0:T(1024)} %copy-done.32) | copy-start | bytes 9220
  347.0 5.2 %copy-start.35 = (f32[768]{0:T(1024)S(1)}, f32[768]{0:T(1024)}, u32[]{:S(2)}) copy-start(f32[768]{0:T(1024)} %copy-done.34) | copy-start | bytes 9220
  347.0 5.1 %copy-start.37 = (f32[1024]{0:T(1024)S(1)}, f32[1024]{0:T(1024)}, u32[]{:S(2)}) copy-start(f32[1024]{0:T(1024)} %param.19) | copy-start | bytes 12292
  347.7 15.9 %collective-permute-start.12 = (bf16[128,1024]{1,0:T(8,128)(2,1)}, bf16[128,1024]{1,0:T(8,128)(2,1)}, u32[]{:S(2)}, u32[]{:S(2)}) collective-permute-start(bf16[128,1024]{1,0:T(8,128)(2,1)} %constant_dynamic-slice_fusion.3), channel_id=1, source_target_pairs={{0,8},{4,12},{8,0},{12,4},{16,24},{20,28},{24,16},{28,20},{1,9},{5... | collective-permute-start | bytes 786440 | tf_op jit(solution)/shard_map/ppermute | solution.py:279
  349.6 15.1 %collective-permute-start.11 = (bf16[128,1536]{1,0:T(8,128)(2,1)}, bf16[128,1536]{1,0:T(8,128)(2,1)}, u32[]{:S(2)}, u32[]{:S(2)}) collective-permute-start(bf16[128,1536]{1,0:T(8,128)(2,1)} %constant_dynamic-slice_fusion.4), channel_id=1, source_target_pairs={{0,4},{4,0},{8,12},{12,8},{16,20},{20,16},{24,28},{28,24},{1,5},{5... | collective-permute-start | bytes 1179656 | tf_op jit(solution)/shard_map/ppermute | solution.py:279
  351.8 8.5 %copy-start.9 = (f32[384,1024]{1,0:T(8,128)S(1)}, f32[384,1024]{1,0:T(8,128)}, u32[]{:S(2)}) copy-start(f32[384,1024]{1,0:T(8,128)} %get-tuple-element.258) | copy-start | bytes 4718596
  351.8 8.5 %copy-start.10 = (f32[384,1024]{1,0:T(8,128)S(1)}, f32[384,1024]{1,0:T(8,128)}, u32[]{:S(2)}) copy-start(f32[384,1024]{1,0:T(8,128)} %get-tuple-element.262) | copy-start | bytes 4718596
  351.8 19.9 %collective-permute-start.10 = (bf16[128,1536]{1,0:T(8,128)(2,1)}, bf16[128,1536]{1,0:T(8,128)(2,1)}, u32[]{:S(2)}, u32[]{:S(2)}) collective-permute-start(bf16[128,1536]{1,0:T(8,128)(2,1)} %constant_dynamic-slice_fusion.5), channel_id=1, source_target_pairs={{0,1},{1,0},{2,3},{3,2},{4,5},{5,4},{6,7},{7,6},{8,9},{9,8},{10,11... | collective-permute-start | bytes 1179656 | tf_op jit(solution)/shard_map/ppermute | solution.py:279
  363.6 8.1 %copy-start.17 = (bf16[256,1536]{1,0:T(8,128)(2,1)S(1)}, bf16[256,1536]{1,0:T(8,128)(2,1)}, u32[]{:S(2)}) copy-start(bf16[256,1536]{1,0:T(8,128)(2,1)} %copy-done.16) | copy-start | bytes 2359300
  372.8 7.0 %collective-permute-start.16 = (f32[12,1024]{1,0:T(8,128)S(1)}, f32[12,1024]{1,0:T(8,128)S(1)}, u32[]{:S(2)}, u32[]{:S(2)}) collective-permute-start(f32[12,1024]{1,0:T(8,128)S(1)} %concatenate.84), channel_id=1, source_target_pairs={{0,16},{4,20},{8,24},{12,28},{16,0},{20,4},{24,8},{28,12},{1,17},{... | collective-permute-start | bytes 147464 | tf_op jit(solution)/shard_map/ppermute | solution.py:279
  375.3 8.1 %collective-permute-start.15 = (bf16[64,1024]{1,0:T(8,128)(2,1)S(1)}, bf16[64,1024]{1,0:T(8,128)(2,1)S(1)}, u32[]{:S(2)}, u32[]{:S(2)}) collective-permute-start(bf16[64,1024]{1,0:T(8,128)(2,1)S(1)} %constant_dynamic-slice_fusion), channel_id=1, source_target_pairs={{0,16},{4,20},{8,24},{12,28},{16,0},{20,4},{24,8},{28,12},{1,17},{... | collective-permute-start | bytes 393224 | tf_op jit(solution)/shard_map/ppermute | solution.py:279
  375.9 10.7 %collective-permute-start.14 = (bf16[64,1536]{1,0:T(8,128)(2,1)S(1)}, bf16[64,1536]{1,0:T(8,128)(2,1)S(1)}, u32[]{:S(2)}, u32[]{:S(2)}) collective-permute-start(bf16[64,1536]{1,0:T(8,128)(2,1)S(1)} %constant_dynamic-slice_fusion.1), channel_id=1, source_target_pairs={{0,1},{1,0},{2,3},{3,2},{4,5},{5,4},{6,7},{7,6},{8,9},{9,8},{10,11... | collective-permute-start | bytes 589832 | tf_op jit(solution)/shard_map/ppermute | solution.py:279
  376.4 10.3 %collective-permute-start.13 = (bf16[64,1536]{1,0:T(8,128)(2,1)S(1)}, bf16[64,1536]{1,0:T(8,128)(2,1)S(1)}, u32[]{:S(2)}, u32[]{:S(2)}) collective-permute-start(bf16[64,1536]{1,0:T(8,128)(2,1)S(1)} %constant_dynamic-slice_fusion.2), channel_id=1, source_target_pairs={{0,8},{4,12},{8,0},{12,4},{16,24},{20,28},{24,16},{28,20},{1,9},{5... | collective-permute-start | bytes 589832 | tf_op jit(solution)/shard_map/ppermute | solution.py:279
  386.8 13.0 %collective-permute-start.18 = (bf16[64,1536]{1,0:T(8,128)(2,1)S(1)}, bf16[64,1536]{1,0:T(8,128)(2,1)S(1)}, u32[]{:S(2)}, u32[]{:S(2)}) collective-permute-start(bf16[64,1536]{1,0:T(8,128)(2,1)S(1)} %dynamic-slice_add_fusion.7), channel_id=1, source_target_pairs={{0,16},{4,20},{8,24},{12,28},{16,0},{20,4},{24,8},{28,12},{1,17},{... | collective-permute-start | bytes 589832 | tf_op jit(solution)/shard_map/ppermute | solution.py:279
  389.2 14.2 %collective-permute-start.17 = (bf16[64,1536]{1,0:T(8,128)(2,1)S(1)}, bf16[64,1536]{1,0:T(8,128)(2,1)S(1)}, u32[]{:S(2)}, u32[]{:S(2)}) collective-permute-start(bf16[64,1536]{1,0:T(8,128)(2,1)S(1)} %dynamic-slice_add_fusion.8), channel_id=1, source_target_pairs={{0,16},{4,20},{8,24},{12,28},{16,0},{20,4},{24,8},{28,12},{1,17},{... | collective-permute-start | bytes 589832 | tf_op jit(solution)/shard_map/ppermute | solution.py:279
  389.8 5.9 %collective-permute-start.19 = (bf16[64,1024]{1,0:T(8,128)(2,1)S(1)}, bf16[64,1024]{1,0:T(8,128)(2,1)S(1)}, u32[]{:S(2)}, u32[]{:S(2)}) collective-permute-start(bf16[64,1024]{1,0:T(8,128)(2,1)S(1)} %dynamic-slice_add_fusion.9), channel_id=1, source_target_pairs={{0,4},{4,0},{8,12},{12,8},{16,20},{20,16},{24,28},{28,24},{1,5},{5... | collective-permute-start | bytes 393224 | tf_op jit(solution)/shard_map/ppermute | solution.py:279
  390.4 5.3 %collective-permute-start.20 = (f32[12,1024]{1,0:T(8,128)S(1)}, f32[12,1024]{1,0:T(8,128)S(1)}, u32[]{:S(2)}, u32[]{:S(2)}) collective-permute-start(f32[12,1024]{1,0:T(8,128)S(1)} %add.471), channel_id=1, source_target_pairs={{0,8},{4,12},{8,0},{12,4},{16,24},{20,28},{24,16},{28,20},{1,9},{5... | collective-permute-start | bytes 147464 | tf_op jit(solution)/shard_map/ppermute | solution.py:279
  403.4 7.9 %collective-permute-start.23 = (bf16[64,1024]{1,0:T(8,128)(2,1)S(1)}, bf16[64,1024]{1,0:T(8,128)(2,1)S(1)}, u32[]{:S(2)}, u32[]{:S(2)}) collective-permute-start(bf16[64,1024]{1,0:T(8,128)(2,1)S(1)} %add.474), channel_id=1, source_target_pairs={{0,16},{4,20},{8,24},{12,28},{16,0},{20,4},{24,8},{28,12},{1,17},{... | collective-permute-start | bytes 393224 | tf_op jit(solution)/shard_map/ppermute | solution.py:279
  403.5 4.3 collective-permute-start.24
  404.1 7.3 %collective-permute-start.22 = (bf16[64,1536]{1,0:T(8,128)(2,1)S(1)}, bf16[64,1536]{1,0:T(8,128)(2,1)S(1)}, u32[]{:S(2)}, u32[]{:S(2)}) collective-permute-start(bf16[64,1536]{1,0:T(8,128)(2,1)S(1)} %add.473), channel_id=1, source_target_pairs={{0,1},{1,0},{2,3},{3,2},{4,5},{5,4},{6,7},{7,6},{8,9},{9,8},{10,11... | collective-permute-start | bytes 589832 | tf_op jit(solution)/shard_map/ppermute | solution.py:279
  405.0 8.9 %collective-permute-start.21 = (bf16[64,1536]{1,0:T(8,128)(2,1)S(1)}, bf16[64,1536]{1,0:T(8,128)(2,1)S(1)}, u32[]{:S(2)}, u32[]{:S(2)}) collective-permute-start(bf16[64,1536]{1,0:T(8,128)(2,1)S(1)} %add.472), channel_id=1, source_target_pairs={{0,8},{4,12},{8,0},{12,4},{16,24},{20,28},{24,16},{28,20},{1,9},{5... | collective-permute-start | bytes 589832 | tf_op jit(solution)/shard_map/ppermute | solution.py:279
  414.7 4.3 collective-permute-start.28
  420.7 7.4 %collective-permute-start.27 = (bf16[128,1024]{1,0:T(8,128)(2,1)S(1)}, bf16[128,1024]{1,0:T(8,128)(2,1)S(1)}, u32[]{:S(2)}, u32[]{:S(2)}) collective-permute-start(bf16[128,1024]{1,0:T(8,128)(2,1)S(1)} %pad_maximum_fusion.9), channel_id=1, source_target_pairs={{0,8},{4,12},{8,0},{12,4},{16,24},{20,28},{24,16},{28,20},{1,9},{5... | collective-permute-start | bytes 786440 | tf_op jit(solution)/shard_map/ppermute | solution.py:279
  420.8 8.2 %collective-permute-start.26 = (bf16[128,1536]{1,0:T(8,128)(2,1)S(1)}, bf16[128,1536]{1,0:T(8,128)(2,1)S(1)}, u32[]{:S(2)}, u32[]{:S(2)}) collective-permute-start(bf16[128,1536]{1,0:T(8,128)(2,1)S(1)} %pad_maximum_fusion.8), channel_id=1, source_target_pairs={{0,4},{4,0},{8,12},{12,8},{16,20},{20,16},{24,28},{28,24},{1,5},{5... | collective-permute-start | bytes 1179656 | tf_op jit(solution)/shard_map/ppermute | solution.py:279
  422.0 9.1 %collective-permute-start.25 = (bf16[128,1536]{1,0:T(8,128)(2,1)S(1)}, bf16[128,1536]{1,0:T(8,128)(2,1)S(1)}, u32[]{:S(2)}, u32[]{:S(2)}) collective-permute-start(bf16[128,1536]{1,0:T(8,128)(2,1)S(1)} %copy-done.23), channel_id=1, source_target_pairs={{0,1},{1,0},{2,3},{3,2},{4,5},{5,4},{6,7},{7,6},{8,9},{9,8},{10,11... | collective-permute-start | bytes 1179656 | tf_op jit(solution)/shard_map/ppermute | solution.py:279
  431.2 10.5 %collective-permute-start.32 = (bf16[256,1024]{1,0:T(8,128)(2,1)S(1)}, bf16[256,1024]{1,0:T(8,128)(2,1)S(1)}, u32[]{:S(2)}, u32[]{:S(2)}) collective-permute-start(bf16[256,1024]{1,0:T(8,128)(2,1)S(1)} %pad_maximum_fusion.6), channel_id=1, source_target_pairs={{0,1},{1,0},{2,3},{3,2},{4,5},{5,4},{6,7},{7,6},{8,9},{9,8},{10,11... | collective-permute-start | bytes 1572872 | tf_op jit(solution)/shard_map/ppermute | solution.py:279
  432.5 15.5 %collective-permute-start.31 = (bf16[256,1536]{1,0:T(8,128)(2,1)S(1)}, bf16[256,1536]{1,0:T(8,128)(2,1)S(1)}, u32[]{:S(2)}, u32[]{:S(2)}) collective-permute-start(bf16[256,1536]{1,0:T(8,128)(2,1)S(1)} %pad_maximum_fusion.5), channel_id=1, source_target_pairs={{0,8},{4,12},{8,0},{12,4},{16,24},{20,28},{24,16},{28,20},{1,9},{5... | collective-permute-start | bytes 2359304 | tf_op jit(solution)/shard_map/ppermute | solution.py:279
  434.3 15.1 %collective-permute-start.30 = (bf16[256,1536]{1,0:T(8,128)(2,1)S(1)}, bf16[256,1536]{1,0:T(8,128)(2,1)S(1)}, u32[]{:S(2)}, u32[]{:S(2)}) collective-permute-start(bf16[256,1536]{1,0:T(8,128)(2,1)S(1)} %pad_maximum_fusion.4), channel_id=1, source_target_pairs={{0,4},{4,0},{8,12},{12,8},{16,20},{20,16},{24,28},{28,24},{1,5},{5... | collective-permute-start | bytes 2359304 | tf_op jit(solution)/shard_map/ppermute | solution.py:279
  441.8 6.3 %copy-start.11 = (bf16[512,1024]{1,0:T(8,128)(2,1)}, bf16[512,1024]{1,0:T(8,128)(2,1)S(1)}, u32[]{:S(2)}) copy-start(bf16[512,1024]{1,0:T(8,128)(2,1)S(1)} %pad_maximum_fusion.3.refs_0_) | copy-start | bytes 3145732
  441.8 9.0 %collective-permute-start.33 = (bf16[512,1024]{1,0:T(8,128)(2,1)S(1)}, bf16[512,1024]{1,0:T(8,128)(2,1)}, u32[]{:S(2)}, u32[]{:S(2)}) collective-permute-start(bf16[512,1024]{1,0:T(8,128)(2,1)S(1)} %pad_maximum_fusion.3.refs_0_), channel_id=1, source_target_pairs={{0,2},{2,0},{1,3},{3,1},{4,6},{6,4},{5,7},{7,5},{8,10},{10,8},{9,1... | collective-permute-start | bytes 3145736 | tf_op jit(solution)/shard_map/ppermute | solution.py:279
  450.8 5.1 %copy-start.15 = (bf16[1,384,1024]{2,1,0:T(8,128)(2,1)S(1)}, bf16[1,384,1024]{2,1,0:T(8,128)(2,1)}, u32[]{:S(2)}) copy-start(bf16[1,384,1024]{2,1,0:T(8,128)(2,1)} %get-tuple-element.281) | copy-start | bytes 2359300
  455.4 4.8 %collective-permute-start.34 = (bf16[512,1536]{1,0:T(8,128)(2,1)}, bf16[512,1536]{1,0:T(8,128)(2,1)}, u32[]{:S(2)}, u32[]{:S(2)}) collective-permute-start(bf16[512,1536]{1,0:T(8,128)(2,1)} %pad_maximum_fusion.1.refs_0_), channel_id=1, source_target_pairs={{0,2},{2,0},{1,3},{3,1},{4,6},{6,4},{5,7},{7,5},{8,10},{10,8},{9,1... | collective-permute-start | bytes 4718600 | tf_op jit(solution)/shard_map/ppermute | solution.py:279
  455.4 6.1 %collective-permute-start.35 = (bf16[512,1536]{1,0:T(8,128)(2,1)}, bf16[512,1536]{1,0:T(8,128)(2,1)}, u32[]{:S(2)}, u32[]{:S(2)}) collective-permute-start(bf16[512,1536]{1,0:T(8,128)(2,1)} %pad_maximum_fusion.2.refs_1_), channel_id=1, source_target_pairs={{0,2},{2,0},{1,3},{3,1},{4,6},{6,4},{5,7},{7,5},{8,10},{10,8},{9,1... | collective-permute-start | bytes 4718600 | tf_op jit(solution)/shard_map/ppermute | solution.py:279
  455.9 3.1 collective-permute-start.29
  (24 other events, 45.1 us)
Sparse Core Ops, SparseCore 0:
  14.6 108.6 all-gather.2
  202.5 72.9 reduce-scatter.2
  300.9 90.2 reduce-scatter.4

commit v4 on v3

--- a/solution.py
+++ b/solution.py
@@ -80,7 +80,7 @@
         ds=(p*(dp-delta)).astype(bf)
         dv=mm(p.astype(bf),do2,NN).astype(bf)
         dk=mm(ds,q2,NN).astype(bf)
-        e=mm(ds,k,TN)
+        e=mm(k,ds,TN)
         dq=e if dq is None else dq+e
         cut=min(max(rows-b,0),kb)
         if cut:
@@ -88,12 +88,13 @@
         if cut<kb:
             at=b+cut-rows
             dx_ref[0,at:at+kb-cut,:]=dk[cut:]; dx_ref[1,at:at+kb-cut,:]=dv[cut:]
+    dq=dq.T
     dq_ref[...]=(jnp.where(lane<64,dq[:rows],dq[rows:])*0.125).astype(bf)
 
 def attn_bwd(joined, other, biast, lset, do, o, mb, kb=None):
     rows=biast.shape[1]; nx=other.shape[0]; D=other.shape[1]//2; G=D//128
     flops=10*rows*(rows+nx)*D
-    kb=kb or rows
+    kb=kb or 2*rows
     return pl.pallas_call(partial(bwd_body,kb),
         grid=(G,),
         in_specs=[pl.BlockSpec(biast.shape,lambda i:(0,0)),
@@ -111,10 +112,19 @@
         name="attn_bwd")(biast,lset,joined,joined,joined,other,other,do,o)
 
 C0=0.7978845608028654; C1=0.044715
-def exp_body(x_ref, g_ref, wi_ref, wo_ref, *refs):
-    act_ref, ig_ref, b_ref, accr, accd = refs[-5:]
+def exp_body(capacity, x_ref, g_ref, wi_ref, wo_ref, *refs):
+    act_ref, ig_ref, b_ref, s_ref, accr, accd = refs[-6:]
     f=pl.program_id(0)
-    x=x_ref[...]; g=g_ref[...]; wi=wi_ref[...].reshape(x_ref.shape[1],wi_ref.shape[3]); wo=wo_ref[0,0]
+    @pl.when(f==0)
+    def _():
+        size=g_ref.shape[2]
+        eye=lax.broadcasted_iota(jnp.int32,(size,128),0)==lax.broadcasted_iota(jnp.int32,(size,128),1)
+        for e in range(g_ref.shape[0]):
+            at=e*size+capacity
+            gate=x_ref[at:at+1,:128].astype(f32)+x_ref[at+1:at+2,:128].astype(f32)
+            column=jnp.sum(jnp.where(eye,gate,0.0),axis=1,keepdims=True)
+            s_ref[e*size:(e+1)*size,:]=(column*g_ref[e,0].astype(f32)).astype(bf)
+    x=x_ref[...]; g=s_ref[...]; wi=wi_ref[...].reshape(x_ref.shape[1],wi_ref.shape[3]); wo=wo_ref[0,0]
     v=mm(x,wi,NN)
     ag=mm(g,wo,NT)
     v2=v*v
@@ -136,17 +146,17 @@
             b_ref[e,:size,:]=accr[e*size:(e+1)*size,:].astype(bf)
             b_ref[e,size:,:]=accd[e*size:(e+1)*size,:].astype(bf)
 
-def expert(x, g, weights, prev, mb, nmb, experts, fb=512):
-    rows,D=x.shape; n,deep,_=weights.shape; part=deep//2; FF=part*n; per=D//fb
+def expert(x, g, weights, prev, mb, nmb, capacity, fb=512):
+    rows,D=x.shape; experts,_,size,_=g.shape; n,deep,_=weights.shape; part=deep//2; FF=part*n; per=D//fb
     blk=pl.BlockSpec((rows,fb),lambda f:(mb,f))
     anyspec=pl.BlockSpec(memory_space=pl.ANY)
     ex=() if prev is None else prev
-    return pl.pallas_call(exp_body, grid=(FF//fb,),
-        in_specs=[pl.BlockSpec((rows,D),lambda f:(0,0)),pl.BlockSpec((rows,D),lambda f:(0,0)),
+    return pl.pallas_call(partial(exp_body,capacity), grid=(FF//fb,),
+        in_specs=[pl.BlockSpec((rows,D),lambda f:(0,0)),pl.BlockSpec((experts,1,size,D),lambda f:(0,mb,0,0)),
                   pl.BlockSpec((n,1,D//n,fb),lambda f:(0,f//per,0,f%per)),
                   pl.BlockSpec((1,1,fb,D),lambda f:(f//(part//fb),part//fb+f%(part//fb),0,0))]+[anyspec]*len(ex),
-        out_specs=[blk,blk,pl.BlockSpec((experts,2*rows//experts,D),lambda f:(0,0,0))],
-        out_shape=[jax.ShapeDtypeStruct((nmb*rows,FF),bf)]*2+[jax.ShapeDtypeStruct((experts,2*rows//experts,D),bf)],
+        out_specs=[blk,blk,pl.BlockSpec((experts,2*size,D),lambda f:(0,0,0)),pl.BlockSpec((rows,D),lambda f:(0,0))],
+        out_shape=[jax.ShapeDtypeStruct((nmb*rows,FF),bf)]*2+[jax.ShapeDtypeStruct((experts,2*size,D),bf),jax.ShapeDtypeStruct((rows,D),bf)],
         scratch_shapes=[pltpu.VMEM((rows,D),f32)]*2,
         input_output_aliases={} if prev is None else {4:0,5:1},
         cost_estimate=pl.CostEstimate(flops=8*rows*D*FF,transcendentals=rows*FF,bytes_accessed=4*D*FF+4*rows*FF),
@@ -188,69 +198,78 @@
         cost_estimate=pl.CostEstimate(flops=2*count*rows*D*FF,transcendentals=0,bytes_accessed=2*D*FF+2*count*rows*FF),
         name="out_grads")(*gs,act)
 
-def project_body(count, parts, first, per, high_ref, x_ref, *refs):
+def project_body(count, parts, per, high_ref, x_ref, *refs):
     j=pl.program_id(0)
-    joined_ref,keep_ref,send_ref,turned=refs[-4:]
-    half=keep_ref.shape[0]
+    joined_ref,*outs,turned=refs[-6:]
+    half=outs[0].shape[0]
     @pl.when(j==0)
     def _(): turned[...]=x_ref[...].T
     rows=x_ref.shape[0]//count
     for m in range(count):
         own=refs[m*(2+parts):(m+1)*(2+parts)]
-        @pl.when(j+first<per)
+        @pl.when(j<per)
         def _(): joined_ref[m*rows:(m+1)*rows,:]=own[0][...]
-        @pl.when(j+first>=per)
+        @pl.when(j>=per)
         def _():
             total=own[1][0].astype(f32)
             for r in own[2:]: total=total+r[0].astype(f32)
             joined_ref[m*rows:(m+1)*rows,:]=total.astype(bf)
     high=high_ref[0]
     right=joined_ref[...]
-    send_ref[...]=mm(turned[pl.ds(pl.multiple_of((1-high)*half,half),half),:],right,NN).astype(bf)
-    keep_ref[...]=mm(turned[pl.ds(pl.multiple_of(high*half,half),half),:],right,NN).astype(bf)
-
-def project_grads(x, groups, high, first, steps, prev, fb=512):
-    rows,D=x.shape; count=len(groups); R=rows//count; per=D//fb; parts=len(groups[0][2])
-    three=pl.BlockSpec((1,R,fb),lambda j,h:(jnp.maximum((j+first)//per-1,0),0,jnp.where(j+first<per,0,(j+first)%per)))
+    send=mm(turned[pl.ds(pl.multiple_of((1-high)*half,half),half),:],right,NN).astype(bf)
+    keep=mm(turned[pl.ds(pl.multiple_of(high*half,half),half),:],right,NN).astype(bf)
+    middle=pl.num_programs(0)//2
+    @pl.when(j<middle)
+    def _(): outs[0][...]=keep; outs[1][...]=send
+    @pl.when(j>=middle)
+    def _(): outs[2][...]=keep; outs[3][...]=send
+
+def project_grads(x, groups, high, fb=512):
+    rows,D=x.shape; count=len(groups); R=rows//count; per=D//fb; parts=len(groups[0][2]); steps=3*per; middle=steps//2
+    three=pl.BlockSpec((1,R,fb),lambda j,h:(jnp.maximum(j//per-1,0),0,jnp.where(j<per,0,j%per)))
     specs=[pl.BlockSpec((rows,D),lambda j,h:(0,0))]; args=[x]
     for dq,own,away in groups:
-        specs+=[pl.BlockSpec((R,fb),lambda j,h:(0,jnp.minimum(j+first,per-1))),three]+[three]*parts
+        specs+=[pl.BlockSpec((R,fb),lambda j,h:(0,jnp.minimum(j,per-1))),three]+[three]*parts
         args+=[dq,own]+list(away)
-    if prev is not None:
-        specs.append(pl.BlockSpec(memory_space=pl.ANY)); args.append(prev)
-    return pl.pallas_call(partial(project_body,count,parts,first,per),
+    early=pl.BlockSpec((D//2,fb),lambda j,h:(0,jnp.minimum(j,middle-1)))
+    late=pl.BlockSpec((D//2,fb),lambda j,h:(0,jnp.maximum(j-middle,0)))
+    return pl.pallas_call(partial(project_body,count,parts,per),
         grid_spec=pltpu.PrefetchScalarGridSpec(num_scalar_prefetch=1,grid=(steps,),in_specs=specs,
-            out_specs=[pl.BlockSpec((rows,fb),lambda j,h:(0,j+first)),pl.BlockSpec((D//2,fb),lambda j,h:(0,j)),pl.BlockSpec((D//2,fb),lambda j,h:(0,j))],
+            out_specs=[pl.BlockSpec((rows,fb),lambda j,h:(0,j)),early,early,late,late],
             scratch_shapes=[pltpu.VMEM((D,rows),bf)]),
-        out_shape=[jax.ShapeDtypeStruct((rows,3*D),bf)]+[jax.ShapeDtypeStruct((D//2,steps*fb),bf)]*2,
-        input_output_aliases={} if prev is None else {len(args):0},
+        out_shape=[jax.ShapeDtypeStruct((rows,3*D),bf)]+[jax.ShapeDtypeStruct((D//2,middle*fb),bf)]*4,
         cost_estimate=pl.CostEstimate(flops=6*rows*D*D,transcendentals=0,bytes_accessed=rows*D*16+6*D*D),
         name="project_grads")(high,*args)
 
-def widen_body(count, per, high_ref, *refs):
-    out_ref=refs[-1]; i=pl.program_id(0)
-    @pl.when(i//per==high_ref[0])
-    def _():
-        start=0
-        for r in refs[:count]:
-            out_ref[:,start:start+r.shape[1]]=r[...].astype(f32); start+=r.shape[1]
-    @pl.when(i//per!=high_ref[0])
-    def _():
-        start=0
-        for r in refs[count:2*count]:
-            out_ref[:,start:start+r.shape[1]]=r[...].astype(f32); start+=r.shape[1]
-
-def widen(mine, other, high, rb=256):
-    half=mine[0].shape[0]; per=half//rb; width=sum(m.shape[1] for m in mine)
-    own=lambda i,h:(jnp.where(i//per==h[0],i%per,jnp.where(h[0]==0,per-1,0)),0)
-    away=lambda i,h:(jnp.where(i//per!=h[0],i%per,jnp.where(h[0]==1,per-1,0)),0)
-    return pl.pallas_call(partial(widen_body,len(mine),per),
-        grid_spec=pltpu.PrefetchScalarGridSpec(num_scalar_prefetch=1,grid=(2*per,),
-            in_specs=[pl.BlockSpec((rb,m.shape[1]),own) for m in mine]+[pl.BlockSpec((rb,m.shape[1]),away) for m in mine],
-            out_specs=pl.BlockSpec((rb,width),lambda i,h:(i,0))),
+def widen_body(count, high_ref, *refs):
+    out_ref=refs[-1]; start=0
+    for r in refs[:count]:
+        out_ref[:,start:start+r.shape[1]]=r[...].astype(f32); start+=r.shape[1]
+
+def widen(values, high, prev=None):
+    half=values[0].shape[0]; rb=half if len(values)==1 else half//2; per=half//rb; width=sum(v.shape[1] for v in values); count=len(values)
+    ex=[] if prev is None else [prev]
+    return pl.pallas_call(partial(widen_body,count),
+        grid_spec=pltpu.PrefetchScalarGridSpec(num_scalar_prefetch=1,grid=(per,),
+            in_specs=[pl.BlockSpec((rb,v.shape[1]),lambda i,h:(i,0)) for v in values]+[pl.BlockSpec(memory_space=pl.ANY)]*len(ex),
+            out_specs=pl.BlockSpec((rb,width),lambda i,h:(h[0]*per+i,0))),
         out_shape=jax.ShapeDtypeStruct((2*half,width),f32),
-        cost_estimate=pl.CostEstimate(flops=half*width,transcendentals=0,bytes_accessed=half*width*12),
-        name="widen")(high,*mine,*other)
+        input_output_aliases={} if prev is None else {1+count:0},
+        cost_estimate=pl.CostEstimate(flops=half*width,transcendentals=0,bytes_accessed=half*width*6),
+        name="widen")(high,*values,*ex)
+
+def stack_body(in_ref, out_ref, both_ref):
+    both_ref[0,0,:,:]=in_ref[...]; both_ref[1,0,:,:]=out_ref[...]
+
+def stack(first, second):
+    short,FF=first.shape; D=second.shape[1]; count=FF//D
+    both=pl.pallas_call(stack_body, grid=(count,),
+        in_specs=[pl.BlockSpec((short,D),lambda k:(0,k)),pl.BlockSpec((short,D),lambda k:(k,0))],
+        out_specs=pl.BlockSpec((2,1,short,D),lambda k:(0,k,0,0)),
+        out_shape=jax.ShapeDtypeStruct((2,count,short,D),bf),
+        cost_estimate=pl.CostEstimate(flops=0,transcendentals=0,bytes_accessed=8*short*FF),
+        name="stack")(first,second)
+    return both.reshape(2*count*short,D)
 
 
 HEADS = 16
@@ -301,18 +320,17 @@
     return [a + swap(b, *order[slot]) for a, b, order in zip(kept, sent, steps)]
 
 
+def join(value, other, step):
+    axis, bit = step
+    high = (lax.axis_index(axis) // bit) % 2
+    return jnp.concatenate(
+        [jnp.where(high == 0, value, other), jnp.where(high == 0, other, value)], axis=0
+    )
+
+
 def double(values, steps, slot):
     sent = [swap(value, *order[slot]) for value, order in zip(values, steps)]
-    joined = []
-    for value, other, order in zip(values, sent, steps):
-        axis, bit = order[slot]
-        high = (lax.axis_index(axis) // bit) % 2
-        joined.append(
-            jnp.concatenate(
-                [jnp.where(high == 0, value, other), jnp.where(high == 0, other, value)], axis=0
-            )
-        )
-    return joined
+    return [join(v, o, order[slot]) for v, o, order in zip(values, sent, steps)]
 
 
 def local(
@@ -340,11 +358,7 @@
     slots = experts * block
 
     devices = contexts * lax.axis_size("dp")
-    hidden = expert_in.shape[2]
-    blocks = [expert_in[0][:, k : k + model] for k in range(0, hidden, model)]
-    weights = lax.all_gather(
-        jnp.concatenate(blocks + [expert_out[0]], axis=0), ("context", "dp"), axis=0
-    )
+    weights = lax.all_gather(stack(expert_in[0], expert_out[0]), ("context", "dp"), axis=0)
 
     router_float = router_weight.astype(f32)
     expert_ids = jnp.arange(experts, dtype=jnp.int32)
@@ -361,9 +375,6 @@
         routes.append(route)
         ranks.append(rank)
         places.append(place.astype(bf))
-        target = (route * (2 * block) + rank)[None, :]
-        wide = jnp.arange(2 * slots, dtype=jnp.int32)[:, None]
-        place_two.append(((target == wide).astype(bf), (target + block == wide).astype(bf)))
         sent_grads.append(
             jnp.dot(places[m], out_grad[m, 0], preferred_element_type=f32)
             .astype(bf)
@@ -403,12 +414,7 @@
                     0.0,
                     -1e30,
                 ).astype(f32),
-                jnp.where(
-                    (key_positions[:, None] <= query_positions[None, :])
-                    & (key_segments[:, None] == query_segments[None, :]),
-                    0.0,
-                    -1e30,
-                ).astype(f32),
+                (key_positions, key_segments),
             )
         )
 
@@ -446,7 +452,25 @@
             sent, others[m + 1] = lax.optimization_barrier((sent, others[m + 1]))
         if m + 1 == micro:
             logs = tuple(state[2] for state in saved) + (log_total,)
-            sent, logs, turned = lax.optimization_barrier((sent, logs, tuple(b[1] for b in biases)))
+            attended, targets, places_in_pack, logs = lax.optimization_barrier(
+                (attended, tuple(r * (2 * block) + k for r, k in zip(routes, ranks)),
+                 tuple(b[1] for b in biases), logs)
+            )
+            wide = jnp.arange(2 * slots, dtype=jnp.int32)[:, None]
+            place_two = [
+                ((t[None, :] == wide).astype(bf), (t[None, :] + block == wide).astype(bf))
+                for t in targets
+            ]
+            turned = [
+                jnp.where(
+                    (p[:, None] <= p[None, :rows]) & (g[:, None] == g[None, :rows]), 0.0, -1e30
+                ).astype(f32)
+                for p, g in places_in_pack
+            ]
+            sent, logs, turned, place_two = lax.optimization_barrier(
+                (sent, logs, turned, place_two)
+            )
+            place_two = list(place_two)
             log_total = logs[-1]
             for n in range(m):
                 saved[n][2] = logs[n]
@@ -469,11 +493,10 @@
     rows_there, scaled_there, returned = [], [], []
     for m in range(micro):
         there = saved[m][-1]
-        gate_there = there[:, capacity, :block].astype(f32) + there[:, capacity + 1, :block].astype(f32)
-        scaled = (gate_there[:, :, None] * grads_there[:, m].astype(f32)).astype(bf)
         there = there.reshape(slots, model)
-        scaled = scaled.reshape(slots, model)
-        active, inner_grad, back = expert(there, scaled, weights, kept, m, micro, experts)
+        active, inner_grad, back, scaled = expert(
+            there, grads_there, weights, kept, m, micro, capacity
+        )
         if m + 1 < micro:
             back, saved[m + 1][-1] = lax.optimization_barrier((back, saved[m + 1][-1]))
         kept = (active, inner_grad)
@@ -539,19 +562,18 @@
     out_sum = lax.dot_general(
         mixed_all, jnp.concatenate(branches, axis=0), TN, preferred_element_type=f32
     ).astype(bf)
-    out_sum, groups[-1][2][0] = lax.optimization_barrier((out_sum, groups[-1][2][0]))
     near, expert_bits, dp_bits = bits_of("context"), bits_of("expert"), bits_of("dp")
+    sent, kept = cut([out_sum], [near], 0)
+    sent, kept, groups[-1][2][0] = lax.optimization_barrier((sent, kept, groups[-1][2][0]))
+    out_half = kept[0] + swap(sent[0], *near[0])
     high = (here % 2).astype(jnp.int32).reshape(1)
-    halves, joined_grad = [], None
-    for first in (0, 3):
-        joined_grad, kept, sent = project_grads(normed_low, groups, high, first, 3, joined_grad)
-        if first == 0:
-            kept, in_term, grad_out_weight = lax.optimization_barrier(
-                (kept, in_term, grad_out_weight)
-            )
-            grad_in = lax.psum_scatter(in_term, ("context", "dp"), scatter_dimension=0, tiled=True)[0]
-        halves.append(kept + swap(sent, *near[0]))
-    halves.append(halve([out_sum], [near], 0)[0])
+    joined_grad, kept, sent, kept_too, sent_too = project_grads(normed_low, groups, high)
+    kept, in_term, grad_out_weight, out_half = lax.optimization_barrier(
+        (kept, in_term, grad_out_weight, out_half)
+    )
+    grad_in = lax.psum_scatter(in_term, ("context", "dp"), scatter_dimension=0, tiled=True)[0]
+    halves = [kept + swap(sent, *near[0]), kept_too + swap(sent_too, *near[0])]
+    halves.append(out_half)
     for slot in range(1, len(near)):
         halves = halve(halves, [near] * 3, slot)
     chunks = tuple(halves)
@@ -586,8 +608,7 @@
         chunks = double(chunks, orders, slot)
         if steps:
             small = small + swap(small, *steps.pop())
-        if slot:
-            chunks, small = lax.optimization_barrier((tuple(chunks), small))
+        chunks, small = lax.optimization_barrier((tuple(chunks), small))
         if slot == count - 2:
             chunks, grad_in, grad_out_weight = lax.optimization_barrier(
                 (chunks, grad_in, grad_out_weight)
@@ -601,9 +622,12 @@
     assert not steps
     for slot in reversed(range(1, len(near))):
         chunks = double(chunks, (near,) * 3, slot)
-    out_sum = widen(chunks[2:], [swap(chunks[2], *near[0])], high)
-    first, last, out_sum = lax.optimization_barrier((chunks[0], chunks[1], out_sum))
-    in_sum = widen([first, last], [swap(first, *near[0]), swap(last, *near[0])], high)
+    arrived = [swap(chunk, *near[0]) for chunk in chunks]
+    out_sum = widen(chunks[2:], high)
+    in_sum = widen(chunks[:2], high)
+    arrived, out_sum, in_sum = lax.optimization_barrier((arrived, out_sum, in_sum))
+    out_sum = widen(arrived[2:], 1 - high, out_sum)
+    in_sum = widen(arrived[:2], 1 - high, in_sum)
     return (
         jnp.stack(outputs)[:, None],
         grad_tokens.reshape(micro, 1, rows, model),

time: 484 us -> 465 us (0.961)
  local copies, waits for them, and re-layouts: 30 us -> 17.4 us
  other arithmetic: 56.7 us -> 50.4 us
  waiting for transfers between devices: 86.4 us -> 81.3 us
  Pallas kernels: 168 us -> 173 us
    ppermute x32, waiting for transfers between devices: 75.4 us -> 64.1 us  [swap(): lax.ppermute(values, axis, [(i, i ^ bit) for i in range(lax.axis_size(axi...]
    pallas_call x6 -> x8, Pallas kernels: 76.8 us -> 82.4 us  [the longest x2 49.7 us: expert(): pl.pallas_call(partial(exp_body, capacity), grid=(FF // fb,), in_specs=[p...]
    ppermute x32, starting transfers between devices: 30.1 us -> 35.1 us  [swap(): lax.ppermute(values, axis, [(i, i ^ bit) for i in range(lax.axis_size(axi...]
  transfers between devices with their start and end apart: 44 -> 44, of which waited for: 22 -> 19; matrix products, arithmetic and copies ran while one was open for 28% -> 25% of each run, Pallas kernels for 33% -> 35%
where the time goes in v4:
time: 465 us; the launch traced here: 458 us
  Pallas kernels  173 us (37%)
  waiting for transfers between devices  81.3 us (17%)
  starting transfers between devices  64.9 us (14%)
  matrix products  56.4 us (12%)
  other arithmetic  50.4 us (11%)
  local copies, waits for them, and re-layouts  17.4 us (4%)
  between operations  15.1 us (3%)
    ppermute x32, waiting for transfers between devices, swap(): lax.ppermute(values, axis, [(i, i ^ bit) for i in range(lax.axis_size(axi...  64.1 us
    pallas_call x2, Pallas kernels, expert(): pl.pallas_call(partial(exp_body, capacity), grid=(FF // fb,), in_specs=[p...  49.7 us
    pallas_call x2, Pallas kernels, attn_bwd(): pl.pallas_call(partial(bwd_body, kb), grid=(G,), in_specs=[pl.BlockSpec(b...  36.1 us
    ppermute x32, starting transfers between devices, swap(): lax.ppermute(values, axis, [(i, i ^ bit) for i in range(lax.axis_size(axi...  35.1 us
    pallas_call x2, Pallas kernels, attn_fwd(): pl.pallas_call(partial(fwd_body, rb), grid=(G,), in_specs=[pl.BlockSpec(b...  25.3 us
    pallas_call x1, Pallas kernels, in_grads(): pl.pallas_call(partial(in_grads_body, count), grid=(FF // fb,), in_specs=...  14.6 us
    pallas_call x1, Pallas kernels, out_grads(): pl.pallas_call(partial(out_grads_body, count), grid=(FF // fb,), in_specs...  14.2 us
    pallas_call x4, Pallas kernels, widen(): pl.pallas_call(partial(widen_body, count), grid_spec=pltpu.PrefetchScalar...  14.1 us
  transfers between devices with their start and end apart: 44, of which 19 were waited for; matrix products, arithmetic and copies ran while one was open for 25% of the time, Pallas kernels for 35%

profile of v4, /device:TPU:0, one launch (start us, length us, event | category | flops | bytes accessed | tf_op | source)
XLA Modules:
  0.0 458.1 jit_solution(13621697495085837560)
XLA Ops:
  7.2 4.8 %stack.13 = bf16[2,4,256,1024]{3,2,1,0:T(8,128)(2,1)} custom-call(bf16[256,4096]{1,0:T(8,128)(2,1)} %bitcast.139, bf16[1024,1024]{1,0:T(8,128)(2,1)} %bitcast.140), custom_call_target="tpu_custom_call" | custom-call | bytes 8388608 | tf_op jit(solution)/shard_map/stack/pallas_call | solution.py:266
  15.2 1.9 convolution_convert_fusion.2
  20.1 2.2 multiply_reduce_fusion.2
  22.3 2.3 add_convert_fusion.x_ref
  24.7 9.6 %convolution_convert_fusion.q_ref.ko_ref.vo_ref = bf16[768,3072]{1,0:T(8,128)(2,1)S(1)} fusion(bf16[768,1024]{1,0:T(8,128)(2,1)S(1)} %add_convert_fusion.x_ref, bf16[1024,3072]{1,0:T(8,128)(2,1)} %param.21), kind=kOutput, calls=%fused_computation | convolution fusion | flops 4834197504 | bytes 12582912 | tf_op jit(solution)/shard_map/dot_general | solution.py:389
  34.3 2.2 fusion.88
  38.0 7.9 %all-to-all-start = ((bf16[8,2,56,1024]{3,2,1,0:T(8,128)(2,1)}), bf16[8,2,56,1024]{3,2,1,0:T(8,128)(2,1)}, u32[]{:S(2)}, u32[]{:S(2)}) async-start(bf16[8,2,56,1024]{3,2,1,0:T(8,128)(2,1)} %pad_maximum_fusion), calls=%async_computation | async-start | bytes 3670016 | tf_op jit(solution)/shard_map/all_to_all | solution.py:384
  52.3 12.7 %attn_fwd.2 = (f32[384,1024]{1,0:T(8,128)}, bf16[384,1024]{1,0:T(8,128)(2,1)}, f32[384,128]{1,0:T(8,128)}) custom-call(f32[384,768]{1,0:T(8,128)} %and_select_fusion.3.bias_ref, bf16[768,3072]{1,0:T(8,128)(2,1)} %copy-done.2, bf16[768,3072]{1,0:T(8,128)(2,1)} %copy-done.2, bf16[768,3072]{1,0:T(8,128)(2,1)} %copy-done.2, ...), custom_call_target="tpu_custom_call" | custom-call | flops 384 | bytes 384 | tf_op jit(solution)/shard_map/attn_fwd/pallas_call | solution.py:45
  65.0 2.4 fusion.92
  69.4 1.8 fusion.22
  71.2 12.6 %attn_fwd.3 = (f32[384,1024]{1,0:T(8,128)}, bf16[384,1024]{1,0:T(8,128)(2,1)}, f32[384,128]{1,0:T(8,128)}) custom-call(f32[384,768]{1,0:T(8,128)} %and_select_fusion.2.bias_ref, bf16[768,3072]{1,0:T(8,128)(2,1)} %copy-done.2, bf16[768,3072]{1,0:T(8,128)(2,1)} %copy-done.2, bf16[768,3072]{1,0:T(8,128)(2,1)} %copy-done.2, ...), custom_call_target="tpu_custom_call" | custom-call | flops 384 | bytes 384 | tf_op jit(solution)/shard_map/attn_fwd/pallas_call | solution.py:45
  86.2 2.5 fusion.94
  91.1 5.9 %all-to-all-start.1 = ((bf16[8,56,1024]{2,1,0:T(8,128)(2,1)}), bf16[8,56,1024]{2,1,0:T(8,128)(2,1)}, u32[]{:S(2)}, u32[]{:S(2)}) async-start(bf16[8,56,1024]{2,1,0:T(8,128)(2,1)} %bitcast.143), calls=%async_computation.1 | async-start | bytes 1835008 | tf_op jit(solution)/shard_map/all_to_all | solution.py:483
  97.0 3.5 fusion.19
  107.5 12.6 %all-to-all-done.1 = bf16[8,56,1024]{2,1,0:T(8,128)(2,1)} async-done(((bf16[8,56,1024]{2,1,0:T(8,128)(2,1)}), bf16[8,56,1024]{2,1,0:T(8,128)(2,1)}, u32[]{:S(2)}, u32[]{:S(2)}) %all-to-all-start.1) | async-done | bytes 917536 | tf_op jit(solution)/shard_map/all_to_all | solution.py:483
  120.0 4.4 all-to-all-start.2
  124.5 24.9 %expert.2 = (bf16[896,4096]{1,0:T(8,128)(2,1)}, bf16[896,4096]{1,0:T(8,128)(2,1)}, bf16[8,112,1024]{2,1,0:T(8,128)(2,1)}, bf16[448,1024]{1,0:T(8,128)(2,1)}) custom-call(bf16[448,1024]{1,0:T(8,128)(2,1)} %bitcast.18.x_ref.refs_0_, bf16[8,2,56,1024]{3,2,1,0:T(8,128)(2,1)} %all-to-all-done.g_ref, bf16[4,8,256,1024]{3,2,1,0:T(8,128)(2,1)} %bitcast.159, ...), custom_call_target="tpu_custom_call" | custom-call | flops 15032385536 | bytes 24117248 | tf_op jit(solution)/shard_map/expert/pallas_call | solution.py:154
  149.3 6.0 %all-to-all-start.3 = ((bf16[8,112,1024]{2,1,0:T(8,128)(2,1)}), bf16[8,112,1024]{2,1,0:T(8,128)(2,1)}, u32[]{:S(2)}, u32[]{:S(2)}) async-start(bf16[8,112,1024]{2,1,0:T(8,128)(2,1)} %get-tuple-element.155), calls=%async_computation.3 | async-start | bytes 3670016 | tf_op jit(solution)/shard_map/all_to_all | solution.py:506
  155.4 24.8 %expert.3 = (bf16[896,4096]{1,0:T(8,128)(2,1)}, bf16[896,4096]{1,0:T(8,128)(2,1)}, bf16[8,112,1024]{2,1,0:T(8,128)(2,1)}, bf16[448,1024]{1,0:T(8,128)(2,1)}) custom-call(bf16[448,1024]{1,0:T(8,128)(2,1)} %bitcast.25.x_ref.refs_1_, bf16[8,2,56,1024]{3,2,1,0:T(8,128)(2,1)} %all-to-all-done.g_ref, ...), custom_call_target="tpu_custom_call", output_to_operand_aliasing={{0}: (4, {}), {1}: (5, {})} | custom-call | flops 15032385536 | bytes 24117248 | tf_op jit(solution)/shard_map/expert/pallas_call | solution.py:154
  180.2 14.2 %out_grads.1 = bf16[4096,1024]{1,0:T(8,128)(2,1)} custom-call(bf16[448,1024]{1,0:T(8,128)(2,1)} %get-tuple-element.146.refs_0_, bf16[448,1024]{1,0:T(8,128)(2,1)} %get-tuple-element.152.refs_1_, bf16[896,4096]{1,0:T(8,128)(2,1)} %get-tuple-element.153.refs_2_), custom_call_target="tpu_custom_call" | custom-call | flops 7516192768 | bytes 15728640 | tf_op jit(solution)/shard_map/out_grads/pallas_call | solution.py:193
  194.4 2.6 all-to-all-done.3
  197.0 4.4 all-to-all-start.4
  201.4 4.6 fusion.29
  206.0 3.1 fusion.96
  212.7 1.9 convolution_convert_fusion.5.do_ref
  214.7 18.1 %attn_bwd.2 = (bf16[384,1024]{1,0:T(8,128)(2,1)}, bf16[2,384,1024]{2,1,0:T(8,128)(2,1)}, bf16[2,384,1024]{2,1,0:T(8,128)(2,1)}) custom-call(f32[768,384]{1,0:T(8,128)} %and_select_fusion.1.biast_ref, f32[16,384]{1,0:T(8,128)} %slice_bitcast_fusion.6.lse_ref, bf16[768,3072]{1,0:T(8,128)(2,1)} %copy-done.2, bf16[768,3072]{1,0:T(8,128)(2,1)} %copy-done.2, ...), custom_call_target="tpu_custom_call" | custom-call | flops 12079595520 | bytes 11796480 | tf_op jit(solution)/shard_map/attn_bwd/pallas_call | solution.py:98
  232.8 14.6 %in_grads.1 = bf16[4,4,256,1024]{3,2,1,0:T(8,128)(2,1)} custom-call(bf16[448,1024]{1,0:T(8,128)(2,1)} %bitcast.18.x_ref.refs_0_, bf16[448,1024]{1,0:T(8,128)(2,1)} %bitcast.25.x_ref.refs_1_, bf16[896,4096]{1,0:T(8,128)(2,1)} %get-tuple-element.163.refs_2_), custom_call_target="tpu_custom_call" | custom-call | flops 7516192768 | bytes 15728640 | tf_op jit(solution)/shard_map/in_grads/pallas_call | solution.py:176
  247.4 3.0 fusion.2
  250.5 2.7 fusion.97
  254.6 2.1 fusion.86
  257.6 1.9 convolution_convert_fusion.4.do_ref
  259.5 18.0 %attn_bwd.3 = (bf16[384,1024]{1,0:T(8,128)(2,1)}, bf16[2,384,1024]{2,1,0:T(8,128)(2,1)}, bf16[2,384,1024]{2,1,0:T(8,128)(2,1)}) custom-call(f32[768,384]{1,0:T(8,128)} %and_select_fusion.biast_ref, f32[16,384]{1,0:T(8,128)} %slice_bitcast_fusion.5.lse_ref, bf16[768,3072]{1,0:T(8,128)(2,1)} %copy-done.2, bf16[768,3072]{1,0:T(8,128)(2,1)} %copy-done.2, ...), custom_call_target="tpu_custom_call" | custom-call | flops 12079595520 | bytes 11796480 | tf_op jit(solution)/shard_map/attn_bwd/pallas_call | solution.py:98
  278.1 3.2 convolution_convert_fusion.1
  281.6 1.9 collective-permute-done.2.refs_2_
  283.6 13.9 %project_grads.1 = (bf16[768,3072]{1,0:T(8,128)(2,1)}, bf16[512,1536]{1,0:T(8,128)(2,1)}, bf16[512,1536]{1,0:T(8,128)(2,1)}, bf16[512,1536]{1,0:T(8,128)(2,1)}, bf16[512,1536]{1,0:T(8,128)(2,1)}) custom-call(s32[1]{0:T(128)} %bitcast.32.high_ref, bf16[768,1024]{1,0:T(8,128)(2,1)} %copy-done.27, bf16[384,1024]{1,0:T(8,128)(2,1)} %get-tuple-element.169.refs_0_, ...), custom_call_target="tpu_custom_call" | custom-call | flops 4831838208 | bytes 18874368 | tf_op jit(solution)/shard_map/project_grads/pallas_call | solution.py:236
  297.5 2.6 add.385
  300.7 3.2 collective-permute-done.7
  303.9 1.8 add.391
  305.8 1.9 collective-permute-start.8
  308.1 2.2 add.386
  315.0 10.5 %collective-permute-done.8 = bf16[256,1536]{1,0:T(8,128)(2,1)S(1)} collective-permute-done((bf16[256,1536]{1,0:T(8,128)(2,1)S(1)}, bf16[256,1536]{1,0:T(8,128)(2,1)S(1)}, u32[]{:S(2)}, u32[]{:S(2)}) %collective-permute-start.8) | collective-permute-done | bytes 786464 | tf_op jit(solution)/shard_map/ppermute | solution.py:298
  326.0 3.5 collective-permute-done.6
  335.8 8.6 %multiply_reduce_fusion = (f32[768]{0:T(1024)S(1)}, f32[1024]{0:T(1024)}, f32[768]{0:T(1024)S(1)}, f32[1024]{0:T(1024)}, f32[768,1024]{1,0:T(8,128)S(1)}) fusion(bf16[2,1,384,1024]{3,2,1,0:T(8,128)(2,1)S(1)} %copy-done.4, f32[1024]{0:T(1024)S(1)} %copy-done.39, f32[768]{0:T(1024)S(1)} %rsqrt.28, f32[768]{0:T(1024)S(1)} %div.101, ...), kind=kOutput, calls=%fused_computation.4 | convolution fusion | flops 4839698432 | bytes 15753216 | tf_op jit(solution)/shard_map/dot_general | solution.py:592
  344.4 2.9 maximum_add_fusion
  347.3 1.9 concatenate.80
  353.3 2.4 collective-permute-start.15
  358.0 5.6 %collective-permute-done.16 = f32[12,1024]{1,0:T(8,128)S(1)} collective-permute-done((f32[12,1024]{1,0:T(8,128)S(1)}, f32[12,1024]{1,0:T(8,128)S(1)}, u32[]{:S(2)}, u32[]{:S(2)}) %collective-permute-start.16) | collective-permute-done | bytes 49184 | tf_op jit(solution)/shard_map/ppermute | solution.py:298
  363.8 3.5 collective-permute-done.14
  367.3 2.4 collective-permute-start.17
  372.3 4.4 collective-permute-done.20
  376.7 3.5 collective-permute-done.17
  380.2 4.1 collective-permute-done.18
  385.9 2.9 collective-permute-start.21
  392.3 2.7 collective-permute-done.21
  397.5 2.6 collective-permute-done.28
  404.5 2.5 maximum_convert_fusion
  407.0 2.5 convert_element_type.227
  414.4 7.1 %collective-permute-done.31 = bf16[256,1024]{1,0:T(8,128)(2,1)S(1)} collective-permute-done((bf16[256,1024]{1,0:T(8,128)(2,1)S(1)}, bf16[256,1024]{1,0:T(8,128)(2,1)S(1)}, u32[]{:S(2)}, u32[]{:S(2)}) %collective-permute-start.31) | collective-permute-done | bytes 524320 | tf_op jit(solution)/shard_map/ppermute | solution.py:298
  421.7 5.6 %collective-permute-done.29 = bf16[256,1536]{1,0:T(8,128)(2,1)S(1)} collective-permute-done((bf16[256,1536]{1,0:T(8,128)(2,1)S(1)}, bf16[256,1536]{1,0:T(8,128)(2,1)S(1)}, u32[]{:S(2)}, u32[]{:S(2)}) %collective-permute-start.29) | collective-permute-done | bytes 786464 | tf_op jit(solution)/shard_map/ppermute | solution.py:298
  427.6 5.1 %collective-permute-done.30 = bf16[256,1536]{1,0:T(8,128)(2,1)S(1)} collective-permute-done((bf16[256,1536]{1,0:T(8,128)(2,1)S(1)}, bf16[256,1536]{1,0:T(8,128)(2,1)S(1)}, u32[]{:S(2)}, u32[]{:S(2)}) %collective-permute-start.30) | collective-permute-done | bytes 786464 | tf_op jit(solution)/shard_map/ppermute | solution.py:298
  436.0 2.7 widen.4.refs_1_
  438.7 4.3 widen.5.refs_2_
  444.2 2.7 widen.7
  446.9 4.4 widen.6
  (299 shorter events, 78.0 us)
Async XLA Ops:
  7.2 57.8 %copy-start = (bf16[1024,1024]{1,0:T(8,128)(2,1)S(1)}, bf16[1024,1024]{1,0:T(8,128)(2,1)}, u32[]{:S(2)}) copy-start(bf16[1024,1024]{1,0:T(8,128)(2,1)} %param.22) | copy-start | bytes 6291460
  7.2 117.3 %all-gather.2.cloned.1.call-start = ((), (), s32[]{:S(2)}) async-start(), calls=%async_computation.7 | async-start | bytes 20971520 | tf_op jit(solution)/shard_map/all_gather | solution.py:361
  24.6 9.6 %copy-start.27 = (bf16[768,1024]{1,0:T(8,128)(2,1)}, bf16[768,1024]{1,0:T(8,128)(2,1)S(1)}, u32[]{:S(2)}) copy-start(bf16[768,1024]{1,0:T(8,128)(2,1)S(1)} %add_convert_fusion.x_ref) | copy-start | bytes 4718596
  37.5 14.9 %collective-permute-start = (bf16[384,2048]{1,0:T(8,128)(2,1)}, bf16[384,2048]{1,0:T(8,128)(2,1)}, u32[]{:S(2)}, u32[]{:S(2)}) collective-permute-start(bf16[384,2048]{1,0:T(8,128)(2,1)} %get-tuple-element.310), channel_id=1, source_target_pairs={{0,2},{2,0},{1,3},{3,1},{4,6},{6,4},{5,7},{7,5},{8,10},{10,8},{9,1... | collective-permute-start | bytes 4718600 | tf_op jit(solution)/shard_map/ppermute | solution.py:394
  37.9 8.0 %copy-start.46 = (s32[2,1,3]{2,1,0:T(1,128)S(1)}, s32[2,1,3]{2,1,0:T(1,128)}, u32[]{:S(2)}) copy-start(s32[2,1,3]{2,1,0:T(1,128)} %param.16) | copy-start | bytes 76
  37.9 8.4 %copy-start.41 = (s32[2,1,768]{2,1,0:T(1,128)S(1)}, s32[2,1,768]{2,1,0:T(1,128)}, u32[]{:S(2)}) copy-start(s32[2,1,768]{2,1,0:T(1,128)} %param.17) | copy-start | bytes 18436
  37.9 33.3 %collective-permute-start.1 = (bf16[384,2048]{1,0:T(8,128)(2,1)}, bf16[384,2048]{1,0:T(8,128)(2,1)}, u32[]{:S(2)}, u32[]{:S(2)}) collective-permute-start(bf16[384,2048]{1,0:T(8,128)(2,1)} %get-tuple-element.309), channel_id=1, source_target_pairs={{0,2},{2,0},{1,3},{3,1},{4,6},{6,4},{5,7},{7,5},{8,10},{10,8},{9,1... | collective-permute-start | bytes 4718600 | tf_op jit(solution)/shard_map/ppermute | solution.py:394
  38.0 53.1 %all-to-all-start = ((bf16[8,2,56,1024]{3,2,1,0:T(8,128)(2,1)}), bf16[8,2,56,1024]{3,2,1,0:T(8,128)(2,1)}, u32[]{:S(2)}, u32[]{:S(2)}) async-start(bf16[8,2,56,1024]{3,2,1,0:T(8,128)(2,1)} %pad_maximum_fusion), calls=%async_computation | async-start | bytes 3670016 | tf_op jit(solution)/shard_map/all_to_all | solution.py:384
  46.7 22.3 %copy-start.44 = (pred[448]{0:T(512)(128)(4,1)}, pred[448]{0:T(512)(128)(4,1)S(1)}, u32[]{:S(2)}) copy-start(pred[448]{0:T(512)(128)(4,1)S(1)} %get-tuple-element.372) | copy-start | bytes 1348
  71.2 12.6 %copy-start.37 = (f32[384,128]{1,0:T(8,128)S(1)}, f32[384,128]{1,0:T(8,128)}, u32[]{:S(2)}) copy-start(f32[384,128]{1,0:T(8,128)} %get-tuple-element.129) | copy-start | bytes 589828
  91.1 28.9 %all-to-all-start.1 = ((bf16[8,56,1024]{2,1,0:T(8,128)(2,1)}), bf16[8,56,1024]{2,1,0:T(8,128)(2,1)}, u32[]{:S(2)}, u32[]{:S(2)}) async-start(bf16[8,56,1024]{2,1,0:T(8,128)(2,1)} %bitcast.143), calls=%async_computation.1 | async-start | bytes 1835008 | tf_op jit(solution)/shard_map/all_to_all | solution.py:483
  120.0 29.3 %all-to-all-start.2 = ((bf16[8,56,1024]{2,1,0:T(8,128)(2,1)}), bf16[8,56,1024]{2,1,0:T(8,128)(2,1)}, u32[]{:S(2)}, u32[]{:S(2)}) async-start(bf16[8,56,1024]{2,1,0:T(8,128)(2,1)} %bitcast.144), calls=%async_computation.2 | async-start | bytes 1835008 | tf_op jit(solution)/shard_map/all_to_all | solution.py:483
  149.3 47.6 %all-to-all-start.3 = ((bf16[8,112,1024]{2,1,0:T(8,128)(2,1)}), bf16[8,112,1024]{2,1,0:T(8,128)(2,1)}, u32[]{:S(2)}, u32[]{:S(2)}) async-start(bf16[8,112,1024]{2,1,0:T(8,128)(2,1)} %get-tuple-element.155), calls=%async_computation.3 | async-start | bytes 3670016 | tf_op jit(solution)/shard_map/all_to_all | solution.py:506
  155.3 144.7 %reduce-scatter.3.cloned.1.call-start = ((), (), s32[]{:S(2)}) async-start(), calls=%async_computation.8 | async-start | bytes 10485760 | tf_op jit(solution)/shard_map/reduce_scatter | solution.py:513
  197.0 50.4 %all-to-all-start.4 = ((bf16[8,112,1024]{2,1,0:T(8,128)(2,1)}), bf16[8,112,1024]{2,1,0:T(8,128)(2,1)}, u32[]{:S(2)}, u32[]{:S(2)}) async-start(bf16[8,112,1024]{2,1,0:T(8,128)(2,1)} %get-tuple-element.168), calls=%async_computation.4 | async-start | bytes 3670016 | tf_op jit(solution)/shard_map/all_to_all | solution.py:506
  201.3 198.8 %reduce-scatter.5.cloned.1.call-start = ((), (), s32[]{:S(2)}) async-start(), calls=%async_computation.9 | async-start | bytes 10485760 | tf_op jit(solution)/shard_map/reduce_scatter | solution.py:574
  201.4 4.6 %copy-start.25 = (bf16[896,384]{1,0:T(8,128)(2,1)S(1)}, bf16[896,384]{1,0:T(8,128)(2,1)}, u32[]{:S(2)}) copy-start(bf16[896,384]{1,0:T(8,128)(2,1)} %fusion.26) | copy-start | bytes 2064388
  259.5 18.6 %copy-start.31 = (bf16[384,1024]{1,0:T(8,128)(2,1)S(1)}, bf16[384,1024]{1,0:T(8,128)(2,1)}, u32[]{:S(2)}) copy-start(bf16[384,1024]{1,0:T(8,128)(2,1)} %copy-done.30) | copy-start | bytes 2359300
  259.5 18.6 %copy-start.35 = (bf16[384,1024]{1,0:T(8,128)(2,1)S(1)}, bf16[384,1024]{1,0:T(8,128)(2,1)}, u32[]{:S(2)}) copy-start(bf16[384,1024]{1,0:T(8,128)(2,1)} %copy-done.34) | copy-start | bytes 2359300
  277.5 4.0 collective-permute-start.3
  277.6 6.0 %collective-permute-start.2 = (bf16[2,384,1024]{2,1,0:T(8,128)(2,1)}, bf16[2,384,1024]{2,1,0:T(8,128)(2,1)}, u32[]{:S(2)}, u32[]{:S(2)}) collective-permute-start(bf16[2,384,1024]{2,1,0:T(8,128)(2,1)} %get-tuple-element.171), channel_id=1, source_target_pairs={{0,2},{2,0},{1,3},{3,1},{4,6},{6,4},{5,7},{7,5},{8,10},{10,8},{9,1... | collective-permute-start | bytes 4718600 | tf_op jit(solution)/shard_map/ppermute | solution.py:540
  281.5 15.9 %collective-permute-start.4 = (bf16[512,1024]{1,0:T(8,128)(2,1)S(1)}, bf16[512,1024]{1,0:T(8,128)(2,1)}, u32[]{:S(2)}, u32[]{:S(2)}) collective-permute-start(bf16[512,1024]{1,0:T(8,128)(2,1)S(1)} %get-tuple-element.184), channel_id=1, source_target_pairs={{0,2},{2,0},{1,3},{3,1},{4,6},{6,4},{5,7},{7,5},{8,10},{10,8},{9,1... | collective-permute-start | bytes 3145736 | tf_op jit(solution)/shard_map/ppermute | solution.py:298
  300.1 3.8 collective-permute-start.7
  300.3 7.9 %collective-permute-start.5 = (bf16[512,1536]{1,0:T(8,128)(2,1)}, bf16[512,1536]{1,0:T(8,128)(2,1)}, u32[]{:S(2)}, u32[]{:S(2)}) collective-permute-start(bf16[512,1536]{1,0:T(8,128)(2,1)} %get-tuple-element.186), channel_id=1, source_target_pairs={{0,2},{2,0},{1,3},{3,1},{4,6},{6,4},{5,7},{7,5},{8,10},{10,8},{9,1... | collective-permute-start | bytes 4718600 | tf_op jit(solution)/shard_map/ppermute | solution.py:298
  305.8 19.8 %collective-permute-start.8 = (bf16[256,1536]{1,0:T(8,128)(2,1)S(1)}, bf16[256,1536]{1,0:T(8,128)(2,1)S(1)}, u32[]{:S(2)}, u32[]{:S(2)}) collective-permute-start(bf16[256,1536]{1,0:T(8,128)(2,1)S(1)} %constant_dynamic-slice_fusion.7), channel_id=1, source_target_pairs={{0,8},{4,12},{8,0},{12,4},{16,24},{20,28},{24,16},{28,20},{1,9},{5... | collective-permute-start | bytes 2359304 | tf_op jit(solution)/shard_map/ppermute | solution.py:298
  310.4 19.1 %collective-permute-start.6 = (bf16[256,1536]{1,0:T(8,128)(2,1)S(1)}, bf16[256,1536]{1,0:T(8,128)(2,1)S(1)}, u32[]{:S(2)}, u32[]{:S(2)}) collective-permute-start(bf16[256,1536]{1,0:T(8,128)(2,1)S(1)} %constant_dynamic-slice_fusion.8), channel_id=1, source_target_pairs={{0,4},{4,0},{8,12},{12,8},{16,20},{20,16},{24,28},{28,24},{1,5},{5... | collective-permute-start | bytes 2359304 | tf_op jit(solution)/shard_map/ppermute | solution.py:298
  311.8 14.0 %collective-permute-start.9 = (bf16[256,1024]{1,0:T(8,128)(2,1)S(1)}, bf16[256,1024]{1,0:T(8,128)(2,1)S(1)}, u32[]{:S(2)}, u32[]{:S(2)}) collective-permute-start(bf16[256,1024]{1,0:T(8,128)(2,1)S(1)} %constant_dynamic-slice_fusion.6), channel_id=1, source_target_pairs={{0,1},{1,0},{2,3},{3,2},{4,5},{5,4},{6,7},{7,6},{8,9},{9,8},{10,11... | collective-permute-start | bytes 1572872 | tf_op jit(solution)/shard_map/ppermute | solution.py:298
  325.6 10.3 %copy-start.47 = (bf16[768,3072]{1,0:T(8,128)(2,1)S(1)}, bf16[768,3072]{1,0:T(8,128)(2,1)}, u32[]{:S(2)}) copy-start(bf16[768,3072]{1,0:T(8,128)(2,1)} %get-tuple-element.194) | copy-start | bytes 14155780
  325.8 6.3 %copy-start.20 = (bf16[256,1536]{1,0:T(8,128)(2,1)}, bf16[256,1536]{1,0:T(8,128)(2,1)S(1)}, u32[]{:S(2)}) copy-start(bf16[256,1536]{1,0:T(8,128)(2,1)S(1)} %dynamic-slice_add_fusion) | copy-start | bytes 2359300
  329.8 4.6 copy-start.22
  329.8 6.0 %copy-start.4 = (bf16[2,1,384,1024]{3,2,1,0:T(8,128)(2,1)S(1)}, bf16[2,1,384,1024]{3,2,1,0:T(8,128)(2,1)}, u32[]{:S(2)}) copy-start(bf16[2,1,384,1024]{3,2,1,0:T(8,128)(2,1)} %param.14) | copy-start | bytes 4718596
  330.6 20.0 %collective-permute-start.10 = (bf16[128,1536]{1,0:T(8,128)(2,1)}, bf16[128,1536]{1,0:T(8,128)(2,1)}, u32[]{:S(2)}, u32[]{:S(2)}) collective-permute-start(bf16[128,1536]{1,0:T(8,128)(2,1)} %constant_dynamic-slice_fusion.5), channel_id=1, source_target_pairs={{0,1},{1,0},{2,3},{3,2},{4,5},{5,4},{6,7},{7,6},{8,9},{9,8},{10,11... | collective-permute-start | bytes 1179656 | tf_op jit(solution)/shard_map/ppermute | solution.py:298
  332.9 18.8 %collective-permute-start.11 = (bf16[128,1536]{1,0:T(8,128)(2,1)}, bf16[128,1536]{1,0:T(8,128)(2,1)S(1)}, u32[]{:S(2)}, u32[]{:S(2)}) collective-permute-start(bf16[128,1536]{1,0:T(8,128)(2,1)} %constant_dynamic-slice_fusion.4), channel_id=1, source_target_pairs={{0,4},{4,0},{8,12},{12,8},{16,20},{20,16},{24,28},{28,24},{1,5},{5... | collective-permute-start | bytes 1179656 | tf_op jit(solution)/shard_map/ppermute | solution.py:298
  334.4 10.0 %copy-start.11 = (f32[384,1024]{1,0:T(8,128)S(1)}, f32[384,1024]{1,0:T(8,128)}, u32[]{:S(2)}) copy-start(f32[384,1024]{1,0:T(8,128)} %get-tuple-element.302) | copy-start | bytes 4718596
  334.4 10.0 %copy-start.12 = (f32[384,1024]{1,0:T(8,128)S(1)}, f32[384,1024]{1,0:T(8,128)}, u32[]{:S(2)}) copy-start(f32[384,1024]{1,0:T(8,128)} %get-tuple-element.304) | copy-start | bytes 4718596
  334.4 14.8 %collective-permute-start.12 = (bf16[128,1024]{1,0:T(8,128)(2,1)S(1)}, bf16[128,1024]{1,0:T(8,128)(2,1)}, u32[]{:S(2)}, u32[]{:S(2)}) collective-permute-start(bf16[128,1024]{1,0:T(8,128)(2,1)S(1)} %constant_dynamic-slice_fusion.3), channel_id=1, source_target_pairs={{0,8},{4,12},{8,0},{12,4},{16,24},{20,28},{24,16},{28,20},{1,9},{5... | collective-permute-start | bytes 786440 | tf_op jit(solution)/shard_map/ppermute | solution.py:298
  344.4 6.2 %copy-start.23 = (bf16[256,1536]{1,0:T(8,128)(2,1)S(1)}, bf16[256,1536]{1,0:T(8,128)(2,1)}, u32[]{:S(2)}) copy-start(bf16[256,1536]{1,0:T(8,128)(2,1)} %copy-done.22) | copy-start | bytes 2359300
  347.3 4.3 copy-start.21
  351.8 11.9 %collective-permute-start.13 = (bf16[64,1536]{1,0:T(8,128)(2,1)S(1)}, bf16[64,1536]{1,0:T(8,128)(2,1)S(1)}, u32[]{:S(2)}, u32[]{:S(2)}) collective-permute-start(bf16[64,1536]{1,0:T(8,128)(2,1)S(1)} %constant_dynamic-slice_fusion.2), channel_id=1, source_target_pairs={{0,8},{4,12},{8,0},{12,4},{16,24},{20,28},{24,16},{28,20},{1,9},{5... | collective-permute-start | bytes 589832 | tf_op jit(solution)/shard_map/ppermute | solution.py:298
  353.3 10.3 %collective-permute-start.15 = (bf16[64,1024]{1,0:T(8,128)(2,1)S(1)}, bf16[64,1024]{1,0:T(8,128)(2,1)S(1)}, u32[]{:S(2)}, u32[]{:S(2)}) collective-permute-start(bf16[64,1024]{1,0:T(8,128)(2,1)S(1)} %constant_dynamic-slice_fusion), channel_id=1, source_target_pairs={{0,16},{4,20},{8,24},{12,28},{16,0},{20,4},{24,8},{28,12},{1,17},{... | collective-permute-start | bytes 393224 | tf_op jit(solution)/shard_map/ppermute | solution.py:298
  355.8 7.9 %collective-permute-start.16 = (f32[12,1024]{1,0:T(8,128)S(1)}, f32[12,1024]{1,0:T(8,128)S(1)}, u32[]{:S(2)}, u32[]{:S(2)}) collective-permute-start(f32[12,1024]{1,0:T(8,128)S(1)} %concatenate.80), channel_id=1, source_target_pairs={{0,16},{4,20},{8,24},{12,28},{16,0},{20,4},{24,8},{28,12},{1,17},{... | collective-permute-start | bytes 147464 | tf_op jit(solution)/shard_map/ppermute | solution.py:298
  356.3 10.9 %collective-permute-start.14 = (bf16[64,1536]{1,0:T(8,128)(2,1)S(1)}, bf16[64,1536]{1,0:T(8,128)(2,1)S(1)}, u32[]{:S(2)}, u32[]{:S(2)}) collective-permute-start(bf16[64,1536]{1,0:T(8,128)(2,1)S(1)} %constant_dynamic-slice_fusion.1), channel_id=1, source_target_pairs={{0,1},{1,0},{2,3},{3,2},{4,5},{5,4},{6,7},{7,6},{8,9},{9,8},{10,11... | collective-permute-start | bytes 589832 | tf_op jit(solution)/shard_map/ppermute | solution.py:298
  367.3 12.9 %collective-permute-start.17 = (bf16[64,1536]{1,0:T(8,128)(2,1)S(1)}, bf16[64,1536]{1,0:T(8,128)(2,1)S(1)}, u32[]{:S(2)}, u32[]{:S(2)}) collective-permute-start(bf16[64,1536]{1,0:T(8,128)(2,1)S(1)} %dynamic-slice_add_fusion.7), channel_id=1, source_target_pairs={{0,16},{4,20},{8,24},{12,28},{16,0},{20,4},{24,8},{28,12},{1,17},{... | collective-permute-start | bytes 589832 | tf_op jit(solution)/shard_map/ppermute | solution.py:298
  369.7 14.6 %collective-permute-start.18 = (bf16[64,1536]{1,0:T(8,128)(2,1)S(1)}, bf16[64,1536]{1,0:T(8,128)(2,1)S(1)}, u32[]{:S(2)}, u32[]{:S(2)}) collective-permute-start(bf16[64,1536]{1,0:T(8,128)(2,1)S(1)} %dynamic-slice_add_fusion.6), channel_id=1, source_target_pairs={{0,16},{4,20},{8,24},{12,28},{16,0},{20,4},{24,8},{28,12},{1,17},{... | collective-permute-start | bytes 589832 | tf_op jit(solution)/shard_map/ppermute | solution.py:298
  370.3 6.4 %collective-permute-start.19 = (bf16[64,1024]{1,0:T(8,128)(2,1)S(1)}, bf16[64,1024]{1,0:T(8,128)(2,1)S(1)}, u32[]{:S(2)}, u32[]{:S(2)}) collective-permute-start(bf16[64,1024]{1,0:T(8,128)(2,1)S(1)} %dynamic-slice_add_fusion.8), channel_id=1, source_target_pairs={{0,4},{4,0},{8,12},{12,8},{16,20},{20,16},{24,28},{28,24},{1,5},{5... | collective-permute-start | bytes 393224 | tf_op jit(solution)/shard_map/ppermute | solution.py:298
  371.8 4.9 %collective-permute-start.20 = (f32[12,1024]{1,0:T(8,128)S(1)}, f32[12,1024]{1,0:T(8,128)S(1)}, u32[]{:S(2)}, u32[]{:S(2)}) collective-permute-start(f32[12,1024]{1,0:T(8,128)S(1)} %add.425), channel_id=1, source_target_pairs={{0,8},{4,12},{8,0},{12,4},{16,24},{20,28},{24,16},{28,20},{1,9},{5... | collective-permute-start | bytes 147464 | tf_op jit(solution)/shard_map/ppermute | solution.py:298
  384.4 7.9 %collective-permute-start.23 = (bf16[64,1024]{1,0:T(8,128)(2,1)S(1)}, bf16[64,1024]{1,0:T(8,128)(2,1)S(1)}, u32[]{:S(2)}, u32[]{:S(2)}) collective-permute-start(bf16[64,1024]{1,0:T(8,128)(2,1)S(1)} %add.428), channel_id=1, source_target_pairs={{0,16},{4,20},{8,24},{12,28},{16,0},{20,4},{24,8},{28,12},{1,17},{... | collective-permute-start | bytes 393224 | tf_op jit(solution)/shard_map/ppermute | solution.py:298
  384.4 6.0 %collective-permute-start.24 = (f32[12,1024]{1,0:T(8,128)S(1)}, f32[12,1024]{1,0:T(8,128)S(1)}, u32[]{:S(2)}, u32[]{:S(2)}) collective-permute-start(f32[12,1024]{1,0:T(8,128)S(1)} %add.429), channel_id=1, source_target_pairs={{0,4},{4,0},{8,12},{12,8},{16,20},{20,16},{24,28},{28,24},{1,5},{5... | collective-permute-start | bytes 147464 | tf_op jit(solution)/shard_map/ppermute | solution.py:298
  385.9 9.0 %collective-permute-start.21 = (bf16[64,1536]{1,0:T(8,128)(2,1)S(1)}, bf16[64,1536]{1,0:T(8,128)(2,1)S(1)}, u32[]{:S(2)}, u32[]{:S(2)}) collective-permute-start(bf16[64,1536]{1,0:T(8,128)(2,1)S(1)} %add.426), channel_id=1, source_target_pairs={{0,8},{4,12},{8,0},{12,4},{16,24},{20,28},{24,16},{28,20},{1,9},{5... | collective-permute-start | bytes 589832 | tf_op jit(solution)/shard_map/ppermute | solution.py:298
  388.8 6.2 %collective-permute-start.22 = (bf16[64,1536]{1,0:T(8,128)(2,1)S(1)}, bf16[64,1536]{1,0:T(8,128)(2,1)S(1)}, u32[]{:S(2)}, u32[]{:S(2)}) collective-permute-start(bf16[64,1536]{1,0:T(8,128)(2,1)S(1)} %add.427), channel_id=1, source_target_pairs={{0,1},{1,0},{2,3},{3,2},{4,5},{5,4},{6,7},{7,6},{8,9},{9,8},{10,11... | collective-permute-start | bytes 589832 | tf_op jit(solution)/shard_map/ppermute | solution.py:298
  395.8 4.3 collective-permute-start.28
  400.2 9.4 %collective-permute-start.25 = (bf16[128,1536]{1,0:T(8,128)(2,1)S(1)}, bf16[128,1536]{1,0:T(8,128)(2,1)S(1)}, u32[]{:S(2)}, u32[]{:S(2)}) collective-permute-start(bf16[128,1536]{1,0:T(8,128)(2,1)S(1)} %pad_maximum_fusion.7), channel_id=1, source_target_pairs={{0,1},{1,0},{2,3},{3,2},{4,5},{5,4},{6,7},{7,6},{8,9},{9,8},{10,11... | collective-permute-start | bytes 1179656 | tf_op jit(solution)/shard_map/ppermute | solution.py:298
  401.8 8.3 %collective-permute-start.26 = (bf16[128,1536]{1,0:T(8,128)(2,1)}, bf16[128,1536]{1,0:T(8,128)(2,1)S(1)}, u32[]{:S(2)}, u32[]{:S(2)}) collective-permute-start(bf16[128,1536]{1,0:T(8,128)(2,1)} %pad_maximum_fusion.8), channel_id=1, source_target_pairs={{0,4},{4,0},{8,12},{12,8},{16,20},{20,16},{24,28},{28,24},{1,5},{5... | collective-permute-start | bytes 1179656 | tf_op jit(solution)/shard_map/ppermute | solution.py:298
  402.8 6.7 %collective-permute-start.27 = (bf16[128,1024]{1,0:T(8,128)(2,1)S(1)}, bf16[128,1024]{1,0:T(8,128)(2,1)S(1)}, u32[]{:S(2)}, u32[]{:S(2)}) collective-permute-start(bf16[128,1024]{1,0:T(8,128)(2,1)S(1)} %pad_maximum_fusion.9), channel_id=1, source_target_pairs={{0,8},{4,12},{8,0},{12,4},{16,24},{20,28},{24,16},{28,20},{1,9},{5... | collective-permute-start | bytes 786440 | tf_op jit(solution)/shard_map/ppermute | solution.py:298
  411.3 10.2 %collective-permute-start.31 = (bf16[256,1024]{1,0:T(8,128)(2,1)S(1)}, bf16[256,1024]{1,0:T(8,128)(2,1)S(1)}, u32[]{:S(2)}, u32[]{:S(2)}) collective-permute-start(bf16[256,1024]{1,0:T(8,128)(2,1)S(1)} %pad_maximum_fusion.6), channel_id=1, source_target_pairs={{0,1},{1,0},{2,3},{3,2},{4,5},{5,4},{6,7},{7,6},{8,9},{9,8},{10,11... | collective-permute-start | bytes 1572872 | tf_op jit(solution)/shard_map/ppermute | solution.py:298
  411.8 15.6 %collective-permute-start.29 = (bf16[256,1536]{1,0:T(8,128)(2,1)S(1)}, bf16[256,1536]{1,0:T(8,128)(2,1)S(1)}, u32[]{:S(2)}, u32[]{:S(2)}) collective-permute-start(bf16[256,1536]{1,0:T(8,128)(2,1)S(1)} %pad_maximum_fusion.4), channel_id=1, source_target_pairs={{0,4},{4,0},{8,12},{12,8},{16,20},{20,16},{24,28},{28,24},{1,5},{5... | collective-permute-start | bytes 2359304 | tf_op jit(solution)/shard_map/ppermute | solution.py:298
  412.8 1.6 collective-permute-start.32
  412.8 20.0 %collective-permute-start.30 = (bf16[256,1536]{1,0:T(8,128)(2,1)S(1)}, bf16[256,1536]{1,0:T(8,128)(2,1)S(1)}, u32[]{:S(2)}, u32[]{:S(2)}) collective-permute-start(bf16[256,1536]{1,0:T(8,128)(2,1)S(1)} %pad_maximum_fusion.5), channel_id=1, source_target_pairs={{0,8},{4,12},{8,0},{12,4},{16,24},{20,28},{24,16},{28,20},{1,9},{5... | collective-permute-start | bytes 2359304 | tf_op jit(solution)/shard_map/ppermute | solution.py:298
  421.7 12.9 %copy-start.15 = (bf16[512,1024]{1,0:T(8,128)(2,1)}, bf16[512,1024]{1,0:T(8,128)(2,1)S(1)}, u32[]{:S(2)}) copy-start(bf16[512,1024]{1,0:T(8,128)(2,1)S(1)} %pad_maximum_fusion.3.refs_0_) | copy-start | bytes 3145732
  427.6 6.5 %copy-start.13 = (bf16[512,1536]{1,0:T(8,128)(2,1)}, bf16[512,1536]{1,0:T(8,128)(2,1)S(1)}, u32[]{:S(2)}) copy-start(bf16[512,1536]{1,0:T(8,128)(2,1)S(1)} %pad_maximum_fusion.1.refs_0_) | copy-start | bytes 4718596
  434.1 10.1 %collective-permute-start.33 = (bf16[512,1536]{1,0:T(8,128)(2,1)S(1)}, bf16[512,1536]{1,0:T(8,128)(2,1)}, u32[]{:S(2)}, u32[]{:S(2)}) collective-permute-start(bf16[512,1536]{1,0:T(8,128)(2,1)S(1)} %pad_maximum_fusion.1.refs_0_), channel_id=1, source_target_pairs={{0,2},{2,0},{1,3},{3,1},{4,6},{6,4},{5,7},{7,5},{8,10},{10,8},{9,1... | collective-permute-start | bytes 4718600 | tf_op jit(solution)/shard_map/ppermute | solution.py:298
  434.1 10.1 %collective-permute-start.34 = (bf16[512,1536]{1,0:T(8,128)(2,1)}, bf16[512,1536]{1,0:T(8,128)(2,1)}, u32[]{:S(2)}, u32[]{:S(2)}) collective-permute-start(bf16[512,1536]{1,0:T(8,128)(2,1)} %pad_maximum_fusion.2.refs_1_), channel_id=1, source_target_pairs={{0,2},{2,0},{1,3},{3,1},{4,6},{6,4},{5,7},{7,5},{8,10},{10,8},{9,1... | collective-permute-start | bytes 4718600 | tf_op jit(solution)/shard_map/ppermute | solution.py:298
  434.6 9.6 %collective-permute-start.35 = (bf16[512,1024]{1,0:T(8,128)(2,1)S(1)}, bf16[512,1024]{1,0:T(8,128)(2,1)}, u32[]{:S(2)}, u32[]{:S(2)}) collective-permute-start(bf16[512,1024]{1,0:T(8,128)(2,1)S(1)} %pad_maximum_fusion.3.refs_0_), channel_id=1, source_target_pairs={{0,2},{2,0},{1,3},{3,1},{4,6},{6,4},{5,7},{7,5},{8,10},{10,8},{9,1... | collective-permute-start | bytes 3145736 | tf_op jit(solution)/shard_map/ppermute | solution.py:298
  446.9 4.4 copy-start.1
  (28 other events, 55.6 us)
Sparse Core Ops, SparseCore 0:
  12.2 108.6 all-gather.1
  197.1 70.7 reduce-scatter.2
  300.2 85.6 reduce-scatter.4

commit v5 on v4

--- a/solution.py
+++ b/solution.py
@@ -146,8 +146,8 @@
             b_ref[e,:size,:]=accr[e*size:(e+1)*size,:].astype(bf)
             b_ref[e,size:,:]=accd[e*size:(e+1)*size,:].astype(bf)
 
-def expert(x, g, weights, prev, mb, nmb, capacity, fb=512):
-    rows,D=x.shape; experts,_,size,_=g.shape; n,deep,_=weights.shape; part=deep//2; FF=part*n; per=D//fb
+def expert(x, g, weights, prev, mb, nmb, capacity):
+    rows,D=x.shape; experts,_,size,_=g.shape; n,deep,_=weights.shape; part=deep//2; FF=part*n; fb=min(D,part); per=D//fb
     blk=pl.BlockSpec((rows,fb),lambda f:(mb,f))
     anyspec=pl.BlockSpec(memory_space=pl.ANY)
     ex=() if prev is None else prev
@@ -171,7 +171,7 @@
     t=mm(turned[...],ig_ref[...],NN).astype(bf)
     for q in range(n): in_ref[q,0,:,:]=t[q*(D//n):(q+1)*(D//n),:]
 
-def in_grads(xs, ig, n, fb=512):
+def in_grads(xs, ig, n, fb=1024):
     rows,D=xs[0].shape; FF=ig.shape[1]; per=D//fb; count=len(xs)
     return pl.pallas_call(partial(in_grads_body,count), grid=(FF//fb,),
         in_specs=[pl.BlockSpec((rows,D),lambda f:(0,0))]*count+[pl.BlockSpec((count*rows,fb),lambda f:(0,f))],
@@ -188,7 +188,7 @@
         for m in range(count): stacked[m*rows:(m+1)*rows,:]=gs[m][...]
     out_ref[...]=mm(act_ref[...],stacked[...],TN).astype(bf)
 
-def out_grads(gs, act, fb=512):
+def out_grads(gs, act, fb=1024):
     rows,D=gs[0].shape; FF=act.shape[1]; count=len(gs)
     return pl.pallas_call(partial(out_grads_body,count), grid=(FF//fb,),
         in_specs=[pl.BlockSpec((rows,D),lambda f:(0,0))]*count+[pl.BlockSpec((count*rows,fb),lambda f:(0,f))],
@@ -598,17 +598,18 @@
         elif slot == 1:
             chunks, small, grad_tokens = lax.optimization_barrier((chunks, small, grad_tokens))
         else:
-            small = small + swap(small, *steps.pop())
-            chunks, small = lax.optimization_barrier((chunks, small))
-    small = small + swap(small, *steps.pop())
-    chunks, small = lax.optimization_barrier(
-        (tuple(chunk + swap(chunk, *order[-1]) for chunk, order in zip(chunks, orders)), small)
+            chunks = lax.optimization_barrier(chunks)
+    for step in steps:
+        small = small + swap(small, *step)
+    chunks = lax.optimization_barrier(
+        tuple(chunk + swap(chunk, *order[-1]) for chunk, order in zip(chunks, orders))
     )
     for slot in reversed(range(count - 1)):
         chunks = double(chunks, orders, slot)
-        if steps:
-            small = small + swap(small, *steps.pop())
-        chunks, small = lax.optimization_barrier((tuple(chunks), small))
+        if slot == 1:
+            chunks, small = lax.optimization_barrier((tuple(chunks), small))
+        else:
+            chunks = lax.optimization_barrier(tuple(chunks))
         if slot == count - 2:
             chunks, grad_in, grad_out_weight = lax.optimization_barrier(
                 (chunks, grad_in, grad_out_weight)
@@ -619,7 +620,6 @@
             chunks, grad_in, grad_out_weight = lax.optimization_barrier(
                 (chunks, grad_in, grad_out_weight)
             )
-    assert not steps
     for slot in reversed(range(1, len(near))):
         chunks = double(chunks, (near,) * 3, slot)
     arrived = [swap(chunk, *near[0]) for chunk in chunks]

time: 465 us -> 461 us (level)
  Pallas kernels: 173 us -> 167 us
  transfers between devices with their start and end apart: 44 -> 44, of which waited for: 19 -> 20; matrix products, arithmetic and copies ran while one was open for 25% -> 26% of each run, Pallas kernels for 35% -> 34%
where the time goes in v5:
time: 461 us; the launch traced here: 454 us
  Pallas kernels  167 us (36%)
  waiting for transfers between devices  82.9 us (18%)
  starting transfers between devices  64.2 us (14%)
  matrix products  56.4 us (12%)
  other arithmetic  50.5 us (11%)
  local copies, waits for them, and re-layouts  17.6 us (4%)
  between operations  15.1 us (3%)
    ppermute x32, waiting for transfers between devices, swap(): lax.ppermute(values, axis, [(i, i ^ bit) for i in range(lax.axis_size(axi...  63.2 us
    pallas_call x2, Pallas kernels, expert(): pl.pallas_call(partial(exp_body, capacity), grid=(FF // fb,), in_specs=[p...  46.8 us
    pallas_call x2, Pallas kernels, attn_bwd(): pl.pallas_call(partial(bwd_body, kb), grid=(G,), in_specs=[pl.BlockSpec(b...  36.1 us
    ppermute x32, starting transfers between devices, swap(): lax.ppermute(values, axis, [(i, i ^ bit) for i in range(lax.axis_size(axi...  34.7 us
    pallas_call x2, Pallas kernels, attn_fwd(): pl.pallas_call(partial(fwd_body, rb), grid=(G,), in_specs=[pl.BlockSpec(b...  25.4 us
    pallas_call x4, Pallas kernels, widen(): pl.pallas_call(partial(widen_body, count), grid_spec=pltpu.PrefetchScalar...  14.1 us
    pallas_call x1, Pallas kernels, project_grads(): pl.pallas_call(partial(project_body, count, parts, per), grid_spec=pltpu....  13.7 us
    pallas_call x1, Pallas kernels, in_grads(): pl.pallas_call(partial(in_grads_body, count), grid=(FF // fb,), in_specs=...  13.5 us
  transfers between devices with their start and end apart: 44, of which 20 were waited for; matrix products, arithmetic and copies ran while one was open for 26% of the time, Pallas kernels for 34%

profile of v5, /device:TPU:0, one launch (start us, length us, event | category | flops | bytes accessed | tf_op | source)
XLA Modules:
  0.0 454.1 jit_solution(11947814148011633611)
XLA Ops:
  7.2 4.8 %stack.13 = bf16[2,4,256,1024]{3,2,1,0:T(8,128)(2,1)} custom-call(bf16[256,4096]{1,0:T(8,128)(2,1)} %bitcast.139, bf16[1024,1024]{1,0:T(8,128)(2,1)} %bitcast.140), custom_call_target="tpu_custom_call" | custom-call | bytes 8388608 | tf_op jit(solution)/shard_map/stack/pallas_call | solution.py:266
  15.2 1.9 convolution_convert_fusion.2
  20.1 2.2 multiply_reduce_fusion.2
  22.3 2.3 add_convert_fusion.x_ref
  24.7 9.6 %convolution_convert_fusion.q_ref.ko_ref.vo_ref = bf16[768,3072]{1,0:T(8,128)(2,1)S(1)} fusion(bf16[768,1024]{1,0:T(8,128)(2,1)S(1)} %add_convert_fusion.x_ref, bf16[1024,3072]{1,0:T(8,128)(2,1)} %param.21), kind=kOutput, calls=%fused_computation | convolution fusion | flops 4834197504 | bytes 12582912 | tf_op jit(solution)/shard_map/dot_general | solution.py:389
  34.3 2.2 fusion.88
  38.0 7.5 %all-to-all-start = ((bf16[8,2,56,1024]{3,2,1,0:T(8,128)(2,1)}), bf16[8,2,56,1024]{3,2,1,0:T(8,128)(2,1)}, u32[]{:S(2)}, u32[]{:S(2)}) async-start(bf16[8,2,56,1024]{3,2,1,0:T(8,128)(2,1)} %pad_maximum_fusion), calls=%async_computation | async-start | bytes 3670016 | tf_op jit(solution)/shard_map/all_to_all | solution.py:384
  52.0 12.8 %attn_fwd.2 = (f32[384,1024]{1,0:T(8,128)}, bf16[384,1024]{1,0:T(8,128)(2,1)}, f32[384,128]{1,0:T(8,128)}) custom-call(f32[384,768]{1,0:T(8,128)} %and_select_fusion.3.bias_ref, bf16[768,3072]{1,0:T(8,128)(2,1)} %copy-done.2, bf16[768,3072]{1,0:T(8,128)(2,1)} %copy-done.2, bf16[768,3072]{1,0:T(8,128)(2,1)} %copy-done.2, ...), custom_call_target="tpu_custom_call" | custom-call | flops 384 | bytes 384 | tf_op jit(solution)/shard_map/attn_fwd/pallas_call | solution.py:45
  64.8 2.4 fusion.92
  69.1 1.8 fusion.22
  70.9 12.6 %attn_fwd.3 = (f32[384,1024]{1,0:T(8,128)}, bf16[384,1024]{1,0:T(8,128)(2,1)}, f32[384,128]{1,0:T(8,128)}) custom-call(f32[384,768]{1,0:T(8,128)} %and_select_fusion.2.bias_ref, bf16[768,3072]{1,0:T(8,128)(2,1)} %copy-done.2, bf16[768,3072]{1,0:T(8,128)(2,1)} %copy-done.2, bf16[768,3072]{1,0:T(8,128)(2,1)} %copy-done.2, ...), custom_call_target="tpu_custom_call" | custom-call | flops 384 | bytes 384 | tf_op jit(solution)/shard_map/attn_fwd/pallas_call | solution.py:45
  86.0 2.5 fusion.94
  90.9 5.8 %all-to-all-start.1 = ((bf16[8,56,1024]{2,1,0:T(8,128)(2,1)}), bf16[8,56,1024]{2,1,0:T(8,128)(2,1)}, u32[]{:S(2)}, u32[]{:S(2)}) async-start(bf16[8,56,1024]{2,1,0:T(8,128)(2,1)} %bitcast.143), calls=%async_computation.1 | async-start | bytes 1835008 | tf_op jit(solution)/shard_map/all_to_all | solution.py:483
  96.7 3.5 fusion.19
  107.2 12.6 %all-to-all-done.1 = bf16[8,56,1024]{2,1,0:T(8,128)(2,1)} async-done(((bf16[8,56,1024]{2,1,0:T(8,128)(2,1)}), bf16[8,56,1024]{2,1,0:T(8,128)(2,1)}, u32[]{:S(2)}, u32[]{:S(2)}) %all-to-all-start.1) | async-done | bytes 917536 | tf_op jit(solution)/shard_map/all_to_all | solution.py:483
  119.7 4.6 %all-to-all-start.2 = ((bf16[8,56,1024]{2,1,0:T(8,128)(2,1)}), bf16[8,56,1024]{2,1,0:T(8,128)(2,1)}, u32[]{:S(2)}, u32[]{:S(2)}) async-start(bf16[8,56,1024]{2,1,0:T(8,128)(2,1)} %bitcast.144), calls=%async_computation.2 | async-start | bytes 1835008 | tf_op jit(solution)/shard_map/all_to_all | solution.py:483
  124.4 23.4 %expert.2 = (bf16[896,4096]{1,0:T(8,128)(2,1)}, bf16[896,4096]{1,0:T(8,128)(2,1)}, bf16[8,112,1024]{2,1,0:T(8,128)(2,1)}, bf16[448,1024]{1,0:T(8,128)(2,1)}) custom-call(bf16[448,1024]{1,0:T(8,128)(2,1)} %bitcast.18.x_ref.refs_0_, bf16[8,2,56,1024]{3,2,1,0:T(8,128)(2,1)} %all-to-all-done.g_ref, bf16[4,8,256,1024]{3,2,1,0:T(8,128)(2,1)} %bitcast.159, ...), custom_call_target="tpu_custom_call" | custom-call | flops 15032385536 | bytes 24117248 | tf_op jit(solution)/shard_map/expert/pallas_call | solution.py:154
  147.8 6.0 %all-to-all-start.3 = ((bf16[8,112,1024]{2,1,0:T(8,128)(2,1)}), bf16[8,112,1024]{2,1,0:T(8,128)(2,1)}, u32[]{:S(2)}, u32[]{:S(2)}) async-start(bf16[8,112,1024]{2,1,0:T(8,128)(2,1)} %get-tuple-element.151), calls=%async_computation.3 | async-start | bytes 3670016 | tf_op jit(solution)/shard_map/all_to_all | solution.py:506
  153.9 23.4 %expert.3 = (bf16[896,4096]{1,0:T(8,128)(2,1)}, bf16[896,4096]{1,0:T(8,128)(2,1)}, bf16[8,112,1024]{2,1,0:T(8,128)(2,1)}, bf16[448,1024]{1,0:T(8,128)(2,1)}) custom-call(bf16[448,1024]{1,0:T(8,128)(2,1)} %bitcast.25.x_ref.refs_1_, bf16[8,2,56,1024]{3,2,1,0:T(8,128)(2,1)} %all-to-all-done.g_ref, ...), custom_call_target="tpu_custom_call", output_to_operand_aliasing={{0}: (4, {}), {1}: (5, {})} | custom-call | flops 15032385536 | bytes 24117248 | tf_op jit(solution)/shard_map/expert/pallas_call | solution.py:154
  177.2 13.1 %out_grads.1 = bf16[4096,1024]{1,0:T(8,128)(2,1)} custom-call(bf16[448,1024]{1,0:T(8,128)(2,1)} %get-tuple-element.142.refs_0_, bf16[448,1024]{1,0:T(8,128)(2,1)} %get-tuple-element.148.refs_1_, bf16[896,4096]{1,0:T(8,128)(2,1)} %get-tuple-element.149.refs_2_), custom_call_target="tpu_custom_call" | custom-call | flops 7516192768 | bytes 15728640 | tf_op jit(solution)/shard_map/out_grads/pallas_call | solution.py:193
  190.3 5.1 %all-to-all-done.3 = bf16[8,112,1024]{2,1,0:T(8,128)(2,1)} async-done(((bf16[8,112,1024]{2,1,0:T(8,128)(2,1)}), bf16[8,112,1024]{2,1,0:T(8,128)(2,1)}, u32[]{:S(2)}, u32[]{:S(2)}) %all-to-all-start.3) | async-done | bytes 1835040 | tf_op jit(solution)/shard_map/all_to_all | solution.py:506
  195.5 4.4 all-to-all-start.4
  199.9 4.6 %fusion.29 = (bf16[1,384,1024]{2,1,0:T(8,128)(2,1)}, f32[384]{0:T(512)S(1)}) fusion(f32[384,1024]{1,0:T(8,128)} %copy-done.7, f32[384]{0:T(512)S(1)} %select_reduce_fusion.1, bf16[2,1,384,1024]{3,2,1,0:T(8,128)(2,1)} %param.15, bf16[896,384]{1,0:T(8,128)(2,1)} %fusion.25, bf16[896,1024]{1,0:T(8,128)(2,1)} %bitcast.26), kind=kOutput, calls=%fused_computation.82 | convolution fusion | flops 707001984 | bytes 5671936 | tf_op jit(solution)/shard_map/dot_general | solution.py:523
  204.5 3.1 fusion.96
  211.2 1.9 convolution_convert_fusion.5.do_ref
  213.1 18.1 %attn_bwd.2 = (bf16[384,1024]{1,0:T(8,128)(2,1)}, bf16[2,384,1024]{2,1,0:T(8,128)(2,1)}, bf16[2,384,1024]{2,1,0:T(8,128)(2,1)}) custom-call(f32[768,384]{1,0:T(8,128)} %and_select_fusion.1.biast_ref, f32[16,384]{1,0:T(8,128)} %slice_bitcast_fusion.6.lse_ref, bf16[768,3072]{1,0:T(8,128)(2,1)} %copy-done.2, bf16[768,3072]{1,0:T(8,128)(2,1)} %copy-done.2, ...), custom_call_target="tpu_custom_call" | custom-call | flops 12079595520 | bytes 11796480 | tf_op jit(solution)/shard_map/attn_bwd/pallas_call | solution.py:98
  231.2 13.5 %in_grads.1 = bf16[4,4,256,1024]{3,2,1,0:T(8,128)(2,1)} custom-call(bf16[448,1024]{1,0:T(8,128)(2,1)} %bitcast.18.x_ref.refs_0_, bf16[448,1024]{1,0:T(8,128)(2,1)} %bitcast.25.x_ref.refs_1_, bf16[896,4096]{1,0:T(8,128)(2,1)} %get-tuple-element.159.refs_2_), custom_call_target="tpu_custom_call" | custom-call | flops 7516192768 | bytes 15728640 | tf_op jit(solution)/shard_map/in_grads/pallas_call | solution.py:176
  244.7 3.0 fusion.2
  247.8 2.6 fusion.97
  251.9 2.1 fusion.86
  254.9 1.9 convolution_convert_fusion.4.do_ref
  256.8 18.0 %attn_bwd.3 = (bf16[384,1024]{1,0:T(8,128)(2,1)}, bf16[2,384,1024]{2,1,0:T(8,128)(2,1)}, bf16[2,384,1024]{2,1,0:T(8,128)(2,1)}) custom-call(f32[768,384]{1,0:T(8,128)} %and_select_fusion.biast_ref, f32[16,384]{1,0:T(8,128)} %slice_bitcast_fusion.5.lse_ref, bf16[768,3072]{1,0:T(8,128)(2,1)} %copy-done.2, bf16[768,3072]{1,0:T(8,128)(2,1)} %copy-done.2, ...), custom_call_target="tpu_custom_call" | custom-call | flops 12079595520 | bytes 11796480 | tf_op jit(solution)/shard_map/attn_bwd/pallas_call | solution.py:98
  275.4 3.2 convolution_convert_fusion.1
  278.9 1.9 collective-permute-done.2.refs_2_
  280.8 13.7 %project_grads.1 = (bf16[768,3072]{1,0:T(8,128)(2,1)}, bf16[512,1536]{1,0:T(8,128)(2,1)}, bf16[512,1536]{1,0:T(8,128)(2,1)}, bf16[512,1536]{1,0:T(8,128)(2,1)}, bf16[512,1536]{1,0:T(8,128)(2,1)}) custom-call(s32[1]{0:T(128)} %bitcast.32.high_ref, bf16[768,1024]{1,0:T(8,128)(2,1)} %copy-done.27, bf16[384,1024]{1,0:T(8,128)(2,1)} %get-tuple-element.165.refs_0_, ...), custom_call_target="tpu_custom_call" | custom-call | flops 4831838208 | bytes 18874368 | tf_op jit(solution)/shard_map/project_grads/pallas_call | solution.py:236
  294.5 2.6 add.385
  297.7 3.2 collective-permute-done.7
  301.0 1.8 add.391
  302.8 2.0 collective-permute-start.8
  305.2 2.2 add.386
  312.0 10.7 %collective-permute-done.8 = bf16[256,1536]{1,0:T(8,128)(2,1)S(1)} collective-permute-done((bf16[256,1536]{1,0:T(8,128)(2,1)S(1)}, bf16[256,1536]{1,0:T(8,128)(2,1)S(1)}, u32[]{:S(2)}, u32[]{:S(2)}) %collective-permute-start.8) | collective-permute-done | bytes 786464 | tf_op jit(solution)/shard_map/ppermute | solution.py:298
  323.1 3.6 collective-permute-done.6
  332.7 8.6 %multiply_reduce_fusion = (f32[768]{0:T(1024)S(1)}, f32[1024]{0:T(1024)}, f32[768]{0:T(1024)S(1)}, f32[1024]{0:T(1024)}, f32[768,1024]{1,0:T(8,128)S(1)}) fusion(bf16[2,1,384,1024]{3,2,1,0:T(8,128)(2,1)S(1)} %copy-done.4, f32[1024]{0:T(1024)S(1)} %copy-done.39, f32[768]{0:T(1024)S(1)} %rsqrt.28, f32[768]{0:T(1024)S(1)} %div.101, ...), kind=kOutput, calls=%fused_computation.4 | convolution fusion | flops 4839698432 | bytes 15753216 | tf_op jit(solution)/shard_map/dot_general | solution.py:592
  341.3 2.9 maximum_add_fusion
  344.2 2.0 concatenate.80
  350.5 2.5 collective-permute-start.15
  354.4 2.6 collective-permute-done.15
  357.3 6.8 %collective-permute-done.14 = bf16[64,1536]{1,0:T(8,128)(2,1)S(1)} collective-permute-done((bf16[64,1536]{1,0:T(8,128)(2,1)S(1)}, bf16[64,1536]{1,0:T(8,128)(2,1)S(1)}, u32[]{:S(2)}, u32[]{:S(2)}) %collective-permute-start.14) | collective-permute-done | bytes 196640 | tf_op jit(solution)/shard_map/ppermute | solution.py:298
  364.7 2.4 collective-permute-start.17
  371.2 4.8 %collective-permute-done.26 = f32[12,1024]{1,0:T(8,128)S(1)} collective-permute-done((f32[12,1024]{1,0:T(8,128)S(1)}, f32[12,1024]{1,0:T(8,128)S(1)}, u32[]{:S(2)}, u32[]{:S(2)}) %collective-permute-start.26) | collective-permute-done | bytes 49184 | tf_op jit(solution)/shard_map/ppermute | solution.py:298
  377.3 4.1 collective-permute-done.17
  382.6 5.9 %collective-permute-done.28 = f32[12,1024]{1,0:T(8,128)S(1)} collective-permute-done((f32[12,1024]{1,0:T(8,128)S(1)}, f32[12,1024]{1,0:T(8,128)S(1)}, u32[]{:S(2)}, u32[]{:S(2)}) %collective-permute-start.28) | collective-permute-done | bytes 49184 | tf_op jit(solution)/shard_map/ppermute | solution.py:298
  388.8 5.3 %collective-permute-done.29 = f32[12,1024]{1,0:T(8,128)S(1)} collective-permute-done((f32[12,1024]{1,0:T(8,128)S(1)}, f32[12,1024]{1,0:T(8,128)S(1)}, u32[]{:S(2)}, u32[]{:S(2)}) %collective-permute-start.29) | collective-permute-done | bytes 49184 | tf_op jit(solution)/shard_map/ppermute | solution.py:298
  395.7 4.2 collective-permute-done.19
  403.5 3.6 collective-permute-start.24
  408.8 2.5 maximum_convert_fusion
  411.3 2.5 convert_element_type.227
  416.5 2.0 collective-permute-start.31
  418.5 5.9 %collective-permute-done.32 = bf16[256,1024]{1,0:T(8,128)(2,1)S(1)} collective-permute-done((bf16[256,1024]{1,0:T(8,128)(2,1)S(1)}, bf16[256,1024]{1,0:T(8,128)(2,1)S(1)}, u32[]{:S(2)}, u32[]{:S(2)}) %collective-permute-start.32) | collective-permute-done | bytes 524320 | tf_op jit(solution)/shard_map/ppermute | solution.py:298
  424.6 3.4 collective-permute-done.30
  433.2 2.7 widen.4.refs_1_
  435.9 4.3 widen.5.refs_2_
  440.2 2.7 widen.7
  442.9 4.4 widen.6
  (299 shorter events, 75.0 us)
Async XLA Ops:
  7.2 57.6 %copy-start = (bf16[1024,1024]{1,0:T(8,128)(2,1)S(1)}, bf16[1024,1024]{1,0:T(8,128)(2,1)}, u32[]{:S(2)}) copy-start(bf16[1024,1024]{1,0:T(8,128)(2,1)} %param.22) | copy-start | bytes 6291460
  7.2 117.2 %all-gather.2.cloned.1.call-start = ((), (), s32[]{:S(2)}) async-start(), calls=%async_computation.7 | async-start | bytes 20971520 | tf_op jit(solution)/shard_map/all_gather | solution.py:361
  24.6 9.6 %copy-start.27 = (bf16[768,1024]{1,0:T(8,128)(2,1)}, bf16[768,1024]{1,0:T(8,128)(2,1)S(1)}, u32[]{:S(2)}) copy-start(bf16[768,1024]{1,0:T(8,128)(2,1)S(1)} %add_convert_fusion.x_ref) | copy-start | bytes 4718596
  37.5 14.5 %collective-permute-start = (bf16[384,2048]{1,0:T(8,128)(2,1)}, bf16[384,2048]{1,0:T(8,128)(2,1)}, u32[]{:S(2)}, u32[]{:S(2)}) collective-permute-start(bf16[384,2048]{1,0:T(8,128)(2,1)} %get-tuple-element.302), channel_id=1, source_target_pairs={{0,2},{2,0},{1,3},{3,1},{4,6},{6,4},{5,7},{7,5},{8,10},{10,8},{9,1... | collective-permute-start | bytes 4718600 | tf_op jit(solution)/shard_map/ppermute | solution.py:394
  37.9 7.7 %copy-start.46 = (s32[2,1,3]{2,1,0:T(1,128)S(1)}, s32[2,1,3]{2,1,0:T(1,128)}, u32[]{:S(2)}) copy-start(s32[2,1,3]{2,1,0:T(1,128)} %param.16) | copy-start | bytes 76
  37.9 8.1 %copy-start.41 = (s32[2,1,768]{2,1,0:T(1,128)S(1)}, s32[2,1,768]{2,1,0:T(1,128)}, u32[]{:S(2)}) copy-start(s32[2,1,768]{2,1,0:T(1,128)} %param.17) | copy-start | bytes 18436
  37.9 33.0 %collective-permute-start.1 = (bf16[384,2048]{1,0:T(8,128)(2,1)}, bf16[384,2048]{1,0:T(8,128)(2,1)}, u32[]{:S(2)}, u32[]{:S(2)}) collective-permute-start(bf16[384,2048]{1,0:T(8,128)(2,1)} %get-tuple-element.301), channel_id=1, source_target_pairs={{0,2},{2,0},{1,3},{3,1},{4,6},{6,4},{5,7},{7,5},{8,10},{10,8},{9,1... | collective-permute-start | bytes 4718600 | tf_op jit(solution)/shard_map/ppermute | solution.py:394
  38.0 52.9 %all-to-all-start = ((bf16[8,2,56,1024]{3,2,1,0:T(8,128)(2,1)}), bf16[8,2,56,1024]{3,2,1,0:T(8,128)(2,1)}, u32[]{:S(2)}, u32[]{:S(2)}) async-start(bf16[8,2,56,1024]{3,2,1,0:T(8,128)(2,1)} %pad_maximum_fusion), calls=%async_computation | async-start | bytes 3670016 | tf_op jit(solution)/shard_map/all_to_all | solution.py:384
  46.4 22.3 %copy-start.44 = (pred[448]{0:T(512)(128)(4,1)}, pred[448]{0:T(512)(128)(4,1)S(1)}, u32[]{:S(2)}) copy-start(pred[448]{0:T(512)(128)(4,1)S(1)} %get-tuple-element.364) | copy-start | bytes 1348
  70.9 12.6 %copy-start.37 = (f32[384,128]{1,0:T(8,128)S(1)}, f32[384,128]{1,0:T(8,128)}, u32[]{:S(2)}) copy-start(f32[384,128]{1,0:T(8,128)} %get-tuple-element.125) | copy-start | bytes 589828
  90.9 28.8 %all-to-all-start.1 = ((bf16[8,56,1024]{2,1,0:T(8,128)(2,1)}), bf16[8,56,1024]{2,1,0:T(8,128)(2,1)}, u32[]{:S(2)}, u32[]{:S(2)}) async-start(bf16[8,56,1024]{2,1,0:T(8,128)(2,1)} %bitcast.143), calls=%async_computation.1 | async-start | bytes 1835008 | tf_op jit(solution)/shard_map/all_to_all | solution.py:483
  119.7 28.1 %all-to-all-start.2 = ((bf16[8,56,1024]{2,1,0:T(8,128)(2,1)}), bf16[8,56,1024]{2,1,0:T(8,128)(2,1)}, u32[]{:S(2)}, u32[]{:S(2)}) async-start(bf16[8,56,1024]{2,1,0:T(8,128)(2,1)} %bitcast.144), calls=%async_computation.2 | async-start | bytes 1835008 | tf_op jit(solution)/shard_map/all_to_all | solution.py:483
  147.8 47.6 %all-to-all-start.3 = ((bf16[8,112,1024]{2,1,0:T(8,128)(2,1)}), bf16[8,112,1024]{2,1,0:T(8,128)(2,1)}, u32[]{:S(2)}, u32[]{:S(2)}) async-start(bf16[8,112,1024]{2,1,0:T(8,128)(2,1)} %get-tuple-element.151), calls=%async_computation.3 | async-start | bytes 3670016 | tf_op jit(solution)/shard_map/all_to_all | solution.py:506
  153.8 143.3 %reduce-scatter.3.cloned.1.call-start = ((), (), s32[]{:S(2)}) async-start(), calls=%async_computation.8 | async-start | bytes 10485760 | tf_op jit(solution)/shard_map/reduce_scatter | solution.py:513
  195.5 49.3 %all-to-all-start.4 = ((bf16[8,112,1024]{2,1,0:T(8,128)(2,1)}), bf16[8,112,1024]{2,1,0:T(8,128)(2,1)}, u32[]{:S(2)}, u32[]{:S(2)}) async-start(bf16[8,112,1024]{2,1,0:T(8,128)(2,1)} %get-tuple-element.164), calls=%async_computation.4 | async-start | bytes 3670016 | tf_op jit(solution)/shard_map/all_to_all | solution.py:506
  199.8 200.9 %reduce-scatter.5.cloned.1.call-start = ((), (), s32[]{:S(2)}) async-start(), calls=%async_computation.9 | async-start | bytes 10485760 | tf_op jit(solution)/shard_map/reduce_scatter | solution.py:574
  199.9 4.6 %copy-start.25 = (bf16[896,384]{1,0:T(8,128)(2,1)S(1)}, bf16[896,384]{1,0:T(8,128)(2,1)}, u32[]{:S(2)}) copy-start(bf16[896,384]{1,0:T(8,128)(2,1)} %fusion.26) | copy-start | bytes 2064388
  256.8 18.6 %copy-start.31 = (bf16[384,1024]{1,0:T(8,128)(2,1)S(1)}, bf16[384,1024]{1,0:T(8,128)(2,1)}, u32[]{:S(2)}) copy-start(bf16[384,1024]{1,0:T(8,128)(2,1)} %copy-done.30) | copy-start | bytes 2359300
  256.8 18.6 %copy-start.35 = (bf16[384,1024]{1,0:T(8,128)(2,1)S(1)}, bf16[384,1024]{1,0:T(8,128)(2,1)}, u32[]{:S(2)}) copy-start(bf16[384,1024]{1,0:T(8,128)(2,1)} %copy-done.34) | copy-start | bytes 2359300
  274.8 4.0 collective-permute-start.3
  274.9 6.0 %collective-permute-start.2 = (bf16[2,384,1024]{2,1,0:T(8,128)(2,1)}, bf16[2,384,1024]{2,1,0:T(8,128)(2,1)}, u32[]{:S(2)}, u32[]{:S(2)}) collective-permute-start(bf16[2,384,1024]{2,1,0:T(8,128)(2,1)} %get-tuple-element.167), channel_id=1, source_target_pairs={{0,2},{2,0},{1,3},{3,1},{4,6},{6,4},{5,7},{7,5},{8,10},{10,8},{9,1... | collective-permute-start | bytes 4718600 | tf_op jit(solution)/shard_map/ppermute | solution.py:540
  278.8 15.8 %collective-permute-start.4 = (bf16[512,1024]{1,0:T(8,128)(2,1)S(1)}, bf16[512,1024]{1,0:T(8,128)(2,1)}, u32[]{:S(2)}, u32[]{:S(2)}) collective-permute-start(bf16[512,1024]{1,0:T(8,128)(2,1)S(1)} %get-tuple-element.180), channel_id=1, source_target_pairs={{0,2},{2,0},{1,3},{3,1},{4,6},{6,4},{5,7},{7,5},{8,10},{10,8},{9,1... | collective-permute-start | bytes 3145736 | tf_op jit(solution)/shard_map/ppermute | solution.py:298
  297.1 3.8 copy-start.29
  297.2 3.8 collective-permute-start.7
  297.3 7.9 %collective-permute-start.5 = (bf16[512,1536]{1,0:T(8,128)(2,1)}, bf16[512,1536]{1,0:T(8,128)(2,1)}, u32[]{:S(2)}, u32[]{:S(2)}) collective-permute-start(bf16[512,1536]{1,0:T(8,128)(2,1)} %get-tuple-element.182), channel_id=1, source_target_pairs={{0,2},{2,0},{1,3},{3,1},{4,6},{6,4},{5,7},{7,5},{8,10},{10,8},{9,1... | collective-permute-start | bytes 4718600 | tf_op jit(solution)/shard_map/ppermute | solution.py:298
  302.8 19.8 %collective-permute-start.8 = (bf16[256,1536]{1,0:T(8,128)(2,1)S(1)}, bf16[256,1536]{1,0:T(8,128)(2,1)S(1)}, u32[]{:S(2)}, u32[]{:S(2)}) collective-permute-start(bf16[256,1536]{1,0:T(8,128)(2,1)S(1)} %constant_dynamic-slice_fusion.7), channel_id=1, source_target_pairs={{0,8},{4,12},{8,0},{12,4},{16,24},{20,28},{24,16},{28,20},{1,9},{5... | collective-permute-start | bytes 2359304 | tf_op jit(solution)/shard_map/ppermute | solution.py:298
  307.5 19.1 %collective-permute-start.6 = (bf16[256,1536]{1,0:T(8,128)(2,1)S(1)}, bf16[256,1536]{1,0:T(8,128)(2,1)S(1)}, u32[]{:S(2)}, u32[]{:S(2)}) collective-permute-start(bf16[256,1536]{1,0:T(8,128)(2,1)S(1)} %constant_dynamic-slice_fusion.8), channel_id=1, source_target_pairs={{0,4},{4,0},{8,12},{12,8},{16,20},{20,16},{24,28},{28,24},{1,5},{5... | collective-permute-start | bytes 2359304 | tf_op jit(solution)/shard_map/ppermute | solution.py:298
  309.0 13.9 %collective-permute-start.9 = (bf16[256,1024]{1,0:T(8,128)(2,1)S(1)}, bf16[256,1024]{1,0:T(8,128)(2,1)S(1)}, u32[]{:S(2)}, u32[]{:S(2)}) collective-permute-start(bf16[256,1024]{1,0:T(8,128)(2,1)S(1)} %constant_dynamic-slice_fusion.6), channel_id=1, source_target_pairs={{0,1},{1,0},{2,3},{3,2},{4,5},{5,4},{6,7},{7,6},{8,9},{9,8},{10,11... | collective-permute-start | bytes 1572872 | tf_op jit(solution)/shard_map/ppermute | solution.py:298
  322.6 10.1 %copy-start.47 = (bf16[768,3072]{1,0:T(8,128)(2,1)S(1)}, bf16[768,3072]{1,0:T(8,128)(2,1)}, u32[]{:S(2)}) copy-start(bf16[768,3072]{1,0:T(8,128)(2,1)} %get-tuple-element.190) | copy-start | bytes 14155780
  322.9 6.2 %copy-start.20 = (bf16[256,1536]{1,0:T(8,128)(2,1)}, bf16[256,1536]{1,0:T(8,128)(2,1)S(1)}, u32[]{:S(2)}) copy-start(bf16[256,1536]{1,0:T(8,128)(2,1)S(1)} %dynamic-slice_add_fusion) | copy-start | bytes 2359300
  326.9 4.4 copy-start.22
  326.9 5.8 %copy-start.4 = (bf16[2,1,384,1024]{3,2,1,0:T(8,128)(2,1)S(1)}, bf16[2,1,384,1024]{3,2,1,0:T(8,128)(2,1)}, u32[]{:S(2)}) copy-start(bf16[2,1,384,1024]{3,2,1,0:T(8,128)(2,1)} %param.14) | copy-start | bytes 4718596
  327.7 20.0 %collective-permute-start.10 = (bf16[128,1536]{1,0:T(8,128)(2,1)}, bf16[128,1536]{1,0:T(8,128)(2,1)}, u32[]{:S(2)}, u32[]{:S(2)}) collective-permute-start(bf16[128,1536]{1,0:T(8,128)(2,1)} %constant_dynamic-slice_fusion.5), channel_id=1, source_target_pairs={{0,1},{1,0},{2,3},{3,2},{4,5},{5,4},{6,7},{7,6},{8,9},{9,8},{10,11... | collective-permute-start | bytes 1179656 | tf_op jit(solution)/shard_map/ppermute | solution.py:298
  329.8 19.0 %collective-permute-start.11 = (bf16[128,1536]{1,0:T(8,128)(2,1)}, bf16[128,1536]{1,0:T(8,128)(2,1)S(1)}, u32[]{:S(2)}, u32[]{:S(2)}) collective-permute-start(bf16[128,1536]{1,0:T(8,128)(2,1)} %constant_dynamic-slice_fusion.4), channel_id=1, source_target_pairs={{0,4},{4,0},{8,12},{12,8},{16,20},{20,16},{24,28},{28,24},{1,5},{5... | collective-permute-start | bytes 1179656 | tf_op jit(solution)/shard_map/ppermute | solution.py:298
  331.3 10.0 %copy-start.11 = (f32[384,1024]{1,0:T(8,128)S(1)}, f32[384,1024]{1,0:T(8,128)}, u32[]{:S(2)}) copy-start(f32[384,1024]{1,0:T(8,128)} %get-tuple-element.294) | copy-start | bytes 4718596
  331.3 10.0 %copy-start.12 = (f32[384,1024]{1,0:T(8,128)S(1)}, f32[384,1024]{1,0:T(8,128)}, u32[]{:S(2)}) copy-start(f32[384,1024]{1,0:T(8,128)} %get-tuple-element.296) | copy-start | bytes 4718596
  331.3 14.9 %collective-permute-start.12 = (bf16[128,1024]{1,0:T(8,128)(2,1)S(1)}, bf16[128,1024]{1,0:T(8,128)(2,1)}, u32[]{:S(2)}, u32[]{:S(2)}) collective-permute-start(bf16[128,1024]{1,0:T(8,128)(2,1)S(1)} %constant_dynamic-slice_fusion.3), channel_id=1, source_target_pairs={{0,8},{4,12},{8,0},{12,4},{16,24},{20,28},{24,16},{28,20},{1,9},{5... | collective-permute-start | bytes 786440 | tf_op jit(solution)/shard_map/ppermute | solution.py:298
  341.3 6.4 %copy-start.23 = (bf16[256,1536]{1,0:T(8,128)(2,1)S(1)}, bf16[256,1536]{1,0:T(8,128)(2,1)}, u32[]{:S(2)}) copy-start(bf16[256,1536]{1,0:T(8,128)(2,1)} %copy-done.22) | copy-start | bytes 2359300
  344.2 4.6 %copy-start.21 = (bf16[256,1536]{1,0:T(8,128)(2,1)S(1)}, bf16[256,1536]{1,0:T(8,128)(2,1)}, u32[]{:S(2)}) copy-start(bf16[256,1536]{1,0:T(8,128)(2,1)} %copy-done.20) | copy-start | bytes 2359300
  348.9 8.3 %collective-permute-start.13 = (bf16[64,1536]{1,0:T(8,128)(2,1)S(1)}, bf16[64,1536]{1,0:T(8,128)(2,1)S(1)}, u32[]{:S(2)}, u32[]{:S(2)}) collective-permute-start(bf16[64,1536]{1,0:T(8,128)(2,1)S(1)} %constant_dynamic-slice_fusion.2), channel_id=1, source_target_pairs={{0,8},{4,12},{8,0},{12,4},{16,24},{20,28},{24,16},{28,20},{1,9},{5... | collective-permute-start | bytes 589832 | tf_op jit(solution)/shard_map/ppermute | solution.py:298
  350.5 6.5 %collective-permute-start.15 = (bf16[64,1024]{1,0:T(8,128)(2,1)S(1)}, bf16[64,1024]{1,0:T(8,128)(2,1)S(1)}, u32[]{:S(2)}, u32[]{:S(2)}) collective-permute-start(bf16[64,1024]{1,0:T(8,128)(2,1)S(1)} %constant_dynamic-slice_fusion), channel_id=1, source_target_pairs={{0,16},{4,20},{8,24},{12,28},{16,0},{20,4},{24,8},{28,12},{1,17},{... | collective-permute-start | bytes 393224 | tf_op jit(solution)/shard_map/ppermute | solution.py:298
  353.0 11.0 %collective-permute-start.14 = (bf16[64,1536]{1,0:T(8,128)(2,1)S(1)}, bf16[64,1536]{1,0:T(8,128)(2,1)S(1)}, u32[]{:S(2)}, u32[]{:S(2)}) collective-permute-start(bf16[64,1536]{1,0:T(8,128)(2,1)S(1)} %constant_dynamic-slice_fusion.1), channel_id=1, source_target_pairs={{0,1},{1,0},{2,3},{3,2},{4,5},{5,4},{6,7},{7,6},{8,9},{9,8},{10,11... | collective-permute-start | bytes 589832 | tf_op jit(solution)/shard_map/ppermute | solution.py:298
  364.1 13.2 %collective-permute-start.16 = (bf16[64,1536]{1,0:T(8,128)(2,1)S(1)}, bf16[64,1536]{1,0:T(8,128)(2,1)S(1)}, u32[]{:S(2)}, u32[]{:S(2)}) collective-permute-start(bf16[64,1536]{1,0:T(8,128)(2,1)S(1)} %dynamic-slice_add_fusion.7), channel_id=1, source_target_pairs={{0,16},{4,20},{8,24},{12,28},{16,0},{20,4},{24,8},{28,12},{1,17},{... | collective-permute-start | bytes 589832 | tf_op jit(solution)/shard_map/ppermute | solution.py:298
  364.7 16.7 %collective-permute-start.17 = (bf16[64,1536]{1,0:T(8,128)(2,1)S(1)}, bf16[64,1536]{1,0:T(8,128)(2,1)S(1)}, u32[]{:S(2)}, u32[]{:S(2)}) collective-permute-start(bf16[64,1536]{1,0:T(8,128)(2,1)S(1)} %dynamic-slice_add_fusion.6), channel_id=1, source_target_pairs={{0,16},{4,20},{8,24},{12,28},{16,0},{20,4},{24,8},{28,12},{1,17},{... | collective-permute-start | bytes 589832 | tf_op jit(solution)/shard_map/ppermute | solution.py:298
  367.1 9.5 %collective-permute-start.18 = (bf16[64,1024]{1,0:T(8,128)(2,1)S(1)}, bf16[64,1024]{1,0:T(8,128)(2,1)S(1)}, u32[]{:S(2)}, u32[]{:S(2)}) collective-permute-start(bf16[64,1024]{1,0:T(8,128)(2,1)S(1)} %dynamic-slice_add_fusion.8), channel_id=1, source_target_pairs={{0,4},{4,0},{8,12},{12,8},{16,20},{20,16},{24,28},{28,24},{1,5},{5... | collective-permute-start | bytes 393224 | tf_op jit(solution)/shard_map/ppermute | solution.py:298
  368.6 1.3 collective-permute-start.25
  369.8 6.1 %collective-permute-start.26 = (f32[12,1024]{1,0:T(8,128)S(1)}, f32[12,1024]{1,0:T(8,128)S(1)}, u32[]{:S(2)}, u32[]{:S(2)}) collective-permute-start(f32[12,1024]{1,0:T(8,128)S(1)} %add.428), channel_id=1, source_target_pairs={{0,1},{1,0},{2,3},{3,2},{4,5},{5,4},{6,7},{7,6},{8,9},{9,8},{10,11... | collective-permute-start | bytes 147464 | tf_op jit(solution)/shard_map/ppermute | solution.py:298
  376.0 5.5 %collective-permute-start.27 = (f32[12,1024]{1,0:T(8,128)S(1)}, f32[12,1024]{1,0:T(8,128)S(1)}, u32[]{:S(2)}, u32[]{:S(2)}) collective-permute-start(f32[12,1024]{1,0:T(8,128)S(1)} %add.429), channel_id=1, source_target_pairs={{0,4},{4,0},{8,12},{12,8},{16,20},{20,16},{24,28},{28,24},{1,5},{5... | collective-permute-start | bytes 147464 | tf_op jit(solution)/shard_map/ppermute | solution.py:298
  381.4 14.2 %collective-permute-start.21 = (bf16[64,1024]{1,0:T(8,128)(2,1)S(1)}, bf16[64,1024]{1,0:T(8,128)(2,1)S(1)}, u32[]{:S(2)}, u32[]{:S(2)}) collective-permute-start(bf16[64,1024]{1,0:T(8,128)(2,1)S(1)} %add.427), channel_id=1, source_target_pairs={{0,16},{4,20},{8,24},{12,28},{16,0},{20,4},{24,8},{28,12},{1,17},{... | collective-permute-start | bytes 393224 | tf_op jit(solution)/shard_map/ppermute | solution.py:298
  381.5 7.0 %collective-permute-start.28 = (f32[12,1024]{1,0:T(8,128)S(1)}, f32[12,1024]{1,0:T(8,128)S(1)}, u32[]{:S(2)}, u32[]{:S(2)}) collective-permute-start(f32[12,1024]{1,0:T(8,128)S(1)} %add.430), channel_id=1, source_target_pairs={{0,8},{4,12},{8,0},{12,4},{16,24},{20,28},{24,16},{28,20},{1,9},{5... | collective-permute-start | bytes 147464 | tf_op jit(solution)/shard_map/ppermute | solution.py:298
  388.5 5.6 %collective-permute-start.29 = (f32[12,1024]{1,0:T(8,128)S(1)}, f32[12,1024]{1,0:T(8,128)S(1)}, u32[]{:S(2)}, u32[]{:S(2)}) collective-permute-start(f32[12,1024]{1,0:T(8,128)S(1)} %add.431), channel_id=1, source_target_pairs={{0,16},{4,20},{8,24},{12,28},{16,0},{20,4},{24,8},{28,12},{1,17},{... | collective-permute-start | bytes 147464 | tf_op jit(solution)/shard_map/ppermute | solution.py:298
  394.1 5.7 %collective-permute-start.19 = (bf16[64,1536]{1,0:T(8,128)(2,1)S(1)}, bf16[64,1536]{1,0:T(8,128)(2,1)S(1)}, u32[]{:S(2)}, u32[]{:S(2)}) collective-permute-start(bf16[64,1536]{1,0:T(8,128)(2,1)S(1)} %add.425), channel_id=1, source_target_pairs={{0,8},{4,12},{8,0},{12,4},{16,24},{20,28},{24,16},{28,20},{1,9},{5... | collective-permute-start | bytes 589832 | tf_op jit(solution)/shard_map/ppermute | solution.py:298
  394.2 5.7 %collective-permute-start.20 = (bf16[64,1536]{1,0:T(8,128)(2,1)S(1)}, bf16[64,1536]{1,0:T(8,128)(2,1)S(1)}, u32[]{:S(2)}, u32[]{:S(2)}) collective-permute-start(bf16[64,1536]{1,0:T(8,128)(2,1)S(1)} %add.426), channel_id=1, source_target_pairs={{0,1},{1,0},{2,3},{3,2},{4,5},{5,4},{6,7},{7,6},{8,9},{9,8},{10,11... | collective-permute-start | bytes 589832 | tf_op jit(solution)/shard_map/ppermute | solution.py:298
  400.8 13.2 %collective-permute-start.22 = (bf16[128,1536]{1,0:T(8,128)(2,1)S(1)}, bf16[128,1536]{1,0:T(8,128)(2,1)S(1)}, u32[]{:S(2)}, u32[]{:S(2)}) collective-permute-start(bf16[128,1536]{1,0:T(8,128)(2,1)S(1)} %pad_maximum_fusion.7), channel_id=1, source_target_pairs={{0,1},{1,0},{2,3},{3,2},{4,5},{5,4},{6,7},{7,6},{8,9},{9,8},{10,11... | collective-permute-start | bytes 1179656 | tf_op jit(solution)/shard_map/ppermute | solution.py:298
  402.1 12.0 %collective-permute-start.23 = (bf16[128,1536]{1,0:T(8,128)(2,1)}, bf16[128,1536]{1,0:T(8,128)(2,1)S(1)}, u32[]{:S(2)}, u32[]{:S(2)}) collective-permute-start(bf16[128,1536]{1,0:T(8,128)(2,1)} %pad_maximum_fusion.8), channel_id=1, source_target_pairs={{0,4},{4,0},{8,12},{12,8},{16,20},{20,16},{24,28},{28,24},{1,5},{5... | collective-permute-start | bytes 1179656 | tf_op jit(solution)/shard_map/ppermute | solution.py:298
  403.5 10.3 %collective-permute-start.24 = (bf16[128,1024]{1,0:T(8,128)(2,1)S(1)}, bf16[128,1024]{1,0:T(8,128)(2,1)S(1)}, u32[]{:S(2)}, u32[]{:S(2)}) collective-permute-start(bf16[128,1024]{1,0:T(8,128)(2,1)S(1)} %pad_maximum_fusion.9), channel_id=1, source_target_pairs={{0,8},{4,12},{8,0},{12,4},{16,24},{20,28},{24,16},{28,20},{1,9},{5... | collective-permute-start | bytes 786440 | tf_op jit(solution)/shard_map/ppermute | solution.py:298
  415.2 9.2 %collective-permute-start.32 = (bf16[256,1024]{1,0:T(8,128)(2,1)S(1)}, bf16[256,1024]{1,0:T(8,128)(2,1)S(1)}, u32[]{:S(2)}, u32[]{:S(2)}) collective-permute-start(bf16[256,1024]{1,0:T(8,128)(2,1)S(1)} %pad_maximum_fusion.6), channel_id=1, source_target_pairs={{0,1},{1,0},{2,3},{3,2},{4,5},{5,4},{6,7},{7,6},{8,9},{9,8},{10,11... | collective-permute-start | bytes 1572872 | tf_op jit(solution)/shard_map/ppermute | solution.py:298
  416.0 12.0 %collective-permute-start.30 = (bf16[256,1536]{1,0:T(8,128)(2,1)S(1)}, bf16[256,1536]{1,0:T(8,128)(2,1)S(1)}, u32[]{:S(2)}, u32[]{:S(2)}) collective-permute-start(bf16[256,1536]{1,0:T(8,128)(2,1)S(1)} %pad_maximum_fusion.4), channel_id=1, source_target_pairs={{0,4},{4,0},{8,12},{12,8},{16,20},{20,16},{24,28},{28,24},{1,5},{5... | collective-permute-start | bytes 2359304 | tf_op jit(solution)/shard_map/ppermute | solution.py:298
  416.5 12.0 %collective-permute-start.31 = (bf16[256,1536]{1,0:T(8,128)(2,1)S(1)}, bf16[256,1536]{1,0:T(8,128)(2,1)S(1)}, u32[]{:S(2)}, u32[]{:S(2)}) collective-permute-start(bf16[256,1536]{1,0:T(8,128)(2,1)S(1)} %pad_maximum_fusion.5), channel_id=1, source_target_pairs={{0,8},{4,12},{8,0},{12,4},{16,24},{20,28},{24,16},{28,20},{1,9},{5... | collective-permute-start | bytes 2359304 | tf_op jit(solution)/shard_map/ppermute | solution.py:298
  424.6 5.8 %copy-start.15 = (bf16[512,1024]{1,0:T(8,128)(2,1)}, bf16[512,1024]{1,0:T(8,128)(2,1)S(1)}, u32[]{:S(2)}) copy-start(bf16[512,1024]{1,0:T(8,128)(2,1)S(1)} %pad_maximum_fusion.3.refs_0_) | copy-start | bytes 3145732
  429.9 10.3 %collective-permute-start.33 = (bf16[512,1536]{1,0:T(8,128)(2,1)S(1)}, bf16[512,1536]{1,0:T(8,128)(2,1)}, u32[]{:S(2)}, u32[]{:S(2)}) collective-permute-start(bf16[512,1536]{1,0:T(8,128)(2,1)S(1)} %pad_maximum_fusion.1.refs_0_), channel_id=1, source_target_pairs={{0,2},{2,0},{1,3},{3,1},{4,6},{6,4},{5,7},{7,5},{8,10},{10,8},{9,1... | collective-permute-start | bytes 4718600 | tf_op jit(solution)/shard_map/ppermute | solution.py:298
  429.9 10.3 %collective-permute-start.34 = (bf16[512,1536]{1,0:T(8,128)(2,1)}, bf16[512,1536]{1,0:T(8,128)(2,1)}, u32[]{:S(2)}, u32[]{:S(2)}) collective-permute-start(bf16[512,1536]{1,0:T(8,128)(2,1)} %pad_maximum_fusion.2.refs_1_), channel_id=1, source_target_pairs={{0,2},{2,0},{1,3},{3,1},{4,6},{6,4},{5,7},{7,5},{8,10},{10,8},{9,1... | collective-permute-start | bytes 4718600 | tf_op jit(solution)/shard_map/ppermute | solution.py:298
  430.4 9.7 %collective-permute-start.35 = (bf16[512,1024]{1,0:T(8,128)(2,1)S(1)}, bf16[512,1024]{1,0:T(8,128)(2,1)}, u32[]{:S(2)}, u32[]{:S(2)}) collective-permute-start(bf16[512,1024]{1,0:T(8,128)(2,1)S(1)} %pad_maximum_fusion.3.refs_0_), channel_id=1, source_target_pairs={{0,2},{2,0},{1,3},{3,1},{4,6},{6,4},{5,7},{7,5},{8,10},{10,8},{9,1... | collective-permute-start | bytes 3145736 | tf_op jit(solution)/shard_map/ppermute | solution.py:298
  442.9 4.4 copy-start.1
  (28 other events, 53.4 us)
Sparse Core Ops, SparseCore 0:
  12.2 108.6 all-gather.1
  195.6 70.6 reduce-scatter.2
  297.3 86.9 reduce-scatter.4

commit v6 on v5

--- a/solution.py
+++ b/solution.py
@@ -241,22 +241,25 @@
         cost_estimate=pl.CostEstimate(flops=6*rows*D*D,transcendentals=0,bytes_accessed=rows*D*16+6*D*D),
         name="project_grads")(high,*args)
 
-def widen_body(count, high_ref, *refs):
-    out_ref=refs[-1]; start=0
-    for r in refs[:count]:
-        out_ref[:,start:start+r.shape[1]]=r[...].astype(f32); start+=r.shape[1]
-
-def widen(values, high, prev=None):
-    half=values[0].shape[0]; rb=half if len(values)==1 else half//2; per=half//rb; width=sum(v.shape[1] for v in values); count=len(values)
-    ex=[] if prev is None else [prev]
-    return pl.pallas_call(partial(widen_body,count),
-        grid_spec=pltpu.PrefetchScalarGridSpec(num_scalar_prefetch=1,grid=(per,),
-            in_specs=[pl.BlockSpec((rb,v.shape[1]),lambda i,h:(i,0)) for v in values]+[pl.BlockSpec(memory_space=pl.ANY)]*len(ex),
-            out_specs=pl.BlockSpec((rb,width),lambda i,h:(h[0]*per+i,0))),
-        out_shape=jax.ShapeDtypeStruct((2*half,width),f32),
-        input_output_aliases={} if prev is None else {1+count:0},
-        cost_estimate=pl.CostEstimate(flops=half*width,transcendentals=0,bytes_accessed=half*width*6),
-        name="widen")(high,*values,*ex)
+def widen_body(counts, high_ref, *refs):
+    outs=refs[len(refs)-len(counts):]; at=0
+    for out_ref,count in zip(outs,counts):
+        start=0
+        for r in refs[at:at+count]:
+            out_ref[:,start:start+r.shape[1]]=r[...].astype(f32); start+=r.shape[1]
+        at+=count
+
+def widen(groups, high, prev=()):
+    half=groups[0][0].shape[0]; rb=half//2; flat=[v for g in groups for v in g]
+    widths=[sum(v.shape[1] for v in g) for g in groups]
+    return pl.pallas_call(partial(widen_body,[len(g) for g in groups]),
+        grid_spec=pltpu.PrefetchScalarGridSpec(num_scalar_prefetch=1,grid=(2,),
+            in_specs=[pl.BlockSpec((rb,v.shape[1]),lambda i,h:(i,0)) for v in flat]+[pl.BlockSpec(memory_space=pl.ANY)]*len(prev),
+            out_specs=[pl.BlockSpec((rb,w),lambda i,h:(h[0]*2+i,0)) for w in widths]),
+        out_shape=[jax.ShapeDtypeStruct((2*half,w),f32) for w in widths],
+        input_output_aliases={1+len(flat)+k:k for k in range(len(prev))},
+        cost_estimate=pl.CostEstimate(flops=half*sum(widths),transcendentals=0,bytes_accessed=half*sum(widths)*6),
+        name="widen")(high,*flat,*prev)
 
 def stack_body(in_ref, out_ref, both_ref):
     both_ref[0,0,:,:]=in_ref[...]; both_ref[1,0,:,:]=out_ref[...]
@@ -623,11 +626,9 @@
     for slot in reversed(range(1, len(near))):
         chunks = double(chunks, (near,) * 3, slot)
     arrived = [swap(chunk, *near[0]) for chunk in chunks]
-    out_sum = widen(chunks[2:], high)
-    in_sum = widen(chunks[:2], high)
+    in_sum, out_sum = widen((chunks[:2], chunks[2:]), high)
     arrived, out_sum, in_sum = lax.optimization_barrier((arrived, out_sum, in_sum))
-    out_sum = widen(arrived[2:], 1 - high, out_sum)
-    in_sum = widen(arrived[:2], 1 - high, in_sum)
+    in_sum, out_sum = widen((arrived[:2], arrived[2:]), 1 - high, (in_sum, out_sum))
     return (
         jnp.stack(outputs)[:, None],
         grad_tokens.reshape(micro, 1, rows, model),

time: 461 us -> 460 us (level)
    pallas_call x4 -> x2, Pallas kernels: 14.1 us -> 10.1 us  [widen(): pl.pallas_call(partial(widen_body, [len(g) for g in groups]), grid_spec=p...]
  transfers between devices with their start and end apart: 44 -> 44, of which waited for: 20 -> 19; matrix products, arithmetic and copies ran while one was open for 26% -> 26% of each run, Pallas kernels for 34% -> 34%
where the time goes in v6:
time: 460 us; the launch traced here: 453 us
  Pallas kernels  163 us (35%)
  waiting for transfers between devices  81.7 us (18%)
  starting transfers between devices  65.1 us (14%)
  matrix products  55.7 us (12%)
  other arithmetic  54.1 us (12%)
  local copies, waits for them, and re-layouts  18 us (4%)
  between operations  15 us (3%)
    ppermute x32, waiting for transfers between devices, swap(): lax.ppermute(values, axis, [(i, i ^ bit) for i in range(lax.axis_size(axi...  63.7 us
    pallas_call x2, Pallas kernels, expert(): pl.pallas_call(partial(exp_body, capacity), grid=(FF // fb,), in_specs=[p...  46.8 us
    pallas_call x2, Pallas kernels, attn_bwd(): pl.pallas_call(partial(bwd_body, kb), grid=(G,), in_specs=[pl.BlockSpec(b...  36 us
    ppermute x32, starting transfers between devices, swap(): lax.ppermute(values, axis, [(i, i ^ bit) for i in range(lax.axis_size(axi...  35.7 us
    pallas_call x2, Pallas kernels, attn_fwd(): pl.pallas_call(partial(fwd_body, rb), grid=(G,), in_specs=[pl.BlockSpec(b...  25.4 us
    pallas_call x1, Pallas kernels, project_grads(): pl.pallas_call(partial(project_body, count, parts, per), grid_spec=pltpu....  13.7 us
    pallas_call x1, Pallas kernels, in_grads(): pl.pallas_call(partial(in_grads_body, count), grid=(FF // fb,), in_specs=...  13.5 us
    pallas_call x1, Pallas kernels, out_grads(): pl.pallas_call(partial(out_grads_body, count), grid=(FF // fb,), in_specs...  13 us
  transfers between devices with their start and end apart: 44, of which 19 were waited for; matrix products, arithmetic and copies ran while one was open for 26% of the time, Pallas kernels for 34%

profile of v6, /device:TPU:0, one launch (start us, length us, event | category | flops | bytes accessed | tf_op | source)
XLA Modules:
  0.0 452.9 jit_solution(5111874569915895956)
XLA Ops:
  7.2 4.8 %stack.13 = bf16[2,4,256,1024]{3,2,1,0:T(8,128)(2,1)} custom-call(bf16[256,4096]{1,0:T(8,128)(2,1)} %bitcast.139, bf16[1024,1024]{1,0:T(8,128)(2,1)} %bitcast.140), custom_call_target="tpu_custom_call" | custom-call | bytes 8388608 | tf_op jit(solution)/shard_map/stack/pallas_call | solution.py:269
  15.2 1.9 convolution_convert_fusion.2
  20.1 2.2 multiply_reduce_fusion.2
  22.3 2.3 add_convert_fusion.x_ref
  24.7 9.6 %convolution_convert_fusion.q_ref.ko_ref.vo_ref = bf16[768,3072]{1,0:T(8,128)(2,1)S(1)} fusion(bf16[768,1024]{1,0:T(8,128)(2,1)S(1)} %add_convert_fusion.x_ref, bf16[1024,3072]{1,0:T(8,128)(2,1)} %param.21), kind=kOutput, calls=%fused_computation | convolution fusion | flops 4834197504 | bytes 12582912 | tf_op jit(solution)/shard_map/dot_general | solution.py:392
  34.3 2.2 fusion.88
  38.0 7.5 %all-to-all-start = ((bf16[8,2,56,1024]{3,2,1,0:T(8,128)(2,1)}), bf16[8,2,56,1024]{3,2,1,0:T(8,128)(2,1)}, u32[]{:S(2)}, u32[]{:S(2)}) async-start(bf16[8,2,56,1024]{3,2,1,0:T(8,128)(2,1)} %pad_maximum_fusion), calls=%async_computation | async-start | bytes 3670016 | tf_op jit(solution)/shard_map/all_to_all | solution.py:387
  52.0 12.8 %attn_fwd.2 = (f32[384,1024]{1,0:T(8,128)}, bf16[384,1024]{1,0:T(8,128)(2,1)}, f32[384,128]{1,0:T(8,128)}) custom-call(f32[384,768]{1,0:T(8,128)} %and_select_fusion.3.bias_ref, bf16[768,3072]{1,0:T(8,128)(2,1)} %copy-done.1, bf16[768,3072]{1,0:T(8,128)(2,1)} %copy-done.1, bf16[768,3072]{1,0:T(8,128)(2,1)} %copy-done.1, ...), custom_call_target="tpu_custom_call" | custom-call | flops 384 | bytes 384 | tf_op jit(solution)/shard_map/attn_fwd/pallas_call | solution.py:45
  64.8 2.4 fusion.92
  69.1 1.8 fusion.22
  71.0 12.6 %attn_fwd.3 = (f32[384,1024]{1,0:T(8,128)}, bf16[384,1024]{1,0:T(8,128)(2,1)}, f32[384,128]{1,0:T(8,128)}) custom-call(f32[384,768]{1,0:T(8,128)} %and_select_fusion.2.bias_ref, bf16[768,3072]{1,0:T(8,128)(2,1)} %copy-done.1, bf16[768,3072]{1,0:T(8,128)(2,1)} %copy-done.1, bf16[768,3072]{1,0:T(8,128)(2,1)} %copy-done.1, ...), custom_call_target="tpu_custom_call" | custom-call | flops 384 | bytes 384 | tf_op jit(solution)/shard_map/attn_fwd/pallas_call | solution.py:45
  86.0 2.5 fusion.94
  90.9 5.8 %all-to-all-start.1 = ((bf16[8,56,1024]{2,1,0:T(8,128)(2,1)}), bf16[8,56,1024]{2,1,0:T(8,128)(2,1)}, u32[]{:S(2)}, u32[]{:S(2)}) async-start(bf16[8,56,1024]{2,1,0:T(8,128)(2,1)} %bitcast.143), calls=%async_computation.1 | async-start | bytes 1835008 | tf_op jit(solution)/shard_map/all_to_all | solution.py:486
  96.8 3.4 fusion.19
  107.2 12.6 %all-to-all-done.1 = bf16[8,56,1024]{2,1,0:T(8,128)(2,1)} async-done(((bf16[8,56,1024]{2,1,0:T(8,128)(2,1)}), bf16[8,56,1024]{2,1,0:T(8,128)(2,1)}, u32[]{:S(2)}, u32[]{:S(2)}) %all-to-all-start.1) | async-done | bytes 917536 | tf_op jit(solution)/shard_map/all_to_all | solution.py:486
  119.8 4.6 %all-to-all-start.2 = ((bf16[8,56,1024]{2,1,0:T(8,128)(2,1)}), bf16[8,56,1024]{2,1,0:T(8,128)(2,1)}, u32[]{:S(2)}, u32[]{:S(2)}) async-start(bf16[8,56,1024]{2,1,0:T(8,128)(2,1)} %bitcast.144), calls=%async_computation.2 | async-start | bytes 1835008 | tf_op jit(solution)/shard_map/all_to_all | solution.py:486
  124.5 23.4 %expert.2 = (bf16[896,4096]{1,0:T(8,128)(2,1)}, bf16[896,4096]{1,0:T(8,128)(2,1)}, bf16[8,112,1024]{2,1,0:T(8,128)(2,1)}, bf16[448,1024]{1,0:T(8,128)(2,1)}) custom-call(bf16[448,1024]{1,0:T(8,128)(2,1)} %bitcast.18.x_ref.refs_0_, bf16[8,2,56,1024]{3,2,1,0:T(8,128)(2,1)} %all-to-all-done.g_ref, bf16[4,8,256,1024]{3,2,1,0:T(8,128)(2,1)} %bitcast.159, ...), custom_call_target="tpu_custom_call" | custom-call | flops 15032385536 | bytes 24117248 | tf_op jit(solution)/shard_map/expert/pallas_call | solution.py:154
  147.9 6.0 %all-to-all-start.3 = ((bf16[8,112,1024]{2,1,0:T(8,128)(2,1)}), bf16[8,112,1024]{2,1,0:T(8,128)(2,1)}, u32[]{:S(2)}, u32[]{:S(2)}) async-start(bf16[8,112,1024]{2,1,0:T(8,128)(2,1)} %get-tuple-element.155), calls=%async_computation.3 | async-start | bytes 3670016 | tf_op jit(solution)/shard_map/all_to_all | solution.py:509
  153.9 23.4 %expert.3 = (bf16[896,4096]{1,0:T(8,128)(2,1)}, bf16[896,4096]{1,0:T(8,128)(2,1)}, bf16[8,112,1024]{2,1,0:T(8,128)(2,1)}, bf16[448,1024]{1,0:T(8,128)(2,1)}) custom-call(bf16[448,1024]{1,0:T(8,128)(2,1)} %bitcast.25.x_ref.refs_1_, bf16[8,2,56,1024]{3,2,1,0:T(8,128)(2,1)} %all-to-all-done.g_ref, ...), custom_call_target="tpu_custom_call", output_to_operand_aliasing={{0}: (4, {}), {1}: (5, {})} | custom-call | flops 15032385536 | bytes 24117248 | tf_op jit(solution)/shard_map/expert/pallas_call | solution.py:154
  177.2 13.0 %out_grads.1 = bf16[4096,1024]{1,0:T(8,128)(2,1)} custom-call(bf16[448,1024]{1,0:T(8,128)(2,1)} %get-tuple-element.146.refs_0_, bf16[448,1024]{1,0:T(8,128)(2,1)} %get-tuple-element.152.refs_1_, bf16[896,4096]{1,0:T(8,128)(2,1)} %get-tuple-element.153.refs_2_), custom_call_target="tpu_custom_call" | custom-call | flops 7516192768 | bytes 15728640 | tf_op jit(solution)/shard_map/out_grads/pallas_call | solution.py:193
  190.3 5.2 %all-to-all-done.3 = bf16[8,112,1024]{2,1,0:T(8,128)(2,1)} async-done(((bf16[8,112,1024]{2,1,0:T(8,128)(2,1)}), bf16[8,112,1024]{2,1,0:T(8,128)(2,1)}, u32[]{:S(2)}, u32[]{:S(2)}) %all-to-all-start.3) | async-done | bytes 1835040 | tf_op jit(solution)/shard_map/all_to_all | solution.py:509
  195.5 4.3 all-to-all-start.4
  199.9 4.6 %fusion.29 = (bf16[1,384,1024]{2,1,0:T(8,128)(2,1)}, f32[384]{0:T(512)S(1)}) fusion(f32[384,1024]{1,0:T(8,128)} %copy-done.6, f32[384]{0:T(512)S(1)} %select_reduce_fusion.1, bf16[2,1,384,1024]{3,2,1,0:T(8,128)(2,1)} %param.15, bf16[896,384]{1,0:T(8,128)(2,1)} %fusion.25, bf16[896,1024]{1,0:T(8,128)(2,1)} %bitcast.26), kind=kOutput, calls=%fused_computation.82 | convolution fusion | flops 707001984 | bytes 5671936 | tf_op jit(solution)/shard_map/dot_general | solution.py:526
  204.5 3.1 fusion.96
  209.5 1.8 fusion.87
  211.3 1.9 convolution_convert_fusion.5.do_ref
  213.2 18.1 %attn_bwd.2 = (bf16[384,1024]{1,0:T(8,128)(2,1)}, bf16[2,384,1024]{2,1,0:T(8,128)(2,1)}, bf16[2,384,1024]{2,1,0:T(8,128)(2,1)}) custom-call(f32[768,384]{1,0:T(8,128)} %and_select_fusion.1.biast_ref, f32[16,384]{1,0:T(8,128)} %slice_bitcast_fusion.6.lse_ref, bf16[768,3072]{1,0:T(8,128)(2,1)} %copy-done.1, bf16[768,3072]{1,0:T(8,128)(2,1)} %copy-done.1, ...), custom_call_target="tpu_custom_call" | custom-call | flops 12079595520 | bytes 11796480 | tf_op jit(solution)/shard_map/attn_bwd/pallas_call | solution.py:98
  231.3 13.5 %in_grads.1 = bf16[4,4,256,1024]{3,2,1,0:T(8,128)(2,1)} custom-call(bf16[448,1024]{1,0:T(8,128)(2,1)} %bitcast.18.x_ref.refs_0_, bf16[448,1024]{1,0:T(8,128)(2,1)} %bitcast.25.x_ref.refs_1_, bf16[896,4096]{1,0:T(8,128)(2,1)} %get-tuple-element.163.refs_2_), custom_call_target="tpu_custom_call" | custom-call | flops 7516192768 | bytes 15728640 | tf_op jit(solution)/shard_map/in_grads/pallas_call | solution.py:176
  244.7 3.0 fusion.2
  247.8 2.6 fusion.97
  251.9 2.1 fusion.86
  254.9 1.9 convolution_convert_fusion.4.do_ref
  256.8 17.9 %attn_bwd.3 = (bf16[384,1024]{1,0:T(8,128)(2,1)}, bf16[2,384,1024]{2,1,0:T(8,128)(2,1)}, bf16[2,384,1024]{2,1,0:T(8,128)(2,1)}) custom-call(f32[768,384]{1,0:T(8,128)} %and_select_fusion.biast_ref, f32[16,384]{1,0:T(8,128)} %slice_bitcast_fusion.5.lse_ref, bf16[768,3072]{1,0:T(8,128)(2,1)} %copy-done.1, bf16[768,3072]{1,0:T(8,128)(2,1)} %copy-done.1, ...), custom_call_target="tpu_custom_call" | custom-call | flops 12079595520 | bytes 11796480 | tf_op jit(solution)/shard_map/attn_bwd/pallas_call | solution.py:98
  275.3 3.7 convolution_convert_fusion.1
  280.8 13.7 %project_grads.1 = (bf16[768,3072]{1,0:T(8,128)(2,1)}, bf16[512,1536]{1,0:T(8,128)(2,1)}, bf16[512,1536]{1,0:T(8,128)(2,1)}, bf16[512,1536]{1,0:T(8,128)(2,1)}, bf16[512,1536]{1,0:T(8,128)(2,1)}) custom-call(s32[1]{0:T(128)} %bitcast.32.high_ref, bf16[768,1024]{1,0:T(8,128)(2,1)} %copy-done.21, bf16[384,1024]{1,0:T(8,128)(2,1)} %get-tuple-element.169.refs_0_, ...), custom_call_target="tpu_custom_call" | custom-call | flops 4831838208 | bytes 18874368 | tf_op jit(solution)/shard_map/project_grads/pallas_call | solution.py:236
  294.5 2.9 add.385
  298.0 3.2 collective-permute-done.7
  301.2 2.3 add.391
  303.6 1.9 collective-permute-start.8
  305.9 2.3 add.386
  311.8 11.7 %collective-permute-done.8 = bf16[256,1536]{1,0:T(8,128)(2,1)S(1)} collective-permute-done((bf16[256,1536]{1,0:T(8,128)(2,1)S(1)}, bf16[256,1536]{1,0:T(8,128)(2,1)S(1)}, u32[]{:S(2)}, u32[]{:S(2)}) %collective-permute-start.8) | collective-permute-done | bytes 786464 | tf_op jit(solution)/shard_map/ppermute | solution.py:301
  323.9 4.0 collective-permute-done.6
  334.5 8.0 %multiply_reduce_fusion = (f32[768]{0:T(1024)S(1)}, f32[1024]{0:T(1024)S(1)}, f32[768]{0:T(1024)S(1)}, f32[1024]{0:T(1024)S(1)}, f32[768,1024]{1,0:T(8,128)S(1)}) fusion(bf16[2,1,384,1024]{3,2,1,0:T(8,128)(2,1)S(1)} %copy-done.3, f32[1024]{0:T(1024)S(1)} %copy-done.30, f32[768]{0:T(1024)S(1)} %rsqrt.28, f32[768]{0:T(1024)S(1)} %div.101, ...), kind=kOutput, calls=%fused_computation.4 | convolution fusion | flops 4839698432 | bytes 15753216 | tf_op jit(solution)/shard_map/dot_general | solution.py:595
  342.5 2.9 maximum_add_fusion
  346.9 2.2 collective-permute-done.10
  352.7 2.4 collective-permute-start.15
  356.7 2.4 collective-permute-done.15
  359.6 6.5 %collective-permute-done.14 = bf16[64,1536]{1,0:T(8,128)(2,1)S(1)} collective-permute-done((bf16[64,1536]{1,0:T(8,128)(2,1)S(1)}, bf16[64,1536]{1,0:T(8,128)(2,1)S(1)}, u32[]{:S(2)}, u32[]{:S(2)}) %collective-permute-start.14) | collective-permute-done | bytes 196640 | tf_op jit(solution)/shard_map/ppermute | solution.py:301
  366.8 2.4 collective-permute-start.17
  373.5 4.6 %collective-permute-done.26 = f32[12,1024]{1,0:T(8,128)S(1)} collective-permute-done((f32[12,1024]{1,0:T(8,128)S(1)}, f32[12,1024]{1,0:T(8,128)S(1)}, u32[]{:S(2)}, u32[]{:S(2)}) %collective-permute-start.26) | collective-permute-done | bytes 49184 | tf_op jit(solution)/shard_map/ppermute | solution.py:301
  379.4 4.1 collective-permute-done.17
  383.7 1.7 collective-permute-start.28
  385.3 5.5 %collective-permute-done.28 = f32[12,1024]{1,0:T(8,128)S(1)} collective-permute-done((f32[12,1024]{1,0:T(8,128)S(1)}, f32[12,1024]{1,0:T(8,128)S(1)}, u32[]{:S(2)}, u32[]{:S(2)}) %collective-permute-start.28) | collective-permute-done | bytes 49184 | tf_op jit(solution)/shard_map/ppermute | solution.py:301
  391.0 5.3 %collective-permute-done.29 = f32[12,1024]{1,0:T(8,128)S(1)} collective-permute-done((f32[12,1024]{1,0:T(8,128)S(1)}, f32[12,1024]{1,0:T(8,128)S(1)}, u32[]{:S(2)}, u32[]{:S(2)}) %collective-permute-start.29) | collective-permute-done | bytes 49184 | tf_op jit(solution)/shard_map/ppermute | solution.py:301
  398.0 4.0 collective-permute-done.19
  405.9 3.6 collective-permute-start.24
  409.5 1.7 slice_bitcast_fusion.3
  411.2 2.5 maximum_convert_fusion
  413.7 2.5 convert_element_type.227
  418.6 2.3 collective-permute-start.31
  420.9 5.8 %collective-permute-done.32 = bf16[256,1024]{1,0:T(8,128)(2,1)S(1)} collective-permute-done((bf16[256,1024]{1,0:T(8,128)(2,1)S(1)}, bf16[256,1024]{1,0:T(8,128)(2,1)S(1)}, u32[]{:S(2)}, u32[]{:S(2)}) %collective-permute-start.32) | collective-permute-done | bytes 524320 | tf_op jit(solution)/shard_map/ppermute | solution.py:301
  427.9 2.2 collective-permute-done.30
  436.0 5.0 %widen.2 = (f32[1024,3072]{1,0:T(8,128)}, f32[1024,1024]{1,0:T(8,128)}) custom-call(s32[1]{0:T(128)} %bitcast.32.high_ref, bf16[512,1536]{1,0:T(8,128)(2,1)} %pad_maximum_fusion.1.refs_0_, bf16[512,1536]{1,0:T(8,128)(2,1)} %pad_maximum_fusion.2.refs_1_, bf16[512,1024]{1,0:T(8,128)(2,1)} %pad_maximum_fusion.3.refs_2_), custom_call_target="tpu_custom_call" | custom-call | flops 2097152 | bytes 12582912 | tf_op jit(solution)/shard_map/widen/pallas_call | solution.py:255
  441.0 5.0 %widen.3 = (f32[1024,3072]{1,0:T(8,128)}, f32[1024,1024]{1,0:T(8,128)}) custom-call(s32[1]{0:T(128)S(6)} %sub.198.high_ref, bf16[512,1536]{1,0:T(8,128)(2,1)} %collective-permute-done.33.refs_0_, bf16[512,1536]{1,0:T(8,128)(2,1)} %collective-permute-done.34.refs_1_, ...), custom_call_target="tpu_custom_call", output_to_operand_aliasing={{0}: (4, {}), {1}: (5, {})} | custom-call | flops 2097152 | bytes 12582912 | tf_op jit(solution)/shard_map/widen/pallas_call | solution.py:255
  (275 shorter events, 74.8 us)
Async XLA Ops:
  7.2 57.6 %copy-start = (bf16[1024,1024]{1,0:T(8,128)(2,1)S(1)}, bf16[1024,1024]{1,0:T(8,128)(2,1)}, u32[]{:S(2)}) copy-start(bf16[1024,1024]{1,0:T(8,128)(2,1)} %param.22) | copy-start | bytes 6291460
  7.2 117.3 %all-gather.2.cloned.1.call-start = ((), (), s32[]{:S(2)}) async-start(), calls=%async_computation.7 | async-start | bytes 20971520 | tf_op jit(solution)/shard_map/all_gather | solution.py:364
  19.8 2.5 copy-start.30
  19.8 2.6 copy-start.33
  24.6 9.6 %copy-start.21 = (bf16[768,1024]{1,0:T(8,128)(2,1)}, bf16[768,1024]{1,0:T(8,128)(2,1)S(1)}, u32[]{:S(2)}) copy-start(bf16[768,1024]{1,0:T(8,128)(2,1)S(1)} %add_convert_fusion.x_ref) | copy-start | bytes 4718596
  34.3 3.2 copy-start.1
  37.5 14.5 %collective-permute-start = (bf16[384,2048]{1,0:T(8,128)(2,1)}, bf16[384,2048]{1,0:T(8,128)(2,1)}, u32[]{:S(2)}, u32[]{:S(2)}) collective-permute-start(bf16[384,2048]{1,0:T(8,128)(2,1)} %get-tuple-element.310), channel_id=1, source_target_pairs={{0,2},{2,0},{1,3},{3,1},{4,6},{6,4},{5,7},{7,5},{8,10},{10,8},{9,1... | collective-permute-start | bytes 4718600 | tf_op jit(solution)/shard_map/ppermute | solution.py:397
  37.9 7.7 %copy-start.35 = (s32[2,1,3]{2,1,0:T(1,128)S(1)}, s32[2,1,3]{2,1,0:T(1,128)}, u32[]{:S(2)}) copy-start(s32[2,1,3]{2,1,0:T(1,128)} %param.16) | copy-start | bytes 76
  37.9 8.1 %copy-start.32 = (s32[2,1,768]{2,1,0:T(1,128)S(1)}, s32[2,1,768]{2,1,0:T(1,128)}, u32[]{:S(2)}) copy-start(s32[2,1,768]{2,1,0:T(1,128)} %param.17) | copy-start | bytes 18436
  37.9 33.1 %collective-permute-start.1 = (bf16[384,2048]{1,0:T(8,128)(2,1)}, bf16[384,2048]{1,0:T(8,128)(2,1)}, u32[]{:S(2)}, u32[]{:S(2)}) collective-permute-start(bf16[384,2048]{1,0:T(8,128)(2,1)} %get-tuple-element.309), channel_id=1, source_target_pairs={{0,2},{2,0},{1,3},{3,1},{4,6},{6,4},{5,7},{7,5},{8,10},{10,8},{9,1... | collective-permute-start | bytes 4718600 | tf_op jit(solution)/shard_map/ppermute | solution.py:397
  38.0 52.9 %all-to-all-start = ((bf16[8,2,56,1024]{3,2,1,0:T(8,128)(2,1)}), bf16[8,2,56,1024]{3,2,1,0:T(8,128)(2,1)}, u32[]{:S(2)}, u32[]{:S(2)}) async-start(bf16[8,2,56,1024]{3,2,1,0:T(8,128)(2,1)} %pad_maximum_fusion), calls=%async_computation | async-start | bytes 3670016 | tf_op jit(solution)/shard_map/all_to_all | solution.py:387
  71.0 12.7 %copy-start.28 = (f32[384,128]{1,0:T(8,128)S(1)}, f32[384,128]{1,0:T(8,128)}, u32[]{:S(2)}) copy-start(f32[384,128]{1,0:T(8,128)} %get-tuple-element.129) | copy-start | bytes 589828
  90.9 28.8 %all-to-all-start.1 = ((bf16[8,56,1024]{2,1,0:T(8,128)(2,1)}), bf16[8,56,1024]{2,1,0:T(8,128)(2,1)}, u32[]{:S(2)}, u32[]{:S(2)}) async-start(bf16[8,56,1024]{2,1,0:T(8,128)(2,1)} %bitcast.143), calls=%async_computation.1 | async-start | bytes 1835008 | tf_op jit(solution)/shard_map/all_to_all | solution.py:486
  119.8 28.1 %all-to-all-start.2 = ((bf16[8,56,1024]{2,1,0:T(8,128)(2,1)}), bf16[8,56,1024]{2,1,0:T(8,128)(2,1)}, u32[]{:S(2)}, u32[]{:S(2)}) async-start(bf16[8,56,1024]{2,1,0:T(8,128)(2,1)} %bitcast.144), calls=%async_computation.2 | async-start | bytes 1835008 | tf_op jit(solution)/shard_map/all_to_all | solution.py:486
  147.9 47.6 %all-to-all-start.3 = ((bf16[8,112,1024]{2,1,0:T(8,128)(2,1)}), bf16[8,112,1024]{2,1,0:T(8,128)(2,1)}, u32[]{:S(2)}, u32[]{:S(2)}) async-start(bf16[8,112,1024]{2,1,0:T(8,128)(2,1)} %get-tuple-element.155), calls=%async_computation.3 | async-start | bytes 3670016 | tf_op jit(solution)/shard_map/all_to_all | solution.py:509
  153.8 143.5 %reduce-scatter.3.cloned.1.call-start = ((), (), s32[]{:S(2)}) async-start(), calls=%async_computation.8 | async-start | bytes 10485760 | tf_op jit(solution)/shard_map/reduce_scatter | solution.py:516
  195.5 49.2 %all-to-all-start.4 = ((bf16[8,112,1024]{2,1,0:T(8,128)(2,1)}), bf16[8,112,1024]{2,1,0:T(8,128)(2,1)}, u32[]{:S(2)}, u32[]{:S(2)}) async-start(bf16[8,112,1024]{2,1,0:T(8,128)(2,1)} %get-tuple-element.168), calls=%async_computation.4 | async-start | bytes 3670016 | tf_op jit(solution)/shard_map/all_to_all | solution.py:509
  199.8 203.1 %reduce-scatter.5.cloned.1.call-start = ((), (), s32[]{:S(2)}) async-start(), calls=%async_computation.9 | async-start | bytes 10485760 | tf_op jit(solution)/shard_map/reduce_scatter | solution.py:577
  199.9 4.6 %copy-start.19 = (bf16[896,384]{1,0:T(8,128)(2,1)S(1)}, bf16[896,384]{1,0:T(8,128)(2,1)}, u32[]{:S(2)}) copy-start(bf16[896,384]{1,0:T(8,128)(2,1)} %fusion.26) | copy-start | bytes 2064388
  204.5 3.1 copy-start.7
  244.7 3.1 copy-start.18
  247.8 2.6 copy-start.5
  274.7 5.8 %collective-permute-start.3 = (bf16[2,384,1024]{2,1,0:T(8,128)(2,1)}, bf16[2,384,1024]{2,1,0:T(8,128)(2,1)}, u32[]{:S(2)}, u32[]{:S(2)}) collective-permute-start(bf16[2,384,1024]{2,1,0:T(8,128)(2,1)} %get-tuple-element.178), channel_id=1, source_target_pairs={{0,2},{2,0},{1,3},{3,1},{4,6},{6,4},{5,7},{7,5},{8,10},{10,8},{9,1... | collective-permute-start | bytes 4718600 | tf_op jit(solution)/shard_map/ppermute | solution.py:543
  274.8 6.0 %collective-permute-start.2 = (bf16[2,384,1024]{2,1,0:T(8,128)(2,1)}, bf16[2,384,1024]{2,1,0:T(8,128)(2,1)}, u32[]{:S(2)}, u32[]{:S(2)}) collective-permute-start(bf16[2,384,1024]{2,1,0:T(8,128)(2,1)} %get-tuple-element.171), channel_id=1, source_target_pairs={{0,2},{2,0},{1,3},{3,1},{4,6},{6,4},{5,7},{7,5},{8,10},{10,8},{9,1... | collective-permute-start | bytes 4718600 | tf_op jit(solution)/shard_map/ppermute | solution.py:543
  280.5 13.9 %collective-permute-start.4 = (bf16[512,1024]{1,0:T(8,128)(2,1)}, bf16[512,1024]{1,0:T(8,128)(2,1)}, u32[]{:S(2)}, u32[]{:S(2)}) collective-permute-start(bf16[512,1024]{1,0:T(8,128)(2,1)} %get-tuple-element.184), channel_id=1, source_target_pairs={{0,2},{2,0},{1,3},{3,1},{4,6},{6,4},{5,7},{7,5},{8,10},{10,8},{9,1... | collective-permute-start | bytes 3145736 | tf_op jit(solution)/shard_map/ppermute | solution.py:301
  297.4 3.8 collective-permute-start.7
  297.7 8.2 %collective-permute-start.5 = (bf16[512,1536]{1,0:T(8,128)(2,1)}, bf16[512,1536]{1,0:T(8,128)(2,1)}, u32[]{:S(2)}, u32[]{:S(2)}) collective-permute-start(bf16[512,1536]{1,0:T(8,128)(2,1)} %get-tuple-element.186), channel_id=1, source_target_pairs={{0,2},{2,0},{1,3},{3,1},{4,6},{6,4},{5,7},{7,5},{8,10},{10,8},{9,1... | collective-permute-start | bytes 4718600 | tf_op jit(solution)/shard_map/ppermute | solution.py:301
  303.6 19.9 %collective-permute-start.8 = (bf16[256,1536]{1,0:T(8,128)(2,1)S(1)}, bf16[256,1536]{1,0:T(8,128)(2,1)S(1)}, u32[]{:S(2)}, u32[]{:S(2)}) collective-permute-start(bf16[256,1536]{1,0:T(8,128)(2,1)S(1)} %constant_dynamic-slice_fusion.7), channel_id=1, source_target_pairs={{0,8},{4,12},{8,0},{12,4},{16,24},{20,28},{24,16},{28,20},{1,9},{5... | collective-permute-start | bytes 2359304 | tf_op jit(solution)/shard_map/ppermute | solution.py:301
  305.9 4.1 copy-start.12
  308.3 3.1 copy-start.9
  308.3 19.6 %collective-permute-start.6 = (bf16[256,1536]{1,0:T(8,128)(2,1)S(1)}, bf16[256,1536]{1,0:T(8,128)(2,1)S(1)}, u32[]{:S(2)}, u32[]{:S(2)}) collective-permute-start(bf16[256,1536]{1,0:T(8,128)(2,1)S(1)} %constant_dynamic-slice_fusion.8), channel_id=1, source_target_pairs={{0,4},{4,0},{8,12},{12,8},{16,20},{20,16},{24,28},{28,24},{1,5},{5... | collective-permute-start | bytes 2359304 | tf_op jit(solution)/shard_map/ppermute | solution.py:301
  310.0 13.7 %collective-permute-start.9 = (bf16[256,1024]{1,0:T(8,128)(2,1)S(1)}, bf16[256,1024]{1,0:T(8,128)(2,1)S(1)}, u32[]{:S(2)}, u32[]{:S(2)}) collective-permute-start(bf16[256,1024]{1,0:T(8,128)(2,1)S(1)} %constant_dynamic-slice_fusion.6), channel_id=1, source_target_pairs={{0,1},{1,0},{2,3},{3,2},{4,5},{5,4},{6,7},{7,6},{8,9},{9,8},{10,11... | collective-permute-start | bytes 1572872 | tf_op jit(solution)/shard_map/ppermute | solution.py:301
  323.5 11.0 %copy-start.36 = (bf16[768,3072]{1,0:T(8,128)(2,1)S(1)}, bf16[768,3072]{1,0:T(8,128)(2,1)}, u32[]{:S(2)}) copy-start(bf16[768,3072]{1,0:T(8,128)(2,1)} %get-tuple-element.194) | copy-start | bytes 14155780
  328.1 4.2 copy-start.17
  328.1 6.4 %copy-start.3 = (bf16[2,1,384,1024]{3,2,1,0:T(8,128)(2,1)S(1)}, bf16[2,1,384,1024]{3,2,1,0:T(8,128)(2,1)}, u32[]{:S(2)}) copy-start(bf16[2,1,384,1024]{3,2,1,0:T(8,128)(2,1)} %param.14) | copy-start | bytes 4718596
  328.9 20.1 %collective-permute-start.10 = (bf16[128,1536]{1,0:T(8,128)(2,1)}, bf16[128,1536]{1,0:T(8,128)(2,1)}, u32[]{:S(2)}, u32[]{:S(2)}) collective-permute-start(bf16[128,1536]{1,0:T(8,128)(2,1)} %constant_dynamic-slice_fusion.5), channel_id=1, source_target_pairs={{0,1},{1,0},{2,3},{3,2},{4,5},{5,4},{6,7},{7,6},{8,9},{9,8},{10,11... | collective-permute-start | bytes 1179656 | tf_op jit(solution)/shard_map/ppermute | solution.py:301
  330.8 19.4 %collective-permute-start.11 = (bf16[128,1536]{1,0:T(8,128)(2,1)}, bf16[128,1536]{1,0:T(8,128)(2,1)}, u32[]{:S(2)}, u32[]{:S(2)}) collective-permute-start(bf16[128,1536]{1,0:T(8,128)(2,1)} %constant_dynamic-slice_fusion.4), channel_id=1, source_target_pairs={{0,4},{4,0},{8,12},{12,8},{16,20},{20,16},{24,28},{28,24},{1,5},{5... | collective-permute-start | bytes 1179656 | tf_op jit(solution)/shard_map/ppermute | solution.py:301
  333.0 9.5 %copy-start.10 = (f32[384,1024]{1,0:T(8,128)S(1)}, f32[384,1024]{1,0:T(8,128)}, u32[]{:S(2)}) copy-start(f32[384,1024]{1,0:T(8,128)} %get-tuple-element.302) | copy-start | bytes 4718596
  333.0 9.5 %copy-start.11 = (f32[384,1024]{1,0:T(8,128)S(1)}, f32[384,1024]{1,0:T(8,128)}, u32[]{:S(2)}) copy-start(f32[384,1024]{1,0:T(8,128)} %get-tuple-element.304) | copy-start | bytes 4718596
  333.0 12.8 %collective-permute-start.12 = (bf16[128,1024]{1,0:T(8,128)(2,1)}, bf16[128,1024]{1,0:T(8,128)(2,1)}, u32[]{:S(2)}, u32[]{:S(2)}) collective-permute-start(bf16[128,1024]{1,0:T(8,128)(2,1)} %constant_dynamic-slice_fusion.3), channel_id=1, source_target_pairs={{0,8},{4,12},{8,0},{12,4},{16,24},{20,28},{24,16},{28,20},{1,9},{5... | collective-permute-start | bytes 786440 | tf_op jit(solution)/shard_map/ppermute | solution.py:301
  351.4 8.1 %collective-permute-start.13 = (bf16[64,1536]{1,0:T(8,128)(2,1)S(1)}, bf16[64,1536]{1,0:T(8,128)(2,1)S(1)}, u32[]{:S(2)}, u32[]{:S(2)}) collective-permute-start(bf16[64,1536]{1,0:T(8,128)(2,1)S(1)} %constant_dynamic-slice_fusion.2), channel_id=1, source_target_pairs={{0,8},{4,12},{8,0},{12,4},{16,24},{20,28},{24,16},{28,20},{1,9},{5... | collective-permute-start | bytes 589832 | tf_op jit(solution)/shard_map/ppermute | solution.py:301
  352.7 6.5 %collective-permute-start.15 = (bf16[64,1024]{1,0:T(8,128)(2,1)S(1)}, bf16[64,1024]{1,0:T(8,128)(2,1)S(1)}, u32[]{:S(2)}, u32[]{:S(2)}) collective-permute-start(bf16[64,1024]{1,0:T(8,128)(2,1)S(1)} %constant_dynamic-slice_fusion), channel_id=1, source_target_pairs={{0,16},{4,20},{8,24},{12,28},{16,0},{20,4},{24,8},{28,12},{1,17},{... | collective-permute-start | bytes 393224 | tf_op jit(solution)/shard_map/ppermute | solution.py:301
  355.1 11.0 %collective-permute-start.14 = (bf16[64,1536]{1,0:T(8,128)(2,1)S(1)}, bf16[64,1536]{1,0:T(8,128)(2,1)S(1)}, u32[]{:S(2)}, u32[]{:S(2)}) collective-permute-start(bf16[64,1536]{1,0:T(8,128)(2,1)S(1)} %constant_dynamic-slice_fusion.1), channel_id=1, source_target_pairs={{0,1},{1,0},{2,3},{3,2},{4,5},{5,4},{6,7},{7,6},{8,9},{9,8},{10,11... | collective-permute-start | bytes 589832 | tf_op jit(solution)/shard_map/ppermute | solution.py:301
  366.2 13.2 %collective-permute-start.16 = (bf16[64,1536]{1,0:T(8,128)(2,1)S(1)}, bf16[64,1536]{1,0:T(8,128)(2,1)S(1)}, u32[]{:S(2)}, u32[]{:S(2)}) collective-permute-start(bf16[64,1536]{1,0:T(8,128)(2,1)S(1)} %dynamic-slice_add_fusion.7), channel_id=1, source_target_pairs={{0,16},{4,20},{8,24},{12,28},{16,0},{20,4},{24,8},{28,12},{1,17},{... | collective-permute-start | bytes 589832 | tf_op jit(solution)/shard_map/ppermute | solution.py:301
  366.8 16.7 %collective-permute-start.17 = (bf16[64,1536]{1,0:T(8,128)(2,1)S(1)}, bf16[64,1536]{1,0:T(8,128)(2,1)S(1)}, u32[]{:S(2)}, u32[]{:S(2)}) collective-permute-start(bf16[64,1536]{1,0:T(8,128)(2,1)S(1)} %dynamic-slice_add_fusion.6), channel_id=1, source_target_pairs={{0,16},{4,20},{8,24},{12,28},{16,0},{20,4},{24,8},{28,12},{1,17},{... | collective-permute-start | bytes 589832 | tf_op jit(solution)/shard_map/ppermute | solution.py:301
  369.2 9.5 %collective-permute-start.18 = (bf16[64,1024]{1,0:T(8,128)(2,1)S(1)}, bf16[64,1024]{1,0:T(8,128)(2,1)S(1)}, u32[]{:S(2)}, u32[]{:S(2)}) collective-permute-start(bf16[64,1024]{1,0:T(8,128)(2,1)S(1)} %dynamic-slice_add_fusion.8), channel_id=1, source_target_pairs={{0,4},{4,0},{8,12},{12,8},{16,20},{20,16},{24,28},{28,24},{1,5},{5... | collective-permute-start | bytes 393224 | tf_op jit(solution)/shard_map/ppermute | solution.py:301
  370.7 1.3 collective-permute-start.25
  371.9 6.1 %collective-permute-start.26 = (f32[12,1024]{1,0:T(8,128)S(1)}, f32[12,1024]{1,0:T(8,128)S(1)}, u32[]{:S(2)}, u32[]{:S(2)}) collective-permute-start(f32[12,1024]{1,0:T(8,128)S(1)} %add.428), channel_id=1, source_target_pairs={{0,1},{1,0},{2,3},{3,2},{4,5},{5,4},{6,7},{7,6},{8,9},{9,8},{10,11... | collective-permute-start | bytes 147464 | tf_op jit(solution)/shard_map/ppermute | solution.py:301
  378.1 5.6 %collective-permute-start.27 = (f32[12,1024]{1,0:T(8,128)S(1)}, f32[12,1024]{1,0:T(8,128)S(1)}, u32[]{:S(2)}, u32[]{:S(2)}) collective-permute-start(f32[12,1024]{1,0:T(8,128)S(1)} %add.429), channel_id=1, source_target_pairs={{0,4},{4,0},{8,12},{12,8},{16,20},{20,16},{24,28},{28,24},{1,5},{5... | collective-permute-start | bytes 147464 | tf_op jit(solution)/shard_map/ppermute | solution.py:301
  383.6 14.4 %collective-permute-start.21 = (bf16[64,1024]{1,0:T(8,128)(2,1)S(1)}, bf16[64,1024]{1,0:T(8,128)(2,1)S(1)}, u32[]{:S(2)}, u32[]{:S(2)}) collective-permute-start(bf16[64,1024]{1,0:T(8,128)(2,1)S(1)} %add.427), channel_id=1, source_target_pairs={{0,16},{4,20},{8,24},{12,28},{16,0},{20,4},{24,8},{28,12},{1,17},{... | collective-permute-start | bytes 393224 | tf_op jit(solution)/shard_map/ppermute | solution.py:301
  383.7 7.1 %collective-permute-start.28 = (f32[12,1024]{1,0:T(8,128)S(1)}, f32[12,1024]{1,0:T(8,128)S(1)}, u32[]{:S(2)}, u32[]{:S(2)}) collective-permute-start(f32[12,1024]{1,0:T(8,128)S(1)} %add.430), channel_id=1, source_target_pairs={{0,8},{4,12},{8,0},{12,4},{16,24},{20,28},{24,16},{28,20},{1,9},{5... | collective-permute-start | bytes 147464 | tf_op jit(solution)/shard_map/ppermute | solution.py:301
  390.8 5.5 %collective-permute-start.29 = (f32[12,1024]{1,0:T(8,128)S(1)}, f32[12,1024]{1,0:T(8,128)S(1)}, u32[]{:S(2)}, u32[]{:S(2)}) collective-permute-start(f32[12,1024]{1,0:T(8,128)S(1)} %add.431), channel_id=1, source_target_pairs={{0,16},{4,20},{8,24},{12,28},{16,0},{20,4},{24,8},{28,12},{1,17},{... | collective-permute-start | bytes 147464 | tf_op jit(solution)/shard_map/ppermute | solution.py:301
  396.3 5.7 %collective-permute-start.19 = (bf16[64,1536]{1,0:T(8,128)(2,1)S(1)}, bf16[64,1536]{1,0:T(8,128)(2,1)S(1)}, u32[]{:S(2)}, u32[]{:S(2)}) collective-permute-start(bf16[64,1536]{1,0:T(8,128)(2,1)S(1)} %add.425), channel_id=1, source_target_pairs={{0,8},{4,12},{8,0},{12,4},{16,24},{20,28},{24,16},{28,20},{1,9},{5... | collective-permute-start | bytes 589832 | tf_op jit(solution)/shard_map/ppermute | solution.py:301
  396.4 5.7 %collective-permute-start.20 = (bf16[64,1536]{1,0:T(8,128)(2,1)S(1)}, bf16[64,1536]{1,0:T(8,128)(2,1)S(1)}, u32[]{:S(2)}, u32[]{:S(2)}) collective-permute-start(bf16[64,1536]{1,0:T(8,128)(2,1)S(1)} %add.426), channel_id=1, source_target_pairs={{0,1},{1,0},{2,3},{3,2},{4,5},{5,4},{6,7},{7,6},{8,9},{9,8},{10,11... | collective-permute-start | bytes 589832 | tf_op jit(solution)/shard_map/ppermute | solution.py:301
  402.9 13.3 %collective-permute-start.22 = (bf16[128,1536]{1,0:T(8,128)(2,1)S(1)}, bf16[128,1536]{1,0:T(8,128)(2,1)S(1)}, u32[]{:S(2)}, u32[]{:S(2)}) collective-permute-start(bf16[128,1536]{1,0:T(8,128)(2,1)S(1)} %pad_maximum_fusion.7), channel_id=1, source_target_pairs={{0,1},{1,0},{2,3},{3,2},{4,5},{5,4},{6,7},{7,6},{8,9},{9,8},{10,11... | collective-permute-start | bytes 1179656 | tf_op jit(solution)/shard_map/ppermute | solution.py:301
  404.5 11.9 %collective-permute-start.23 = (bf16[128,1536]{1,0:T(8,128)(2,1)}, bf16[128,1536]{1,0:T(8,128)(2,1)S(1)}, u32[]{:S(2)}, u32[]{:S(2)}) collective-permute-start(bf16[128,1536]{1,0:T(8,128)(2,1)} %pad_maximum_fusion.8), channel_id=1, source_target_pairs={{0,4},{4,0},{8,12},{12,8},{16,20},{20,16},{24,28},{28,24},{1,5},{5... | collective-permute-start | bytes 1179656 | tf_op jit(solution)/shard_map/ppermute | solution.py:301
  405.9 10.2 %collective-permute-start.24 = (bf16[128,1024]{1,0:T(8,128)(2,1)S(1)}, bf16[128,1024]{1,0:T(8,128)(2,1)S(1)}, u32[]{:S(2)}, u32[]{:S(2)}) collective-permute-start(bf16[128,1024]{1,0:T(8,128)(2,1)S(1)} %pad_maximum_fusion.9), channel_id=1, source_target_pairs={{0,8},{4,12},{8,0},{12,4},{16,24},{20,28},{24,16},{28,20},{1,9},{5... | collective-permute-start | bytes 786440 | tf_op jit(solution)/shard_map/ppermute | solution.py:301
  411.1 2.5 copy-start.20
  417.5 9.2 %collective-permute-start.32 = (bf16[256,1024]{1,0:T(8,128)(2,1)S(1)}, bf16[256,1024]{1,0:T(8,128)(2,1)S(1)}, u32[]{:S(2)}, u32[]{:S(2)}) collective-permute-start(bf16[256,1024]{1,0:T(8,128)(2,1)S(1)} %pad_maximum_fusion.6), channel_id=1, source_target_pairs={{0,1},{1,0},{2,3},{3,2},{4,5},{5,4},{6,7},{7,6},{8,9},{9,8},{10,11... | collective-permute-start | bytes 1572872 | tf_op jit(solution)/shard_map/ppermute | solution.py:301
  418.1 12.0 %collective-permute-start.30 = (bf16[256,1536]{1,0:T(8,128)(2,1)S(1)}, bf16[256,1536]{1,0:T(8,128)(2,1)S(1)}, u32[]{:S(2)}, u32[]{:S(2)}) collective-permute-start(bf16[256,1536]{1,0:T(8,128)(2,1)S(1)} %pad_maximum_fusion.4), channel_id=1, source_target_pairs={{0,4},{4,0},{8,12},{12,8},{16,20},{20,16},{24,28},{28,24},{1,5},{5... | collective-permute-start | bytes 2359304 | tf_op jit(solution)/shard_map/ppermute | solution.py:301
  418.6 12.8 %collective-permute-start.31 = (bf16[256,1536]{1,0:T(8,128)(2,1)S(1)}, bf16[256,1536]{1,0:T(8,128)(2,1)S(1)}, u32[]{:S(2)}, u32[]{:S(2)}) collective-permute-start(bf16[256,1536]{1,0:T(8,128)(2,1)S(1)} %pad_maximum_fusion.5), channel_id=1, source_target_pairs={{0,8},{4,12},{8,0},{12,4},{16,24},{20,28},{24,16},{28,20},{1,9},{5... | collective-permute-start | bytes 2359304 | tf_op jit(solution)/shard_map/ppermute | solution.py:301
  432.8 8.2 %collective-permute-start.33 = (bf16[512,1536]{1,0:T(8,128)(2,1)}, bf16[512,1536]{1,0:T(8,128)(2,1)}, u32[]{:S(2)}, u32[]{:S(2)}) collective-permute-start(bf16[512,1536]{1,0:T(8,128)(2,1)} %pad_maximum_fusion.1.refs_0_), channel_id=1, source_target_pairs={{0,2},{2,0},{1,3},{3,1},{4,6},{6,4},{5,7},{7,5},{8,10},{10,8},{9,1... | collective-permute-start | bytes 4718600 | tf_op jit(solution)/shard_map/ppermute | solution.py:301
  432.8 8.2 %collective-permute-start.34 = (bf16[512,1536]{1,0:T(8,128)(2,1)}, bf16[512,1536]{1,0:T(8,128)(2,1)}, u32[]{:S(2)}, u32[]{:S(2)}) collective-permute-start(bf16[512,1536]{1,0:T(8,128)(2,1)} %pad_maximum_fusion.2.refs_1_), channel_id=1, source_target_pairs={{0,2},{2,0},{1,3},{3,1},{4,6},{6,4},{5,7},{7,5},{8,10},{10,8},{9,1... | collective-permute-start | bytes 4718600 | tf_op jit(solution)/shard_map/ppermute | solution.py:301
  433.3 7.7 %collective-permute-start.35 = (bf16[512,1024]{1,0:T(8,128)(2,1)}, bf16[512,1024]{1,0:T(8,128)(2,1)}, u32[]{:S(2)}, u32[]{:S(2)}) collective-permute-start(bf16[512,1024]{1,0:T(8,128)(2,1)} %pad_maximum_fusion.3.refs_2_), channel_id=1, source_target_pairs={{0,2},{2,0},{1,3},{3,1},{4,6},{6,4},{5,7},{7,5},{8,10},{10,8},{9,1... | collective-permute-start | bytes 3145736 | tf_op jit(solution)/shard_map/ppermute | solution.py:301
  (17 other events, 23.7 us)
Sparse Core Ops, SparseCore 0:
  12.2 108.6 all-gather.1
  195.6 70.7 reduce-scatter.2
  297.5 86.9 reduce-scatter.4

commit v7 on v6

--- a/solution.py
+++ b/solution.py
@@ -609,6 +609,10 @@
     )
     for slot in reversed(range(count - 1)):
         chunks = double(chunks, orders, slot)
+        if slot == 0:
+            done = (small[0], small[1], small[2], small[3], small[4:].T, jnp.stack(outputs)[:, None])
+            chunks, done = lax.optimization_barrier((tuple(chunks), done))
+            continue
         if slot == 1:
             chunks, small = lax.optimization_barrier((tuple(chunks), small))
         else:
@@ -630,15 +634,15 @@
     arrived, out_sum, in_sum = lax.optimization_barrier((arrived, out_sum, in_sum))
     in_sum, out_sum = widen((arrived[:2], arrived[2:]), 1 - high, (in_sum, out_sum))
     return (
-        jnp.stack(outputs)[:, None],
+        done[5],
         grad_tokens.reshape(micro, 1, rows, model),
-        small[0],
-        small[1],
+        done[0],
+        done[1],
         in_sum,
         out_sum,
-        small[2],
-        small[3],
-        small[4:].T,
+        done[2],
+        done[3],
+        done[4],
         grad_in[None],
         grad_out_weight[None],
     )

time: 460 us -> 460 us (level)
  transfers between devices with their start and end apart: 44 -> 44, of which waited for: 19 -> 22; matrix products, arithmetic and copies ran while one was open for 26% -> 26% of each run, Pallas kernels for 34% -> 34%
where the time goes in v7:
time: 460 us; the launch traced here: 454 us
  Pallas kernels  163 us (35%)
  waiting for transfers between devices  83.9 us (18%)
  starting transfers between devices  65.1 us (14%)
  matrix products  57.2 us (12%)
  other arithmetic  51 us (11%)
  local copies, waits for them, and re-layouts  18.5 us (4%)
  between operations  15 us (3%)
    ppermute x32, waiting for transfers between devices, swap(): lax.ppermute(values, axis, [(i, i ^ bit) for i in range(lax.axis_size(axi...  65.8 us
    pallas_call x2, Pallas kernels, expert(): pl.pallas_call(partial(exp_body, capacity), grid=(FF // fb,), in_specs=[p...  46.8 us
    pallas_call x2, Pallas kernels, attn_bwd(): pl.pallas_call(partial(bwd_body, kb), grid=(G,), in_specs=[pl.BlockSpec(b...  35.9 us
    ppermute x32, starting transfers between devices, swap(): lax.ppermute(values, axis, [(i, i ^ bit) for i in range(lax.axis_size(axi...  35.6 us
    pallas_call x2, Pallas kernels, attn_fwd(): pl.pallas_call(partial(fwd_body, rb), grid=(G,), in_specs=[pl.BlockSpec(b...  25.4 us
    pallas_call x1, Pallas kernels, project_grads(): pl.pallas_call(partial(project_body, count, parts, per), grid_spec=pltpu....  13.7 us
    pallas_call x1, Pallas kernels, in_grads(): pl.pallas_call(partial(in_grads_body, count), grid=(FF // fb,), in_specs=...  13.5 us
    pallas_call x1, Pallas kernels, out_grads(): pl.pallas_call(partial(out_grads_body, count), grid=(FF // fb,), in_specs...  13 us
  transfers between devices with their start and end apart: 44, of which 22 were waited for; matrix products, arithmetic and copies ran while one was open for 26% of the time, Pallas kernels for 34%

profile of v7, /device:TPU:0, one launch (start us, length us, event | category | flops | bytes accessed | tf_op | source)
XLA Modules:
  0.0 454.0 jit_solution(5721753021170064185)
XLA Ops:
  7.2 4.8 %stack.13 = bf16[2,4,256,1024]{3,2,1,0:T(8,128)(2,1)} custom-call(bf16[256,4096]{1,0:T(8,128)(2,1)} %bitcast.138, bf16[1024,1024]{1,0:T(8,128)(2,1)} %bitcast.139), custom_call_target="tpu_custom_call" | custom-call | bytes 8388608 | tf_op jit(solution)/shard_map/stack/pallas_call | solution.py:269
  15.2 1.9 convolution_convert_fusion.2
  20.1 2.2 multiply_reduce_fusion.2
  22.3 2.3 add_convert_fusion.x_ref
  24.7 9.6 %convolution_convert_fusion.q_ref.ko_ref.vo_ref = bf16[768,3072]{1,0:T(8,128)(2,1)S(1)} fusion(bf16[768,1024]{1,0:T(8,128)(2,1)S(1)} %add_convert_fusion.x_ref, bf16[1024,3072]{1,0:T(8,128)(2,1)} %param.21), kind=kOutput, calls=%fused_computation | convolution fusion | flops 4834197504 | bytes 12582912 | tf_op jit(solution)/shard_map/dot_general | solution.py:392
  34.3 2.2 fusion.88
  38.0 7.5 %all-to-all-start = ((bf16[8,2,56,1024]{3,2,1,0:T(8,128)(2,1)}), bf16[8,2,56,1024]{3,2,1,0:T(8,128)(2,1)}, u32[]{:S(2)}, u32[]{:S(2)}) async-start(bf16[8,2,56,1024]{3,2,1,0:T(8,128)(2,1)} %pad_maximum_fusion), calls=%async_computation | async-start | bytes 3670016 | tf_op jit(solution)/shard_map/all_to_all | solution.py:387
  52.0 12.8 %attn_fwd.2 = (f32[384,1024]{1,0:T(8,128)}, bf16[384,1024]{1,0:T(8,128)(2,1)}, f32[384,128]{1,0:T(8,128)}) custom-call(f32[384,768]{1,0:T(8,128)} %and_select_fusion.2.bias_ref, bf16[768,3072]{1,0:T(8,128)(2,1)} %copy-done.1, bf16[768,3072]{1,0:T(8,128)(2,1)} %copy-done.1, bf16[768,3072]{1,0:T(8,128)(2,1)} %copy-done.1, ...), custom_call_target="tpu_custom_call" | custom-call | flops 384 | bytes 384 | tf_op jit(solution)/shard_map/attn_fwd/pallas_call | solution.py:45
  64.8 2.4 fusion.92
  69.1 1.8 fusion.22
  71.0 12.6 %attn_fwd.3 = (f32[384,1024]{1,0:T(8,128)}, bf16[384,1024]{1,0:T(8,128)(2,1)}, f32[384,128]{1,0:T(8,128)}) custom-call(f32[384,768]{1,0:T(8,128)} %and_select_fusion.3.bias_ref, bf16[768,3072]{1,0:T(8,128)(2,1)} %copy-done.1, bf16[768,3072]{1,0:T(8,128)(2,1)} %copy-done.1, bf16[768,3072]{1,0:T(8,128)(2,1)} %copy-done.1, ...), custom_call_target="tpu_custom_call" | custom-call | flops 384 | bytes 384 | tf_op jit(solution)/shard_map/attn_fwd/pallas_call | solution.py:45
  86.0 2.5 fusion.94
  90.9 5.8 %all-to-all-start.1 = ((bf16[8,56,1024]{2,1,0:T(8,128)(2,1)}), bf16[8,56,1024]{2,1,0:T(8,128)(2,1)}, u32[]{:S(2)}, u32[]{:S(2)}) async-start(bf16[8,56,1024]{2,1,0:T(8,128)(2,1)} %bitcast.143), calls=%async_computation.1 | async-start | bytes 1835008 | tf_op jit(solution)/shard_map/all_to_all | solution.py:486
  96.8 3.5 fusion.19
  107.2 12.6 %all-to-all-done.1 = bf16[8,56,1024]{2,1,0:T(8,128)(2,1)} async-done(((bf16[8,56,1024]{2,1,0:T(8,128)(2,1)}), bf16[8,56,1024]{2,1,0:T(8,128)(2,1)}, u32[]{:S(2)}, u32[]{:S(2)}) %all-to-all-start.1) | async-done | bytes 917536 | tf_op jit(solution)/shard_map/all_to_all | solution.py:486
  119.8 4.6 %all-to-all-start.2 = ((bf16[8,56,1024]{2,1,0:T(8,128)(2,1)}), bf16[8,56,1024]{2,1,0:T(8,128)(2,1)}, u32[]{:S(2)}, u32[]{:S(2)}) async-start(bf16[8,56,1024]{2,1,0:T(8,128)(2,1)} %bitcast.144), calls=%async_computation.2 | async-start | bytes 1835008 | tf_op jit(solution)/shard_map/all_to_all | solution.py:486
  124.5 23.4 %expert.2 = (bf16[896,4096]{1,0:T(8,128)(2,1)}, bf16[896,4096]{1,0:T(8,128)(2,1)}, bf16[8,112,1024]{2,1,0:T(8,128)(2,1)}, bf16[448,1024]{1,0:T(8,128)(2,1)}) custom-call(bf16[448,1024]{1,0:T(8,128)(2,1)} %bitcast.19.x_ref.refs_0_, bf16[8,2,56,1024]{3,2,1,0:T(8,128)(2,1)} %all-to-all-done.g_ref, bf16[4,8,256,1024]{3,2,1,0:T(8,128)(2,1)} %bitcast.159, ...), custom_call_target="tpu_custom_call" | custom-call | flops 15032385536 | bytes 24117248 | tf_op jit(solution)/shard_map/expert/pallas_call | solution.py:154
  147.9 6.0 %all-to-all-start.3 = ((bf16[8,112,1024]{2,1,0:T(8,128)(2,1)}), bf16[8,112,1024]{2,1,0:T(8,128)(2,1)}, u32[]{:S(2)}, u32[]{:S(2)}) async-start(bf16[8,112,1024]{2,1,0:T(8,128)(2,1)} %get-tuple-element.160), calls=%async_computation.3 | async-start | bytes 3670016 | tf_op jit(solution)/shard_map/all_to_all | solution.py:509
  153.9 23.4 %expert.3 = (bf16[896,4096]{1,0:T(8,128)(2,1)}, bf16[896,4096]{1,0:T(8,128)(2,1)}, bf16[8,112,1024]{2,1,0:T(8,128)(2,1)}, bf16[448,1024]{1,0:T(8,128)(2,1)}) custom-call(bf16[448,1024]{1,0:T(8,128)(2,1)} %bitcast.26.x_ref.refs_1_, bf16[8,2,56,1024]{3,2,1,0:T(8,128)(2,1)} %all-to-all-done.g_ref, ...), custom_call_target="tpu_custom_call", output_to_operand_aliasing={{0}: (4, {}), {1}: (5, {})} | custom-call | flops 15032385536 | bytes 24117248 | tf_op jit(solution)/shard_map/expert/pallas_call | solution.py:154
  177.3 13.0 %out_grads.1 = bf16[4096,1024]{1,0:T(8,128)(2,1)} custom-call(bf16[448,1024]{1,0:T(8,128)(2,1)} %get-tuple-element.154.refs_0_, bf16[448,1024]{1,0:T(8,128)(2,1)} %get-tuple-element.157.refs_1_, bf16[896,4096]{1,0:T(8,128)(2,1)} %get-tuple-element.158.refs_2_), custom_call_target="tpu_custom_call" | custom-call | flops 7516192768 | bytes 15728640 | tf_op jit(solution)/shard_map/out_grads/pallas_call | solution.py:193
  190.3 5.2 %all-to-all-done.3 = bf16[8,112,1024]{2,1,0:T(8,128)(2,1)} async-done(((bf16[8,112,1024]{2,1,0:T(8,128)(2,1)}), bf16[8,112,1024]{2,1,0:T(8,128)(2,1)}, u32[]{:S(2)}, u32[]{:S(2)}) %all-to-all-start.3) | async-done | bytes 1835040 | tf_op jit(solution)/shard_map/all_to_all | solution.py:509
  195.5 4.3 all-to-all-start.4
  199.9 4.6 %fusion.29 = (bf16[1,384,1024]{2,1,0:T(8,128)(2,1)}, f32[384]{0:T(512)S(1)}) fusion(f32[384,1024]{1,0:T(8,128)} %copy-done.4, f32[384]{0:T(512)S(1)} %select_reduce_fusion.1, bf16[2,1,384,1024]{3,2,1,0:T(8,128)(2,1)} %param.15, bf16[896,384]{1,0:T(8,128)(2,1)} %fusion.25, bf16[896,1024]{1,0:T(8,128)(2,1)} %bitcast.27), kind=kOutput, calls=%fused_computation.82 | convolution fusion | flops 707001984 | bytes 5671936 | tf_op jit(solution)/shard_map/dot_general | solution.py:526
  204.5 3.1 fusion.96
  209.5 1.8 fusion.87
  211.3 1.9 convolution_convert_fusion.5.do_ref
  213.2 18.1 %attn_bwd.2 = (bf16[384,1024]{1,0:T(8,128)(2,1)}, bf16[2,384,1024]{2,1,0:T(8,128)(2,1)}, bf16[2,384,1024]{2,1,0:T(8,128)(2,1)}) custom-call(f32[768,384]{1,0:T(8,128)} %and_select_fusion.1.biast_ref, f32[16,384]{1,0:T(8,128)} %slice_bitcast_fusion.6.lse_ref, bf16[768,3072]{1,0:T(8,128)(2,1)} %copy-done.1, bf16[768,3072]{1,0:T(8,128)(2,1)} %copy-done.1, ...), custom_call_target="tpu_custom_call" | custom-call | flops 12079595520 | bytes 11796480 | tf_op jit(solution)/shard_map/attn_bwd/pallas_call | solution.py:98
  231.3 13.5 %in_grads.1 = bf16[4,4,256,1024]{3,2,1,0:T(8,128)(2,1)} custom-call(bf16[448,1024]{1,0:T(8,128)(2,1)} %bitcast.19.x_ref.refs_0_, bf16[448,1024]{1,0:T(8,128)(2,1)} %bitcast.26.x_ref.refs_1_, bf16[896,4096]{1,0:T(8,128)(2,1)} %get-tuple-element.169.refs_2_), custom_call_target="tpu_custom_call" | custom-call | flops 7516192768 | bytes 15728640 | tf_op jit(solution)/shard_map/in_grads/pallas_call | solution.py:176
  244.7 4.4 fusion.30
  249.2 2.7 fusion.97
  253.4 1.8 fusion.86
  256.1 1.9 convolution_convert_fusion.4.do_ref
  258.0 17.9 %attn_bwd.3 = (bf16[384,1024]{1,0:T(8,128)(2,1)}, bf16[2,384,1024]{2,1,0:T(8,128)(2,1)}, bf16[2,384,1024]{2,1,0:T(8,128)(2,1)}) custom-call(f32[768,384]{1,0:T(8,128)} %and_select_fusion.biast_ref, f32[16,384]{1,0:T(8,128)} %slice_bitcast_fusion.5.lse_ref, bf16[768,3072]{1,0:T(8,128)(2,1)} %copy-done.1, bf16[768,3072]{1,0:T(8,128)(2,1)} %copy-done.1, ...), custom_call_target="tpu_custom_call" | custom-call | flops 12079595520 | bytes 11796480 | tf_op jit(solution)/shard_map/attn_bwd/pallas_call | solution.py:98
  276.5 3.7 convolution_convert_fusion.1
  281.9 13.7 %project_grads.1 = (bf16[768,3072]{1,0:T(8,128)(2,1)}, bf16[512,1536]{1,0:T(8,128)(2,1)}, bf16[512,1536]{1,0:T(8,128)(2,1)}, bf16[512,1536]{1,0:T(8,128)(2,1)}, bf16[512,1536]{1,0:T(8,128)(2,1)}) custom-call(s32[1]{0:T(128)} %bitcast.high_ref, bf16[768,1024]{1,0:T(8,128)(2,1)} %copy-done.18, bf16[384,1024]{1,0:T(8,128)(2,1)} %get-tuple-element.173.refs_0_, ...), custom_call_target="tpu_custom_call" | custom-call | flops 4831838208 | bytes 18874368 | tf_op jit(solution)/shard_map/project_grads/pallas_call | solution.py:236
  295.6 2.9 add.386
  299.1 3.2 collective-permute-done.7
  302.4 2.3 add.391
  304.7 1.9 collective-permute-start.8
  307.1 2.3 add.387
  312.9 11.7 %collective-permute-done.8 = bf16[256,1536]{1,0:T(8,128)(2,1)S(1)} collective-permute-done((bf16[256,1536]{1,0:T(8,128)(2,1)S(1)}, bf16[256,1536]{1,0:T(8,128)(2,1)S(1)}, u32[]{:S(2)}, u32[]{:S(2)}) %collective-permute-start.8) | collective-permute-done | bytes 786464 | tf_op jit(solution)/shard_map/ppermute | solution.py:301
  325.0 4.0 collective-permute-done.6
  335.6 8.0 %multiply_reduce_fusion = (f32[768]{0:T(1024)S(1)}, f32[1024]{0:T(1024)S(1)}, f32[768]{0:T(1024)S(1)}, f32[1024]{0:T(1024)S(1)}, f32[768,1024]{1,0:T(8,128)S(1)}) fusion(bf16[2,1,384,1024]{3,2,1,0:T(8,128)(2,1)S(1)} %copy-done.3, f32[1024]{0:T(1024)S(1)} %copy-done.31, f32[768]{0:T(1024)S(1)} %rsqrt.28, f32[768]{0:T(1024)S(1)} %div.104, ...), kind=kOutput, calls=%fused_computation.4 | convolution fusion | flops 4839698432 | bytes 15753216 | tf_op jit(solution)/shard_map/dot_general | solution.py:595
  343.6 2.9 maximum_add_fusion
  348.0 2.2 collective-permute-done.10
  353.7 2.5 collective-permute-start.15
  357.8 2.4 collective-permute-done.15
  360.8 6.5 %collective-permute-done.14 = bf16[64,1536]{1,0:T(8,128)(2,1)S(1)} collective-permute-done((bf16[64,1536]{1,0:T(8,128)(2,1)S(1)}, bf16[64,1536]{1,0:T(8,128)(2,1)S(1)}, u32[]{:S(2)}, u32[]{:S(2)}) %collective-permute-start.14) | collective-permute-done | bytes 196640 | tf_op jit(solution)/shard_map/ppermute | solution.py:301
  367.9 2.4 collective-permute-start.17
  374.6 4.6 %collective-permute-done.26 = f32[12,1024]{1,0:T(8,128)S(1)} collective-permute-done((f32[12,1024]{1,0:T(8,128)S(1)}, f32[12,1024]{1,0:T(8,128)S(1)}, u32[]{:S(2)}, u32[]{:S(2)}) %collective-permute-start.26) | collective-permute-done | bytes 49184 | tf_op jit(solution)/shard_map/ppermute | solution.py:301
  380.5 4.1 collective-permute-done.17
  384.7 1.8 collective-permute-start.28
  386.5 5.4 %collective-permute-done.28 = f32[12,1024]{1,0:T(8,128)S(1)} collective-permute-done((f32[12,1024]{1,0:T(8,128)S(1)}, f32[12,1024]{1,0:T(8,128)S(1)}, u32[]{:S(2)}, u32[]{:S(2)}) %collective-permute-start.28) | collective-permute-done | bytes 49184 | tf_op jit(solution)/shard_map/ppermute | solution.py:301
  392.0 5.3 %collective-permute-done.29 = f32[12,1024]{1,0:T(8,128)S(1)} collective-permute-done((f32[12,1024]{1,0:T(8,128)S(1)}, f32[12,1024]{1,0:T(8,128)S(1)}, u32[]{:S(2)}, u32[]{:S(2)}) %collective-permute-start.29) | collective-permute-done | bytes 49184 | tf_op jit(solution)/shard_map/ppermute | solution.py:301
  399.0 4.1 collective-permute-done.19
  406.9 3.5 collective-permute-start.24
  410.4 1.7 slice_bitcast_fusion.3
  412.1 2.5 maximum_convert_fusion
  414.6 2.5 convert_element_type.225
  420.5 2.5 collective-permute-start.31
  424.2 2.5 collective-permute-done.32
  426.8 5.1 %collective-permute-done.30 = bf16[256,1536]{1,0:T(8,128)(2,1)S(1)} collective-permute-done((bf16[256,1536]{1,0:T(8,128)(2,1)S(1)}, bf16[256,1536]{1,0:T(8,128)(2,1)S(1)}, u32[]{:S(2)}, u32[]{:S(2)}) %collective-permute-start.30) | collective-permute-done | bytes 786464 | tf_op jit(solution)/shard_map/ppermute | solution.py:301
  435.2 5.0 %widen.2 = (f32[1024,3072]{1,0:T(8,128)}, f32[1024,1024]{1,0:T(8,128)}) custom-call(s32[1]{0:T(128)} %bitcast.high_ref, bf16[512,1536]{1,0:T(8,128)(2,1)} %pad_maximum_fusion.1.refs_0_, bf16[512,1536]{1,0:T(8,128)(2,1)} %pad_maximum_fusion.2.refs_1_, bf16[512,1024]{1,0:T(8,128)(2,1)} %copy-done.12), custom_call_target="tpu_custom_call" | custom-call | flops 2097152 | bytes 12582912 | tf_op jit(solution)/shard_map/widen/pallas_call | solution.py:255
  442.1 5.0 %widen.3 = (f32[1024,3072]{1,0:T(8,128)}, f32[1024,1024]{1,0:T(8,128)}) custom-call(s32[1]{0:T(128)S(6)} %sub.198.high_ref, bf16[512,1536]{1,0:T(8,128)(2,1)} %collective-permute-done.33.refs_0_, bf16[512,1536]{1,0:T(8,128)(2,1)} %collective-permute-done.34.refs_1_, ...), custom_call_target="tpu_custom_call", output_to_operand_aliasing={{0}: (4, {}), {1}: (5, {})} | custom-call | flops 2097152 | bytes 12582912 | tf_op jit(solution)/shard_map/widen/pallas_call | solution.py:255
  (277 shorter events, 75.0 us)
Async XLA Ops:
  7.2 57.6 %copy-start = (bf16[1024,1024]{1,0:T(8,128)(2,1)S(1)}, bf16[1024,1024]{1,0:T(8,128)(2,1)}, u32[]{:S(2)}) copy-start(bf16[1024,1024]{1,0:T(8,128)(2,1)} %param.22) | copy-start | bytes 6291460
  7.2 117.3 %all-gather.2.cloned.1.call-start = ((), (), s32[]{:S(2)}) async-start(), calls=%async_computation.7 | async-start | bytes 20971520 | tf_op jit(solution)/shard_map/all_gather | solution.py:364
  19.8 2.5 copy-start.31
  19.8 2.6 copy-start.34
  24.6 9.6 %copy-start.18 = (bf16[768,1024]{1,0:T(8,128)(2,1)}, bf16[768,1024]{1,0:T(8,128)(2,1)S(1)}, u32[]{:S(2)}) copy-start(bf16[768,1024]{1,0:T(8,128)(2,1)S(1)} %add_convert_fusion.x_ref) | copy-start | bytes 4718596
  34.3 3.2 copy-start.1
  37.5 14.5 %collective-permute-start = (bf16[384,2048]{1,0:T(8,128)(2,1)}, bf16[384,2048]{1,0:T(8,128)(2,1)}, u32[]{:S(2)}, u32[]{:S(2)}) collective-permute-start(bf16[384,2048]{1,0:T(8,128)(2,1)} %get-tuple-element.322), channel_id=1, source_target_pairs={{0,2},{2,0},{1,3},{3,1},{4,6},{6,4},{5,7},{7,5},{8,10},{10,8},{9,1... | collective-permute-start | bytes 4718600 | tf_op jit(solution)/shard_map/ppermute | solution.py:397
  37.9 7.7 %copy-start.36 = (s32[2,1,3]{2,1,0:T(1,128)S(1)}, s32[2,1,3]{2,1,0:T(1,128)}, u32[]{:S(2)}) copy-start(s32[2,1,3]{2,1,0:T(1,128)} %param.16) | copy-start | bytes 76
  37.9 8.1 %copy-start.33 = (s32[2,1,768]{2,1,0:T(1,128)S(1)}, s32[2,1,768]{2,1,0:T(1,128)}, u32[]{:S(2)}) copy-start(s32[2,1,768]{2,1,0:T(1,128)} %param.17) | copy-start | bytes 18436
  37.9 33.1 %collective-permute-start.1 = (bf16[384,2048]{1,0:T(8,128)(2,1)}, bf16[384,2048]{1,0:T(8,128)(2,1)}, u32[]{:S(2)}, u32[]{:S(2)}) collective-permute-start(bf16[384,2048]{1,0:T(8,128)(2,1)} %get-tuple-element.321), channel_id=1, source_target_pairs={{0,2},{2,0},{1,3},{3,1},{4,6},{6,4},{5,7},{7,5},{8,10},{10,8},{9,1... | collective-permute-start | bytes 4718600 | tf_op jit(solution)/shard_map/ppermute | solution.py:397
  38.0 52.9 %all-to-all-start = ((bf16[8,2,56,1024]{3,2,1,0:T(8,128)(2,1)}), bf16[8,2,56,1024]{3,2,1,0:T(8,128)(2,1)}, u32[]{:S(2)}, u32[]{:S(2)}) async-start(bf16[8,2,56,1024]{3,2,1,0:T(8,128)(2,1)} %pad_maximum_fusion), calls=%async_computation | async-start | bytes 3670016 | tf_op jit(solution)/shard_map/all_to_all | solution.py:387
  71.0 12.7 %copy-start.29 = (f32[384,128]{1,0:T(8,128)S(1)}, f32[384,128]{1,0:T(8,128)}, u32[]{:S(2)}) copy-start(f32[384,128]{1,0:T(8,128)} %get-tuple-element.135) | copy-start | bytes 589828
  90.9 28.9 %all-to-all-start.1 = ((bf16[8,56,1024]{2,1,0:T(8,128)(2,1)}), bf16[8,56,1024]{2,1,0:T(8,128)(2,1)}, u32[]{:S(2)}, u32[]{:S(2)}) async-start(bf16[8,56,1024]{2,1,0:T(8,128)(2,1)} %bitcast.143), calls=%async_computation.1 | async-start | bytes 1835008 | tf_op jit(solution)/shard_map/all_to_all | solution.py:486
  119.8 28.1 %all-to-all-start.2 = ((bf16[8,56,1024]{2,1,0:T(8,128)(2,1)}), bf16[8,56,1024]{2,1,0:T(8,128)(2,1)}, u32[]{:S(2)}, u32[]{:S(2)}) async-start(bf16[8,56,1024]{2,1,0:T(8,128)(2,1)} %bitcast.144), calls=%async_computation.2 | async-start | bytes 1835008 | tf_op jit(solution)/shard_map/all_to_all | solution.py:486
  147.9 47.6 %all-to-all-start.3 = ((bf16[8,112,1024]{2,1,0:T(8,128)(2,1)}), bf16[8,112,1024]{2,1,0:T(8,128)(2,1)}, u32[]{:S(2)}, u32[]{:S(2)}) async-start(bf16[8,112,1024]{2,1,0:T(8,128)(2,1)} %get-tuple-element.160), calls=%async_computation.3 | async-start | bytes 3670016 | tf_op jit(solution)/shard_map/all_to_all | solution.py:509
  153.8 144.7 %reduce-scatter.3.cloned.1.call-start = ((), (), s32[]{:S(2)}) async-start(), calls=%async_computation.8 | async-start | bytes 10485760 | tf_op jit(solution)/shard_map/reduce_scatter | solution.py:516
  195.5 49.2 %all-to-all-start.4 = ((bf16[8,112,1024]{2,1,0:T(8,128)(2,1)}), bf16[8,112,1024]{2,1,0:T(8,128)(2,1)}, u32[]{:S(2)}, u32[]{:S(2)}) async-start(bf16[8,112,1024]{2,1,0:T(8,128)(2,1)} %get-tuple-element.179), calls=%async_computation.4 | async-start | bytes 3670016 | tf_op jit(solution)/shard_map/all_to_all | solution.py:509
  199.8 204.0 %reduce-scatter.5.cloned.1.call-start = ((), (), s32[]{:S(2)}) async-start(), calls=%async_computation.9 | async-start | bytes 10485760 | tf_op jit(solution)/shard_map/reduce_scatter | solution.py:577
  199.9 4.6 %copy-start.16 = (bf16[896,384]{1,0:T(8,128)(2,1)S(1)}, bf16[896,384]{1,0:T(8,128)(2,1)}, u32[]{:S(2)}) copy-start(bf16[896,384]{1,0:T(8,128)(2,1)} %fusion.26) | copy-start | bytes 2064388
  204.5 3.1 copy-start.5
  244.7 4.4 copy-start.15
  249.1 2.7 copy-start.7
  275.9 5.8 %collective-permute-start.3 = (bf16[2,384,1024]{2,1,0:T(8,128)(2,1)}, bf16[2,384,1024]{2,1,0:T(8,128)(2,1)}, u32[]{:S(2)}, u32[]{:S(2)}) collective-permute-start(bf16[2,384,1024]{2,1,0:T(8,128)(2,1)} %get-tuple-element.184), channel_id=1, source_target_pairs={{0,2},{2,0},{1,3},{3,1},{4,6},{6,4},{5,7},{7,5},{8,10},{10,8},{9,1... | collective-permute-start | bytes 4718600 | tf_op jit(solution)/shard_map/ppermute | solution.py:543
  276.0 6.0 %collective-permute-start.2 = (bf16[2,384,1024]{2,1,0:T(8,128)(2,1)}, bf16[2,384,1024]{2,1,0:T(8,128)(2,1)}, u32[]{:S(2)}, u32[]{:S(2)}) collective-permute-start(bf16[2,384,1024]{2,1,0:T(8,128)(2,1)} %get-tuple-element.175), channel_id=1, source_target_pairs={{0,2},{2,0},{1,3},{3,1},{4,6},{6,4},{5,7},{7,5},{8,10},{10,8},{9,1... | collective-permute-start | bytes 4718600 | tf_op jit(solution)/shard_map/ppermute | solution.py:543
  281.7 13.9 %collective-permute-start.4 = (bf16[512,1024]{1,0:T(8,128)(2,1)}, bf16[512,1024]{1,0:T(8,128)(2,1)}, u32[]{:S(2)}, u32[]{:S(2)}) collective-permute-start(bf16[512,1024]{1,0:T(8,128)(2,1)} %get-tuple-element.190), channel_id=1, source_target_pairs={{0,2},{2,0},{1,3},{3,1},{4,6},{6,4},{5,7},{7,5},{8,10},{10,8},{9,1... | collective-permute-start | bytes 3145736 | tf_op jit(solution)/shard_map/ppermute | solution.py:301
  298.6 3.8 collective-permute-start.7
  298.9 8.1 %collective-permute-start.5 = (bf16[512,1536]{1,0:T(8,128)(2,1)}, bf16[512,1536]{1,0:T(8,128)(2,1)}, u32[]{:S(2)}, u32[]{:S(2)}) collective-permute-start(bf16[512,1536]{1,0:T(8,128)(2,1)} %get-tuple-element.192), channel_id=1, source_target_pairs={{0,2},{2,0},{1,3},{3,1},{4,6},{6,4},{5,7},{7,5},{8,10},{10,8},{9,1... | collective-permute-start | bytes 4718600 | tf_op jit(solution)/shard_map/ppermute | solution.py:301
  304.7 19.9 %collective-permute-start.8 = (bf16[256,1536]{1,0:T(8,128)(2,1)S(1)}, bf16[256,1536]{1,0:T(8,128)(2,1)S(1)}, u32[]{:S(2)}, u32[]{:S(2)}) collective-permute-start(bf16[256,1536]{1,0:T(8,128)(2,1)S(1)} %constant_dynamic-slice_fusion.7), channel_id=1, source_target_pairs={{0,8},{4,12},{8,0},{12,4},{16,24},{20,28},{24,16},{28,20},{1,9},{5... | collective-permute-start | bytes 2359304 | tf_op jit(solution)/shard_map/ppermute | solution.py:301
  307.0 4.0 copy-start.13
  309.3 3.1 copy-start.9
  309.4 19.6 %collective-permute-start.6 = (bf16[256,1536]{1,0:T(8,128)(2,1)S(1)}, bf16[256,1536]{1,0:T(8,128)(2,1)S(1)}, u32[]{:S(2)}, u32[]{:S(2)}) collective-permute-start(bf16[256,1536]{1,0:T(8,128)(2,1)S(1)} %constant_dynamic-slice_fusion.8), channel_id=1, source_target_pairs={{0,4},{4,0},{8,12},{12,8},{16,20},{20,16},{24,28},{28,24},{1,5},{5... | collective-permute-start | bytes 2359304 | tf_op jit(solution)/shard_map/ppermute | solution.py:301
  311.1 13.7 %collective-permute-start.9 = (bf16[256,1024]{1,0:T(8,128)(2,1)S(1)}, bf16[256,1024]{1,0:T(8,128)(2,1)S(1)}, u32[]{:S(2)}, u32[]{:S(2)}) collective-permute-start(bf16[256,1024]{1,0:T(8,128)(2,1)S(1)} %constant_dynamic-slice_fusion.6), channel_id=1, source_target_pairs={{0,1},{1,0},{2,3},{3,2},{4,5},{5,4},{6,7},{7,6},{8,9},{9,8},{10,11... | collective-permute-start | bytes 1572872 | tf_op jit(solution)/shard_map/ppermute | solution.py:301
  324.6 11.0 %copy-start.37 = (bf16[768,3072]{1,0:T(8,128)(2,1)S(1)}, bf16[768,3072]{1,0:T(8,128)(2,1)}, u32[]{:S(2)}) copy-start(bf16[768,3072]{1,0:T(8,128)(2,1)} %get-tuple-element.200) | copy-start | bytes 14155780
  329.2 4.2 copy-start.14
  329.2 6.3 %copy-start.3 = (bf16[2,1,384,1024]{3,2,1,0:T(8,128)(2,1)S(1)}, bf16[2,1,384,1024]{3,2,1,0:T(8,128)(2,1)}, u32[]{:S(2)}) copy-start(bf16[2,1,384,1024]{3,2,1,0:T(8,128)(2,1)} %param.14) | copy-start | bytes 4718596
  330.0 20.2 %collective-permute-start.10 = (bf16[128,1536]{1,0:T(8,128)(2,1)}, bf16[128,1536]{1,0:T(8,128)(2,1)}, u32[]{:S(2)}, u32[]{:S(2)}) collective-permute-start(bf16[128,1536]{1,0:T(8,128)(2,1)} %constant_dynamic-slice_fusion.5), channel_id=1, source_target_pairs={{0,1},{1,0},{2,3},{3,2},{4,5},{5,4},{6,7},{7,6},{8,9},{9,8},{10,11... | collective-permute-start | bytes 1179656 | tf_op jit(solution)/shard_map/ppermute | solution.py:301
  332.0 19.4 %collective-permute-start.11 = (bf16[128,1536]{1,0:T(8,128)(2,1)}, bf16[128,1536]{1,0:T(8,128)(2,1)}, u32[]{:S(2)}, u32[]{:S(2)}) collective-permute-start(bf16[128,1536]{1,0:T(8,128)(2,1)} %constant_dynamic-slice_fusion.4), channel_id=1, source_target_pairs={{0,4},{4,0},{8,12},{12,8},{16,20},{20,16},{24,28},{28,24},{1,5},{5... | collective-permute-start | bytes 1179656 | tf_op jit(solution)/shard_map/ppermute | solution.py:301
  334.1 9.5 %copy-start.10 = (f32[384,1024]{1,0:T(8,128)S(1)}, f32[384,1024]{1,0:T(8,128)}, u32[]{:S(2)}) copy-start(f32[384,1024]{1,0:T(8,128)} %get-tuple-element.316) | copy-start | bytes 4718596
  334.1 9.5 %copy-start.11 = (f32[384,1024]{1,0:T(8,128)S(1)}, f32[384,1024]{1,0:T(8,128)}, u32[]{:S(2)}) copy-start(f32[384,1024]{1,0:T(8,128)} %get-tuple-element.314) | copy-start | bytes 4718596
  334.1 12.8 %collective-permute-start.12 = (bf16[128,1024]{1,0:T(8,128)(2,1)}, bf16[128,1024]{1,0:T(8,128)(2,1)}, u32[]{:S(2)}, u32[]{:S(2)}) collective-permute-start(bf16[128,1024]{1,0:T(8,128)(2,1)} %constant_dynamic-slice_fusion.3), channel_id=1, source_target_pairs={{0,8},{4,12},{8,0},{12,4},{16,24},{20,28},{24,16},{28,20},{1,9},{5... | collective-permute-start | bytes 786440 | tf_op jit(solution)/shard_map/ppermute | solution.py:301
  352.6 8.1 %collective-permute-start.13 = (bf16[64,1536]{1,0:T(8,128)(2,1)S(1)}, bf16[64,1536]{1,0:T(8,128)(2,1)S(1)}, u32[]{:S(2)}, u32[]{:S(2)}) collective-permute-start(bf16[64,1536]{1,0:T(8,128)(2,1)S(1)} %constant_dynamic-slice_fusion.2), channel_id=1, source_target_pairs={{0,8},{4,12},{8,0},{12,4},{16,24},{20,28},{24,16},{28,20},{1,9},{5... | collective-permute-start | bytes 589832 | tf_op jit(solution)/shard_map/ppermute | solution.py:301
  353.7 6.5 %collective-permute-start.15 = (bf16[64,1024]{1,0:T(8,128)(2,1)S(1)}, bf16[64,1024]{1,0:T(8,128)(2,1)S(1)}, u32[]{:S(2)}, u32[]{:S(2)}) collective-permute-start(bf16[64,1024]{1,0:T(8,128)(2,1)S(1)} %constant_dynamic-slice_fusion), channel_id=1, source_target_pairs={{0,16},{4,20},{8,24},{12,28},{16,0},{20,4},{24,8},{28,12},{1,17},{... | collective-permute-start | bytes 393224 | tf_op jit(solution)/shard_map/ppermute | solution.py:301
  356.2 11.0 %collective-permute-start.14 = (bf16[64,1536]{1,0:T(8,128)(2,1)S(1)}, bf16[64,1536]{1,0:T(8,128)(2,1)S(1)}, u32[]{:S(2)}, u32[]{:S(2)}) collective-permute-start(bf16[64,1536]{1,0:T(8,128)(2,1)S(1)} %constant_dynamic-slice_fusion.1), channel_id=1, source_target_pairs={{0,1},{1,0},{2,3},{3,2},{4,5},{5,4},{6,7},{7,6},{8,9},{9,8},{10,11... | collective-permute-start | bytes 589832 | tf_op jit(solution)/shard_map/ppermute | solution.py:301
  367.3 13.2 %collective-permute-start.16 = (bf16[64,1536]{1,0:T(8,128)(2,1)S(1)}, bf16[64,1536]{1,0:T(8,128)(2,1)S(1)}, u32[]{:S(2)}, u32[]{:S(2)}) collective-permute-start(bf16[64,1536]{1,0:T(8,128)(2,1)S(1)} %dynamic-slice_add_fusion.7), channel_id=1, source_target_pairs={{0,16},{4,20},{8,24},{12,28},{16,0},{20,4},{24,8},{28,12},{1,17},{... | collective-permute-start | bytes 589832 | tf_op jit(solution)/shard_map/ppermute | solution.py:301
  367.9 16.7 %collective-permute-start.17 = (bf16[64,1536]{1,0:T(8,128)(2,1)S(1)}, bf16[64,1536]{1,0:T(8,128)(2,1)S(1)}, u32[]{:S(2)}, u32[]{:S(2)}) collective-permute-start(bf16[64,1536]{1,0:T(8,128)(2,1)S(1)} %dynamic-slice_add_fusion.6), channel_id=1, source_target_pairs={{0,16},{4,20},{8,24},{12,28},{16,0},{20,4},{24,8},{28,12},{1,17},{... | collective-permute-start | bytes 589832 | tf_op jit(solution)/shard_map/ppermute | solution.py:301
  370.3 9.5 %collective-permute-start.18 = (bf16[64,1024]{1,0:T(8,128)(2,1)S(1)}, bf16[64,1024]{1,0:T(8,128)(2,1)S(1)}, u32[]{:S(2)}, u32[]{:S(2)}) collective-permute-start(bf16[64,1024]{1,0:T(8,128)(2,1)S(1)} %dynamic-slice_add_fusion.8), channel_id=1, source_target_pairs={{0,4},{4,0},{8,12},{12,8},{16,20},{20,16},{24,28},{28,24},{1,5},{5... | collective-permute-start | bytes 393224 | tf_op jit(solution)/shard_map/ppermute | solution.py:301
  371.7 1.3 collective-permute-start.25
  373.0 6.1 %collective-permute-start.26 = (f32[12,1024]{1,0:T(8,128)S(1)}, f32[12,1024]{1,0:T(8,128)S(1)}, u32[]{:S(2)}, u32[]{:S(2)}) collective-permute-start(f32[12,1024]{1,0:T(8,128)S(1)} %add.426), channel_id=1, source_target_pairs={{0,1},{1,0},{2,3},{3,2},{4,5},{5,4},{6,7},{7,6},{8,9},{9,8},{10,11... | collective-permute-start | bytes 147464 | tf_op jit(solution)/shard_map/ppermute | solution.py:301
  379.1 5.6 %collective-permute-start.27 = (f32[12,1024]{1,0:T(8,128)S(1)}, f32[12,1024]{1,0:T(8,128)S(1)}, u32[]{:S(2)}, u32[]{:S(2)}) collective-permute-start(f32[12,1024]{1,0:T(8,128)S(1)} %add.427), channel_id=1, source_target_pairs={{0,4},{4,0},{8,12},{12,8},{16,20},{20,16},{24,28},{28,24},{1,5},{5... | collective-permute-start | bytes 147464 | tf_op jit(solution)/shard_map/ppermute | solution.py:301
  384.6 14.3 %collective-permute-start.21 = (bf16[64,1024]{1,0:T(8,128)(2,1)S(1)}, bf16[64,1024]{1,0:T(8,128)(2,1)S(1)}, u32[]{:S(2)}, u32[]{:S(2)}) collective-permute-start(bf16[64,1024]{1,0:T(8,128)(2,1)S(1)} %add.425), channel_id=1, source_target_pairs={{0,16},{4,20},{8,24},{12,28},{16,0},{20,4},{24,8},{28,12},{1,17},{... | collective-permute-start | bytes 393224 | tf_op jit(solution)/shard_map/ppermute | solution.py:301
  384.7 7.1 %collective-permute-start.28 = (f32[12,1024]{1,0:T(8,128)S(1)}, f32[12,1024]{1,0:T(8,128)S(1)}, u32[]{:S(2)}, u32[]{:S(2)}) collective-permute-start(f32[12,1024]{1,0:T(8,128)S(1)} %add.428), channel_id=1, source_target_pairs={{0,8},{4,12},{8,0},{12,4},{16,24},{20,28},{24,16},{28,20},{1,9},{5... | collective-permute-start | bytes 147464 | tf_op jit(solution)/shard_map/ppermute | solution.py:301
  391.9 5.5 %collective-permute-start.29 = (f32[12,1024]{1,0:T(8,128)S(1)}, f32[12,1024]{1,0:T(8,128)S(1)}, u32[]{:S(2)}, u32[]{:S(2)}) collective-permute-start(f32[12,1024]{1,0:T(8,128)S(1)} %add.429), channel_id=1, source_target_pairs={{0,16},{4,20},{8,24},{12,28},{16,0},{20,4},{24,8},{28,12},{1,17},{... | collective-permute-start | bytes 147464 | tf_op jit(solution)/shard_map/ppermute | solution.py:301
  397.3 5.7 %collective-permute-start.19 = (bf16[64,1536]{1,0:T(8,128)(2,1)S(1)}, bf16[64,1536]{1,0:T(8,128)(2,1)S(1)}, u32[]{:S(2)}, u32[]{:S(2)}) collective-permute-start(bf16[64,1536]{1,0:T(8,128)(2,1)S(1)} %add.423), channel_id=1, source_target_pairs={{0,8},{4,12},{8,0},{12,4},{16,24},{20,28},{24,16},{28,20},{1,9},{5... | collective-permute-start | bytes 589832 | tf_op jit(solution)/shard_map/ppermute | solution.py:301
  397.4 6.3 %collective-permute-start.20 = (bf16[64,1536]{1,0:T(8,128)(2,1)S(1)}, bf16[64,1536]{1,0:T(8,128)(2,1)S(1)}, u32[]{:S(2)}, u32[]{:S(2)}) collective-permute-start(bf16[64,1536]{1,0:T(8,128)(2,1)S(1)} %add.424), channel_id=1, source_target_pairs={{0,1},{1,0},{2,3},{3,2},{4,5},{5,4},{6,7},{7,6},{8,9},{9,8},{10,11... | collective-permute-start | bytes 589832 | tf_op jit(solution)/shard_map/ppermute | solution.py:301
  403.8 13.3 %collective-permute-start.22 = (bf16[128,1536]{1,0:T(8,128)(2,1)S(1)}, bf16[128,1536]{1,0:T(8,128)(2,1)S(1)}, u32[]{:S(2)}, u32[]{:S(2)}) collective-permute-start(bf16[128,1536]{1,0:T(8,128)(2,1)S(1)} %pad_maximum_fusion.7), channel_id=1, source_target_pairs={{0,1},{1,0},{2,3},{3,2},{4,5},{5,4},{6,7},{7,6},{8,9},{9,8},{10,11... | collective-permute-start | bytes 1179656 | tf_op jit(solution)/shard_map/ppermute | solution.py:301
  405.4 11.9 %collective-permute-start.23 = (bf16[128,1536]{1,0:T(8,128)(2,1)S(1)}, bf16[128,1536]{1,0:T(8,128)(2,1)S(1)}, u32[]{:S(2)}, u32[]{:S(2)}) collective-permute-start(bf16[128,1536]{1,0:T(8,128)(2,1)S(1)} %pad_maximum_fusion.8), channel_id=1, source_target_pairs={{0,4},{4,0},{8,12},{12,8},{16,20},{20,16},{24,28},{28,24},{1,5},{5... | collective-permute-start | bytes 1179656 | tf_op jit(solution)/shard_map/ppermute | solution.py:301
  406.9 10.2 %collective-permute-start.24 = (bf16[128,1024]{1,0:T(8,128)(2,1)S(1)}, bf16[128,1024]{1,0:T(8,128)(2,1)S(1)}, u32[]{:S(2)}, u32[]{:S(2)}) collective-permute-start(bf16[128,1024]{1,0:T(8,128)(2,1)S(1)} %pad_maximum_fusion.9), channel_id=1, source_target_pairs={{0,8},{4,12},{8,0},{12,4},{16,24},{20,28},{24,16},{28,20},{1,9},{5... | collective-permute-start | bytes 786440 | tf_op jit(solution)/shard_map/ppermute | solution.py:301
  417.4 9.2 %collective-permute-start.32 = (bf16[256,1024]{1,0:T(8,128)(2,1)S(1)}, bf16[256,1024]{1,0:T(8,128)(2,1)S(1)}, u32[]{:S(2)}, u32[]{:S(2)}) collective-permute-start(bf16[256,1024]{1,0:T(8,128)(2,1)S(1)} %pad_maximum_fusion.6), channel_id=1, source_target_pairs={{0,1},{1,0},{2,3},{3,2},{4,5},{5,4},{6,7},{7,6},{8,9},{9,8},{10,11... | collective-permute-start | bytes 1572872 | tf_op jit(solution)/shard_map/ppermute | solution.py:301
  419.9 12.0 %collective-permute-start.30 = (bf16[256,1536]{1,0:T(8,128)(2,1)S(1)}, bf16[256,1536]{1,0:T(8,128)(2,1)S(1)}, u32[]{:S(2)}, u32[]{:S(2)}) collective-permute-start(bf16[256,1536]{1,0:T(8,128)(2,1)S(1)} %pad_maximum_fusion.4), channel_id=1, source_target_pairs={{0,4},{4,0},{8,12},{12,8},{16,20},{20,16},{24,28},{28,24},{1,5},{5... | collective-permute-start | bytes 2359304 | tf_op jit(solution)/shard_map/ppermute | solution.py:301
  420.5 12.8 %collective-permute-start.31 = (bf16[256,1536]{1,0:T(8,128)(2,1)S(1)}, bf16[256,1536]{1,0:T(8,128)(2,1)S(1)}, u32[]{:S(2)}, u32[]{:S(2)}) collective-permute-start(bf16[256,1536]{1,0:T(8,128)(2,1)S(1)} %pad_maximum_fusion.5), channel_id=1, source_target_pairs={{0,8},{4,12},{8,0},{12,4},{16,24},{20,28},{24,16},{28,20},{1,9},{5... | collective-permute-start | bytes 2359304 | tf_op jit(solution)/shard_map/ppermute | solution.py:301
  426.8 8.3 %copy-start.12 = (bf16[512,1024]{1,0:T(8,128)(2,1)}, bf16[512,1024]{1,0:T(8,128)(2,1)S(1)}, u32[]{:S(2)}) copy-start(bf16[512,1024]{1,0:T(8,128)(2,1)S(1)} %pad_maximum_fusion.3.refs_2_) | copy-start | bytes 3145732
  434.6 6.5 %collective-permute-start.33 = (bf16[512,1536]{1,0:T(8,128)(2,1)}, bf16[512,1536]{1,0:T(8,128)(2,1)}, u32[]{:S(2)}, u32[]{:S(2)}) collective-permute-start(bf16[512,1536]{1,0:T(8,128)(2,1)} %pad_maximum_fusion.1.refs_0_), channel_id=1, source_target_pairs={{0,2},{2,0},{1,3},{3,1},{4,6},{6,4},{5,7},{7,5},{8,10},{10,8},{9,1... | collective-permute-start | bytes 4718600 | tf_op jit(solution)/shard_map/ppermute | solution.py:301
  434.6 7.5 %collective-permute-start.34 = (bf16[512,1536]{1,0:T(8,128)(2,1)}, bf16[512,1536]{1,0:T(8,128)(2,1)}, u32[]{:S(2)}, u32[]{:S(2)}) collective-permute-start(bf16[512,1536]{1,0:T(8,128)(2,1)} %pad_maximum_fusion.2.refs_1_), channel_id=1, source_target_pairs={{0,2},{2,0},{1,3},{3,1},{4,6},{6,4},{5,7},{7,5},{8,10},{10,8},{9,1... | collective-permute-start | bytes 4718600 | tf_op jit(solution)/shard_map/ppermute | solution.py:301
  435.1 6.0 %collective-permute-start.35 = (bf16[512,1024]{1,0:T(8,128)(2,1)S(1)}, bf16[512,1024]{1,0:T(8,128)(2,1)}, u32[]{:S(2)}, u32[]{:S(2)}) collective-permute-start(bf16[512,1024]{1,0:T(8,128)(2,1)S(1)} %pad_maximum_fusion.3.refs_2_), channel_id=1, source_target_pairs={{0,2},{2,0},{1,3},{3,1},{4,6},{6,4},{5,7},{7,5},{8,10},{10,8},{9,1... | collective-permute-start | bytes 3145736 | tf_op jit(solution)/shard_map/ppermute | solution.py:301
  (18 other events, 25.0 us)
Sparse Core Ops, SparseCore 0:
  12.2 108.6 all-gather.1
  195.6 70.7 reduce-scatter.2
  298.7 86.9 reduce-scatter.4
